TPU v7x, 256 devices: a whole 4x4x8 slice. The times are simulated.
256 devices in a mesh: mem: 4 (over z_lo), hor: 16 (over y, x), grp: 4 (over z_hi, core).
Axes of the slice: x: 4, y: 4, z: 8 (z_hi: 2, z_lo: 4; z = z_hi * 4 + z_lo), core: 2. Of those that a mesh axis runs over, the one named last changes fastest.
Arguments:
- ensemble: float32 [128, 2, 32, 8192], P(('mem', 'grp'), None, None, 'hor'), may hold values from -1 to 1
- coupling: float32 [32, 32], replicated, may hold values from -1 to 1
- obs_column: int32 [2, 16, 16, 512], P(None, ('mem', 'grp'), 'hor'), may hold values from 0 to 511
- obs_level: int32 [2, 16, 16, 512], P(None, ('mem', 'grp'), 'hor'), may hold values from 0 to 1
- obs_value: float32 [2, 16, 16, 512], P(None, ('mem', 'grp'), 'hor'), may hold values from -6 to 6
- obs_error: float32 [2, 16, 16, 512], P(None, ('mem', 'grp'), 'hor'), may hold values from 0.25 to 4
- obs_live: int32 [2, 16, 16, 512], P(None, ('mem', 'grp'), 'hor'), may hold values 0 or 1
- partners: int32 [16, 16, 2], P(('mem', 'grp'), 'hor'), may hold values from 0 to 15, as said below
Outputs:
- analysed: float32 [128, 2, 32, 8192], P(('mem', 'grp'), None, None, 'hor')
Inputs may be any that keep to these rules, and one draw needn't show every extreme that they name: `partners`: each row holds 2 different slab numbers, none of them the row's own slab.
All inputs are finite; a program needn't handle non-finite values. No bound on the sum of `obs_live` on one device may be relied on, other than what follows from the above.
Results may differ from a plain program's by a relative error of at most 0.0003.
Values sent between devices are 32-bit elements; how exact they have to be, the bound alone decides.
No kernel may reach another device: no remote copies, remote signals or barrier semaphores. Data moves between devices by JAX's collectives and lax.ppermute only.
A program may use at most 64 MiB of HBM per device.

v0:
```python
import functools
import math

import jax
import jax.numpy as jnp
from jax import lax
from jax.experimental import pallas as pl
from jax.experimental.pallas import tpu as pltpu
from jax.sharding import Mesh, PartitionSpec as P

SUBSTEPS = 4
ROOT_STEPS = 8
TIME_STEP = 0.2
GROUP = 16
WIDTH = 128
LEVELS = 32
COLS = 512
MINE = COLS // GROUP
HALO = 2 * SUBSTEPS
WIDE = MINE + 2 * HALO
FOLD = 72
F32 = jnp.float32
BF16 = jnp.bfloat16
VMEM_LIMIT = 48 * 1024 * 1024
ALL = ("mem", "hor", "zh", "core")
TILE = ("mem", "zh", "core")
CHIPS = ("mem", "zh")


def block_of(g):
    return ((g >> 1) & 1) * 8 + (g >> 2) * 2 + (g & 1)


MEMBER_AT = {block_of(g): g for g in range(GROUP)}


def split(a):
    high = a.astype(BF16)
    return high, (a - high.astype(F32)).astype(BF16)


def dot_split(a, b, dims=((1,), (0,))):
    dims = (dims, ((), ()))
    dot = functools.partial(lax.dot_general, dimension_numbers=dims, preferred_element_type=F32)
    return dot(a[0], b[0]) + (dot(a[0], b[1]) + dot(a[1], b[0]))


def iota(shape, dim):
    return lax.broadcasted_iota(jnp.int32, shape, dim)


def chunk_transpose(rows):
    lane = iota(rows[0].shape, 1)
    out = []
    for p in range(4):
        total = None
        for q in range(4):
            piece = rows[q] if p == q else pltpu.roll(rows[q], (32 * (q - p)) % 128, 1)
            total = piece if total is None else jnp.where(lane >= 32 * q, piece, total)
        out.append(total)
    return out


def pack_kernel(ens, column, level, value, error, live, partner, out, tiles):
    for t in range(4):
        tiles[pl.ds(512 * t, 512), :] = ens[:, pl.ds(128 * t, 128)]
    for m in range(8):
        for t in range(4):
            rows = []
            for f in range(2):
                for j in range(2):
                    rows.append(tiles[pl.ds(512 * t + (m * 2 + f) * LEVELS + j, 16, stride=2), :])
            for p, block in enumerate(chunk_transpose(rows)):
                g = MEMBER_AT[4 * t + p]
                out[pl.ds(g * 136 + m, 16, stride=8), :] = block
    member = iota((GROUP, COLS), 0)
    place = ((member >> 1) & 1) * 8 + (member >> 2) * 2 + (member & 1)
    spot = iota((64, COLS), 0)
    zero = jnp.zeros((64, COLS), F32)
    for cycle in range(2):
        col = column[cycle : cycle + 1, :]
        weight = live[cycle : cycle + 1, :].astype(F32) / error[cycle : cycle + 1, :]
        weighted = weight * value[cycle : cycle + 1, :]
        here = (col >> 5) == place
        left = jnp.concatenate([jnp.where(here, weight, 0.0), jnp.where(here, weighted, 0.0)], axis=1)
        hit = jnp.where(level[cycle : cycle + 1, :] * 32 + (col & 31) == spot, 1.0, 0.0)
        right = jnp.concatenate(
            [jnp.concatenate([hit, zero], axis=1), jnp.concatenate([zero, hit], axis=1)], axis=0
        )
        sums = lax.dot_general(
            left, right, (((1,), (1,)), ((), ())), precision=lax.Precision.HIGHEST, preferred_element_type=F32
        )
        out[pl.ds(128 + cycle, GROUP, stride=136), :] = sums
    lane = iota((GROUP, 128), 1)
    first = partner[0].astype(F32)
    second = partner[1].astype(F32)
    out[pl.ds(130, GROUP, stride=136), :] = jnp.where(lane == 0, first, second)


def unpack_kernel(got, state, low, high, hist, table):
    for s in range(GROUP):
        square = jnp.concatenate([got[pl.ds(g * 136 + s * 8, 8), :] for g in range(GROUP)], axis=0).T
        for f in range(2):
            for j in range(2):
                at = (f * 2 + j) * 32
                state[pl.ds(f * MINE * LEVELS + 2 * s + j, MINE, stride=LEVELS), :] = square[at : at + 32, :]
    for f in range(2):
        edge = HALO * LEVELS
        low[pl.ds(f * edge, edge), :] = state[pl.ds(f * MINE * LEVELS, edge), :]
        high[pl.ds(f * edge, edge), :] = state[pl.ds((f + 1) * MINE * LEVELS - edge, edge), :]
    for cycle in range(2):
        rows = got[pl.ds(128 + cycle, GROUP, stride=136), :]
        hist[pl.ds(cycle * 128, 128), :] = jnp.concatenate([rows, jnp.zeros((128 - GROUP, 128), F32)], axis=0).T
    table[...] = got[pl.ds(130, GROUP, stride=136), :].astype(jnp.int32)


def fold(top, bottom, vector):
    row, lane = iota((64, 128), 0), iota((64, 128), 1)
    body = jnp.where((lane >= 64) | (row <= lane), top, pltpu.roll(bottom, 64, 1))
    diagonal = jnp.sum(jnp.where(lane == row + 64, bottom, 0.0), axis=0, keepdims=True)
    tail = jnp.where(iota((8, 128), 0) == 0, diagonal, vector)
    return body, tail


def unfold(body, tail):
    row, lane = iota((64, 128), 0), iota((64, 128), 1)
    top = jnp.where((lane >= 64) | (row < lane), body, jnp.where(row == lane, 0.5 * body, 0.0))
    moved = pltpu.roll(body, 64, 1)
    bottom = jnp.where(row > lane - 64, moved, jnp.where(row == lane - 64, 0.5 * tail[0:1, :], 0.0))
    bottom = jnp.where(lane >= 64, bottom, 0.0)
    half = jnp.concatenate([top, bottom], axis=0)
    return half + half.T, tail[1:2, :]


def forecast_kernel(cycle, table, core, state, low, high, hist, mixing, out, keep, send, us, hs, ps, fs):
    edge = HALO * LEVELS
    span = MINE * LEVELS
    for f, ref in enumerate((us, hs)):
        ref[pl.ds(0, edge), :] = low[pl.ds(f * edge, edge), :]
        ref[pl.ds(edge, span), :] = state[pl.ds(f * span, span), :]
        ref[pl.ds(edge + span, edge), :] = high[pl.ds(f * edge, edge), :]
    rate = 0.5 * TIME_STEP
    mix = (mixing[pl.ds(0, 256), :].astype(BF16), mixing[pl.ds(256, 256), :].astype(BF16))

    def col(ref, c):
        return ref[pl.ds(c * LEVELS, LEVELS), :]

    for step in range(SUBSTEPS):
        lo, hi = 2 * step, WIDE - 2 * step
        for pair in range(3):
            block = jnp.concatenate(
                [hs[pl.ds(pair * 512, 256), :], hs[pl.ds(pair * 512 + 256, 256), :]], axis=1
            )
            pressure = dot_split(mix, split(block))
            ps[pl.ds(pair * 512, 256), :] = pressure[:, :128]
            ps[pl.ds(pair * 512 + 256, 256), :] = pressure[:, 128:]
        before, here = col(us, lo), col(us, lo + 1)
        flux_two, flux_one, height_one = None, None, None
        for c in range(lo + 1, hi - 1):
            after = col(us, c + 1)
            moved = here - rate * (here * (after - before) + (col(ps, c + 1) - col(ps, c - 1)))
            height = col(hs, c)
            flux = moved * height
            if c >= lo + 3:
                hs[pl.ds((c - 1) * LEVELS, LEVELS), :] = height_one - rate * (flux - flux_two)
            us[pl.ds(c * LEVELS, LEVELS), :] = moved
            before, here = here, after
            flux_two, flux_one, height_one = flux_one, flux, height
    out[pl.ds(0, span), :] = us[pl.ds(edge, span), :]
    out[pl.ds(span, span), :] = hs[pl.ds(edge, span), :]

    for q in range(GROUP):
        field = jnp.concatenate(
            [hs[pl.ds(edge + 2 * q + j, MINE, stride=LEVELS), :] for j in range(2)], axis=0
        )
        mean = jnp.mean(field, axis=1, keepdims=True)
        anomaly = field - mean
        weight = hist[pl.ds(cycle * 128, 64), q : q + 1]
        pull = hist[pl.ds(cycle * 128 + 64, 64), q : q + 1] - weight * mean
        vector = jnp.sum(anomaly * pull, axis=0, keepdims=True)
        flipped = split(anomaly.T)
        gram = dot_split(flipped, split(anomaly * weight))
        body, tail = fold(gram[:64], gram[64:], vector)
        fs[q, pl.ds(0, 64), :] = body
        fs[q, pl.ds(64, 8), :] = tail
    mine = core[0]
    for j in range(GROUP // 2):
        for which, ref in ((mine, keep), (1 - mine, send)):
            s = 2 * j + which
            ref[j] = fs[s] + fs[table[s, 0]] + fs[table[s, 1]]


def root_kernel(got, out):
    total = got[0]
    for j in range(1, 8):
        total = total + got[j]
    gram, vector = unfold(total[:64], total[64:])
    eye = jnp.where(iota((WIDTH, WIDTH), 0) == iota((WIDTH, WIDTH), 1), 1.0, 0.0)
    third = 1.0 / 3.0
    blended = (WIDTH - 1.0) * eye + gram * third
    pull = vector * third
    squared = jnp.sum(jnp.sum(blended * blended, axis=0, keepdims=True), axis=1, keepdims=True)
    norm = jnp.sqrt(squared)
    a = blended / norm
    newton = 1.5 * eye - 0.5 * a
    s = split(newton)
    a = dot_split(split(a), s)
    z = newton
    for step in range(1, ROOT_STEPS):
        newton = 1.5 * eye - 0.5 * dot_split(split(z), split(a))
        s = split(newton)
        if step < ROOT_STEPS - 1:
            a = dot_split(split(a), s)
        z = dot_split(s, split(z))
    halves = split(z)
    wide = jnp.broadcast_to(pull, (8, WIDTH))
    inner = dot_split(split(wide), halves, ((1,), (1,)))
    shift = dot_split(split(inner), halves, ((1,), (1,)))[0:1, :] / norm
    spread = z * (math.sqrt(WIDTH - 1.0) / jnp.sqrt(norm))
    body, tail = fold(spread[:64], spread[64:], shift)
    for j in range(8):
        out[j, pl.ds(0, 64), :] = body
        out[j, pl.ds(64, 8), :] = tail


def apply_kernel(last, core, state, same, other, *outs):
    mine = core[0]
    both = outs[-1]
    for j in range(GROUP // 2):
        both[2 * j + mine] = same[j]
        both[2 * j + 1 - mine] = other[j]
    span = MINE * LEVELS
    for s in range(GROUP):
        spread, shift = unfold(both[s, pl.ds(0, 64), :], both[s, pl.ds(64, 8), :])
        field = jnp.concatenate(
            [
                state[pl.ds(f * span + 2 * s + j, MINE, stride=LEVELS), :]
                for f in range(2)
                for j in range(2)
            ],
            axis=0,
        )
        mean = jnp.mean(field, axis=1, keepdims=True)
        anomaly = field - mean
        centre = mean + jnp.sum(anomaly * shift, axis=1, keepdims=True)
        result = centre + dot_split(split(anomaly), split(spread))
        if last:
            result = result.T
            for g in range(GROUP):
                outs[0][pl.ds((g * GROUP + s) * 8, 8), :] = result[g * 8 : g * 8 + 8, :]
        else:
            for f in range(2):
                for j in range(2):
                    at = (f * 2 + j) * 32
                    outs[0][pl.ds(f * span + 2 * s + j, MINE, stride=LEVELS), :] = result[at : at + 32, :]
    if not last:
        edge = HALO * LEVELS
        for f in range(2):
            outs[1][pl.ds(f * edge, edge), :] = outs[0][pl.ds(f * span, edge), :]
            outs[2][pl.ds(f * edge, edge), :] = outs[0][pl.ds((f + 1) * span - edge, edge), :]


def place_kernel(got, out, tiles):
    for n in range(8):
        for t in range(4):
            rows = [got[pl.ds(MEMBER_AT[4 * t + p] * 128 + n, 16, stride=8), :] for p in range(4)]
            for fj, block in enumerate(chunk_transpose(rows)):
                f, j = fj // 2, fj % 2
                tiles[pl.ds(512 * t + (n * 2 + f) * LEVELS + j, 16, stride=2), :] = block
    for t in range(4):
        out[:, pl.ds(128 * t, 128)] = tiles[pl.ds(512 * t, 512), :]


def vmem():
    return pl.BlockSpec(memory_space=pltpu.VMEM)


def smem():
    return pl.BlockSpec(memory_space=pltpu.SMEM)


def call(kernel, out, ins, name, scratch=()):
    return pl.pallas_call(
        kernel,
        out_shape=out,
        in_specs=ins,
        out_specs=jax.tree.map(lambda _: vmem(), out),
        scratch_shapes=scratch,
        compiler_params=pltpu.CompilerParams(vmem_limit_bytes=VMEM_LIMIT),
        name=name,
    )


def arr(*shape, dtype=F32):
    return jax.ShapeDtypeStruct(shape, dtype)


def across(x, forward):
    pairs = []
    for hor in range(16):
        for block in range(GROUP):
            here = MEMBER_AT[block]
            nxt = MEMBER_AT[(block + 1) % GROUP]
            nhor = (hor + (block + 1) // GROUP) % 16

            def flat(g, h):
                return ((g >> 2) * 16 + h) * 4 + (g & 3)

            pair = (flat(here, hor), flat(nxt, nhor))
            pairs.append(pair if forward else pair[::-1])
    return lax.ppermute(x, ALL, pairs)


def swap(x):
    return lax.ppermute(x, "core", [(0, 1), (1, 0)])


def exchange(x, axes):
    return lax.all_to_all(x, axes, split_axis=0, concat_axis=0, tiled=True)


def shards(ensemble, coupling, obs_column, obs_level, obs_value, obs_error, obs_live, partners):
    rows = MINE * LEVELS
    edges = 2 * HALO * LEVELS
    core = lax.axis_index("core").astype(jnp.int32).reshape(1)
    blocks = jnp.kron(jnp.eye(8, dtype=F32), coupling)
    blocks_high = lax.reduce_precision(blocks, 8, 7)
    mixing = jnp.concatenate([blocks_high, blocks - blocks_high], axis=0)
    packed = call(
        pack_kernel,
        arr(GROUP * 136, 128),
        [vmem()] * 6 + [smem()],
        "pack",
        [pltpu.VMEM((2048, 128), F32)],
    )(
        ensemble.reshape(512, 512),
        obs_column.reshape(2, COLS),
        obs_level.reshape(2, COLS),
        obs_value.reshape(2, COLS),
        obs_error.reshape(2, COLS),
        obs_live.reshape(2, COLS),
        partners.reshape(2),
    )
    got = exchange(packed.reshape(GROUP, 136, 128), TILE).reshape(GROUP * 136, 128)
    state, low, high, hist, table = call(
        unpack_kernel,
        (
            arr(2 * rows, WIDTH),
            arr(edges, WIDTH),
            arr(edges, WIDTH),
            arr(256, 128),
            arr(GROUP, 128, dtype=jnp.int32),
        ),
        [vmem()],
        "unpack",
    )(got)
    for cycle in range(2):
        from_low = across(high, True)
        from_high = across(low, False)
        state, keep, send = call(
            functools.partial(forecast_kernel, cycle),
            (arr(2 * rows, WIDTH), arr(8, FOLD, 128), arr(8, FOLD, 128)),
            [smem(), smem()] + [vmem()] * 5,
            "forecast",
            [
                pltpu.VMEM((WIDE * LEVELS, WIDTH), F32),
                pltpu.VMEM((WIDE * LEVELS, WIDTH), F32),
                pltpu.VMEM((WIDE * LEVELS, WIDTH), F32),
                pltpu.VMEM((GROUP, FOLD, 128), F32),
            ],
        )(table, core, state, from_low, from_high, hist, mixing)
        parts = exchange(keep + swap(send), CHIPS)
        copies = call(root_kernel, arr(8, FOLD, 128), [vmem()], "root")(parts)
        same = exchange(copies, CHIPS)
        other = swap(same)
        last = cycle == 1
        scratch = [pltpu.VMEM((GROUP, FOLD, 128), F32)]
        if last:
            outs = (arr(GROUP * 128, 128),)
        else:
            outs = (arr(2 * rows, WIDTH), arr(edges, WIDTH), arr(edges, WIDTH))
        result = call(
            functools.partial(apply_kernel, last), outs, [smem()] + [vmem()] * 3, "apply", scratch
        )(core, state, same, other)
        if not last:
            state, low, high = result
    got = exchange(result[0].reshape(GROUP, 128, 128), TILE).reshape(GROUP * 128, 128)
    placed = call(place_kernel, arr(512, 512), [vmem()], "place", [pltpu.VMEM((2048, 128), F32)])(got)
    return placed.reshape(ensemble.shape)


def solution(mesh):
    fine = Mesh(mesh.devices.reshape(4, 16, 2, 2), ALL)
    group = TILE
    in_specs = (
        P(group, None, None, "hor"),
        P(),
        P(None, group, "hor", None),
        P(None, group, "hor", None),
        P(None, group, "hor", None),
        P(None, group, "hor", None),
        P(None, group, "hor", None),
        P(group, "hor", None),
    )
    out_specs = P(group, None, None, "hor")
    return jax.shard_map(shards, mesh=fine, in_specs=in_specs, out_specs=out_specs, check_vma=False)
```

profile of v0, /device:TPU:1, one launch (start us, length us, event | category | flops | bytes accessed | tf_op | source)
XLA Modules:
  0.0 188.6 jit_solution(5678344975463551685)
XLA Ops:
  0.7 0.7 copy_bitcast_fusion
  1.4 0.7 copy_bitcast_fusion.1
  2.1 1.2 copy-done
  4.0 2.5 %pack.1 = f32[2176,128]{1,0:T(8,128)} custom-call(f32[512,512]{1,0:T(8,128)S(1)} %bitcast.24, s32[2,512]{1,0:T(2,128)S(1)} %bitcast.25, s32[2,512]{1,0:T(2,128)S(1)} %get-tuple-element.36.level, f32[2,512]{1,0:T(2,128)S(1)} %get-tuple-element.38.value, f32[2,512]{1,0:T(2,128)S(1)} %get-tuple-element.37.error, s32[2,512]{1,0:T(2,128)S(1)} %get-tuple-element.35.live, ...), custom_call_target="tpu_custom_call" | custom-call | tf_op jit(solution)/shard_map/pack/pallas_call | solution.py:329
  6.5 10.1 %all-to-all-start = ((f32[16,136,128]{2,1,0:T(8,128)}), f32[16,136,128]{2,1,0:T(8,128)S(1)}, u32[]{:S(2)}, u32[]{:S(2)}) async-start(f32[16,136,128]{2,1,0:T(8,128)} %bitcast.3), calls=%async_computation | async-start | bytes 2228224 | tf_op jit(solution)/shard_map/all_to_all | solution.py:319
  17.1 28.4 %all-to-all-done = f32[16,136,128]{2,1,0:T(8,128)S(1)} async-done(((f32[16,136,128]{2,1,0:T(8,128)}), f32[16,136,128]{2,1,0:T(8,128)S(1)}, u32[]{:S(2)}, u32[]{:S(2)}) %all-to-all-start) | async-done | bytes 1114144 | tf_op jit(solution)/shard_map/all_to_all | solution.py:319
  45.5 0.8 unpack.1
  46.9 2.7 %collective-permute-done.low = f32[512,128]{1,0:T(8,128)S(1)} collective-permute-done((f32[512,128]{1,0:T(8,128)S(1)}, f32[512,128]{1,0:T(8,128)S(1)}, u32[]{:S(2)}, u32[]{:S(2)}) %collective-permute-start) | collective-permute-done | bytes 262176 | tf_op jit(solution)/shard_map/ppermute | solution.py:311
  49.7 2.6 %collective-permute-done.1.high = f32[512,128]{1,0:T(8,128)S(1)} collective-permute-done((f32[512,128]{1,0:T(8,128)S(1)}, f32[512,128]{1,0:T(8,128)S(1)}, u32[]{:S(2)}, u32[]{:S(2)}) %collective-permute-start.1) | collective-permute-done | bytes 262176 | tf_op jit(solution)/shard_map/ppermute | solution.py:311
  52.2 4.1 %forecast.2 = (f32[2048,128]{1,0:T(8,128)S(1)}, f32[8,72,128]{2,1,0:T(8,128)S(1)}, f32[8,72,128]{2,1,0:T(8,128)S(1)}) custom-call(s32[16,128]{1,0:T(8,128)S(1)} %get-tuple-element.19.table, s32[1]{0:T(128)} %bitcast.core, f32[2048,128]{1,0:T(8,128)S(1)} %get-tuple-element.20.state, f32[512,128]{1,0:T(8,128)S(1)} %collective-permute-done.low, ...), custom_call_target="tpu_custom_call" | custom-call | tf_op jit(solution)/shard_map/forecast/pallas_call | solution.py:360
  56.4 5.6 %collective-permute-start.2 = (f32[8,72,128]{2,1,0:T(8,128)S(1)}, f32[8,72,128]{2,1,0:T(8,128)S(1)}, u32[]{:S(2)}, u32[]{:S(2)}) collective-permute-start(f32[8,72,128]{2,1,0:T(8,128)S(1)} %get-tuple-element.26), channel_id=1, source_target_pairs={{0,1},{1,0},{2,3},{3,2},{4,5},{5,4},{6,7},{7,6},{8,9},{9,8},{10,11... | collective-permute-start | bytes 884744 | tf_op jit(solution)/shard_map/ppermute | solution.py:315
  62.0 1.2 collective-permute-done.2
  63.2 12.9 %all_to_all.30.got = f32[8,72,128]{2,1,0:T(8,128)S(1)} all-to-all(f32[8,72,128]{2,1,0:T(8,128)S(1)} %add.6), channel_id=1, replica_groups=mesh['mem'=4,'hor'=16,'zh'=2,'core'=2] {'mem','zh'}, dimensions={0} | all-to-all | bytes 589824 | tf_op jit(solution)/shard_map/all_to_all | solution.py:319
  76.2 3.2 %root.2 = f32[8,72,128]{2,1,0:T(8,128)S(1)} custom-call(f32[8,72,128]{2,1,0:T(8,128)S(1)} %all_to_all.30.got), custom_call_target="tpu_custom_call" | custom-call | tf_op jit(solution)/shard_map/root/pallas_call | solution.py:373
  79.4 13.2 %all_to_all.31.same = f32[8,72,128]{2,1,0:T(8,128)S(1)} all-to-all(f32[8,72,128]{2,1,0:T(8,128)S(1)} %root.2), channel_id=1, replica_groups=mesh['mem'=4,'hor'=16,'zh'=2,'core'=2] {'mem','zh'}, dimensions={0} | all-to-all | bytes 589824 | tf_op jit(solution)/shard_map/all_to_all | solution.py:319
  92.6 3.0 %collective-permute-start.3 = (f32[8,72,128]{2,1,0:T(8,128)S(1)}, f32[8,72,128]{2,1,0:T(8,128)S(1)}, u32[]{:S(2)}, u32[]{:S(2)}) collective-permute-start(f32[8,72,128]{2,1,0:T(8,128)S(1)} %all_to_all.31.same), channel_id=1, source_target_pairs={{0,1},{1,0},{2,3},{3,2},{4,5},{5,4},{6,7},{7,6},{8,9},{9,8},{10,11... | collective-permute-start | bytes 884744 | tf_op jit(solution)/shard_map/ppermute | solution.py:315
  95.5 1.2 collective-permute-done.3.other
  96.7 3.8 %apply.2 = (f32[2048,128]{1,0:T(8,128)S(1)}, f32[512,128]{1,0:T(8,128)S(1)}, f32[512,128]{1,0:T(8,128)S(1)}) custom-call(s32[1]{0:T(128)} %bitcast.core, f32[2048,128]{1,0:T(8,128)S(1)} %get-tuple-element.24.state, f32[8,72,128]{2,1,0:T(8,128)S(1)} %all_to_all.31.same, f32[8,72,128]{2,1,0:T(8,128)S(1)} %collective-permute-done.3.other), custom_call_target="tpu_custom_call" | custom-call | tf_op jit(solution)/shard_map/apply/pallas_call | solution.py:382
  100.5 1.4 collective-permute-start.4
  102.0 3.3 %collective-permute-done.4.low = f32[512,128]{1,0:T(8,128)S(1)} collective-permute-done((f32[512,128]{1,0:T(8,128)S(1)}, f32[512,128]{1,0:T(8,128)S(1)}, u32[]{:S(2)}, u32[]{:S(2)}) %collective-permute-start.4) | collective-permute-done | bytes 262176 | tf_op jit(solution)/shard_map/ppermute | solution.py:311
  105.3 2.5 %collective-permute-done.5.high = f32[512,128]{1,0:T(8,128)S(1)} collective-permute-done((f32[512,128]{1,0:T(8,128)S(1)}, f32[512,128]{1,0:T(8,128)S(1)}, u32[]{:S(2)}, u32[]{:S(2)}) %collective-permute-start.5) | collective-permute-done | bytes 262176 | tf_op jit(solution)/shard_map/ppermute | solution.py:311
  107.8 4.1 %forecast.3 = (f32[2048,128]{1,0:T(8,128)S(1)}, f32[8,72,128]{2,1,0:T(8,128)S(1)}, f32[8,72,128]{2,1,0:T(8,128)S(1)}) custom-call(s32[16,128]{1,0:T(8,128)S(1)} %get-tuple-element.19.table, s32[1]{0:T(128)} %bitcast.core, f32[2048,128]{1,0:T(8,128)S(1)} %get-tuple-element.27.state, f32[512,128]{1,0:T(8,128)S(1)} %collective-permute-done.4.low, ...), custom_call_target="tpu_custom_call" | custom-call | tf_op jit(solution)/shard_map/forecast/pallas_call | solution.py:360
  111.9 4.5 %collective-permute-start.6 = (f32[8,72,128]{2,1,0:T(8,128)S(1)}, f32[8,72,128]{2,1,0:T(8,128)S(1)}, u32[]{:S(2)}, u32[]{:S(2)}) collective-permute-start(f32[8,72,128]{2,1,0:T(8,128)S(1)} %get-tuple-element.32), channel_id=1, source_target_pairs={{0,1},{1,0},{2,3},{3,2},{4,5},{5,4},{6,7},{7,6},{8,9},{9,8},{10,11... | collective-permute-start | bytes 884744 | tf_op jit(solution)/shard_map/ppermute | solution.py:315
  116.4 1.2 collective-permute-done.6
  117.7 12.9 %all_to_all.32.got = f32[8,72,128]{2,1,0:T(8,128)S(1)} all-to-all(f32[8,72,128]{2,1,0:T(8,128)S(1)} %add.7), channel_id=1, replica_groups=mesh['mem'=4,'hor'=16,'zh'=2,'core'=2] {'mem','zh'}, dimensions={0} | all-to-all | bytes 589824 | tf_op jit(solution)/shard_map/all_to_all | solution.py:319
  130.6 3.2 %root.3 = f32[8,72,128]{2,1,0:T(8,128)S(1)} custom-call(f32[8,72,128]{2,1,0:T(8,128)S(1)} %all_to_all.32.got), custom_call_target="tpu_custom_call" | custom-call | tf_op jit(solution)/shard_map/root/pallas_call | solution.py:373
  133.9 13.2 %all_to_all.33.same = f32[8,72,128]{2,1,0:T(8,128)S(1)} all-to-all(f32[8,72,128]{2,1,0:T(8,128)S(1)} %root.3), channel_id=1, replica_groups=mesh['mem'=4,'hor'=16,'zh'=2,'core'=2] {'mem','zh'}, dimensions={0} | all-to-all | bytes 589824 | tf_op jit(solution)/shard_map/all_to_all | solution.py:319
  147.0 3.0 %collective-permute-start.7 = (f32[8,72,128]{2,1,0:T(8,128)S(1)}, f32[8,72,128]{2,1,0:T(8,128)S(1)}, u32[]{:S(2)}, u32[]{:S(2)}) collective-permute-start(f32[8,72,128]{2,1,0:T(8,128)S(1)} %all_to_all.33.same), channel_id=1, source_target_pairs={{0,1},{1,0},{2,3},{3,2},{4,5},{5,4},{6,7},{7,6},{8,9},{9,8},{10,11... | collective-permute-start | bytes 884744 | tf_op jit(solution)/shard_map/ppermute | solution.py:315
  150.0 1.2 collective-permute-done.7.other
  151.2 4.3 %apply.3 = f32[2048,128]{1,0:T(8,128)S(1)} custom-call(s32[1]{0:T(128)} %bitcast.core, f32[2048,128]{1,0:T(8,128)S(1)} %get-tuple-element.30.state, f32[8,72,128]{2,1,0:T(8,128)S(1)} %all_to_all.33.same, f32[8,72,128]{2,1,0:T(8,128)S(1)} %collective-permute-done.7.other), custom_call_target="tpu_custom_call" | custom-call | tf_op jit(solution)/shard_map/apply/pallas_call | solution.py:382
  155.5 31.1 %all_to_all.34 = f32[16,128,128]{2,1,0:T(8,128)S(1)} all-to-all(f32[16,128,128]{2,1,0:T(8,128)S(1)} %bitcast.22), channel_id=1, replica_groups=mesh['mem'=4,'hor'=16,'zh'=2,'core'=2] {'mem','zh','core'}, dimensions={0} | all-to-all | bytes 2097152 | tf_op jit(solution)/shard_map/all_to_all | solution.py:319
  186.6 1.9 %place.1 = f32[512,512]{1,0:T(8,128)} custom-call(f32[2048,128]{1,0:T(8,128)S(1)} %bitcast.23), custom_call_target="tpu_custom_call" | custom-call | tf_op jit(solution)/shard_map/place/pallas_call | solution.py:388
  (16 shorter events, 2.5 us)
Async XLA Ops:
  2.1 1.2 copy-start
  3.3 0.7 copy-start.1
  6.5 10.1 %copy-start.2 = (f32[32,32]{1,0:T(8,128)S(1)}, f32[32,32]{1,0:T(8,128)}, u32[]{:S(2)}) copy-start(f32[32,32]{1,0:T(8,128)} %param.9) | copy-start | bytes 12292
  6.5 39.0 %all-to-all-start = ((f32[16,136,128]{2,1,0:T(8,128)}), f32[16,136,128]{2,1,0:T(8,128)S(1)}, u32[]{:S(2)}, u32[]{:S(2)}) async-start(f32[16,136,128]{2,1,0:T(8,128)} %bitcast.3), calls=%async_computation | async-start | bytes 2228224 | tf_op jit(solution)/shard_map/all_to_all | solution.py:319
  46.3 3.4 %collective-permute-start = (f32[512,128]{1,0:T(8,128)S(1)}, f32[512,128]{1,0:T(8,128)S(1)}, u32[]{:S(2)}, u32[]{:S(2)}) collective-permute-start(f32[512,128]{1,0:T(8,128)S(1)} %get-tuple-element.21), channel_id=1, source_target_pairs={{0,1},{1,64},{64,65},{65,128},{128,129},{129,192},{192,193},{193,2... | collective-permute-start | bytes 786440 | tf_op jit(solution)/shard_map/ppermute | solution.py:311
  46.4 5.9 %collective-permute-start.1 = (f32[512,128]{1,0:T(8,128)S(1)}, f32[512,128]{1,0:T(8,128)S(1)}, u32[]{:S(2)}, u32[]{:S(2)}) collective-permute-start(f32[512,128]{1,0:T(8,128)S(1)} %get-tuple-element.22), channel_id=1, source_target_pairs={{1,0},{64,1},{65,64},{128,65},{129,128},{192,129},{193,192},{2,193... | collective-permute-start | bytes 786440 | tf_op jit(solution)/shard_map/ppermute | solution.py:311
  56.4 6.8 %collective-permute-start.2 = (f32[8,72,128]{2,1,0:T(8,128)S(1)}, f32[8,72,128]{2,1,0:T(8,128)S(1)}, u32[]{:S(2)}, u32[]{:S(2)}) collective-permute-start(f32[8,72,128]{2,1,0:T(8,128)S(1)} %get-tuple-element.26), channel_id=1, source_target_pairs={{0,1},{1,0},{2,3},{3,2},{4,5},{5,4},{6,7},{7,6},{8,9},{9,8},{10,11... | collective-permute-start | bytes 884744 | tf_op jit(solution)/shard_map/ppermute | solution.py:315
  92.6 4.2 %collective-permute-start.3 = (f32[8,72,128]{2,1,0:T(8,128)S(1)}, f32[8,72,128]{2,1,0:T(8,128)S(1)}, u32[]{:S(2)}, u32[]{:S(2)}) collective-permute-start(f32[8,72,128]{2,1,0:T(8,128)S(1)} %all_to_all.31.same), channel_id=1, source_target_pairs={{0,1},{1,0},{2,3},{3,2},{4,5},{5,4},{6,7},{7,6},{8,9},{9,8},{10,11... | collective-permute-start | bytes 884744 | tf_op jit(solution)/shard_map/ppermute | solution.py:315
  100.5 4.8 %collective-permute-start.4 = (f32[512,128]{1,0:T(8,128)S(1)}, f32[512,128]{1,0:T(8,128)S(1)}, u32[]{:S(2)}, u32[]{:S(2)}) collective-permute-start(f32[512,128]{1,0:T(8,128)S(1)} %get-tuple-element.28), channel_id=1, source_target_pairs={{0,1},{1,64},{64,65},{65,128},{128,129},{129,192},{192,193},{193,2... | collective-permute-start | bytes 786440 | tf_op jit(solution)/shard_map/ppermute | solution.py:311
  102.0 5.8 %collective-permute-start.5 = (f32[512,128]{1,0:T(8,128)S(1)}, f32[512,128]{1,0:T(8,128)S(1)}, u32[]{:S(2)}, u32[]{:S(2)}) collective-permute-start(f32[512,128]{1,0:T(8,128)S(1)} %get-tuple-element.29), channel_id=1, source_target_pairs={{1,0},{64,1},{65,64},{128,65},{129,128},{192,129},{193,192},{2,193... | collective-permute-start | bytes 786440 | tf_op jit(solution)/shard_map/ppermute | solution.py:311
  111.9 5.7 %collective-permute-start.6 = (f32[8,72,128]{2,1,0:T(8,128)S(1)}, f32[8,72,128]{2,1,0:T(8,128)S(1)}, u32[]{:S(2)}, u32[]{:S(2)}) collective-permute-start(f32[8,72,128]{2,1,0:T(8,128)S(1)} %get-tuple-element.32), channel_id=1, source_target_pairs={{0,1},{1,0},{2,3},{3,2},{4,5},{5,4},{6,7},{7,6},{8,9},{9,8},{10,11... | collective-permute-start | bytes 884744 | tf_op jit(solution)/shard_map/ppermute | solution.py:315
  147.0 4.2 %collective-permute-start.7 = (f32[8,72,128]{2,1,0:T(8,128)S(1)}, f32[8,72,128]{2,1,0:T(8,128)S(1)}, u32[]{:S(2)}, u32[]{:S(2)}) collective-permute-start(f32[8,72,128]{2,1,0:T(8,128)S(1)} %all_to_all.33.same), channel_id=1, source_target_pairs={{0,1},{1,0},{2,3},{3,2},{4,5},{5,4},{6,7},{7,6},{8,9},{9,8},{10,11... | collective-permute-start | bytes 884744 | tf_op jit(solution)/shard_map/ppermute | solution.py:315
where the time goes:
time: 190 us; the launch traced here: 189 us
  blocking collectives  83.3 us (44%)
  waiting for transfers between devices  44.3 us (23%)
  starting transfers between devices  28.2 us (15%)
  Pallas kernels  28.1 us (15%)
  local copies, waits for them, and re-layouts  4.3 us (2%)
    all_to_all x5, blocking collectives, exchange(): return lax.all_to_all(x, axes, split_axis=0, concat_axis=0, tiled=True)  83.3 us
    all_to_all x1, waiting for transfers between devices, exchange(): return lax.all_to_all(x, axes, split_axis=0, concat_axis=0, tiled=True)  28.4 us
    ppermute x4, starting transfers between devices, swap(): return lax.ppermute(x, 'core', [(0, 1), (1, 0)])  16 us
    ppermute x4, waiting for transfers between devices, across(): return lax.ppermute(x, ALL, pairs)  11.1 us
    all_to_all x1, starting transfers between devices, exchange(): return lax.all_to_all(x, axes, split_axis=0, concat_axis=0, tiled=True)  10.1 us
    pallas_call x2, Pallas kernels, shards(): call(functools.partial(forecast_kernel, cycle), (arr(2 * rows, WIDTH), ar...  8.27 us
    pallas_call x2, Pallas kernels, shards(): call(functools.partial(apply_kernel, last), outs, [smem()] + [vmem()] * 3...  8.1 us
    pallas_call x2, Pallas kernels, shards(): copies = call(root_kernel, arr(8, FOLD, 128), [vmem()], 'root')(parts)  6.49 us
  transfers between devices with their start and end apart: 9, of which 9 were waited for; matrix products, arithmetic and copies ran while one was open for 0% of the time, Pallas kernels for 0%

commit v1 on v0

v1 whole, which is shorter than its diff:
```python
import functools
import math

import jax
import jax.numpy as jnp
from jax import lax
from jax.experimental import pallas as pl
from jax.experimental.pallas import tpu as pltpu
from jax.sharding import Mesh, PartitionSpec as P

SUBSTEPS = 4
ROOT_STEPS = 8
TIME_STEP = 0.2
GROUP = 16
WIDTH = 128
LEVELS = 32
COLS = 512
MINE = COLS // GROUP
HALO = 2 * SUBSTEPS
WIDE = MINE + 2 * HALO
FOLD = 72
F32 = jnp.float32
BF16 = jnp.bfloat16
VMEM_LIMIT = 48 * 1024 * 1024
ALL = ("mem", "hor", "zh", "core")
TILE = ("mem", "zh", "core")
CHIPS = ("mem", "zh")


def block_of(g):
    return ((g >> 1) & 1) * 8 + (g >> 2) * 2 + (g & 1)


MEMBER_AT = {block_of(g): g for g in range(GROUP)}


def split(a):
    high = a.astype(BF16)
    return high, (a - high.astype(F32)).astype(BF16)


def dot_split(a, b, dims=((1,), (0,))):
    dims = (dims, ((), ()))
    dot = functools.partial(lax.dot_general, dimension_numbers=dims, preferred_element_type=F32)
    return dot(a[0], b[0]) + (dot(a[0], b[1]) + dot(a[1], b[0]))


def iota(shape, dim):
    return lax.broadcasted_iota(jnp.int32, shape, dim)


def chunk_transpose(rows):
    lane = iota(rows[0].shape, 1)
    out = []
    for p in range(4):
        total = None
        for q in range(4):
            piece = rows[q] if p == q else pltpu.roll(rows[q], (32 * (q - p)) % 128, 1)
            total = piece if total is None else jnp.where(lane >= 32 * q, piece, total)
        out.append(total)
    return out


def edges_kernel(left, right, first, last):
    first[...] = left[...].T[0:HALO, :]
    last[...] = right[...].T[128 - HALO :, :]


def observe_kernel(info, partner, column, level, value, error, live, coupling, out, mixing):
    member = jnp.bitwise_xor(iota((GROUP, COLS), 0), info[1])
    place = ((member >> 1) & 1) * 8 + (member >> 2) * 2 + (member & 1)
    spot = iota((64, COLS), 0)
    zero = jnp.zeros((64, COLS), F32)
    for cycle in range(2):
        col = column[cycle, 0]
        weight = live[cycle, 0].astype(F32) / error[cycle, 0]
        weighted = weight * value[cycle, 0]
        here = (col >> 5) == place
        left = jnp.concatenate([jnp.where(here, weight, 0.0), jnp.where(here, weighted, 0.0)], axis=1)
        hit = jnp.where(level[cycle, 0] * 32 + (col & 31) == spot, 1.0, 0.0)
        right = jnp.concatenate(
            [jnp.concatenate([hit, zero], axis=1), jnp.concatenate([zero, hit], axis=1)], axis=0
        )
        sums = lax.dot_general(
            left, right, (((1,), (1,)), ((), ())), precision=lax.Precision.HIGHEST, preferred_element_type=F32
        )
        out[pl.ds(cycle, GROUP, stride=8), :] = sums
    lane = iota((GROUP, 128), 1)
    first = partner[0, 0, 0].astype(F32)
    second = partner[0, 0, 1].astype(F32)
    out[pl.ds(2, GROUP, stride=8), :] = jnp.where(lane == 0, first, second)
    wide = jnp.concatenate([coupling[...]] * 8, axis=1)
    wide = jnp.concatenate([wide] * 8, axis=0)
    wide = jnp.where((iota((256, 256), 0) >> 5) == (iota((256, 256), 1) >> 5), wide, 0.0)
    high, rest = split(wide)
    mixing[pl.ds(0, 256), :] = high
    mixing[pl.ds(256, 256), :] = rest


def first_kernel(info, ens, before, after, sums, mixing, heights, speeds, us, hs, tiles):
    ring = COLS + 128
    middle = jnp.zeros((128 - 2 * HALO, COLS), F32)
    halo = jnp.concatenate([after[...], middle, before[...]], axis=0).T
    for m in range(8):
        for f, ref in enumerate((us, hs)):
            at = (m * 2 + f) * LEVELS
            ref[pl.ds(m * LEVELS, LEVELS), pl.ds(0, COLS)] = ens[pl.ds(at, LEVELS), :]
            ref[pl.ds(m * LEVELS, LEVELS), pl.ds(COLS, 128)] = halo[at : at + LEVELS, :]
    rate = 0.5 * TIME_STEP
    mix = (mixing[pl.ds(0, 256), :], mixing[pl.ds(256, 256), :])

    def slope(x):
        return pltpu.roll(x, ring - 1, 1) - pltpu.roll(x, 1, 1)

    for step in range(SUBSTEPS):
        pressure = dot_split(mix, split(hs[...]))
        for r in range(32):
            rows = pl.ds(8 * r, 8)
            u, h = us[rows, :], hs[rows, :]
            moved = u - rate * (u * slope(u) + slope(pressure[8 * r : 8 * r + 8, :]))
            height = h - rate * slope(moved * h)
            if step < SUBSTEPS - 1:
                us[rows, :] = moved
                hs[rows, :] = height
            else:
                for t in range(4):
                    for f, done in enumerate((moved, height)):
                        tiles[pl.ds((f * 4 + t) * 256 + 8 * r, 8), :] = done[:, 128 * t : 128 * t + 128]
    for f, (ref, size) in enumerate(((speeds, 64), (heights, 72))):
        for t in range(4):
            for m in range(8):
                at = (f * 4 + t) * 256 + m * LEVELS
                rows = [tiles[pl.ds(at + i, 8, stride=4), :] for i in range(4)]
                for p, block in enumerate(chunk_transpose(rows)):
                    g = jnp.bitwise_xor(MEMBER_AT[4 * t + p], info[1])
                    ref[pl.ds(g * size + m, 8, stride=8), :] = block
    for g in range(GROUP):
        heights[pl.ds(g * 72 + 64, 8), :] = sums[pl.ds(g * 8, 8), :]


def square_of(ref, at, size):
    return jnp.concatenate([ref[pl.ds(g * size + at * 8, 8), :] for g in range(GROUP)], axis=0)


def blend(fs, table, core, keep, send):
    mine = core
    for j in range(GROUP // 2):
        for which, ref in ((mine, keep), (1 - mine, send)):
            s = 2 * j + which
            ref[j] = fs[s] + fs[table[s, 0]] + fs[table[s, 1]]


def partial_gram(fs, q, flipped, anomaly, mean, weight, total):
    pull = total - weight * mean
    vector = jnp.sum(anomaly * pull, axis=0, keepdims=True)
    gram = dot_split(split(flipped), split(anomaly * weight))
    body, tail = fold(gram[:64], gram[64:], vector)
    fs[q, pl.ds(0, 64), :] = body
    fs[q, pl.ds(64, 8), :] = tail


def first_gram_kernel(info, got, keep, send, later, table_out, fs, table, sem):
    rows = got[pl.ds(66, GROUP, stride=72), :].astype(jnp.int32)
    table_out[...] = rows
    copy = pltpu.make_async_copy(table_out, table, sem)
    copy.start()
    hist = []
    for cycle in range(2):
        lines = got[pl.ds(64 + cycle, GROUP, stride=72), :]
        hist.append(jnp.concatenate([lines, jnp.zeros((128 - GROUP, 128), F32)], axis=0).T)
    later[...] = hist[1]
    for four in range(8):
        square = square_of(got, four, 72)
        square = square - jnp.mean(square, axis=0, keepdims=True)
        mean = jnp.mean(square_of(got, four, 72).T, axis=1, keepdims=True)
        turned = square.T
        for half in range(2):
            q = 2 * four + half
            at = slice(64 * half, 64 * half + 64)
            partial_gram(
                fs, q, square[:, at], turned[at, :], mean[at], hist[0][:64, q : q + 1], hist[0][64:, q : q + 1]
            )
    copy.wait()
    blend(fs, table, info[0], keep, send)


def fold(top, bottom, vector):
    row, lane = iota((64, 128), 0), iota((64, 128), 1)
    body = jnp.where((lane >= 64) | (row <= lane), top, pltpu.roll(bottom, 64, 1))
    diagonal = jnp.sum(jnp.where(lane == row + 64, bottom, 0.0), axis=0, keepdims=True)
    tail = jnp.where(iota((8, 128), 0) == 0, diagonal, vector)
    return body, tail


def unfold(body, tail):
    row, lane = iota((64, 128), 0), iota((64, 128), 1)
    top = jnp.where((lane >= 64) | (row < lane), body, jnp.where(row == lane, 0.5 * body, 0.0))
    moved = pltpu.roll(body, 64, 1)
    bottom = jnp.where(row > lane - 64, moved, jnp.where(row == lane - 64, 0.5 * tail[0:1, :], 0.0))
    bottom = jnp.where(lane >= 64, bottom, 0.0)
    half = jnp.concatenate([top, bottom], axis=0)
    return half + half.T, tail[1:2, :]


def forecast_kernel(table, info, state, low, high, hist, mixing, out, keep, send, us, hs, ps, fs):
    edge = HALO * LEVELS
    span = MINE * LEVELS
    for f, ref in enumerate((us, hs)):
        ref[pl.ds(0, edge), :] = low[pl.ds(f * edge, edge), :]
        ref[pl.ds(edge, span), :] = state[pl.ds(f * span, span), :]
        ref[pl.ds(edge + span, edge), :] = high[pl.ds(f * edge, edge), :]
    rate = 0.5 * TIME_STEP
    mix = (mixing[pl.ds(0, 256), :], mixing[pl.ds(256, 256), :])

    def col(ref, c):
        return ref[pl.ds(c * LEVELS, LEVELS), :]

    for step in range(SUBSTEPS):
        lo, hi = 2 * step, WIDE - 2 * step
        for pair in range(3):
            block = jnp.concatenate(
                [hs[pl.ds(pair * 512, 256), :], hs[pl.ds(pair * 512 + 256, 256), :]], axis=1
            )
            pressure = dot_split(mix, split(block))
            ps[pl.ds(pair * 512, 256), :] = pressure[:, :128]
            ps[pl.ds(pair * 512 + 256, 256), :] = pressure[:, 128:]
        before, here = col(us, lo), col(us, lo + 1)
        flux_two, flux_one, height_one = None, None, None
        for c in range(lo + 1, hi - 1):
            after = col(us, c + 1)
            moved = here - rate * (here * (after - before) + (col(ps, c + 1) - col(ps, c - 1)))
            height = col(hs, c)
            flux = moved * height
            if c >= lo + 3:
                hs[pl.ds((c - 1) * LEVELS, LEVELS), :] = height_one - rate * (flux - flux_two)
            us[pl.ds(c * LEVELS, LEVELS), :] = moved
            before, here = here, after
            flux_two, flux_one, height_one = flux_one, flux, height
    out[pl.ds(0, span), :] = us[pl.ds(edge, span), :]
    out[pl.ds(span, span), :] = hs[pl.ds(edge, span), :]

    for q in range(GROUP):
        field = jnp.concatenate(
            [hs[pl.ds(edge + 2 * q + j, MINE, stride=LEVELS), :] for j in range(2)], axis=0
        )
        mean = jnp.mean(field, axis=1, keepdims=True)
        anomaly = field - mean
        partial_gram(fs, q, anomaly.T, anomaly, mean, hist[pl.ds(0, 64), q : q + 1], hist[pl.ds(64, 64), q : q + 1])
    blend(fs, table, info[0], keep, send)


def root_kernel(got, out):
    total = got[0]
    for j in range(1, 8):
        total = total + got[j]
    gram, vector = unfold(total[:64], total[64:])
    eye = jnp.where(iota((WIDTH, WIDTH), 0) == iota((WIDTH, WIDTH), 1), 1.0, 0.0)
    third = 1.0 / 3.0
    blended = (WIDTH - 1.0) * eye + gram * third
    pull = vector * third
    squared = jnp.sum(jnp.sum(blended * blended, axis=0, keepdims=True), axis=1, keepdims=True)
    norm = jnp.sqrt(squared)
    a = blended / norm
    newton = 1.5 * eye - 0.5 * a
    s = split(newton)
    a = dot_split(split(a), s)
    z = newton
    for step in range(1, ROOT_STEPS):
        newton = 1.5 * eye - 0.5 * dot_split(split(z), split(a))
        s = split(newton)
        if step < ROOT_STEPS - 1:
            a = dot_split(split(a), s)
        z = dot_split(s, split(z))
    halves = split(z)
    wide = jnp.broadcast_to(pull, (8, WIDTH))
    inner = dot_split(split(wide), halves, ((1,), (1,)))
    shift = dot_split(split(inner), halves, ((1,), (1,)))[0:1, :] / norm
    spread = z * (math.sqrt(WIDTH - 1.0) / jnp.sqrt(norm))
    body, tail = fold(spread[:64], spread[64:], shift)
    for j in range(8):
        out[j, pl.ds(0, 64), :] = body
        out[j, pl.ds(64, 8), :] = tail


def gather_roots(info, same, other, both):
    for j in range(GROUP // 2):
        both[2 * j + info[0]] = same[j]
        both[2 * j + 1 - info[0]] = other[j]


def first_apply_kernel(info, heights, speeds, same, other, out, low, high, both):
    gather_roots(info, same, other, both)
    span = MINE * LEVELS
    edge = HALO * LEVELS
    for four in range(8):
        fields = (square_of(speeds, four, 64), square_of(heights, four, 72))
        for half in range(2):
            s = 2 * four + half
            spread, shift = unfold(both[s, pl.ds(0, 64), :], both[s, pl.ds(64, 8), :])
            field = jnp.concatenate([x[:, 64 * half : 64 * half + 64] for x in fields], axis=1)
            mean = jnp.mean(field, axis=0, keepdims=True)
            result = mean + dot_split(split(spread + shift), split(field - mean))
            result = result.T
            for f in range(2):
                for j in range(2):
                    at = (f * 2 + j) * 32
                    out[pl.ds(f * span + 2 * s + j, MINE, stride=LEVELS), :] = result[at : at + 32, :]
    for f in range(2):
        low[pl.ds(f * edge, edge), :] = out[pl.ds(f * span, edge), :]
        high[pl.ds(f * edge, edge), :] = out[pl.ds((f + 1) * span - edge, edge), :]


def last_apply_kernel(info, state, same, other, out, both):
    gather_roots(info, same, other, both)
    span = MINE * LEVELS
    for s in range(GROUP):
        spread, shift = unfold(both[s, pl.ds(0, 64), :], both[s, pl.ds(64, 8), :])
        field = jnp.concatenate(
            [
                state[pl.ds(f * span + 2 * s + j, MINE, stride=LEVELS), :]
                for f in range(2)
                for j in range(2)
            ],
            axis=0,
        ).T
        mean = jnp.mean(field, axis=0, keepdims=True)
        result = mean + dot_split(split(spread + shift), split(field - mean))
        for g in range(GROUP):
            out[pl.ds((g * GROUP + s) * 8, 8), :] = result[g * 8 : g * 8 + 8, :]


def place_kernel(info, got, out, tiles):
    for n in range(8):
        for t in range(4):
            members = [jnp.bitwise_xor(MEMBER_AT[4 * t + p], info[1]) for p in range(4)]
            rows = [got[pl.ds(g * 128 + n, 16, stride=8), :] for g in members]
            for fj, block in enumerate(chunk_transpose(rows)):
                f, j = fj // 2, fj % 2
                tiles[pl.ds(512 * t + (n * 2 + f) * LEVELS + j, 16, stride=2), :] = block
    for t in range(4):
        out[:, pl.ds(128 * t, 128)] = tiles[pl.ds(512 * t, 512), :]


def vmem():
    return pl.BlockSpec(memory_space=pltpu.VMEM)


def smem():
    return pl.BlockSpec(memory_space=pltpu.SMEM)


def call(kernel, out, ins, name, scratch=()):
    return pl.pallas_call(
        kernel,
        out_shape=out,
        in_specs=ins,
        out_specs=jax.tree.map(lambda _: vmem(), out),
        scratch_shapes=scratch,
        compiler_params=pltpu.CompilerParams(vmem_limit_bytes=VMEM_LIMIT),
        name=name,
    )


def arr(*shape, dtype=F32):
    return jax.ShapeDtypeStruct(shape, dtype)


def across(x, forward):
    pairs = []
    for hor in range(16):
        for block in range(GROUP):
            here = MEMBER_AT[block]
            nxt = MEMBER_AT[(block + 1) % GROUP]
            nhor = (hor + (block + 1) // GROUP) % 16

            def flat(g, h):
                return ((g >> 2) * 16 + h) * 4 + (g & 3)

            pair = (flat(here ^ (15 * (hor & 1)), hor), flat(nxt ^ (15 * (nhor & 1)), nhor))
            pairs.append(pair if forward else pair[::-1])
    return lax.ppermute(x, ALL, pairs)


def swap(x):
    return lax.ppermute(x, "core", [(0, 1), (1, 0)])


def exchange(x, axes):
    return lax.all_to_all(x, axes, split_axis=0, concat_axis=0, tiled=True)


def shards(ensemble, coupling, obs_column, obs_level, obs_value, obs_error, obs_live, partners):
    rows = MINE * LEVELS
    edges = 2 * HALO * LEVELS
    members = ensemble.reshape(512, COLS)
    info = jnp.stack([lax.axis_index("core"), 15 * (lax.axis_index("hor") & 1)]).astype(jnp.int32)
    first, last = pl.pallas_call(
        edges_kernel,
        grid=(1,),
        out_shape=(arr(HALO, COLS), arr(HALO, COLS)),
        in_specs=[pl.BlockSpec((512, 128), lambda i: (0, 0)), pl.BlockSpec((512, 128), lambda i: (0, 3))],
        out_specs=(pl.BlockSpec((HALO, COLS), lambda i: (0, 0)),) * 2,
        name="edges",
    )(members, members)
    ring = [(i, (i + 1) % 16) for i in range(16)]
    before = lax.ppermute(last, "hor", ring)
    after = lax.ppermute(first, "hor", [(b, a) for a, b in ring])
    sums, mixing = call(
        observe_kernel, (arr(128, 128), arr(512, 256, dtype=BF16)), [smem()] * 2 + [vmem()] * 6, "observe"
    )(info, partners, obs_column, obs_level, obs_value, obs_error, obs_live, coupling)
    heights, speeds = call(
        first_kernel,
        (arr(GROUP * 72, 128), arr(GROUP * 64, 128)),
        [smem()] + [vmem()] * 5,
        "first",
        [pltpu.VMEM((256, COLS + 128), F32), pltpu.VMEM((256, COLS + 128), F32), pltpu.VMEM((2048, 128), F32)],
    )(info, members, before, after, sums, mixing)
    heights = exchange(heights.reshape(GROUP, 72, 128), TILE)
    speeds, heights = lax.optimization_barrier((speeds, heights))
    heights = heights.reshape(GROUP * 72, 128)
    speeds = exchange(speeds.reshape(GROUP, 64, 128), TILE).reshape(GROUP * 64, 128)
    folded = pltpu.VMEM((GROUP, FOLD, 128), F32)
    keep, send, hist, table = call(
        first_gram_kernel,
        (arr(8, FOLD, 128), arr(8, FOLD, 128), arr(128, 128), arr(GROUP, 128, dtype=jnp.int32)),
        [smem(), vmem()],
        "gram",
        [folded, pltpu.SMEM((GROUP, 128), jnp.int32), pltpu.SemaphoreType.DMA(())],
    )(info, heights)

    def roots(keep, send):
        parts = exchange(keep + swap(send), CHIPS)
        copies = call(root_kernel, arr(8, FOLD, 128), [vmem()], "root")(parts)
        same = exchange(copies, CHIPS)
        return same, swap(same)

    same, other = roots(keep, send)
    state, low, high = call(
        first_apply_kernel,
        (arr(2 * rows, WIDTH), arr(edges, WIDTH), arr(edges, WIDTH)),
        [smem()] + [vmem()] * 4,
        "apply",
        [folded],
    )(info, heights, speeds, same, other)
    from_low = across(high, True)
    from_high = across(low, False)
    wide = pltpu.VMEM((WIDE * LEVELS, WIDTH), F32)
    state, keep, send = call(
        forecast_kernel,
        (arr(2 * rows, WIDTH), arr(8, FOLD, 128), arr(8, FOLD, 128)),
        [smem(), smem()] + [vmem()] * 5,
        "forecast",
        [wide, wide, wide, folded],
    )(table, info, state, from_low, from_high, hist, mixing)
    same, other = roots(keep, send)
    analysed = call(
        last_apply_kernel, arr(GROUP * 128, 128), [smem()] + [vmem()] * 3, "analyse", [folded]
    )(info, state, same, other)
    got = exchange(analysed.reshape(GROUP, 128, 128), TILE).reshape(GROUP * 128, 128)
    placed = call(place_kernel, arr(512, 512), [smem(), vmem()], "place", [pltpu.VMEM((2048, 128), F32)])(info, got)
    return placed.reshape(ensemble.shape)


def solution(mesh):
    fine = Mesh(mesh.devices.reshape(4, 16, 2, 2), ALL)
    group = TILE
    in_specs = (
        P(group, None, None, "hor"),
        P(),
        P(None, group, "hor", None),
        P(None, group, "hor", None),
        P(None, group, "hor", None),
        P(None, group, "hor", None),
        P(None, group, "hor", None),
        P(group, "hor", None),
    )
    out_specs = P(group, None, None, "hor")
    return jax.shard_map(shards, mesh=fine, in_specs=in_specs, out_specs=out_specs, check_vma=False)
```

time: 190 us -> 202 us (1.063)
  blocking collectives: 83.3 us -> 112 us
  waiting for transfers between devices: 44.3 us -> 26 us
  Pallas kernels: 28.1 us -> 42.5 us
  starting transfers between devices: 28.2 us -> 19.5 us
  local copies, waits for them, and re-layouts: 4.3 us -> 0.63 us
    all_to_all x5 -> x6, blocking collectives: 83.3 us -> 112 us  [exchange(): return lax.all_to_all(x, axes, split_axis=0, concat_axis=0, tiled=True)]
    pallas_call x9 -> x10, Pallas kernels: 28.1 us -> 42.5 us  [the longest x1 15.8 us: shards(): call(first_kernel, (arr(GROUP * 72, 128), arr(GROUP * 64, 128)), [smem()]...]
    all_to_all x1, waiting for transfers between devices: 28.4 us -> 16.6 us  [exchange(): return lax.all_to_all(x, axes, split_axis=0, concat_axis=0, tiled=True)]
    ppermute x4, starting transfers between devices: 16 us -> 7.21 us  [swap(): return lax.ppermute(x, 'core', [(0, 1), (1, 0)])]
    ppermute x0 -> x2, starting transfers between devices: none -> 5.79 us  [the longest x1 3.74 us: shards(): after = lax.ppermute(first, 'hor', [(b, a) for a, b in ring])]
    ppermute x4 -> x2, waiting for transfers between devices: 11.1 us -> 5.39 us  [across(): return lax.ppermute(x, ALL, pairs)]
    all_to_all x1, starting transfers between devices: 10.1 us -> 5.96 us  [exchange(): return lax.all_to_all(x, axes, split_axis=0, concat_axis=0, tiled=True)]
    unnamed x9 -> x16, local copies, waits for them, and re-layouts: 3.99 us -> 0.63 us
  transfers between devices with their start and end apart: 9 -> 9, of which waited for: 9 -> 6; matrix products, arithmetic and copies ran while one was open for 0% -> 0% of each run, Pallas kernels for 0% -> 1%
where the time goes in v1:
time: 202 us; the launch traced here: 201 us
  blocking collectives  112 us (55%)
  Pallas kernels  42.5 us (21%)
  waiting for transfers between devices  26 us (13%)
  starting transfers between devices  19.5 us (10%)
    all_to_all x6, blocking collectives, exchange(): return lax.all_to_all(x, axes, split_axis=0, concat_axis=0, tiled=True)  112 us
    all_to_all x1, waiting for transfers between devices, exchange(): return lax.all_to_all(x, axes, split_axis=0, concat_axis=0, tiled=True)  16.6 us
    pallas_call x1, Pallas kernels, shards(): call(first_kernel, (arr(GROUP * 72, 128), arr(GROUP * 64, 128)), [smem()]...  15.8 us
    ppermute x4, starting transfers between devices, swap(): return lax.ppermute(x, 'core', [(0, 1), (1, 0)])  7.21 us
    pallas_call x2, Pallas kernels, roots(): copies = call(root_kernel, arr(8, FOLD, 128), [vmem()], 'root')(parts)  6.49 us
    all_to_all x1, starting transfers between devices, exchange(): return lax.all_to_all(x, axes, split_axis=0, concat_axis=0, tiled=True)  5.96 us
    pallas_call x1, Pallas kernels, shards(): call(first_gram_kernel, (arr(8, FOLD, 128), arr(8, FOLD, 128), arr(128, 1...  5.4 us
    ppermute x2, waiting for transfers between devices, across(): return lax.ppermute(x, ALL, pairs)  5.39 us
  transfers between devices with their start and end apart: 9, of which 6 were waited for; matrix products, arithmetic and copies ran while one was open for 0% of the time, Pallas kernels for 1%

profile of v1, /device:TPU:1, one launch (start us, length us, event | category | flops | bytes accessed | tf_op | source)
XLA Modules:
  0.0 201.4 jit_solution(4804162516865999819)
XLA Ops:
  0.0 1.9 edges.1
  1.9 2.0 %collective-permute-start = (f32[8,512]{1,0:T(8,128)}, f32[8,512]{1,0:T(8,128)S(1)}, u32[]{:S(2)}, u32[]{:S(2)}) collective-permute-start(f32[8,512]{1,0:T(8,128)} %get-tuple-element.23), channel_id=1, source_target_pairs={{0,4},{4,8},{8,12},{12,16},{16,20},{20,24},{24,28},{28,32},{32,36}... | collective-permute-start | bytes 49160 | tf_op jit(solution)/shard_map/ppermute | solution.py:406
  4.0 3.7 %collective-permute-start.1 = (f32[8,512]{1,0:T(8,128)}, f32[8,512]{1,0:T(8,128)S(1)}, u32[]{:S(2)}, u32[]{:S(2)}) collective-permute-start(f32[8,512]{1,0:T(8,128)} %get-tuple-element.24), channel_id=1, source_target_pairs={{4,0},{8,4},{12,8},{16,12},{20,16},{24,20},{28,24},{32,28},{36,32}... | collective-permute-start | bytes 49160 | tf_op jit(solution)/shard_map/ppermute | solution.py:407
  7.8 0.6 copy-done.3
  8.4 1.3 observe.1
  9.8 15.8 %first.1 = (f32[1152,128]{1,0:T(8,128)S(1)}, f32[1024,128]{1,0:T(8,128)}) custom-call(s32[2]{0:T(128)S(1)} %pad_add_fusion.info, f32[512,512]{1,0:T(8,128)S(1)} %bitcast.12, f32[8,512]{1,0:T(8,128)S(1)} %collective-permute-done.before, f32[8,512]{1,0:T(8,128)S(1)} %collective-permute-done.1.after, f32[128,128]{1,0:T(8,128)S(1)} %get-tuple-element.25.sums, ...), custom_call_target="tpu_custom_call" | custom-call | tf_op jit(solution)/shard_map/first/pallas_call | solution.py:411
  25.6 28.3 %all_to_all.35 = f32[16,72,128]{2,1,0:T(8,128)S(1)} all-to-all(f32[16,72,128]{2,1,0:T(8,128)S(1)} %bitcast.18), channel_id=1, replica_groups=mesh['mem'=4,'hor'=16,'zh'=2,'core'=2] {'mem','zh','core'}, dimensions={0} | all-to-all | bytes 1179648 | tf_op jit(solution)/shard_map/all_to_all | solution.py:389
  53.9 5.4 %gram.1 = (f32[8,72,128]{2,1,0:T(8,128)S(1)}, f32[8,72,128]{2,1,0:T(8,128)S(1)}, f32[128,128]{1,0:T(8,128)S(1)}, s32[16,128]{1,0:T(8,128)S(1)}) custom-call(s32[2]{0:T(128)S(1)} %pad_add_fusion.info, f32[1152,128]{1,0:T(8,128)S(1)} %bitcast.13), custom_call_target="tpu_custom_call" | custom-call | tf_op jit(solution)/shard_map/gram/pallas_call | solution.py:423
  59.3 0.1 collective-permute-start.2
  59.4 1.6 collective-permute-done.2
  61.0 13.4 %all_to_all.36.got = f32[8,72,128]{2,1,0:T(8,128)S(1)} all-to-all(f32[8,72,128]{2,1,0:T(8,128)S(1)} %add.6), channel_id=1, replica_groups=mesh['mem'=4,'hor'=16,'zh'=2,'core'=2] {'mem','zh'}, dimensions={0} | all-to-all | bytes 589824 | tf_op jit(solution)/shard_map/all_to_all | solution.py:389
  74.4 3.2 %root.2 = f32[8,72,128]{2,1,0:T(8,128)S(1)} custom-call(f32[8,72,128]{2,1,0:T(8,128)S(1)} %all_to_all.36.got), custom_call_target="tpu_custom_call" | custom-call | tf_op jit(solution)/shard_map/root/pallas_call | solution.py:433
  77.6 13.3 %all_to_all.37.same = f32[8,72,128]{2,1,0:T(8,128)S(1)} all-to-all(f32[8,72,128]{2,1,0:T(8,128)S(1)} %root.2), channel_id=1, replica_groups=mesh['mem'=4,'hor'=16,'zh'=2,'core'=2] {'mem','zh'}, dimensions={0} | all-to-all | bytes 589824 | tf_op jit(solution)/shard_map/all_to_all | solution.py:389
  90.9 6.0 %all-to-all-start.1 = ((f32[16,64,128]{2,1,0:T(8,128)}), f32[16,64,128]{2,1,0:T(8,128)S(1)}, u32[]{:S(2)}, u32[]{:S(2)}) async-start(f32[16,64,128]{2,1,0:T(8,128)} %bitcast.5), calls=%async_computation.1 | async-start | bytes 1048576 | tf_op jit(solution)/shard_map/all_to_all | solution.py:389
  96.9 0.3 collective-permute-start.3
  97.2 16.6 %all-to-all-done.1 = f32[16,64,128]{2,1,0:T(8,128)S(1)} async-done(((f32[16,64,128]{2,1,0:T(8,128)}), f32[16,64,128]{2,1,0:T(8,128)S(1)}, u32[]{:S(2)}, u32[]{:S(2)}) %all-to-all-start.1) | async-done | bytes 524320 | tf_op jit(solution)/shard_map/all_to_all | solution.py:389
  113.8 2.7 %apply.1 = (f32[2048,128]{1,0:T(8,128)S(1)}, f32[512,128]{1,0:T(8,128)S(1)}, f32[512,128]{1,0:T(8,128)S(1)}) custom-call(s32[2]{0:T(128)S(1)} %pad_add_fusion.info, f32[1152,128]{1,0:T(8,128)S(1)} %bitcast.14, f32[1024,128]{1,0:T(8,128)S(1)} %bitcast.17, f32[8,72,128]{2,1,0:T(8,128)S(1)} %all_to_all.37.same, f32[8,72,128]{2,1,0:T(8,128)S(1)} %collective-permute-done.3.other), custom_call_target="tpu_custom_call" | custom-call | tf_op jit(solution)/shard_map/apply/pallas_call | solution.py:438
  116.5 0.1 collective-permute-start.4
  116.6 0.5 collective-permute-start.5
  117.1 2.8 %collective-permute-done.4.low = f32[512,128]{1,0:T(8,128)S(1)} collective-permute-done((f32[512,128]{1,0:T(8,128)S(1)}, f32[512,128]{1,0:T(8,128)S(1)}, u32[]{:S(2)}, u32[]{:S(2)}) %collective-permute-start.4) | collective-permute-done | bytes 262176 | tf_op jit(solution)/shard_map/ppermute | solution.py:381
  119.9 2.6 %collective-permute-done.5.high = f32[512,128]{1,0:T(8,128)S(1)} collective-permute-done((f32[512,128]{1,0:T(8,128)S(1)}, f32[512,128]{1,0:T(8,128)S(1)}, u32[]{:S(2)}, u32[]{:S(2)}) %collective-permute-start.5) | collective-permute-done | bytes 262176 | tf_op jit(solution)/shard_map/ppermute | solution.py:381
  122.5 4.1 %forecast.1 = (f32[2048,128]{1,0:T(8,128)S(1)}, f32[8,72,128]{2,1,0:T(8,128)S(1)}, f32[8,72,128]{2,1,0:T(8,128)S(1)}) custom-call(s32[16,128]{1,0:T(8,128)S(1)} %get-tuple-element.30.table, s32[2]{0:T(128)S(1)} %pad_add_fusion.info, f32[2048,128]{1,0:T(8,128)S(1)} %get-tuple-element.34.state, f32[512,128]{1,0:T(8,128)S(1)} %collective-permute-done.4.low, ...), custom_call_target="tpu_custom_call" | custom-call | tf_op jit(solution)/shard_map/forecast/pallas_call | solution.py:448
  126.6 4.0 %collective-permute-start.6 = (f32[8,72,128]{2,1,0:T(8,128)S(1)}, f32[8,72,128]{2,1,0:T(8,128)S(1)}, u32[]{:S(2)}, u32[]{:S(2)}) collective-permute-start(f32[8,72,128]{2,1,0:T(8,128)S(1)} %get-tuple-element.40), channel_id=1, source_target_pairs={{0,1},{1,0},{2,3},{3,2},{4,5},{5,4},{6,7},{7,6},{8,9},{9,8},{10,11... | collective-permute-start | bytes 884744 | tf_op jit(solution)/shard_map/ppermute | solution.py:385
  130.6 1.2 collective-permute-done.6
  131.9 13.1 %all_to_all.38.got = f32[8,72,128]{2,1,0:T(8,128)S(1)} all-to-all(f32[8,72,128]{2,1,0:T(8,128)S(1)} %add.7), channel_id=1, replica_groups=mesh['mem'=4,'hor'=16,'zh'=2,'core'=2] {'mem','zh'}, dimensions={0} | all-to-all | bytes 589824 | tf_op jit(solution)/shard_map/all_to_all | solution.py:389
  145.0 3.2 %root.3 = f32[8,72,128]{2,1,0:T(8,128)S(1)} custom-call(f32[8,72,128]{2,1,0:T(8,128)S(1)} %all_to_all.38.got), custom_call_target="tpu_custom_call" | custom-call | tf_op jit(solution)/shard_map/root/pallas_call | solution.py:433
  148.2 13.3 %all_to_all.39.same = f32[8,72,128]{2,1,0:T(8,128)S(1)} all-to-all(f32[8,72,128]{2,1,0:T(8,128)S(1)} %root.3), channel_id=1, replica_groups=mesh['mem'=4,'hor'=16,'zh'=2,'core'=2] {'mem','zh'}, dimensions={0} | all-to-all | bytes 589824 | tf_op jit(solution)/shard_map/all_to_all | solution.py:389
  161.6 2.8 %collective-permute-start.7 = (f32[8,72,128]{2,1,0:T(8,128)S(1)}, f32[8,72,128]{2,1,0:T(8,128)S(1)}, u32[]{:S(2)}, u32[]{:S(2)}) collective-permute-start(f32[8,72,128]{2,1,0:T(8,128)S(1)} %all_to_all.39.same), channel_id=1, source_target_pairs={{0,1},{1,0},{2,3},{3,2},{4,5},{5,4},{6,7},{7,6},{8,9},{9,8},{10,11... | collective-permute-start | bytes 884744 | tf_op jit(solution)/shard_map/ppermute | solution.py:385
  164.4 1.2 collective-permute-done.7.other
  165.6 2.2 %analyse.1 = f32[2048,128]{1,0:T(8,128)S(1)} custom-call(s32[2]{0:T(128)S(1)} %pad_add_fusion.info, f32[2048,128]{1,0:T(8,128)S(1)} %get-tuple-element.38.state, f32[8,72,128]{2,1,0:T(8,128)S(1)} %all_to_all.39.same, f32[8,72,128]{2,1,0:T(8,128)S(1)} %collective-permute-done.7.other), custom_call_target="tpu_custom_call" | custom-call | tf_op jit(solution)/shard_map/analyse/pallas_call | solution.py:456
  167.8 31.1 %all_to_all.40 = f32[16,128,128]{2,1,0:T(8,128)S(1)} all-to-all(f32[16,128,128]{2,1,0:T(8,128)S(1)} %bitcast.16), channel_id=1, replica_groups=mesh['mem'=4,'hor'=16,'zh'=2,'core'=2] {'mem','zh','core'}, dimensions={0} | all-to-all | bytes 2097152 | tf_op jit(solution)/shard_map/all_to_all | solution.py:389
  198.9 2.5 %place.1 = f32[512,512]{1,0:T(8,128)} custom-call(s32[2]{0:T(128)S(1)} %pad_add_fusion.info, f32[2048,128]{1,0:T(8,128)S(1)} %bitcast.15), custom_call_target="tpu_custom_call" | custom-call | tf_op jit(solution)/shard_map/place/pallas_call | solution.py:460
  (21 shorter events, 0.2 us)
Async XLA Ops:
  0.0 7.8 %copy-start.4 = (f32[2,1,1,512]{3,2,1,0:T(1,128)S(1)}, f32[2,1,1,512]{3,2,1,0:T(1,128)}, u32[]{:S(2)}) copy-start(f32[2,1,1,512]{3,2,1,0:T(1,128)} %value.1) | copy-start | bytes 12292
  0.0 7.8 %copy-start.5 = (f32[2,1,1,512]{3,2,1,0:T(1,128)S(1)}, f32[2,1,1,512]{3,2,1,0:T(1,128)}, u32[]{:S(2)}) copy-start(f32[2,1,1,512]{3,2,1,0:T(1,128)} %error.1) | copy-start | bytes 12292
  0.0 7.8 %copy-start.6 = (s32[2,1,1,512]{3,2,1,0:T(1,128)S(1)}, s32[2,1,1,512]{3,2,1,0:T(1,128)}, u32[]{:S(2)}) copy-start(s32[2,1,1,512]{3,2,1,0:T(1,128)} %live.1) | copy-start | bytes 12292
  0.0 9.7 %copy-start = (f32[8,2,32,512]{3,2,1,0:T(8,128)S(1)}, f32[8,2,32,512]{3,2,1,0:T(8,128)}, u32[]{:S(2)}) copy-start(f32[8,2,32,512]{3,2,1,0:T(8,128)} %param.8) | copy-start | bytes 3145732
  1.9 5.9 %copy-start.1 = (f32[32,32]{1,0:T(8,128)S(1)}, f32[32,32]{1,0:T(8,128)}, u32[]{:S(2)}) copy-start(f32[32,32]{1,0:T(8,128)} %coupling.1) | copy-start | bytes 12292
  1.9 7.8 %collective-permute-start = (f32[8,512]{1,0:T(8,128)}, f32[8,512]{1,0:T(8,128)S(1)}, u32[]{:S(2)}, u32[]{:S(2)}) collective-permute-start(f32[8,512]{1,0:T(8,128)} %get-tuple-element.23), channel_id=1, source_target_pairs={{0,4},{4,8},{8,12},{12,16},{16,20},{20,24},{24,28},{28,32},{32,36}... | collective-permute-start | bytes 49160 | tf_op jit(solution)/shard_map/ppermute | solution.py:406
  4.0 5.8 %collective-permute-start.1 = (f32[8,512]{1,0:T(8,128)}, f32[8,512]{1,0:T(8,128)S(1)}, u32[]{:S(2)}, u32[]{:S(2)}) collective-permute-start(f32[8,512]{1,0:T(8,128)} %get-tuple-element.24), channel_id=1, source_target_pairs={{4,0},{8,4},{12,8},{16,12},{20,16},{24,20},{28,24},{32,28},{36,32}... | collective-permute-start | bytes 49160 | tf_op jit(solution)/shard_map/ppermute | solution.py:407
  7.7 0.7 copy-start.3
  7.7 0.7 copy-start.2
  7.7 0.7 copy-start.7
  59.3 1.7 collective-permute-start.2
  90.9 22.9 %all-to-all-start.1 = ((f32[16,64,128]{2,1,0:T(8,128)}), f32[16,64,128]{2,1,0:T(8,128)S(1)}, u32[]{:S(2)}, u32[]{:S(2)}) async-start(f32[16,64,128]{2,1,0:T(8,128)} %bitcast.5), calls=%async_computation.1 | async-start | bytes 1048576 | tf_op jit(solution)/shard_map/all_to_all | solution.py:389
  96.9 16.9 %collective-permute-start.3 = (f32[8,72,128]{2,1,0:T(8,128)S(1)}, f32[8,72,128]{2,1,0:T(8,128)S(1)}, u32[]{:S(2)}, u32[]{:S(2)}) collective-permute-start(f32[8,72,128]{2,1,0:T(8,128)S(1)} %all_to_all.37.same), channel_id=1, source_target_pairs={{0,1},{1,0},{2,3},{3,2},{4,5},{5,4},{6,7},{7,6},{8,9},{9,8},{10,11... | collective-permute-start | bytes 884744 | tf_op jit(solution)/shard_map/ppermute | solution.py:385
  116.5 3.4 %collective-permute-start.4 = (f32[512,128]{1,0:T(8,128)S(1)}, f32[512,128]{1,0:T(8,128)S(1)}, u32[]{:S(2)}, u32[]{:S(2)}) collective-permute-start(f32[512,128]{1,0:T(8,128)S(1)} %get-tuple-element.35), channel_id=1, source_target_pairs={{0,1},{1,64},{64,65},{65,128},{128,129},{129,192},{192,193},{193,2... | collective-permute-start | bytes 786440 | tf_op jit(solution)/shard_map/ppermute | solution.py:381
  116.6 5.9 %collective-permute-start.5 = (f32[512,128]{1,0:T(8,128)S(1)}, f32[512,128]{1,0:T(8,128)S(1)}, u32[]{:S(2)}, u32[]{:S(2)}) collective-permute-start(f32[512,128]{1,0:T(8,128)S(1)} %get-tuple-element.36), channel_id=1, source_target_pairs={{1,0},{64,1},{65,64},{128,65},{129,128},{192,129},{193,192},{2,193... | collective-permute-start | bytes 786440 | tf_op jit(solution)/shard_map/ppermute | solution.py:381
  126.6 5.2 %collective-permute-start.6 = (f32[8,72,128]{2,1,0:T(8,128)S(1)}, f32[8,72,128]{2,1,0:T(8,128)S(1)}, u32[]{:S(2)}, u32[]{:S(2)}) collective-permute-start(f32[8,72,128]{2,1,0:T(8,128)S(1)} %get-tuple-element.40), channel_id=1, source_target_pairs={{0,1},{1,0},{2,3},{3,2},{4,5},{5,4},{6,7},{7,6},{8,9},{9,8},{10,11... | collective-permute-start | bytes 884744 | tf_op jit(solution)/shard_map/ppermute | solution.py:385
  161.6 4.0 %collective-permute-start.7 = (f32[8,72,128]{2,1,0:T(8,128)S(1)}, f32[8,72,128]{2,1,0:T(8,128)S(1)}, u32[]{:S(2)}, u32[]{:S(2)}) collective-permute-start(f32[8,72,128]{2,1,0:T(8,128)S(1)} %all_to_all.39.same), channel_id=1, source_target_pairs={{0,1},{1,0},{2,3},{3,2},{4,5},{5,4},{6,7},{7,6},{8,9},{9,8},{10,11... | collective-permute-start | bytes 884744 | tf_op jit(solution)/shard_map/ppermute | solution.py:385

commit v2 on v1

--- a/solution.py
+++ b/solution.py
@@ -39,10 +39,11 @@
     return high, (a - high.astype(F32)).astype(BF16)
 
 
-def dot_split(a, b, dims=((1,), (0,))):
-    dims = (dims, ((), ()))
-    dot = functools.partial(lax.dot_general, dimension_numbers=dims, preferred_element_type=F32)
-    return dot(a[0], b[0]) + (dot(a[0], b[1]) + dot(a[1], b[0]))
+def dot_split(a, b, turned=False):
+    left = jnp.concatenate([a[0], a[0], a[1]], axis=1)
+    right = jnp.concatenate([b[0], b[1], b[0]], axis=1 if turned else 0)
+    dims = (((1,), (1 if turned else 0,)), ((), ()))
+    return lax.dot_general(left, right, dims, preferred_element_type=F32)
 
 
 def iota(shape, dim):
@@ -66,7 +67,23 @@
     last[...] = right[...].T[128 - HALO :, :]
 
 
-def observe_kernel(info, partner, column, level, value, error, live, coupling, out, mixing):
+def prepare_kernel(
+    info, partner, ens, column, level, value, error, live, coupling, state, out, mixing, tiles, blocks
+):
+    for t in range(4):
+        tiles[pl.ds(512 * t, 512), :] = ens[:, pl.ds(128 * t, 128)]
+    for f in range(2):
+        for t in range(4):
+            for m in range(8):
+                at = t * 512 + (m * 2 + f) * LEVELS
+                rows = [tiles[pl.ds(at + i, 8, stride=4), :] for i in range(4)]
+                for p, block in enumerate(chunk_transpose(rows)):
+                    blocks[pl.ds(f * 1024 + (4 * t + p) * 8 + m, 8, stride=128), :] = block
+        for four in range(8):
+            turned = blocks[pl.ds(f * 1024 + four * 128, 128), :].T
+            for i in range(4):
+                at = f * MINE * LEVELS + 4 * four + i
+                state[pl.ds(at, MINE, stride=LEVELS), :] = turned[32 * i : 32 * i + 32, :]
     member = jnp.bitwise_xor(iota((GROUP, COLS), 0), info[1])
     place = ((member >> 1) & 1) * 8 + (member >> 2) * 2 + (member & 1)
     spot = iota((64, COLS), 0)
@@ -97,118 +114,7 @@
     mixing[pl.ds(256, 256), :] = rest
 
 
-def first_kernel(info, ens, before, after, sums, mixing, heights, speeds, us, hs, tiles):
-    ring = COLS + 128
-    middle = jnp.zeros((128 - 2 * HALO, COLS), F32)
-    halo = jnp.concatenate([after[...], middle, before[...]], axis=0).T
-    for m in range(8):
-        for f, ref in enumerate((us, hs)):
-            at = (m * 2 + f) * LEVELS
-            ref[pl.ds(m * LEVELS, LEVELS), pl.ds(0, COLS)] = ens[pl.ds(at, LEVELS), :]
-            ref[pl.ds(m * LEVELS, LEVELS), pl.ds(COLS, 128)] = halo[at : at + LEVELS, :]
-    rate = 0.5 * TIME_STEP
-    mix = (mixing[pl.ds(0, 256), :], mixing[pl.ds(256, 256), :])
-
-    def slope(x):
-        return pltpu.roll(x, ring - 1, 1) - pltpu.roll(x, 1, 1)
-
-    for step in range(SUBSTEPS):
-        pressure = dot_split(mix, split(hs[...]))
-        for r in range(32):
-            rows = pl.ds(8 * r, 8)
-            u, h = us[rows, :], hs[rows, :]
-            moved = u - rate * (u * slope(u) + slope(pressure[8 * r : 8 * r + 8, :]))
-            height = h - rate * slope(moved * h)
-            if step < SUBSTEPS - 1:
-                us[rows, :] = moved
-                hs[rows, :] = height
-            else:
-                for t in range(4):
-                    for f, done in enumerate((moved, height)):
-                        tiles[pl.ds((f * 4 + t) * 256 + 8 * r, 8), :] = done[:, 128 * t : 128 * t + 128]
-    for f, (ref, size) in enumerate(((speeds, 64), (heights, 72))):
-        for t in range(4):
-            for m in range(8):
-                at = (f * 4 + t) * 256 + m * LEVELS
-                rows = [tiles[pl.ds(at + i, 8, stride=4), :] for i in range(4)]
-                for p, block in enumerate(chunk_transpose(rows)):
-                    g = jnp.bitwise_xor(MEMBER_AT[4 * t + p], info[1])
-                    ref[pl.ds(g * size + m, 8, stride=8), :] = block
-    for g in range(GROUP):
-        heights[pl.ds(g * 72 + 64, 8), :] = sums[pl.ds(g * 8, 8), :]
-
-
-def square_of(ref, at, size):
-    return jnp.concatenate([ref[pl.ds(g * size + at * 8, 8), :] for g in range(GROUP)], axis=0)
-
-
-def blend(fs, table, core, keep, send):
-    mine = core
-    for j in range(GROUP // 2):
-        for which, ref in ((mine, keep), (1 - mine, send)):
-            s = 2 * j + which
-            ref[j] = fs[s] + fs[table[s, 0]] + fs[table[s, 1]]
-
-
-def partial_gram(fs, q, flipped, anomaly, mean, weight, total):
-    pull = total - weight * mean
-    vector = jnp.sum(anomaly * pull, axis=0, keepdims=True)
-    gram = dot_split(split(flipped), split(anomaly * weight))
-    body, tail = fold(gram[:64], gram[64:], vector)
-    fs[q, pl.ds(0, 64), :] = body
-    fs[q, pl.ds(64, 8), :] = tail
-
-
-def first_gram_kernel(info, got, keep, send, later, table_out, fs, table, sem):
-    rows = got[pl.ds(66, GROUP, stride=72), :].astype(jnp.int32)
-    table_out[...] = rows
-    copy = pltpu.make_async_copy(table_out, table, sem)
-    copy.start()
-    hist = []
-    for cycle in range(2):
-        lines = got[pl.ds(64 + cycle, GROUP, stride=72), :]
-        hist.append(jnp.concatenate([lines, jnp.zeros((128 - GROUP, 128), F32)], axis=0).T)
-    later[...] = hist[1]
-    for four in range(8):
-        square = square_of(got, four, 72)
-        square = square - jnp.mean(square, axis=0, keepdims=True)
-        mean = jnp.mean(square_of(got, four, 72).T, axis=1, keepdims=True)
-        turned = square.T
-        for half in range(2):
-            q = 2 * four + half
-            at = slice(64 * half, 64 * half + 64)
-            partial_gram(
-                fs, q, square[:, at], turned[at, :], mean[at], hist[0][:64, q : q + 1], hist[0][64:, q : q + 1]
-            )
-    copy.wait()
-    blend(fs, table, info[0], keep, send)
-
-
-def fold(top, bottom, vector):
-    row, lane = iota((64, 128), 0), iota((64, 128), 1)
-    body = jnp.where((lane >= 64) | (row <= lane), top, pltpu.roll(bottom, 64, 1))
-    diagonal = jnp.sum(jnp.where(lane == row + 64, bottom, 0.0), axis=0, keepdims=True)
-    tail = jnp.where(iota((8, 128), 0) == 0, diagonal, vector)
-    return body, tail
-
-
-def unfold(body, tail):
-    row, lane = iota((64, 128), 0), iota((64, 128), 1)
-    top = jnp.where((lane >= 64) | (row < lane), body, jnp.where(row == lane, 0.5 * body, 0.0))
-    moved = pltpu.roll(body, 64, 1)
-    bottom = jnp.where(row > lane - 64, moved, jnp.where(row == lane - 64, 0.5 * tail[0:1, :], 0.0))
-    bottom = jnp.where(lane >= 64, bottom, 0.0)
-    half = jnp.concatenate([top, bottom], axis=0)
-    return half + half.T, tail[1:2, :]
-
-
-def forecast_kernel(table, info, state, low, high, hist, mixing, out, keep, send, us, hs, ps, fs):
-    edge = HALO * LEVELS
-    span = MINE * LEVELS
-    for f, ref in enumerate((us, hs)):
-        ref[pl.ds(0, edge), :] = low[pl.ds(f * edge, edge), :]
-        ref[pl.ds(edge, span), :] = state[pl.ds(f * span, span), :]
-        ref[pl.ds(edge + span, edge), :] = high[pl.ds(f * edge, edge), :]
+def substeps(us, hs, ps, mixing):
     rate = 0.5 * TIME_STEP
     mix = (mixing[pl.ds(0, 256), :], mixing[pl.ds(256, 256), :])
 
@@ -236,16 +142,116 @@
             us[pl.ds(c * LEVELS, LEVELS), :] = moved
             before, here = here, after
             flux_two, flux_one, height_one = flux_one, flux, height
+
+
+def four_levels(ref, at, four):
+    rows = [ref[pl.ds(at + 4 * four + i, MINE, stride=LEVELS), :] for i in range(4)]
+    return jnp.concatenate(rows, axis=0)
+
+
+def first_kernel(info, state, before, after, sums, mixing, packed, us, hs, ps, spare):
+    span = MINE * LEVELS
+    edge = HALO * LEVELS
+    pieces = []
+    for ref in (before, after):
+        for m in range(8):
+            line = ref[:, pl.ds(128 * (m // 2), 128)]
+            spare[pl.ds(8 * m, 8), :] = line if m % 2 == 0 else pltpu.roll(line, 64, 1)
+        pieces += [spare[pl.ds(c, 8, stride=8), :] for c in range(8)]
+    halo = jnp.concatenate(pieces, axis=0).T
+    lane = iota((LEVELS, 128), 1)
+    for f, ref in enumerate((us, hs)):
+        ref[pl.ds(edge, span), :] = state[pl.ds(f * span, span), :]
+        line = halo[f * LEVELS : (f + 1) * LEVELS, :]
+        for c in range(HALO):
+            inner = pltpu.roll(state[pl.ds(f * span + (MINE - HALO + c) * LEVELS, LEVELS), :], 8, 1)
+            outer = pltpu.roll(line, (128 - 8 * c) % 128, 1)
+            ref[pl.ds(c * LEVELS, LEVELS), :] = jnp.where(lane < 8, outer, inner)
+            inner = pltpu.roll(state[pl.ds(f * span + c * LEVELS, LEVELS), :], 120, 1)
+            outer = pltpu.roll(line, (56 - 8 * c) % 128, 1)
+            ref[pl.ds(edge + span + c * LEVELS, LEVELS), :] = jnp.where(lane >= 120, outer, inner)
+    substeps(us, hs, ps, mixing)
+    starts = [jnp.bitwise_xor(MEMBER_AT[k], info[1]) * 136 for k in range(GROUP)]
+    for base, ref in ((72, us), (0, hs)):
+        for four in range(8):
+            square = four_levels(ref, edge, four).T
+            for k in range(GROUP):
+                packed[pl.ds(starts[k] + (base + 8 * four), 8), :] = square[8 * k : 8 * k + 8, :]
+    for g in range(GROUP):
+        packed[pl.ds(g * 136 + 64, 8), :] = sums[pl.ds(g * 8, 8), :]
+
+
+def square_of(ref, base, four):
+    return jnp.concatenate([ref[pl.ds(g * 136 + base + four * 8, 8), :] for g in range(GROUP)], axis=0)
+
+
+def blend(fs, table, core, keep, send):
+    for j in range(GROUP // 2):
+        for which, ref in ((core, keep), (1 - core, send)):
+            s = 2 * j + which
+            ref[j] = fs[s] + fs[table[s, 0]] + fs[table[s, 1]]
+
+
+def gram_pair(fs, four, square, lines):
+    mean = jnp.mean(square, axis=0, keepdims=True)
+    anomaly = square - mean
+    halves = split(anomaly)
+    lane = iota((1, 128), 1)
+    for half in range(2):
+        q = 2 * four + half
+        line = lines(q)
+        swapped = pltpu.roll(line, 64, 1)
+        mine = (lane >= 64) if half else (lane < 64)
+        weight = jnp.where(mine, swapped if half else line, 0.0)
+        pull = jnp.where(mine, line if half else swapped, 0.0) - weight * mean
+        left = jnp.concatenate([anomaly * weight, jnp.broadcast_to(pull, (8, 128))], axis=0)
+        gram = dot_split(split(left), halves, turned=True)
+        body, tail = fold(gram[:64], gram[64:128], gram[128:129])
+        fs[q, pl.ds(0, 64), :] = body
+        fs[q, pl.ds(64, 8), :] = tail
+
+
+def first_gram_kernel(info, got, keep, send, later, table_out, fs, table, sem):
+    table_out[...] = got[pl.ds(66, GROUP, stride=136), :].astype(jnp.int32)
+    copy = pltpu.make_async_copy(table_out, table, sem)
+    copy.start()
+    later[...] = got[pl.ds(65, GROUP, stride=136), :]
+    for four in range(8):
+        gram_pair(fs, four, square_of(got, 0, four), lambda q: got[pl.ds(q * 136 + 64, 1), :])
+    copy.wait()
+    blend(fs, table, info[0], keep, send)
+
+
+def fold(top, bottom, vector):
+    row, lane = iota((64, 128), 0), iota((64, 128), 1)
+    body = jnp.where((lane >= 64) | (row <= lane), top, pltpu.roll(bottom, 64, 1))
+    diagonal = jnp.sum(jnp.where(lane == row + 64, bottom, 0.0), axis=0, keepdims=True)
+    tail = jnp.where(iota((8, 128), 0) == 0, diagonal, vector)
+    return body, tail
+
+
+def unfold(body, tail):
+    row, lane = iota((64, 128), 0), iota((64, 128), 1)
+    top = jnp.where((lane >= 64) | (row < lane), body, jnp.where(row == lane, 0.5 * body, 0.0))
+    moved = pltpu.roll(body, 64, 1)
+    bottom = jnp.where(row > lane - 64, moved, jnp.where(row == lane - 64, 0.5 * tail[0:1, :], 0.0))
+    bottom = jnp.where(lane >= 64, bottom, 0.0)
+    half = jnp.concatenate([top, bottom], axis=0)
+    return half + half.T, tail[1:2, :]
+
+
+def forecast_kernel(table, info, state, low, high, hist, mixing, out, keep, send, us, hs, ps, fs):
+    edge = HALO * LEVELS
+    span = MINE * LEVELS
+    for f, ref in enumerate((us, hs)):
+        ref[pl.ds(0, edge), :] = low[pl.ds(f * edge, edge), :]
+        ref[pl.ds(edge, span), :] = state[pl.ds(f * span, span), :]
+        ref[pl.ds(edge + span, edge), :] = high[pl.ds(f * edge, edge), :]
+    substeps(us, hs, ps, mixing)
     out[pl.ds(0, span), :] = us[pl.ds(edge, span), :]
     out[pl.ds(span, span), :] = hs[pl.ds(edge, span), :]
-
-    for q in range(GROUP):
-        field = jnp.concatenate(
-            [hs[pl.ds(edge + 2 * q + j, MINE, stride=LEVELS), :] for j in range(2)], axis=0
-        )
-        mean = jnp.mean(field, axis=1, keepdims=True)
-        anomaly = field - mean
-        partial_gram(fs, q, anomaly.T, anomaly, mean, hist[pl.ds(0, 64), q : q + 1], hist[pl.ds(64, 64), q : q + 1])
+    for four in range(8):
+        gram_pair(fs, four, four_levels(hs, edge, four).T, lambda q: hist[pl.ds(q, 1), :])
     blend(fs, table, info[0], keep, send)
 
 
@@ -262,19 +268,19 @@
     norm = jnp.sqrt(squared)
     a = blended / norm
     newton = 1.5 * eye - 0.5 * a
-    s = split(newton)
-    a = dot_split(split(a), s)
+    a = dot_split(split(a), split(newton))
     z = newton
     for step in range(1, ROOT_STEPS):
         newton = 1.5 * eye - 0.5 * dot_split(split(z), split(a))
-        s = split(newton)
         if step < ROOT_STEPS - 1:
-            a = dot_split(split(a), s)
-        z = dot_split(s, split(z))
+            both = dot_split(split(jnp.concatenate([a, z], axis=0)), split(newton))
+            a, z = both[:WIDTH], both[WIDTH:]
+        else:
+            z = dot_split(split(z), split(newton))
     halves = split(z)
     wide = jnp.broadcast_to(pull, (8, WIDTH))
-    inner = dot_split(split(wide), halves, ((1,), (1,)))
-    shift = dot_split(split(inner), halves, ((1,), (1,)))[0:1, :] / norm
+    inner = dot_split(split(wide), halves, turned=True)
+    shift = dot_split(split(inner), halves, turned=True)[0:1, :] / norm
     spread = z * (math.sqrt(WIDTH - 1.0) / jnp.sqrt(norm))
     body, tail = fold(spread[:64], spread[64:], shift)
     for j in range(8):
@@ -288,12 +294,12 @@
         both[2 * j + 1 - info[0]] = other[j]
 
 
-def first_apply_kernel(info, heights, speeds, same, other, out, low, high, both):
+def first_apply_kernel(info, got, same, other, out, low, high, both):
     gather_roots(info, same, other, both)
     span = MINE * LEVELS
     edge = HALO * LEVELS
     for four in range(8):
-        fields = (square_of(speeds, four, 64), square_of(heights, four, 72))
+        fields = (square_of(got, 72, four), square_of(got, 0, four))
         for half in range(2):
             s = 2 * four + half
             spread, shift = unfold(both[s, pl.ds(0, 64), :], both[s, pl.ds(64, 8), :])
@@ -330,10 +336,10 @@
 
 
 def place_kernel(info, got, out, tiles):
-    for n in range(8):
-        for t in range(4):
-            members = [jnp.bitwise_xor(MEMBER_AT[4 * t + p], info[1]) for p in range(4)]
-            rows = [got[pl.ds(g * 128 + n, 16, stride=8), :] for g in members]
+    starts = [jnp.bitwise_xor(MEMBER_AT[k], info[1]) * 128 for k in range(GROUP)]
+    for t in range(4):
+        for n in range(8):
+            rows = [got[pl.ds(starts[4 * t + p] + n, 16, stride=8), :] for p in range(4)]
             for fj, block in enumerate(chunk_transpose(rows)):
                 f, j = fj // 2, fj % 2
                 tiles[pl.ds(512 * t + (n * 2 + f) * LEVELS + j, 16, stride=2), :] = block
@@ -405,28 +411,30 @@
     ring = [(i, (i + 1) % 16) for i in range(16)]
     before = lax.ppermute(last, "hor", ring)
     after = lax.ppermute(first, "hor", [(b, a) for a, b in ring])
-    sums, mixing = call(
-        observe_kernel, (arr(128, 128), arr(512, 256, dtype=BF16)), [smem()] * 2 + [vmem()] * 6, "observe"
-    )(info, partners, obs_column, obs_level, obs_value, obs_error, obs_live, coupling)
-    heights, speeds = call(
+    state, sums, mixing = call(
+        prepare_kernel,
+        (arr(2 * rows, 128), arr(128, 128), arr(512, 256, dtype=BF16)),
+        [smem()] * 2 + [vmem()] * 7,
+        "prepare",
+        [pltpu.VMEM((2048, 128), F32), pltpu.VMEM((2048, 128), F32)],
+    )(info, partners, members, obs_column, obs_level, obs_value, obs_error, obs_live, coupling)
+    wide = pltpu.VMEM((WIDE * LEVELS, WIDTH), F32)
+    packed = call(
         first_kernel,
-        (arr(GROUP * 72, 128), arr(GROUP * 64, 128)),
+        arr(GROUP * 136, 128),
         [smem()] + [vmem()] * 5,
         "first",
-        [pltpu.VMEM((256, COLS + 128), F32), pltpu.VMEM((256, COLS + 128), F32), pltpu.VMEM((2048, 128), F32)],
-    )(info, members, before, after, sums, mixing)
-    heights = exchange(heights.reshape(GROUP, 72, 128), TILE)
-    speeds, heights = lax.optimization_barrier((speeds, heights))
-    heights = heights.reshape(GROUP * 72, 128)
-    speeds = exchange(speeds.reshape(GROUP, 64, 128), TILE).reshape(GROUP * 64, 128)
+        [wide, wide, wide, pltpu.VMEM((64, 128), F32)],
+    )(info, state, before, after, sums, mixing)
+    received = exchange(packed.reshape(GROUP, 136, 128), TILE).reshape(GROUP * 136, 128)
     folded = pltpu.VMEM((GROUP, FOLD, 128), F32)
     keep, send, hist, table = call(
         first_gram_kernel,
-        (arr(8, FOLD, 128), arr(8, FOLD, 128), arr(128, 128), arr(GROUP, 128, dtype=jnp.int32)),
+        (arr(8, FOLD, 128), arr(8, FOLD, 128), arr(GROUP, 128), arr(GROUP, 128, dtype=jnp.int32)),
         [smem(), vmem()],
         "gram",
         [folded, pltpu.SMEM((GROUP, 128), jnp.int32), pltpu.SemaphoreType.DMA(())],
-    )(info, heights)
+    )(info, received)
 
     def roots(keep, send):
         parts = exchange(keep + swap(send), CHIPS)
@@ -438,13 +446,12 @@
     state, low, high = call(
         first_apply_kernel,
         (arr(2 * rows, WIDTH), arr(edges, WIDTH), arr(edges, WIDTH)),
-        [smem()] + [vmem()] * 4,
+        [smem()] + [vmem()] * 3,
         "apply",
         [folded],
-    )(info, heights, speeds, same, other)
+    )(info, received, same, other)
     from_low = across(high, True)
     from_high = across(low, False)
-    wide = pltpu.VMEM((WIDE * LEVELS, WIDTH), F32)
     state, keep, send = call(
         forecast_kernel,
         (arr(2 * rows, WIDTH), arr(8, FOLD, 128), arr(8, FOLD, 128)),

time: 202 us -> 178 us (0.88)
  Pallas kernels: 42.5 us -> 27.4 us
  waiting for transfers between devices: 26 us -> 11.3 us
  blocking collectives: 112 us -> 123 us
  starting transfers between devices: 19.5 us -> 15.7 us
    all_to_all x1 -> x0, waiting for transfers between devices: 16.6 us -> none  [exchange(): return lax.all_to_all(x, axes, split_axis=0, concat_axis=0, tiled=True)]
    pallas_call x3, Pallas kernels: 22.5 us -> 8.01 us  [the longest x1 3.45 us: shards(): call(first_kernel, arr(GROUP * 136, 128), [smem()] + [vmem()] * 5, 'first...]
    all_to_all x6, blocking collectives: 112 us -> 123 us  [exchange(): return lax.all_to_all(x, axes, split_axis=0, concat_axis=0, tiled=True)]
    all_to_all x1 -> x0, starting transfers between devices: 5.96 us -> none  [exchange(): return lax.all_to_all(x, axes, split_axis=0, concat_axis=0, tiled=True)]
  transfers between devices with their start and end apart: 9 -> 8, of which waited for: 6 -> 6; matrix products, arithmetic and copies ran while one was open for 0% -> 0% of each run, Pallas kernels for 1% -> 1%
where the time goes in v2:
time: 178 us
  blocking collectives  123 us (69%)
  Pallas kernels  27.4 us (15%)
  starting transfers between devices  15.7 us (9%)
  waiting for transfers between devices  11.3 us (6%)
    all_to_all x6, blocking collectives, exchange(): return lax.all_to_all(x, axes, split_axis=0, concat_axis=0, tiled=True)  123 us
    ppermute x4, starting transfers between devices, swap(): return lax.ppermute(x, 'core', [(0, 1), (1, 0)])  8.32 us
    pallas_call x2, Pallas kernels, roots(): copies = call(root_kernel, arr(8, FOLD, 128), [vmem()], 'root')(parts)  6.1 us
    ppermute x2, waiting for transfers between devices, across(): return lax.ppermute(x, ALL, pairs)  6.09 us
    ppermute x4, waiting for transfers between devices, swap(): return lax.ppermute(x, 'core', [(0, 1), (1, 0)])  5.19 us
    pallas_call x1, Pallas kernels, shards(): call(forecast_kernel, (arr(2 * rows, WIDTH), arr(8, FOLD, 128), arr(8, FO...  3.99 us
    ppermute x1, starting transfers between devices, shards(): after = lax.ppermute(first, 'hor', [(b, a) for a, b in ring])  3.72 us
  transfers between devices with their start and end apart: 8, of which 6 were waited for; matrix products, arithmetic and copies ran while one was open for 0% of the time, Pallas kernels for 1%

profile of v2, /device:TPU:1, one launch (start us, length us, event | category | flops | bytes accessed | tf_op | source)
XLA Modules:
  0.0 178.2 jit_solution(9387210913679646013)
XLA Ops:
  0.1 1.9 %edges.1 = (f32[8,512]{1,0:T(8,128)}, f32[8,512]{1,0:T(8,128)}) custom-call(f32[512,512]{1,0:T(8,128)} %bitcast.10, f32[512,512]{1,0:T(8,128)} %bitcast.11), custom_call_target="tpu_custom_call" | custom-call | tf_op jit(solution)/shard_map/edges/pallas_call | solution.py:403
  2.0 2.0 %collective-permute-start = (f32[8,512]{1,0:T(8,128)}, f32[8,512]{1,0:T(8,128)S(1)}, u32[]{:S(2)}, u32[]{:S(2)}) collective-permute-start(f32[8,512]{1,0:T(8,128)} %get-tuple-element.21), channel_id=1, source_target_pairs={{0,4},{4,8},{8,12},{12,16},{16,20},{20,24},{24,28},{28,32},{32,36}... | collective-permute-start | bytes 49160 | tf_op jit(solution)/shard_map/ppermute | solution.py:412
  4.0 3.7 %collective-permute-start.1 = (f32[8,512]{1,0:T(8,128)}, f32[8,512]{1,0:T(8,128)S(1)}, u32[]{:S(2)}, u32[]{:S(2)}) collective-permute-start(f32[8,512]{1,0:T(8,128)} %get-tuple-element.22), channel_id=1, source_target_pairs={{4,0},{8,4},{12,8},{16,12},{20,16},{24,20},{28,24},{32,28},{36,32}... | collective-permute-start | bytes 49160 | tf_op jit(solution)/shard_map/ppermute | solution.py:413
  7.7 0.1 pad_add_fusion.info
  7.9 2.4 %prepare.1 = (f32[2048,128]{1,0:T(8,128)S(1)}, f32[128,128]{1,0:T(8,128)S(1)}, bf16[512,256]{1,0:T(8,128)(2,1)S(1)}) custom-call(s32[2]{0:T(128)S(1)} %pad_add_fusion.info, s32[1,1,2]{2,1,0:T(1,128)S(1)} %copy-done.7, f32[512,512]{1,0:T(8,128)S(1)} %bitcast.12, s32[2,1,1,512]{3,2,1,0:T(1,128)S(1)} %copy-done.2, s32[2,1,1,512]{3,2,1,0:T(1,128)S(1)} %copy-done.3, ...), custom_call_target="tpu_custom_call" | custom-call | tf_op jit(solution)/shard_map/prepare/pallas_call | solution.py:414
  10.3 0.0 collective-permute-done.before
  10.3 0.0 collective-permute-done.1.after
  10.3 3.5 %first.1 = f32[2176,128]{1,0:T(8,128)S(1)} custom-call(s32[2]{0:T(128)S(1)} %pad_add_fusion.info, f32[2048,128]{1,0:T(8,128)S(1)} %get-tuple-element.20.state, f32[8,512]{1,0:T(8,128)S(1)} %collective-permute-done.before, f32[8,512]{1,0:T(8,128)S(1)} %collective-permute-done.1.after, f32[128,128]{1,0:T(8,128)S(1)} %get-tuple-element.23.sums, ...), custom_call_target="tpu_custom_call" | custom-call | tf_op jit(solution)/shard_map/first/pallas_call | solution.py:422
  13.8 39.6 %all_to_all.30 = f32[16,136,128]{2,1,0:T(8,128)S(1)} all-to-all(f32[16,136,128]{2,1,0:T(8,128)S(1)} %bitcast.13), channel_id=1, replica_groups=mesh['mem'=4,'hor'=16,'zh'=2,'core'=2] {'mem','zh','core'}, dimensions={0} | all-to-all | bytes 2228224 | tf_op jit(solution)/shard_map/all_to_all | solution.py:395
  53.3 2.2 %gram.1 = (f32[8,72,128]{2,1,0:T(8,128)S(1)}, f32[8,72,128]{2,1,0:T(8,128)S(1)}, f32[16,128]{1,0:T(8,128)S(1)}, s32[16,128]{1,0:T(8,128)S(1)}) custom-call(s32[2]{0:T(128)S(1)} %pad_add_fusion.info, f32[2176,128]{1,0:T(8,128)S(1)} %bitcast.8), custom_call_target="tpu_custom_call" | custom-call | tf_op jit(solution)/shard_map/gram/pallas_call | solution.py:431
  55.5 0.1 collective-permute-start.2
  55.6 1.6 collective-permute-done.2
  57.2 13.4 %all_to_all.31.got = f32[8,72,128]{2,1,0:T(8,128)S(1)} all-to-all(f32[8,72,128]{2,1,0:T(8,128)S(1)} %add.6), channel_id=1, replica_groups=mesh['mem'=4,'hor'=16,'zh'=2,'core'=2] {'mem','zh'}, dimensions={0} | all-to-all | bytes 589824 | tf_op jit(solution)/shard_map/all_to_all | solution.py:395
  70.6 3.1 %root.2 = f32[8,72,128]{2,1,0:T(8,128)S(1)} custom-call(f32[8,72,128]{2,1,0:T(8,128)S(1)} %all_to_all.31.got), custom_call_target="tpu_custom_call" | custom-call | tf_op jit(solution)/shard_map/root/pallas_call | solution.py:441
  73.6 13.3 %all_to_all.32.same = f32[8,72,128]{2,1,0:T(8,128)S(1)} all-to-all(f32[8,72,128]{2,1,0:T(8,128)S(1)} %root.2), channel_id=1, replica_groups=mesh['mem'=4,'hor'=16,'zh'=2,'core'=2] {'mem','zh'}, dimensions={0} | all-to-all | bytes 589824 | tf_op jit(solution)/shard_map/all_to_all | solution.py:395
  86.9 2.6 %collective-permute-start.3 = (f32[8,72,128]{2,1,0:T(8,128)S(1)}, f32[8,72,128]{2,1,0:T(8,128)S(1)}, u32[]{:S(2)}, u32[]{:S(2)}) collective-permute-start(f32[8,72,128]{2,1,0:T(8,128)S(1)} %all_to_all.32.same), channel_id=1, source_target_pairs={{0,1},{1,0},{2,3},{3,2},{4,5},{5,4},{6,7},{7,6},{8,9},{9,8},{10,11... | collective-permute-start | bytes 884744 | tf_op jit(solution)/shard_map/ppermute | solution.py:391
  89.5 1.2 collective-permute-done.3.other
  90.7 2.6 %apply.1 = (f32[2048,128]{1,0:T(8,128)S(1)}, f32[512,128]{1,0:T(8,128)S(1)}, f32[512,128]{1,0:T(8,128)S(1)}) custom-call(s32[2]{0:T(128)S(1)} %pad_add_fusion.info, f32[2176,128]{1,0:T(8,128)S(1)} %bitcast.9, f32[8,72,128]{2,1,0:T(8,128)S(1)} %all_to_all.32.same, f32[8,72,128]{2,1,0:T(8,128)S(1)} %collective-permute-done.3.other), custom_call_target="tpu_custom_call" | custom-call | tf_op jit(solution)/shard_map/apply/pallas_call | solution.py:446
  93.3 1.6 collective-permute-start.4
  95.0 3.3 %collective-permute-done.4.low = f32[512,128]{1,0:T(8,128)S(1)} collective-permute-done((f32[512,128]{1,0:T(8,128)S(1)}, f32[512,128]{1,0:T(8,128)S(1)}, u32[]{:S(2)}, u32[]{:S(2)}) %collective-permute-start.4) | collective-permute-done | bytes 262176 | tf_op jit(solution)/shard_map/ppermute | solution.py:387
  98.3 2.8 %collective-permute-done.5.high = f32[512,128]{1,0:T(8,128)S(1)} collective-permute-done((f32[512,128]{1,0:T(8,128)S(1)}, f32[512,128]{1,0:T(8,128)S(1)}, u32[]{:S(2)}, u32[]{:S(2)}) %collective-permute-start.5) | collective-permute-done | bytes 262176 | tf_op jit(solution)/shard_map/ppermute | solution.py:387
  101.1 4.0 %forecast.1 = (f32[2048,128]{1,0:T(8,128)S(1)}, f32[8,72,128]{2,1,0:T(8,128)S(1)}, f32[8,72,128]{2,1,0:T(8,128)S(1)}) custom-call(s32[16,128]{1,0:T(8,128)S(1)} %get-tuple-element.25.table, s32[2]{0:T(128)S(1)} %pad_add_fusion.info, f32[2048,128]{1,0:T(8,128)S(1)} %get-tuple-element.28.state, f32[512,128]{1,0:T(8,128)S(1)} %collective-permute-done.4.low, ...), custom_call_target="tpu_custom_call" | custom-call | tf_op jit(solution)/shard_map/forecast/pallas_call | solution.py:455
  105.1 2.7 %collective-permute-start.6 = (f32[8,72,128]{2,1,0:T(8,128)S(1)}, f32[8,72,128]{2,1,0:T(8,128)S(1)}, u32[]{:S(2)}, u32[]{:S(2)}) collective-permute-start(f32[8,72,128]{2,1,0:T(8,128)S(1)} %get-tuple-element.34), channel_id=1, source_target_pairs={{0,1},{1,0},{2,3},{3,2},{4,5},{5,4},{6,7},{7,6},{8,9},{9,8},{10,11... | collective-permute-start | bytes 884744 | tf_op jit(solution)/shard_map/ppermute | solution.py:391
  107.7 1.2 collective-permute-done.6
  109.0 12.9 %all_to_all.33.got = f32[8,72,128]{2,1,0:T(8,128)S(1)} all-to-all(f32[8,72,128]{2,1,0:T(8,128)S(1)} %add.7), channel_id=1, replica_groups=mesh['mem'=4,'hor'=16,'zh'=2,'core'=2] {'mem','zh'}, dimensions={0} | all-to-all | bytes 589824 | tf_op jit(solution)/shard_map/all_to_all | solution.py:395
  121.9 3.1 %root.3 = f32[8,72,128]{2,1,0:T(8,128)S(1)} custom-call(f32[8,72,128]{2,1,0:T(8,128)S(1)} %all_to_all.33.got), custom_call_target="tpu_custom_call" | custom-call | tf_op jit(solution)/shard_map/root/pallas_call | solution.py:441
  125.0 13.2 %all_to_all.34.same = f32[8,72,128]{2,1,0:T(8,128)S(1)} all-to-all(f32[8,72,128]{2,1,0:T(8,128)S(1)} %root.3), channel_id=1, replica_groups=mesh['mem'=4,'hor'=16,'zh'=2,'core'=2] {'mem','zh'}, dimensions={0} | all-to-all | bytes 589824 | tf_op jit(solution)/shard_map/all_to_all | solution.py:395
  138.1 2.9 %collective-permute-start.7 = (f32[8,72,128]{2,1,0:T(8,128)S(1)}, f32[8,72,128]{2,1,0:T(8,128)S(1)}, u32[]{:S(2)}, u32[]{:S(2)}) collective-permute-start(f32[8,72,128]{2,1,0:T(8,128)S(1)} %all_to_all.34.same), channel_id=1, source_target_pairs={{0,1},{1,0},{2,3},{3,2},{4,5},{5,4},{6,7},{7,6},{8,9},{9,8},{10,11... | collective-permute-start | bytes 884744 | tf_op jit(solution)/shard_map/ppermute | solution.py:391
  141.1 1.2 collective-permute-done.7.other
  142.3 2.3 %analyse.1 = f32[2048,128]{1,0:T(8,128)S(1)} custom-call(s32[2]{0:T(128)S(1)} %pad_add_fusion.info, f32[2048,128]{1,0:T(8,128)S(1)} %get-tuple-element.32.state, f32[8,72,128]{2,1,0:T(8,128)S(1)} %all_to_all.34.same, f32[8,72,128]{2,1,0:T(8,128)S(1)} %collective-permute-done.7.other), custom_call_target="tpu_custom_call" | custom-call | tf_op jit(solution)/shard_map/analyse/pallas_call | solution.py:463
  144.6 31.1 %all_to_all.35 = f32[16,128,128]{2,1,0:T(8,128)S(1)} all-to-all(f32[16,128,128]{2,1,0:T(8,128)S(1)} %bitcast.15), channel_id=1, replica_groups=mesh['mem'=4,'hor'=16,'zh'=2,'core'=2] {'mem','zh','core'}, dimensions={0} | all-to-all | bytes 2097152 | tf_op jit(solution)/shard_map/all_to_all | solution.py:395
  175.7 2.5 %place.1 = f32[512,512]{1,0:T(8,128)} custom-call(s32[2]{0:T(128)S(1)} %pad_add_fusion.info, f32[2048,128]{1,0:T(8,128)S(1)} %bitcast.14), custom_call_target="tpu_custom_call" | custom-call | tf_op jit(solution)/shard_map/place/pallas_call | solution.py:467
  (19 shorter events, 0.1 us)
Async XLA Ops:
  0.0 7.8 %copy-start = (f32[8,2,32,512]{3,2,1,0:T(8,128)S(1)}, f32[8,2,32,512]{3,2,1,0:T(8,128)}, u32[]{:S(2)}) copy-start(f32[8,2,32,512]{3,2,1,0:T(8,128)} %param.8) | copy-start | bytes 3145732
  0.0 7.8 %copy-start.7 = (s32[1,1,2]{2,1,0:T(1,128)S(1)}, s32[1,1,2]{2,1,0:T(1,128)}, u32[]{:S(2)}) copy-start(s32[1,1,2]{2,1,0:T(1,128)} %partner.1) | copy-start | bytes 28
  0.0 7.8 %copy-start.6 = (s32[2,1,1,512]{3,2,1,0:T(1,128)S(1)}, s32[2,1,1,512]{3,2,1,0:T(1,128)}, u32[]{:S(2)}) copy-start(s32[2,1,1,512]{3,2,1,0:T(1,128)} %live.1) | copy-start | bytes 12292
  0.0 7.8 %copy-start.5 = (f32[2,1,1,512]{3,2,1,0:T(1,128)S(1)}, f32[2,1,1,512]{3,2,1,0:T(1,128)}, u32[]{:S(2)}) copy-start(f32[2,1,1,512]{3,2,1,0:T(1,128)} %error.1) | copy-start | bytes 12292
  0.0 7.8 %copy-start.4 = (f32[2,1,1,512]{3,2,1,0:T(1,128)S(1)}, f32[2,1,1,512]{3,2,1,0:T(1,128)}, u32[]{:S(2)}) copy-start(f32[2,1,1,512]{3,2,1,0:T(1,128)} %value.1) | copy-start | bytes 12292
  0.0 7.8 %copy-start.3 = (s32[2,1,1,512]{3,2,1,0:T(1,128)S(1)}, s32[2,1,1,512]{3,2,1,0:T(1,128)}, u32[]{:S(2)}) copy-start(s32[2,1,1,512]{3,2,1,0:T(1,128)} %level.1) | copy-start | bytes 12292
  0.0 7.8 %copy-start.2 = (s32[2,1,1,512]{3,2,1,0:T(1,128)S(1)}, s32[2,1,1,512]{3,2,1,0:T(1,128)}, u32[]{:S(2)}) copy-start(s32[2,1,1,512]{3,2,1,0:T(1,128)} %column.1) | copy-start | bytes 12292
  0.0 7.8 %copy-start.1 = (f32[32,32]{1,0:T(8,128)S(1)}, f32[32,32]{1,0:T(8,128)}, u32[]{:S(2)}) copy-start(f32[32,32]{1,0:T(8,128)} %coupling.1) | copy-start | bytes 12292
  2.0 8.3 %collective-permute-start = (f32[8,512]{1,0:T(8,128)}, f32[8,512]{1,0:T(8,128)S(1)}, u32[]{:S(2)}, u32[]{:S(2)}) collective-permute-start(f32[8,512]{1,0:T(8,128)} %get-tuple-element.21), channel_id=1, source_target_pairs={{0,4},{4,8},{8,12},{12,16},{16,20},{20,24},{24,28},{28,32},{32,36}... | collective-permute-start | bytes 49160 | tf_op jit(solution)/shard_map/ppermute | solution.py:412
  4.0 6.3 %collective-permute-start.1 = (f32[8,512]{1,0:T(8,128)}, f32[8,512]{1,0:T(8,128)S(1)}, u32[]{:S(2)}, u32[]{:S(2)}) collective-permute-start(f32[8,512]{1,0:T(8,128)} %get-tuple-element.22), channel_id=1, source_target_pairs={{4,0},{8,4},{12,8},{16,12},{20,16},{24,20},{28,24},{32,28},{36,32}... | collective-permute-start | bytes 49160 | tf_op jit(solution)/shard_map/ppermute | solution.py:413
  55.5 1.7 collective-permute-start.2
  86.9 3.8 %collective-permute-start.3 = (f32[8,72,128]{2,1,0:T(8,128)S(1)}, f32[8,72,128]{2,1,0:T(8,128)S(1)}, u32[]{:S(2)}, u32[]{:S(2)}) collective-permute-start(f32[8,72,128]{2,1,0:T(8,128)S(1)} %all_to_all.32.same), channel_id=1, source_target_pairs={{0,1},{1,0},{2,3},{3,2},{4,5},{5,4},{6,7},{7,6},{8,9},{9,8},{10,11... | collective-permute-start | bytes 884744 | tf_op jit(solution)/shard_map/ppermute | solution.py:391
  93.3 5.0 %collective-permute-start.4 = (f32[512,128]{1,0:T(8,128)S(1)}, f32[512,128]{1,0:T(8,128)S(1)}, u32[]{:S(2)}, u32[]{:S(2)}) collective-permute-start(f32[512,128]{1,0:T(8,128)S(1)} %get-tuple-element.29), channel_id=1, source_target_pairs={{0,1},{1,64},{64,65},{65,128},{128,129},{129,192},{192,193},{193,2... | collective-permute-start | bytes 786440 | tf_op jit(solution)/shard_map/ppermute | solution.py:387
  95.0 6.1 %collective-permute-start.5 = (f32[512,128]{1,0:T(8,128)S(1)}, f32[512,128]{1,0:T(8,128)S(1)}, u32[]{:S(2)}, u32[]{:S(2)}) collective-permute-start(f32[512,128]{1,0:T(8,128)S(1)} %get-tuple-element.30), channel_id=1, source_target_pairs={{1,0},{64,1},{65,64},{128,65},{129,128},{192,129},{193,192},{2,193... | collective-permute-start | bytes 786440 | tf_op jit(solution)/shard_map/ppermute | solution.py:387
  105.1 3.9 %collective-permute-start.6 = (f32[8,72,128]{2,1,0:T(8,128)S(1)}, f32[8,72,128]{2,1,0:T(8,128)S(1)}, u32[]{:S(2)}, u32[]{:S(2)}) collective-permute-start(f32[8,72,128]{2,1,0:T(8,128)S(1)} %get-tuple-element.34), channel_id=1, source_target_pairs={{0,1},{1,0},{2,3},{3,2},{4,5},{5,4},{6,7},{7,6},{8,9},{9,8},{10,11... | collective-permute-start | bytes 884744 | tf_op jit(solution)/shard_map/ppermute | solution.py:391
  138.1 4.1 %collective-permute-start.7 = (f32[8,72,128]{2,1,0:T(8,128)S(1)}, f32[8,72,128]{2,1,0:T(8,128)S(1)}, u32[]{:S(2)}, u32[]{:S(2)}) collective-permute-start(f32[8,72,128]{2,1,0:T(8,128)S(1)} %all_to_all.34.same), channel_id=1, source_target_pairs={{0,1},{1,0},{2,3},{3,2},{4,5},{5,4},{6,7},{7,6},{8,9},{9,8},{10,11... | collective-permute-start | bytes 884744 | tf_op jit(solution)/shard_map/ppermute | solution.py:391

commit v3 on v2

--- a/solution.py
+++ b/solution.py
@@ -114,33 +114,42 @@
     mixing[pl.ds(256, 256), :] = rest
 
 
-def substeps(us, hs, ps, mixing):
+def substeps(sources, both, ps, mixing):
     rate = 0.5 * TIME_STEP
     mix = (mixing[pl.ds(0, 256), :], mixing[pl.ds(256, 256), :])
-
-    def col(ref, c):
-        return ref[pl.ds(c * LEVELS, LEVELS), :]
+    wide = WIDE * LEVELS
+    for c in (0, WIDE - 2):
+        both[pl.ds(wide + c * LEVELS, 2 * LEVELS), :] = jnp.zeros((2 * LEVELS, WIDTH), F32)
+
+    def rows(step, f, c, count):
+        if step == 0:
+            ref, at = sources(f, c)
+            return ref[pl.ds(at, count * LEVELS), :]
+        return both[pl.ds(f * wide + c * LEVELS, count * LEVELS), :]
 
     for step in range(SUBSTEPS):
         lo, hi = 2 * step, WIDE - 2 * step
         for pair in range(3):
             block = jnp.concatenate(
-                [hs[pl.ds(pair * 512, 256), :], hs[pl.ds(pair * 512 + 256, 256), :]], axis=1
+                [rows(step, 1, 16 * pair, 8), rows(step, 1, 16 * pair + 8, 8)], axis=1
             )
             pressure = dot_split(mix, split(block))
             ps[pl.ds(pair * 512, 256), :] = pressure[:, :128]
             ps[pl.ds(pair * 512 + 256, 256), :] = pressure[:, 128:]
-        before, here = col(us, lo), col(us, lo + 1)
+        before, here = rows(step, 0, lo, 1), rows(step, 0, lo + 1, 1)
+        slope_one, slope_two = ps[pl.ds(lo * LEVELS, LEVELS), :], ps[pl.ds((lo + 1) * LEVELS, LEVELS), :]
         flux_two, flux_one, height_one = None, None, None
         for c in range(lo + 1, hi - 1):
-            after = col(us, c + 1)
-            moved = here - rate * (here * (after - before) + (col(ps, c + 1) - col(ps, c - 1)))
-            height = col(hs, c)
+            after = rows(step, 0, c + 1, 1)
+            slope = ps[pl.ds((c + 1) * LEVELS, LEVELS), :]
+            moved = here - rate * (here * (after - before) + (slope - slope_one))
+            height = rows(step, 1, c, 1)
             flux = moved * height
             if c >= lo + 3:
-                hs[pl.ds((c - 1) * LEVELS, LEVELS), :] = height_one - rate * (flux - flux_two)
-            us[pl.ds(c * LEVELS, LEVELS), :] = moved
+                both[pl.ds(wide + (c - 1) * LEVELS, LEVELS), :] = height_one - rate * (flux - flux_two)
+            both[pl.ds(c * LEVELS, LEVELS), :] = moved
             before, here = here, after
+            slope_one, slope_two = slope_two, slope
             flux_two, flux_one, height_one = flux_one, flux, height
 
 
@@ -149,7 +158,14 @@
     return jnp.concatenate(rows, axis=0)
 
 
-def first_kernel(info, state, before, after, sums, mixing, packed, us, hs, ps, spare):
+def slab_rows(ref, at, s):
+    rows = [
+        ref[pl.ds(f * WIDE * LEVELS + at + 2 * s + j, MINE, stride=LEVELS), :] for f in range(2) for j in range(2)
+    ]
+    return jnp.concatenate(rows, axis=0)
+
+
+def first_kernel(info, state, before, after, sums, mixing, packed, both, ps, sides, spare):
     span = MINE * LEVELS
     edge = HALO * LEVELS
     pieces = []
@@ -160,29 +176,53 @@
         pieces += [spare[pl.ds(c, 8, stride=8), :] for c in range(8)]
     halo = jnp.concatenate(pieces, axis=0).T
     lane = iota((LEVELS, 128), 1)
-    for f, ref in enumerate((us, hs)):
-        ref[pl.ds(edge, span), :] = state[pl.ds(f * span, span), :]
+    for f in range(2):
         line = halo[f * LEVELS : (f + 1) * LEVELS, :]
         for c in range(HALO):
             inner = pltpu.roll(state[pl.ds(f * span + (MINE - HALO + c) * LEVELS, LEVELS), :], 8, 1)
             outer = pltpu.roll(line, (128 - 8 * c) % 128, 1)
-            ref[pl.ds(c * LEVELS, LEVELS), :] = jnp.where(lane < 8, outer, inner)
+            sides[pl.ds((2 * f) * edge + c * LEVELS, LEVELS), :] = jnp.where(lane < 8, outer, inner)
             inner = pltpu.roll(state[pl.ds(f * span + c * LEVELS, LEVELS), :], 120, 1)
             outer = pltpu.roll(line, (56 - 8 * c) % 128, 1)
-            ref[pl.ds(edge + span + c * LEVELS, LEVELS), :] = jnp.where(lane >= 120, outer, inner)
-    substeps(us, hs, ps, mixing)
+            sides[pl.ds((2 * f + 1) * edge + c * LEVELS, LEVELS), :] = jnp.where(lane >= 120, outer, inner)
+
+    def sources(f, c):
+        if c < HALO:
+            return sides, 2 * f * edge + c * LEVELS
+        if c < HALO + MINE:
+            return state, f * span + (c - HALO) * LEVELS
+        return sides, (2 * f + 1) * edge + (c - HALO - MINE) * LEVELS
+
+    substeps(sources, both, ps, mixing)
     starts = [jnp.bitwise_xor(MEMBER_AT[k], info[1]) * 136 for k in range(GROUP)]
-    for base, ref in ((72, us), (0, hs)):
-        for four in range(8):
-            square = four_levels(ref, edge, four).T
-            for k in range(GROUP):
-                packed[pl.ds(starts[k] + (base + 8 * four), 8), :] = square[8 * k : 8 * k + 8, :]
+    for s in range(GROUP):
+        square = slab_rows(both, edge, s).T
+        for k in range(GROUP):
+            packed[pl.ds(starts[k] + 8 * s, 8), :] = square[8 * k : 8 * k + 8, :]
     for g in range(GROUP):
-        packed[pl.ds(g * 136 + 64, 8), :] = sums[pl.ds(g * 8, 8), :]
-
-
-def square_of(ref, base, four):
-    return jnp.concatenate([ref[pl.ds(g * 136 + base + four * 8, 8), :] for g in range(GROUP)], axis=0)
+        packed[pl.ds(g * 136 + 128, 8), :] = sums[pl.ds(g * 8, 8), :]
+
+
+def square_of(ref, s):
+    return jnp.concatenate([ref[pl.ds(g * 136 + s * 8, 8), :] for g in range(GROUP)], axis=0)
+
+
+def fold(top, bottom, vector, extra=0.0):
+    row, lane = iota((64, 128), 0), iota((64, 128), 1)
+    body = jnp.where((lane >= 64) | (row <= lane), top, pltpu.roll(bottom, 64, 1))
+    diagonal = jnp.sum(jnp.where(lane == row + 64, bottom, 0.0), axis=0, keepdims=True)
+    at = iota((8, 128), 0)
+    tail = jnp.where(at == 0, diagonal, jnp.where(at == 1, vector, extra))
+    return body, tail
+
+
+def half_of(body, tail):
+    row, lane = iota((64, 128), 0), iota((64, 128), 1)
+    top = jnp.where((lane >= 64) | (row < lane), body, jnp.where(row == lane, 0.5 * body, 0.0))
+    moved = pltpu.roll(body, 64, 1)
+    bottom = jnp.where(row > lane - 64, moved, jnp.where(row == lane - 64, 0.5 * tail[0:1, :], 0.0))
+    bottom = jnp.where(lane >= 64, bottom, 0.0)
+    return jnp.concatenate([top, bottom], axis=0)
 
 
 def blend(fs, table, core, keep, send):
@@ -192,66 +232,53 @@
             ref[j] = fs[s] + fs[table[s, 0]] + fs[table[s, 1]]
 
 
-def gram_pair(fs, four, square, lines):
+def gram_of(fs, q, anomaly, halves, mean, line, upper):
+    lane = iota((1, 128), 1)
+    swapped = pltpu.roll(line, 64, 1)
+    mine = (lane >= 64) if upper else (lane < 64)
+    weight = jnp.where(mine, swapped if upper else line, 0.0)
+    pull = jnp.where(mine, line if upper else swapped, 0.0) - weight * mean
+    left = jnp.concatenate([anomaly * weight, jnp.broadcast_to(pull, (8, 128))], axis=0)
+    gram = dot_split(split(left), halves, turned=True)
+    body, tail = fold(gram[:64], gram[64:128], gram[128:129])
+    fs[q, pl.ds(0, 64), :] = body
+    fs[q, pl.ds(64, 8), :] = tail
+
+
+def centred(square):
     mean = jnp.mean(square, axis=0, keepdims=True)
     anomaly = square - mean
-    halves = split(anomaly)
-    lane = iota((1, 128), 1)
-    for half in range(2):
-        q = 2 * four + half
-        line = lines(q)
-        swapped = pltpu.roll(line, 64, 1)
-        mine = (lane >= 64) if half else (lane < 64)
-        weight = jnp.where(mine, swapped if half else line, 0.0)
-        pull = jnp.where(mine, line if half else swapped, 0.0) - weight * mean
-        left = jnp.concatenate([anomaly * weight, jnp.broadcast_to(pull, (8, 128))], axis=0)
-        gram = dot_split(split(left), halves, turned=True)
-        body, tail = fold(gram[:64], gram[64:128], gram[128:129])
-        fs[q, pl.ds(0, 64), :] = body
-        fs[q, pl.ds(64, 8), :] = tail
+    return anomaly, split(anomaly), mean
 
 
 def first_gram_kernel(info, got, keep, send, later, table_out, fs, table, sem):
-    table_out[...] = got[pl.ds(66, GROUP, stride=136), :].astype(jnp.int32)
+    table_out[...] = got[pl.ds(130, GROUP, stride=136), :].astype(jnp.int32)
     copy = pltpu.make_async_copy(table_out, table, sem)
     copy.start()
-    later[...] = got[pl.ds(65, GROUP, stride=136), :]
-    for four in range(8):
-        gram_pair(fs, four, square_of(got, 0, four), lambda q: got[pl.ds(q * 136 + 64, 1), :])
+    later[...] = got[pl.ds(129, GROUP, stride=136), :]
+    for q in range(GROUP):
+        gram_of(fs, q, *centred(square_of(got, q)), got[pl.ds(q * 136 + 128, 1), :], True)
     copy.wait()
     blend(fs, table, info[0], keep, send)
 
 
-def fold(top, bottom, vector):
-    row, lane = iota((64, 128), 0), iota((64, 128), 1)
-    body = jnp.where((lane >= 64) | (row <= lane), top, pltpu.roll(bottom, 64, 1))
-    diagonal = jnp.sum(jnp.where(lane == row + 64, bottom, 0.0), axis=0, keepdims=True)
-    tail = jnp.where(iota((8, 128), 0) == 0, diagonal, vector)
-    return body, tail
-
-
-def unfold(body, tail):
-    row, lane = iota((64, 128), 0), iota((64, 128), 1)
-    top = jnp.where((lane >= 64) | (row < lane), body, jnp.where(row == lane, 0.5 * body, 0.0))
-    moved = pltpu.roll(body, 64, 1)
-    bottom = jnp.where(row > lane - 64, moved, jnp.where(row == lane - 64, 0.5 * tail[0:1, :], 0.0))
-    bottom = jnp.where(lane >= 64, bottom, 0.0)
-    half = jnp.concatenate([top, bottom], axis=0)
-    return half + half.T, tail[1:2, :]
-
-
-def forecast_kernel(table, info, state, low, high, hist, mixing, out, keep, send, us, hs, ps, fs):
+def forecast_kernel(table, info, state, low, high, hist, mixing, both, keep, send, ps, fs):
     edge = HALO * LEVELS
     span = MINE * LEVELS
-    for f, ref in enumerate((us, hs)):
-        ref[pl.ds(0, edge), :] = low[pl.ds(f * edge, edge), :]
-        ref[pl.ds(edge, span), :] = state[pl.ds(f * span, span), :]
-        ref[pl.ds(edge + span, edge), :] = high[pl.ds(f * edge, edge), :]
-    substeps(us, hs, ps, mixing)
-    out[pl.ds(0, span), :] = us[pl.ds(edge, span), :]
-    out[pl.ds(span, span), :] = hs[pl.ds(edge, span), :]
+
+    def sources(f, c):
+        if c < HALO:
+            return low, f * edge + c * LEVELS
+        if c < HALO + MINE:
+            return state, f * span + (c - HALO) * LEVELS
+        return high, f * edge + (c - HALO - MINE) * LEVELS
+
+    substeps(sources, both, ps, mixing)
     for four in range(8):
-        gram_pair(fs, four, four_levels(hs, edge, four).T, lambda q: hist[pl.ds(q, 1), :])
+        parts = centred(four_levels(both, WIDE * LEVELS + edge, four).T)
+        for half in range(2):
+            q = 2 * four + half
+            gram_of(fs, q, *parts, hist[pl.ds(q, 1), :], half == 1)
     blend(fs, table, info[0], keep, send)
 
 
@@ -259,7 +286,8 @@
     total = got[0]
     for j in range(1, 8):
         total = total + got[j]
-    gram, vector = unfold(total[:64], total[64:])
+    half = half_of(total[:64], total[64:])
+    gram, vector = half + half.T, total[65:66]
     eye = jnp.where(iota((WIDTH, WIDTH), 0) == iota((WIDTH, WIDTH), 1), 1.0, 0.0)
     third = 1.0 / 3.0
     blended = (WIDTH - 1.0) * eye + gram * third
@@ -282,67 +310,70 @@
     inner = dot_split(split(wide), halves, turned=True)
     shift = dot_split(split(inner), halves, turned=True)[0:1, :] / norm
     spread = z * (math.sqrt(WIDTH - 1.0) / jnp.sqrt(norm))
-    body, tail = fold(spread[:64], spread[64:], shift)
+    sums = jnp.sum(spread, axis=0, keepdims=True) + jnp.sum(shift, axis=1, keepdims=True)
+    body, tail = fold(spread[:64], spread[64:], shift, (1.0 - sums) * (1.0 / WIDTH))
     for j in range(8):
         out[j, pl.ds(0, 64), :] = body
         out[j, pl.ds(64, 8), :] = tail
 
 
-def gather_roots(info, same, other, both):
-    for j in range(GROUP // 2):
-        both[2 * j + info[0]] = same[j]
-        both[2 * j + 1 - info[0]] = other[j]
-
-
-def first_apply_kernel(info, got, same, other, out, low, high, both):
-    gather_roots(info, same, other, both)
+def weights_of(roots, j):
+    body, tail = roots[j, pl.ds(0, 64), :], roots[j, pl.ds(64, 8), :]
+    half = half_of(body, tail)
+    return split((half + tail[1:2, :]) + (half + tail[2:3, :]).T)
+
+
+def first_apply_kernel(second, info, got, roots, *refs):
+    out = refs[1] if second else refs[0]
     span = MINE * LEVELS
     edge = HALO * LEVELS
-    for four in range(8):
-        fields = (square_of(got, 72, four), square_of(got, 0, four))
-        for half in range(2):
-            s = 2 * four + half
-            spread, shift = unfold(both[s, pl.ds(0, 64), :], both[s, pl.ds(64, 8), :])
-            field = jnp.concatenate([x[:, 64 * half : 64 * half + 64] for x in fields], axis=1)
-            mean = jnp.mean(field, axis=0, keepdims=True)
-            result = mean + dot_split(split(spread + shift), split(field - mean))
-            result = result.T
-            for f in range(2):
-                for j in range(2):
-                    at = (f * 2 + j) * 32
-                    out[pl.ds(f * span + 2 * s + j, MINE, stride=LEVELS), :] = result[at : at + 32, :]
-    for f in range(2):
-        low[pl.ds(f * edge, edge), :] = out[pl.ds(f * span, edge), :]
-        high[pl.ds(f * edge, edge), :] = out[pl.ds((f + 1) * span - edge, edge), :]
-
-
-def last_apply_kernel(info, state, same, other, out, both):
-    gather_roots(info, same, other, both)
-    span = MINE * LEVELS
-    for s in range(GROUP):
-        spread, shift = unfold(both[s, pl.ds(0, 64), :], both[s, pl.ds(64, 8), :])
+    parity = 1 - info[0] if second else info[0]
+    for j in range(8):
+        s = 2 * j + parity
+        square = jnp.concatenate(
+            [got[pl.ds(pl.multiple_of(g * 136 + s * 8, 8), 8), :] for g in range(GROUP)], axis=0
+        )
+        result = dot_split(weights_of(roots, j), split(square)).T
+        for fj in range(4):
+            at = (fj // 2) * span + 2 * s + fj % 2
+            out[pl.ds(at, MINE, stride=LEVELS), :] = result[fj * 32 : fj * 32 + 32, :]
+    if second:
+        low, high = refs[2:]
+        for f in range(2):
+            low[pl.ds(f * edge, edge), :] = out[pl.ds(f * span, edge), :]
+            high[pl.ds(f * edge, edge), :] = out[pl.ds((f + 1) * span - edge, edge), :]
+
+
+def last_apply_kernel(second, info, both, roots, *refs):
+    out = refs[-1]
+    parity = 1 - info[0] if second else info[0]
+    starts = []
+    for chunk in range(4):
+        fj = (chunk + 4 - info[2]) & 3
+        starts.append((fj >> 1) * (WIDE * LEVELS) + (fj & 1) + HALO * LEVELS)
+    for j in range(8):
+        s = 2 * j + parity
         field = jnp.concatenate(
-            [
-                state[pl.ds(f * span + 2 * s + j, MINE, stride=LEVELS), :]
-                for f in range(2)
-                for j in range(2)
-            ],
-            axis=0,
-        ).T
-        mean = jnp.mean(field, axis=0, keepdims=True)
-        result = mean + dot_split(split(spread + shift), split(field - mean))
+            [both[pl.ds(at + 2 * s, MINE, stride=LEVELS), :] for at in starts], axis=0
+        )
+        result = dot_split(weights_of(roots, j), split(field), turned=True)
         for g in range(GROUP):
-            out[pl.ds((g * GROUP + s) * 8, 8), :] = result[g * 8 : g * 8 + 8, :]
+            out[pl.ds(pl.multiple_of((g * GROUP + s) * 8, 8), 8), :] = result[g * 8 : g * 8 + 8, :]
 
 
 def place_kernel(info, got, out, tiles):
     starts = [jnp.bitwise_xor(MEMBER_AT[k], info[1]) * 128 for k in range(GROUP)]
+    lane = iota((16, 128), 1)
     for t in range(4):
         for n in range(8):
             rows = [got[pl.ds(starts[4 * t + p] + n, 16, stride=8), :] for p in range(4)]
-            for fj, block in enumerate(chunk_transpose(rows)):
-                f, j = fj // 2, fj % 2
-                tiles[pl.ds(512 * t + (n * 2 + f) * LEVELS + j, 16, stride=2), :] = block
+            for fj in range(4):
+                block = rows[(0 - fj) % 4]
+                for chunk in range(1, 4):
+                    block = jnp.where(lane >= 32 * chunk, rows[(chunk - fj) % 4], block)
+                if fj > 0:
+                    block = pltpu.roll(block, 128 - 32 * fj, 1)
+                tiles[pl.ds(512 * t + (n * 2 + fj // 2) * LEVELS + fj % 2, 16, stride=2), :] = block
     for t in range(4):
         out[:, pl.ds(128 * t, 128)] = tiles[pl.ds(512 * t, 512), :]
 
@@ -355,13 +386,15 @@
     return pl.BlockSpec(memory_space=pltpu.SMEM)
 
 
-def call(kernel, out, ins, name, scratch=()):
+def call(kernel, out, ins, name, scratch=(), aliases=None, cost=None):
     return pl.pallas_call(
         kernel,
         out_shape=out,
         in_specs=ins,
         out_specs=jax.tree.map(lambda _: vmem(), out),
         scratch_shapes=scratch,
+        input_output_aliases=aliases or {},
+        cost_estimate=cost,
         compiler_params=pltpu.CompilerParams(vmem_limit_bytes=VMEM_LIMIT),
         name=name,
     )
@@ -399,7 +432,9 @@
     rows = MINE * LEVELS
     edges = 2 * HALO * LEVELS
     members = ensemble.reshape(512, COLS)
-    info = jnp.stack([lax.axis_index("core"), 15 * (lax.axis_index("hor") & 1)]).astype(jnp.int32)
+    flip = 15 * (lax.axis_index("hor") & 1)
+    block = block_of(lax.axis_index(TILE) ^ flip)
+    info = jnp.stack([lax.axis_index("core"), flip, block & 3]).astype(jnp.int32)
     first, last = pl.pallas_call(
         edges_kernel,
         grid=(1,),
@@ -419,12 +454,13 @@
         [pltpu.VMEM((2048, 128), F32), pltpu.VMEM((2048, 128), F32)],
     )(info, partners, members, obs_column, obs_level, obs_value, obs_error, obs_live, coupling)
     wide = pltpu.VMEM((WIDE * LEVELS, WIDTH), F32)
+    fields = pltpu.VMEM((2 * WIDE * LEVELS, WIDTH), F32)
     packed = call(
         first_kernel,
         arr(GROUP * 136, 128),
         [smem()] + [vmem()] * 5,
         "first",
-        [wide, wide, wide, pltpu.VMEM((64, 128), F32)],
+        [fields, wide, pltpu.VMEM((4 * HALO * LEVELS, 128), F32), pltpu.VMEM((64, 128), F32)],
     )(info, state, before, after, sums, mixing)
     received = exchange(packed.reshape(GROUP, 136, 128), TILE).reshape(GROUP * 136, 128)
     folded = pltpu.VMEM((GROUP, FOLD, 128), F32)
@@ -442,27 +478,46 @@
         same = exchange(copies, CHIPS)
         return same, swap(same)
 
+    cost = pl.CostEstimate(flops=10**9, bytes_accessed=3 * 2**20, transcendentals=0)
     same, other = roots(keep, send)
+    part = call(
+        functools.partial(first_apply_kernel, False),
+        arr(2 * rows, WIDTH),
+        [smem()] + [vmem()] * 2,
+        "apply",
+        cost=cost,
+    )(info, received, same)
     state, low, high = call(
-        first_apply_kernel,
+        functools.partial(first_apply_kernel, True),
         (arr(2 * rows, WIDTH), arr(edges, WIDTH), arr(edges, WIDTH)),
         [smem()] + [vmem()] * 3,
         "apply",
-        [folded],
-    )(info, received, same, other)
+        aliases={3: 0},
+    )(info, received, other, part)
     from_low = across(high, True)
     from_high = across(low, False)
-    state, keep, send = call(
+    both, keep, send = call(
         forecast_kernel,
-        (arr(2 * rows, WIDTH), arr(8, FOLD, 128), arr(8, FOLD, 128)),
+        (arr(2 * WIDE * LEVELS, WIDTH), arr(8, FOLD, 128), arr(8, FOLD, 128)),
         [smem(), smem()] + [vmem()] * 5,
         "forecast",
-        [wide, wide, wide, folded],
+        [wide, folded],
     )(table, info, state, from_low, from_high, hist, mixing)
     same, other = roots(keep, send)
+    part = call(
+        functools.partial(last_apply_kernel, False),
+        arr(GROUP * 128, 128),
+        [smem()] + [vmem()] * 2,
+        "analyse",
+        cost=cost,
+    )(info, both, same)
     analysed = call(
-        last_apply_kernel, arr(GROUP * 128, 128), [smem()] + [vmem()] * 3, "analyse", [folded]
-    )(info, state, same, other)
+        functools.partial(last_apply_kernel, True),
+        arr(GROUP * 128, 128),
+        [smem()] + [vmem()] * 3,
+        "analyse",
+        aliases={3: 0},
+    )(info, both, other, part)
     got = exchange(analysed.reshape(GROUP, 128, 128), TILE).reshape(GROUP * 128, 128)
     placed = call(place_kernel, arr(512, 512), [smem(), vmem()], "place", [pltpu.VMEM((2048, 128), F32)])(info, got)
     return placed.reshape(ensemble.shape)

time: 178 us -> 176 us (0.989)
  waiting for transfers between devices: 11.3 us -> 8.88 us
    ppermute x4, waiting for transfers between devices: 5.19 us -> 2.78 us  [swap(): return lax.ppermute(x, 'core', [(0, 1), (1, 0)])]
    pallas_call x3 -> x5, Pallas kernels: 8.87 us -> 9.83 us  [the longest x1 4.01 us: shards(): call(forecast_kernel, (arr(2 * WIDE * LEVELS, WIDTH), arr(8, FOLD, 128),...]
  transfers between devices with their start and end apart: 8 -> 8, of which waited for: 6 -> 4; matrix products, arithmetic and copies ran while one was open for 0% -> 0% of each run, Pallas kernels for 1% -> 3%
where the time goes in v3:
time: 176 us
  blocking collectives  123 us (70%)
  Pallas kernels  27.9 us (16%)
  starting transfers between devices  15.4 us (9%)
  waiting for transfers between devices  8.88 us (5%)
    all_to_all x6, blocking collectives, exchange(): return lax.all_to_all(x, axes, split_axis=0, concat_axis=0, tiled=True)  123 us
    ppermute x4, starting transfers between devices, swap(): return lax.ppermute(x, 'core', [(0, 1), (1, 0)])  8.32 us
    pallas_call x2, Pallas kernels, roots(): copies = call(root_kernel, arr(8, FOLD, 128), [vmem()], 'root')(parts)  6.24 us
    ppermute x2, waiting for transfers between devices, across(): return lax.ppermute(x, ALL, pairs)  6.09 us
    pallas_call x1, Pallas kernels, shards(): call(forecast_kernel, (arr(2 * WIDE * LEVELS, WIDTH), arr(8, FOLD, 128),...  4.01 us
    ppermute x1, starting transfers between devices, shards(): after = lax.ppermute(first, 'hor', [(b, a) for a, b in ring])  3.72 us
  transfers between devices with their start and end apart: 8, of which 4 were waited for; matrix products, arithmetic and copies ran while one was open for 0% of the time, Pallas kernels for 3%

profile of v3, /device:TPU:1, one launch (start us, length us, event | category | flops | bytes accessed | tf_op | source)
XLA Modules:
  0.0 175.8 jit_solution(14237219551370383765)
XLA Ops:
  0.1 1.9 %edges.1 = (f32[8,512]{1,0:T(8,128)}, f32[8,512]{1,0:T(8,128)}) custom-call(f32[512,512]{1,0:T(8,128)} %bitcast.12, f32[512,512]{1,0:T(8,128)} %bitcast.13), custom_call_target="tpu_custom_call" | custom-call | tf_op jit(solution)/shard_map/edges/pallas_call | solution.py:438
  2.0 2.0 %collective-permute-start = (f32[8,512]{1,0:T(8,128)}, f32[8,512]{1,0:T(8,128)S(1)}, u32[]{:S(2)}, u32[]{:S(2)}) collective-permute-start(f32[8,512]{1,0:T(8,128)} %get-tuple-element.21), channel_id=1, source_target_pairs={{0,4},{4,8},{8,12},{12,16},{16,20},{20,24},{24,28},{28,32},{32,36}... | collective-permute-start | bytes 49160 | tf_op jit(solution)/shard_map/ppermute | solution.py:447
  4.0 3.7 %collective-permute-start.1 = (f32[8,512]{1,0:T(8,128)}, f32[8,512]{1,0:T(8,128)S(1)}, u32[]{:S(2)}, u32[]{:S(2)}) collective-permute-start(f32[8,512]{1,0:T(8,128)} %get-tuple-element.22), channel_id=1, source_target_pairs={{4,0},{8,4},{12,8},{16,12},{20,16},{24,20},{28,24},{32,28},{36,32}... | collective-permute-start | bytes 49160 | tf_op jit(solution)/shard_map/ppermute | solution.py:448
  7.7 0.1 pad_add_fusion.info
  7.9 2.4 %prepare.1 = (f32[2048,128]{1,0:T(8,128)S(1)}, f32[128,128]{1,0:T(8,128)S(1)}, bf16[512,256]{1,0:T(8,128)(2,1)S(1)}) custom-call(s32[3]{0:T(128)S(1)} %pad_add_fusion.info, s32[1,1,2]{2,1,0:T(1,128)S(1)} %copy-done.7, f32[512,512]{1,0:T(8,128)S(1)} %bitcast.14, s32[2,1,1,512]{3,2,1,0:T(1,128)S(1)} %copy-done.2, s32[2,1,1,512]{3,2,1,0:T(1,128)S(1)} %copy-done.3, ...), custom_call_target="tpu_custom_call" | custom-call | tf_op jit(solution)/shard_map/prepare/pallas_call | solution.py:449
  10.3 0.0 collective-permute-done.before
  10.3 0.0 collective-permute-done.1.after
  10.3 3.4 %first.1 = f32[2176,128]{1,0:T(8,128)S(1)} custom-call(s32[3]{0:T(128)S(1)} %pad_add_fusion.info, f32[2048,128]{1,0:T(8,128)S(1)} %get-tuple-element.20.state, f32[8,512]{1,0:T(8,128)S(1)} %collective-permute-done.before, f32[8,512]{1,0:T(8,128)S(1)} %collective-permute-done.1.after, f32[128,128]{1,0:T(8,128)S(1)} %get-tuple-element.23.sums, ...), custom_call_target="tpu_custom_call" | custom-call | tf_op jit(solution)/shard_map/first/pallas_call | solution.py:458
  13.7 39.6 %all_to_all.30 = f32[16,136,128]{2,1,0:T(8,128)S(1)} all-to-all(f32[16,136,128]{2,1,0:T(8,128)S(1)} %bitcast.15), channel_id=1, replica_groups=mesh['mem'=4,'hor'=16,'zh'=2,'core'=2] {'mem','zh','core'}, dimensions={0} | all-to-all | bytes 2228224 | tf_op jit(solution)/shard_map/all_to_all | solution.py:428
  53.3 2.2 %gram.1 = (f32[8,72,128]{2,1,0:T(8,128)S(1)}, f32[8,72,128]{2,1,0:T(8,128)S(1)}, f32[16,128]{1,0:T(8,128)S(1)}, s32[16,128]{1,0:T(8,128)S(1)}) custom-call(s32[3]{0:T(128)S(1)} %pad_add_fusion.info, f32[2176,128]{1,0:T(8,128)S(1)} %bitcast.9), custom_call_target="tpu_custom_call" | custom-call | tf_op jit(solution)/shard_map/gram/pallas_call | solution.py:467
  55.5 0.1 collective-permute-start.2
  55.6 1.6 collective-permute-done.2
  57.2 13.4 %all_to_all.31.got = f32[8,72,128]{2,1,0:T(8,128)S(1)} all-to-all(f32[8,72,128]{2,1,0:T(8,128)S(1)} %add.22), channel_id=1, replica_groups=mesh['mem'=4,'hor'=16,'zh'=2,'core'=2] {'mem','zh'}, dimensions={0} | all-to-all | bytes 589824 | tf_op jit(solution)/shard_map/all_to_all | solution.py:428
  70.5 3.1 %root.2 = f32[8,72,128]{2,1,0:T(8,128)S(1)} custom-call(f32[8,72,128]{2,1,0:T(8,128)S(1)} %all_to_all.31.got), custom_call_target="tpu_custom_call" | custom-call | tf_op jit(solution)/shard_map/root/pallas_call | solution.py:477
  73.7 13.3 %all_to_all.32.roots = f32[8,72,128]{2,1,0:T(8,128)S(1)} all-to-all(f32[8,72,128]{2,1,0:T(8,128)S(1)} %root.2), channel_id=1, replica_groups=mesh['mem'=4,'hor'=16,'zh'=2,'core'=2] {'mem','zh'}, dimensions={0} | all-to-all | bytes 589824 | tf_op jit(solution)/shard_map/all_to_all | solution.py:428
  86.9 2.6 %collective-permute-start.3 = (f32[8,72,128]{2,1,0:T(8,128)S(1)}, f32[8,72,128]{2,1,0:T(8,128)S(1)}, u32[]{:S(2)}, u32[]{:S(2)}) collective-permute-start(f32[8,72,128]{2,1,0:T(8,128)S(1)} %all_to_all.32.roots), channel_id=1, source_target_pairs={{0,1},{1,0},{2,3},{3,2},{4,5},{5,4},{6,7},{7,6},{8,9},{9,8},{10,11... | collective-permute-start | bytes 884744 | tf_op jit(solution)/shard_map/ppermute | solution.py:424
  89.5 1.5 apply.2.refs_0_
  91.1 1.5 apply.3
  92.6 1.3 collective-permute-start.4
  94.0 3.3 %collective-permute-done.4.low = f32[512,128]{1,0:T(8,128)S(1)} collective-permute-done((f32[512,128]{1,0:T(8,128)S(1)}, f32[512,128]{1,0:T(8,128)S(1)}, u32[]{:S(2)}, u32[]{:S(2)}) %collective-permute-start.4) | collective-permute-done | bytes 262176 | tf_op jit(solution)/shard_map/ppermute | solution.py:420
  97.3 2.8 %collective-permute-done.5.high = f32[512,128]{1,0:T(8,128)S(1)} collective-permute-done((f32[512,128]{1,0:T(8,128)S(1)}, f32[512,128]{1,0:T(8,128)S(1)}, u32[]{:S(2)}, u32[]{:S(2)}) %collective-permute-start.5) | collective-permute-done | bytes 262176 | tf_op jit(solution)/shard_map/ppermute | solution.py:420
  100.0 4.0 %forecast.1 = (f32[3072,128]{1,0:T(8,128)S(1)}, f32[8,72,128]{2,1,0:T(8,128)S(1)}, f32[8,72,128]{2,1,0:T(8,128)S(1)}) custom-call(s32[16,128]{1,0:T(8,128)S(1)} %get-tuple-element.25.table, s32[3]{0:T(128)S(1)} %pad_add_fusion.info, f32[2048,128]{1,0:T(8,128)S(1)} %get-tuple-element.28.state, f32[512,128]{1,0:T(8,128)S(1)} %collective-permute-done.4.low, ...), custom_call_target="tpu_custom_call" | custom-call | tf_op jit(solution)/shard_map/forecast/pallas_call | solution.py:499
  104.1 2.7 %collective-permute-start.6 = (f32[8,72,128]{2,1,0:T(8,128)S(1)}, f32[8,72,128]{2,1,0:T(8,128)S(1)}, u32[]{:S(2)}, u32[]{:S(2)}) collective-permute-start(f32[8,72,128]{2,1,0:T(8,128)S(1)} %get-tuple-element.34), channel_id=1, source_target_pairs={{0,1},{1,0},{2,3},{3,2},{4,5},{5,4},{6,7},{7,6},{8,9},{9,8},{10,11... | collective-permute-start | bytes 884744 | tf_op jit(solution)/shard_map/ppermute | solution.py:424
  106.7 1.2 collective-permute-done.6
  108.0 12.9 %all_to_all.33.got = f32[8,72,128]{2,1,0:T(8,128)S(1)} all-to-all(f32[8,72,128]{2,1,0:T(8,128)S(1)} %add.23), channel_id=1, replica_groups=mesh['mem'=4,'hor'=16,'zh'=2,'core'=2] {'mem','zh'}, dimensions={0} | all-to-all | bytes 589824 | tf_op jit(solution)/shard_map/all_to_all | solution.py:428
  120.9 3.1 %root.3 = f32[8,72,128]{2,1,0:T(8,128)S(1)} custom-call(f32[8,72,128]{2,1,0:T(8,128)S(1)} %all_to_all.33.got), custom_call_target="tpu_custom_call" | custom-call | tf_op jit(solution)/shard_map/root/pallas_call | solution.py:477
  124.0 13.2 %all_to_all.34.roots = f32[8,72,128]{2,1,0:T(8,128)S(1)} all-to-all(f32[8,72,128]{2,1,0:T(8,128)S(1)} %root.3), channel_id=1, replica_groups=mesh['mem'=4,'hor'=16,'zh'=2,'core'=2] {'mem','zh'}, dimensions={0} | all-to-all | bytes 589824 | tf_op jit(solution)/shard_map/all_to_all | solution.py:428
  137.2 2.9 %collective-permute-start.7 = (f32[8,72,128]{2,1,0:T(8,128)S(1)}, f32[8,72,128]{2,1,0:T(8,128)S(1)}, u32[]{:S(2)}, u32[]{:S(2)}) collective-permute-start(f32[8,72,128]{2,1,0:T(8,128)S(1)} %all_to_all.34.roots), channel_id=1, source_target_pairs={{0,1},{1,0},{2,3},{3,2},{4,5},{5,4},{6,7},{7,6},{8,9},{9,8},{10,11... | collective-permute-start | bytes 884744 | tf_op jit(solution)/shard_map/ppermute | solution.py:424
  140.2 1.4 analyse.2.refs_0_
  141.5 1.4 analyse.3
  143.0 30.9 %all_to_all.35 = f32[16,128,128]{2,1,0:T(8,128)S(1)} all-to-all(f32[16,128,128]{2,1,0:T(8,128)S(1)} %bitcast.17), channel_id=1, replica_groups=mesh['mem'=4,'hor'=16,'zh'=2,'core'=2] {'mem','zh','core'}, dimensions={0} | all-to-all | bytes 2097152 | tf_op jit(solution)/shard_map/all_to_all | solution.py:428
  173.9 1.9 %place.1 = f32[512,512]{1,0:T(8,128)} custom-call(s32[3]{0:T(128)S(1)} %pad_add_fusion.info, f32[2048,128]{1,0:T(8,128)S(1)} %bitcast.16), custom_call_target="tpu_custom_call" | custom-call | tf_op jit(solution)/shard_map/place/pallas_call | solution.py:522
  (21 shorter events, 0.1 us)
Async XLA Ops:
  0.0 7.8 %copy-start = (f32[8,2,32,512]{3,2,1,0:T(8,128)S(1)}, f32[8,2,32,512]{3,2,1,0:T(8,128)}, u32[]{:S(2)}) copy-start(f32[8,2,32,512]{3,2,1,0:T(8,128)} %param.8) | copy-start | bytes 3145732
  0.0 7.8 %copy-start.7 = (s32[1,1,2]{2,1,0:T(1,128)S(1)}, s32[1,1,2]{2,1,0:T(1,128)}, u32[]{:S(2)}) copy-start(s32[1,1,2]{2,1,0:T(1,128)} %partner.1) | copy-start | bytes 28
  0.0 7.8 %copy-start.6 = (s32[2,1,1,512]{3,2,1,0:T(1,128)S(1)}, s32[2,1,1,512]{3,2,1,0:T(1,128)}, u32[]{:S(2)}) copy-start(s32[2,1,1,512]{3,2,1,0:T(1,128)} %live.1) | copy-start | bytes 12292
  0.0 7.8 %copy-start.5 = (f32[2,1,1,512]{3,2,1,0:T(1,128)S(1)}, f32[2,1,1,512]{3,2,1,0:T(1,128)}, u32[]{:S(2)}) copy-start(f32[2,1,1,512]{3,2,1,0:T(1,128)} %error.1) | copy-start | bytes 12292
  0.0 7.8 %copy-start.4 = (f32[2,1,1,512]{3,2,1,0:T(1,128)S(1)}, f32[2,1,1,512]{3,2,1,0:T(1,128)}, u32[]{:S(2)}) copy-start(f32[2,1,1,512]{3,2,1,0:T(1,128)} %value.1) | copy-start | bytes 12292
  0.0 7.8 %copy-start.3 = (s32[2,1,1,512]{3,2,1,0:T(1,128)S(1)}, s32[2,1,1,512]{3,2,1,0:T(1,128)}, u32[]{:S(2)}) copy-start(s32[2,1,1,512]{3,2,1,0:T(1,128)} %level.1) | copy-start | bytes 12292
  0.0 7.8 %copy-start.2 = (s32[2,1,1,512]{3,2,1,0:T(1,128)S(1)}, s32[2,1,1,512]{3,2,1,0:T(1,128)}, u32[]{:S(2)}) copy-start(s32[2,1,1,512]{3,2,1,0:T(1,128)} %column.1) | copy-start | bytes 12292
  0.0 7.8 %copy-start.1 = (f32[32,32]{1,0:T(8,128)S(1)}, f32[32,32]{1,0:T(8,128)}, u32[]{:S(2)}) copy-start(f32[32,32]{1,0:T(8,128)} %coupling.1) | copy-start | bytes 12292
  2.0 8.3 %collective-permute-start = (f32[8,512]{1,0:T(8,128)}, f32[8,512]{1,0:T(8,128)S(1)}, u32[]{:S(2)}, u32[]{:S(2)}) collective-permute-start(f32[8,512]{1,0:T(8,128)} %get-tuple-element.21), channel_id=1, source_target_pairs={{0,4},{4,8},{8,12},{12,16},{16,20},{20,24},{24,28},{28,32},{32,36}... | collective-permute-start | bytes 49160 | tf_op jit(solution)/shard_map/ppermute | solution.py:447
  4.0 6.3 %collective-permute-start.1 = (f32[8,512]{1,0:T(8,128)}, f32[8,512]{1,0:T(8,128)S(1)}, u32[]{:S(2)}, u32[]{:S(2)}) collective-permute-start(f32[8,512]{1,0:T(8,128)} %get-tuple-element.22), channel_id=1, source_target_pairs={{4,0},{8,4},{12,8},{16,12},{20,16},{24,20},{28,24},{32,28},{36,32}... | collective-permute-start | bytes 49160 | tf_op jit(solution)/shard_map/ppermute | solution.py:448
  55.5 1.7 collective-permute-start.2
  86.9 4.1 %collective-permute-start.3 = (f32[8,72,128]{2,1,0:T(8,128)S(1)}, f32[8,72,128]{2,1,0:T(8,128)S(1)}, u32[]{:S(2)}, u32[]{:S(2)}) collective-permute-start(f32[8,72,128]{2,1,0:T(8,128)S(1)} %all_to_all.32.roots), channel_id=1, source_target_pairs={{0,1},{1,0},{2,3},{3,2},{4,5},{5,4},{6,7},{7,6},{8,9},{9,8},{10,11... | collective-permute-start | bytes 884744 | tf_op jit(solution)/shard_map/ppermute | solution.py:424
  92.6 4.7 %collective-permute-start.4 = (f32[512,128]{1,0:T(8,128)S(1)}, f32[512,128]{1,0:T(8,128)S(1)}, u32[]{:S(2)}, u32[]{:S(2)}) collective-permute-start(f32[512,128]{1,0:T(8,128)S(1)} %get-tuple-element.29), channel_id=1, source_target_pairs={{0,1},{1,64},{64,65},{65,128},{128,129},{129,192},{192,193},{193,2... | collective-permute-start | bytes 786440 | tf_op jit(solution)/shard_map/ppermute | solution.py:420
  93.9 6.1 %collective-permute-start.5 = (f32[512,128]{1,0:T(8,128)S(1)}, f32[512,128]{1,0:T(8,128)S(1)}, u32[]{:S(2)}, u32[]{:S(2)}) collective-permute-start(f32[512,128]{1,0:T(8,128)S(1)} %get-tuple-element.30), channel_id=1, source_target_pairs={{1,0},{64,1},{65,64},{128,65},{129,128},{192,129},{193,192},{2,193... | collective-permute-start | bytes 786440 | tf_op jit(solution)/shard_map/ppermute | solution.py:420
  104.1 3.9 %collective-permute-start.6 = (f32[8,72,128]{2,1,0:T(8,128)S(1)}, f32[8,72,128]{2,1,0:T(8,128)S(1)}, u32[]{:S(2)}, u32[]{:S(2)}) collective-permute-start(f32[8,72,128]{2,1,0:T(8,128)S(1)} %get-tuple-element.34), channel_id=1, source_target_pairs={{0,1},{1,0},{2,3},{3,2},{4,5},{5,4},{6,7},{7,6},{8,9},{9,8},{10,11... | collective-permute-start | bytes 884744 | tf_op jit(solution)/shard_map/ppermute | solution.py:424
  137.2 4.3 %collective-permute-start.7 = (f32[8,72,128]{2,1,0:T(8,128)S(1)}, f32[8,72,128]{2,1,0:T(8,128)S(1)}, u32[]{:S(2)}, u32[]{:S(2)}) collective-permute-start(f32[8,72,128]{2,1,0:T(8,128)S(1)} %all_to_all.34.roots), channel_id=1, source_target_pairs={{0,1},{1,0},{2,3},{3,2},{4,5},{5,4},{6,7},{7,6},{8,9},{9,8},{10,11... | collective-permute-start | bytes 884744 | tf_op jit(solution)/shard_map/ppermute | solution.py:424

commit v4 on v3

--- a/solution.py
+++ b/solution.py
@@ -10,7 +10,8 @@
 
 SUBSTEPS = 4
 ROOT_STEPS = 8
-TIME_STEP = 0.2
+RATE = 0.5 * 0.2
+MIX = 128
 GROUP = 16
 WIDTH = 128
 LEVELS = 32
@@ -62,9 +63,9 @@
     return out
 
 
-def edges_kernel(left, right, first, last):
-    first[...] = left[...].T[0:HALO, :]
-    last[...] = right[...].T[128 - HALO :, :]
+def edges_kernel(ens, first, last):
+    first[...] = ens[:, 0:128].T[0:HALO, :]
+    last[...] = ens[:, COLS - 128 : COLS].T[128 - HALO :, :]
 
 
 def prepare_kernel(
@@ -106,17 +107,16 @@
     first = partner[0, 0, 0].astype(F32)
     second = partner[0, 0, 1].astype(F32)
     out[pl.ds(2, GROUP, stride=8), :] = jnp.where(lane == 0, first, second)
-    wide = jnp.concatenate([coupling[...]] * 8, axis=1)
-    wide = jnp.concatenate([wide] * 8, axis=0)
-    wide = jnp.where((iota((256, 256), 0) >> 5) == (iota((256, 256), 1) >> 5), wide, 0.0)
+    wide = jnp.concatenate([coupling[...]] * (MIX // LEVELS), axis=1)
+    wide = jnp.concatenate([wide] * (MIX // LEVELS), axis=0)
+    wide = jnp.where((iota((MIX, MIX), 0) >> 5) == (iota((MIX, MIX), 1) >> 5), RATE * RATE * wide, 0.0)
     high, rest = split(wide)
-    mixing[pl.ds(0, 256), :] = high
-    mixing[pl.ds(256, 256), :] = rest
+    mixing[pl.ds(0, MIX), :] = high
+    mixing[pl.ds(MIX, MIX), :] = rest
 
 
 def substeps(sources, both, ps, mixing):
-    rate = 0.5 * TIME_STEP
-    mix = (mixing[pl.ds(0, 256), :], mixing[pl.ds(256, 256), :])
+    mix = (mixing[pl.ds(0, MIX), :], mixing[pl.ds(MIX, MIX), :])
     wide = WIDE * LEVELS
     for c in (0, WIDE - 2):
         both[pl.ds(wide + c * LEVELS, 2 * LEVELS), :] = jnp.zeros((2 * LEVELS, WIDTH), F32)
@@ -127,27 +127,29 @@
             return ref[pl.ds(at, count * LEVELS), :]
         return both[pl.ds(f * wide + c * LEVELS, count * LEVELS), :]
 
+    def speed(step, c):
+        return RATE * rows(0, 0, c, 1) if step == 0 else rows(step, 0, c, 1)
+
+    many = MIX // LEVELS
     for step in range(SUBSTEPS):
         lo, hi = 2 * step, WIDE - 2 * step
-        for pair in range(3):
-            block = jnp.concatenate(
-                [rows(step, 1, 16 * pair, 8), rows(step, 1, 16 * pair + 8, 8)], axis=1
-            )
+        for c in range(0, WIDE, 2 * many):
+            block = jnp.concatenate([rows(step, 1, c, many), rows(step, 1, c + many, many)], axis=1)
             pressure = dot_split(mix, split(block))
-            ps[pl.ds(pair * 512, 256), :] = pressure[:, :128]
-            ps[pl.ds(pair * 512 + 256, 256), :] = pressure[:, 128:]
-        before, here = rows(step, 0, lo, 1), rows(step, 0, lo + 1, 1)
+            ps[pl.ds(c * LEVELS, MIX), :] = pressure[:, :128]
+            ps[pl.ds(c * LEVELS + MIX, MIX), :] = pressure[:, 128:]
+        before, here = speed(step, lo), speed(step, lo + 1)
         slope_one, slope_two = ps[pl.ds(lo * LEVELS, LEVELS), :], ps[pl.ds((lo + 1) * LEVELS, LEVELS), :]
         flux_two, flux_one, height_one = None, None, None
         for c in range(lo + 1, hi - 1):
-            after = rows(step, 0, c + 1, 1)
+            after = speed(step, c + 1)
             slope = ps[pl.ds((c + 1) * LEVELS, LEVELS), :]
-            moved = here - rate * (here * (after - before) + (slope - slope_one))
+            moved = (here - here * (after - before)) - (slope - slope_one)
             height = rows(step, 1, c, 1)
             flux = moved * height
             if c >= lo + 3:
-                both[pl.ds(wide + (c - 1) * LEVELS, LEVELS), :] = height_one - rate * (flux - flux_two)
-            both[pl.ds(c * LEVELS, LEVELS), :] = moved
+                both[pl.ds(wide + (c - 1) * LEVELS, LEVELS), :] = height_one - (flux - flux_two)
+            both[pl.ds(c * LEVELS, LEVELS), :] = moved if step < SUBSTEPS - 1 else moved * (1.0 / RATE)
             before, here = here, after
             slope_one, slope_two = slope_two, slope
             flux_two, flux_one, height_one = flux_one, flux, height
@@ -435,20 +437,13 @@
     flip = 15 * (lax.axis_index("hor") & 1)
     block = block_of(lax.axis_index(TILE) ^ flip)
     info = jnp.stack([lax.axis_index("core"), flip, block & 3]).astype(jnp.int32)
-    first, last = pl.pallas_call(
-        edges_kernel,
-        grid=(1,),
-        out_shape=(arr(HALO, COLS), arr(HALO, COLS)),
-        in_specs=[pl.BlockSpec((512, 128), lambda i: (0, 0)), pl.BlockSpec((512, 128), lambda i: (0, 3))],
-        out_specs=(pl.BlockSpec((HALO, COLS), lambda i: (0, 0)),) * 2,
-        name="edges",
-    )(members, members)
+    first, last = call(edges_kernel, (arr(HALO, COLS), arr(HALO, COLS)), [vmem()], "edges")(members)
     ring = [(i, (i + 1) % 16) for i in range(16)]
     before = lax.ppermute(last, "hor", ring)
     after = lax.ppermute(first, "hor", [(b, a) for a, b in ring])
     state, sums, mixing = call(
         prepare_kernel,
-        (arr(2 * rows, 128), arr(128, 128), arr(512, 256, dtype=BF16)),
+        (arr(2 * rows, 128), arr(128, 128), arr(2 * MIX, MIX, dtype=BF16)),
         [smem()] * 2 + [vmem()] * 7,
         "prepare",
         [pltpu.VMEM((2048, 128), F32), pltpu.VMEM((2048, 128), F32)],

time: 176 us -> 175 us (level)
  Pallas kernels: 27.9 us -> 25.1 us
where the time goes in v4:
time: 175 us; the launch traced here: 174 us
  blocking collectives  123 us (70%)
  Pallas kernels  25.1 us (14%)
  starting transfers between devices  15.4 us (9%)
  waiting for transfers between devices  8.87 us (5%)
    all_to_all x6, blocking collectives, exchange(): return lax.all_to_all(x, axes, split_axis=0, concat_axis=0, tiled=True)  123 us
    ppermute x4, starting transfers between devices, swap(): return lax.ppermute(x, 'core', [(0, 1), (1, 0)])  8.32 us
    pallas_call x2, Pallas kernels, roots(): copies = call(root_kernel, arr(8, FOLD, 128), [vmem()], 'root')(parts)  6.24 us
    ppermute x2, waiting for transfers between devices, across(): return lax.ppermute(x, ALL, pairs)  6.09 us
    ppermute x1, starting transfers between devices, shards(): after = lax.ppermute(first, 'hor', [(b, a) for a, b in ring])  3.81 us
  transfers between devices with their start and end apart: 8, of which 4 were waited for; matrix products, arithmetic and copies ran while one was open for 0% of the time, Pallas kernels for 3%

profile of v4, /device:TPU:1, one launch (start us, length us, event | category | flops | bytes accessed | tf_op | source)
XLA Modules:
  0.0 174.2 jit_solution(8525777355425489809)
XLA Ops:
  0.0 1.2 copy-done
  1.3 0.2 edges.1
  1.5 2.1 %collective-permute-start = (f32[8,512]{1,0:T(8,128)S(1)}, f32[8,512]{1,0:T(8,128)S(1)}, u32[]{:S(2)}, u32[]{:S(2)}) collective-permute-start(f32[8,512]{1,0:T(8,128)S(1)} %get-tuple-element.21), channel_id=1, source_target_pairs={{0,4},{4,8},{8,12},{12,16},{16,20},{20,24},{24,28},{28,32},{32,36}... | collective-permute-start | bytes 49160 | tf_op jit(solution)/shard_map/ppermute | solution.py:442
  3.6 3.8 %collective-permute-start.1 = (f32[8,512]{1,0:T(8,128)S(1)}, f32[8,512]{1,0:T(8,128)S(1)}, u32[]{:S(2)}, u32[]{:S(2)}) collective-permute-start(f32[8,512]{1,0:T(8,128)S(1)} %get-tuple-element.22), channel_id=1, source_target_pairs={{4,0},{8,4},{12,8},{16,12},{20,16},{24,20},{28,24},{32,28},{36,32}... | collective-permute-start | bytes 49160 | tf_op jit(solution)/shard_map/ppermute | solution.py:443
  7.4 0.1 pad_add_fusion.info
  7.5 2.4 %prepare.1 = (f32[2048,128]{1,0:T(8,128)S(1)}, f32[128,128]{1,0:T(8,128)S(1)}, bf16[256,128]{1,0:T(8,128)(2,1)S(1)}) custom-call(s32[3]{0:T(128)S(1)} %pad_add_fusion.info, s32[1,1,2]{2,1,0:T(1,128)S(1)} %copy-done.8, f32[512,512]{1,0:T(8,128)S(1)} %bitcast.15, s32[2,1,1,512]{3,2,1,0:T(1,128)S(1)} %copy-done.3, s32[2,1,1,512]{3,2,1,0:T(1,128)S(1)} %copy-done.4, ...), custom_call_target="tpu_custom_call" | custom-call | tf_op jit(solution)/shard_map/prepare/pallas_call | solution.py:444
  9.9 2.9 %first.1 = f32[2176,128]{1,0:T(8,128)S(1)} custom-call(s32[3]{0:T(128)S(1)} %pad_add_fusion.info, f32[2048,128]{1,0:T(8,128)S(1)} %get-tuple-element.20.state, f32[8,512]{1,0:T(8,128)S(1)} %collective-permute-done.before, f32[8,512]{1,0:T(8,128)S(1)} %collective-permute-done.1.after, f32[128,128]{1,0:T(8,128)S(1)} %get-tuple-element.23.sums, ...), custom_call_target="tpu_custom_call" | custom-call | tf_op jit(solution)/shard_map/first/pallas_call | solution.py:453
  12.9 39.5 %all_to_all.30 = f32[16,136,128]{2,1,0:T(8,128)S(1)} all-to-all(f32[16,136,128]{2,1,0:T(8,128)S(1)} %bitcast.12), channel_id=1, replica_groups=mesh['mem'=4,'hor'=16,'zh'=2,'core'=2] {'mem','zh','core'}, dimensions={0} | all-to-all | bytes 2228224 | tf_op jit(solution)/shard_map/all_to_all | solution.py:430
  52.4 2.2 %gram.1 = (f32[8,72,128]{2,1,0:T(8,128)S(1)}, f32[8,72,128]{2,1,0:T(8,128)S(1)}, f32[16,128]{1,0:T(8,128)S(1)}, s32[16,128]{1,0:T(8,128)S(1)}) custom-call(s32[3]{0:T(128)S(1)} %pad_add_fusion.info, f32[2176,128]{1,0:T(8,128)S(1)} %bitcast.9), custom_call_target="tpu_custom_call" | custom-call | tf_op jit(solution)/shard_map/gram/pallas_call | solution.py:462
  54.6 0.1 collective-permute-start.2
  54.7 1.6 collective-permute-done.2
  56.3 13.4 %all_to_all.31.got = f32[8,72,128]{2,1,0:T(8,128)S(1)} all-to-all(f32[8,72,128]{2,1,0:T(8,128)S(1)} %add.22), channel_id=1, replica_groups=mesh['mem'=4,'hor'=16,'zh'=2,'core'=2] {'mem','zh'}, dimensions={0} | all-to-all | bytes 589824 | tf_op jit(solution)/shard_map/all_to_all | solution.py:430
  69.6 3.1 %root.2 = f32[8,72,128]{2,1,0:T(8,128)S(1)} custom-call(f32[8,72,128]{2,1,0:T(8,128)S(1)} %all_to_all.31.got), custom_call_target="tpu_custom_call" | custom-call | tf_op jit(solution)/shard_map/root/pallas_call | solution.py:472
  72.8 13.3 %all_to_all.32.roots = f32[8,72,128]{2,1,0:T(8,128)S(1)} all-to-all(f32[8,72,128]{2,1,0:T(8,128)S(1)} %root.2), channel_id=1, replica_groups=mesh['mem'=4,'hor'=16,'zh'=2,'core'=2] {'mem','zh'}, dimensions={0} | all-to-all | bytes 589824 | tf_op jit(solution)/shard_map/all_to_all | solution.py:430
  86.0 2.6 %collective-permute-start.3 = (f32[8,72,128]{2,1,0:T(8,128)S(1)}, f32[8,72,128]{2,1,0:T(8,128)S(1)}, u32[]{:S(2)}, u32[]{:S(2)}) collective-permute-start(f32[8,72,128]{2,1,0:T(8,128)S(1)} %all_to_all.32.roots), channel_id=1, source_target_pairs={{0,1},{1,0},{2,3},{3,2},{4,5},{5,4},{6,7},{7,6},{8,9},{9,8},{10,11... | collective-permute-start | bytes 884744 | tf_op jit(solution)/shard_map/ppermute | solution.py:426
  88.6 1.5 apply.2.refs_0_
  90.1 1.5 apply.3
  91.7 1.2 collective-permute-start.4
  92.9 0.0 collective-permute-start.5
  92.9 3.3 %collective-permute-done.4.low = f32[512,128]{1,0:T(8,128)S(1)} collective-permute-done((f32[512,128]{1,0:T(8,128)S(1)}, f32[512,128]{1,0:T(8,128)S(1)}, u32[]{:S(2)}, u32[]{:S(2)}) %collective-permute-start.4) | collective-permute-done | bytes 262176 | tf_op jit(solution)/shard_map/ppermute | solution.py:422
  96.2 2.8 %collective-permute-done.5.high = f32[512,128]{1,0:T(8,128)S(1)} collective-permute-done((f32[512,128]{1,0:T(8,128)S(1)}, f32[512,128]{1,0:T(8,128)S(1)}, u32[]{:S(2)}, u32[]{:S(2)}) %collective-permute-start.5) | collective-permute-done | bytes 262176 | tf_op jit(solution)/shard_map/ppermute | solution.py:422
  99.0 3.5 %forecast.1 = (f32[3072,128]{1,0:T(8,128)S(1)}, f32[8,72,128]{2,1,0:T(8,128)S(1)}, f32[8,72,128]{2,1,0:T(8,128)S(1)}) custom-call(s32[16,128]{1,0:T(8,128)S(1)} %get-tuple-element.25.table, s32[3]{0:T(128)S(1)} %pad_add_fusion.info, f32[2048,128]{1,0:T(8,128)S(1)} %get-tuple-element.28.state, f32[512,128]{1,0:T(8,128)S(1)} %collective-permute-done.4.low, ...), custom_call_target="tpu_custom_call" | custom-call | tf_op jit(solution)/shard_map/forecast/pallas_call | solution.py:494
  102.4 2.7 %collective-permute-start.6 = (f32[8,72,128]{2,1,0:T(8,128)S(1)}, f32[8,72,128]{2,1,0:T(8,128)S(1)}, u32[]{:S(2)}, u32[]{:S(2)}) collective-permute-start(f32[8,72,128]{2,1,0:T(8,128)S(1)} %get-tuple-element.34), channel_id=1, source_target_pairs={{0,1},{1,0},{2,3},{3,2},{4,5},{5,4},{6,7},{7,6},{8,9},{9,8},{10,11... | collective-permute-start | bytes 884744 | tf_op jit(solution)/shard_map/ppermute | solution.py:426
  105.1 1.2 collective-permute-done.6
  106.4 12.9 %all_to_all.33.got = f32[8,72,128]{2,1,0:T(8,128)S(1)} all-to-all(f32[8,72,128]{2,1,0:T(8,128)S(1)} %add.23), channel_id=1, replica_groups=mesh['mem'=4,'hor'=16,'zh'=2,'core'=2] {'mem','zh'}, dimensions={0} | all-to-all | bytes 589824 | tf_op jit(solution)/shard_map/all_to_all | solution.py:430
  119.3 3.1 %root.3 = f32[8,72,128]{2,1,0:T(8,128)S(1)} custom-call(f32[8,72,128]{2,1,0:T(8,128)S(1)} %all_to_all.33.got), custom_call_target="tpu_custom_call" | custom-call | tf_op jit(solution)/shard_map/root/pallas_call | solution.py:472
  122.4 13.2 %all_to_all.34.roots = f32[8,72,128]{2,1,0:T(8,128)S(1)} all-to-all(f32[8,72,128]{2,1,0:T(8,128)S(1)} %root.3), channel_id=1, replica_groups=mesh['mem'=4,'hor'=16,'zh'=2,'core'=2] {'mem','zh'}, dimensions={0} | all-to-all | bytes 589824 | tf_op jit(solution)/shard_map/all_to_all | solution.py:430
  135.6 2.9 %collective-permute-start.7 = (f32[8,72,128]{2,1,0:T(8,128)S(1)}, f32[8,72,128]{2,1,0:T(8,128)S(1)}, u32[]{:S(2)}, u32[]{:S(2)}) collective-permute-start(f32[8,72,128]{2,1,0:T(8,128)S(1)} %all_to_all.34.roots), channel_id=1, source_target_pairs={{0,1},{1,0},{2,3},{3,2},{4,5},{5,4},{6,7},{7,6},{8,9},{9,8},{10,11... | collective-permute-start | bytes 884744 | tf_op jit(solution)/shard_map/ppermute | solution.py:426
  138.5 1.4 analyse.2.refs_0_
  139.9 1.4 analyse.3
  141.3 30.9 %all_to_all.35 = f32[16,128,128]{2,1,0:T(8,128)S(1)} all-to-all(f32[16,128,128]{2,1,0:T(8,128)S(1)} %bitcast.16), channel_id=1, replica_groups=mesh['mem'=4,'hor'=16,'zh'=2,'core'=2] {'mem','zh','core'}, dimensions={0} | all-to-all | bytes 2097152 | tf_op jit(solution)/shard_map/all_to_all | solution.py:430
  172.3 1.9 %place.1 = f32[512,512]{1,0:T(8,128)} custom-call(s32[3]{0:T(128)S(1)} %pad_add_fusion.info, f32[2048,128]{1,0:T(8,128)S(1)} %bitcast.13), custom_call_target="tpu_custom_call" | custom-call | tf_op jit(solution)/shard_map/place/pallas_call | solution.py:517
  (23 shorter events, 0.1 us)
Async XLA Ops:
  0.0 7.5 %copy-start.8 = (s32[1,1,2]{2,1,0:T(1,128)S(1)}, s32[1,1,2]{2,1,0:T(1,128)}, u32[]{:S(2)}) copy-start(s32[1,1,2]{2,1,0:T(1,128)} %partner.1) | copy-start | bytes 28
  0.0 1.2 copy-start
  1.2 6.2 %copy-start.1 = (f32[8,2,32,512]{3,2,1,0:T(8,128)S(1)}, f32[8,2,32,512]{3,2,1,0:T(8,128)}, u32[]{:S(2)}) copy-start(f32[8,2,32,512]{3,2,1,0:T(8,128)} %param.8) | copy-start | bytes 3145732
  1.2 6.2 %copy-start.2 = (f32[32,32]{1,0:T(8,128)S(1)}, f32[32,32]{1,0:T(8,128)}, u32[]{:S(2)}) copy-start(f32[32,32]{1,0:T(8,128)} %coupling.1) | copy-start | bytes 12292
  1.2 6.3 %copy-start.3 = (s32[2,1,1,512]{3,2,1,0:T(1,128)S(1)}, s32[2,1,1,512]{3,2,1,0:T(1,128)}, u32[]{:S(2)}) copy-start(s32[2,1,1,512]{3,2,1,0:T(1,128)} %column.1) | copy-start | bytes 12292
  1.2 6.3 %copy-start.4 = (s32[2,1,1,512]{3,2,1,0:T(1,128)S(1)}, s32[2,1,1,512]{3,2,1,0:T(1,128)}, u32[]{:S(2)}) copy-start(s32[2,1,1,512]{3,2,1,0:T(1,128)} %level.1) | copy-start | bytes 12292
  1.3 6.3 %copy-start.5 = (f32[2,1,1,512]{3,2,1,0:T(1,128)S(1)}, f32[2,1,1,512]{3,2,1,0:T(1,128)}, u32[]{:S(2)}) copy-start(f32[2,1,1,512]{3,2,1,0:T(1,128)} %value.1) | copy-start | bytes 12292
  1.3 6.3 %copy-start.6 = (f32[2,1,1,512]{3,2,1,0:T(1,128)S(1)}, f32[2,1,1,512]{3,2,1,0:T(1,128)}, u32[]{:S(2)}) copy-start(f32[2,1,1,512]{3,2,1,0:T(1,128)} %error.1) | copy-start | bytes 12292
  1.3 6.3 %copy-start.7 = (s32[2,1,1,512]{3,2,1,0:T(1,128)S(1)}, s32[2,1,1,512]{3,2,1,0:T(1,128)}, u32[]{:S(2)}) copy-start(s32[2,1,1,512]{3,2,1,0:T(1,128)} %live.1) | copy-start | bytes 12292
  1.5 8.4 %collective-permute-start = (f32[8,512]{1,0:T(8,128)S(1)}, f32[8,512]{1,0:T(8,128)S(1)}, u32[]{:S(2)}, u32[]{:S(2)}) collective-permute-start(f32[8,512]{1,0:T(8,128)S(1)} %get-tuple-element.21), channel_id=1, source_target_pairs={{0,4},{4,8},{8,12},{12,16},{16,20},{20,24},{24,28},{28,32},{32,36}... | collective-permute-start | bytes 49160 | tf_op jit(solution)/shard_map/ppermute | solution.py:442
  3.6 6.3 %collective-permute-start.1 = (f32[8,512]{1,0:T(8,128)S(1)}, f32[8,512]{1,0:T(8,128)S(1)}, u32[]{:S(2)}, u32[]{:S(2)}) collective-permute-start(f32[8,512]{1,0:T(8,128)S(1)} %get-tuple-element.22), channel_id=1, source_target_pairs={{4,0},{8,4},{12,8},{16,12},{20,16},{24,20},{28,24},{32,28},{36,32}... | collective-permute-start | bytes 49160 | tf_op jit(solution)/shard_map/ppermute | solution.py:443
  54.6 1.7 collective-permute-start.2
  86.0 4.1 %collective-permute-start.3 = (f32[8,72,128]{2,1,0:T(8,128)S(1)}, f32[8,72,128]{2,1,0:T(8,128)S(1)}, u32[]{:S(2)}, u32[]{:S(2)}) collective-permute-start(f32[8,72,128]{2,1,0:T(8,128)S(1)} %all_to_all.32.roots), channel_id=1, source_target_pairs={{0,1},{1,0},{2,3},{3,2},{4,5},{5,4},{6,7},{7,6},{8,9},{9,8},{10,11... | collective-permute-start | bytes 884744 | tf_op jit(solution)/shard_map/ppermute | solution.py:426
  91.7 4.5 %collective-permute-start.4 = (f32[512,128]{1,0:T(8,128)S(1)}, f32[512,128]{1,0:T(8,128)S(1)}, u32[]{:S(2)}, u32[]{:S(2)}) collective-permute-start(f32[512,128]{1,0:T(8,128)S(1)} %get-tuple-element.29), channel_id=1, source_target_pairs={{0,1},{1,64},{64,65},{65,128},{128,129},{129,192},{192,193},{193,2... | collective-permute-start | bytes 786440 | tf_op jit(solution)/shard_map/ppermute | solution.py:422
  92.9 6.1 %collective-permute-start.5 = (f32[512,128]{1,0:T(8,128)S(1)}, f32[512,128]{1,0:T(8,128)S(1)}, u32[]{:S(2)}, u32[]{:S(2)}) collective-permute-start(f32[512,128]{1,0:T(8,128)S(1)} %get-tuple-element.30), channel_id=1, source_target_pairs={{1,0},{64,1},{65,64},{128,65},{129,128},{192,129},{193,192},{2,193... | collective-permute-start | bytes 786440 | tf_op jit(solution)/shard_map/ppermute | solution.py:422
  102.4 3.9 %collective-permute-start.6 = (f32[8,72,128]{2,1,0:T(8,128)S(1)}, f32[8,72,128]{2,1,0:T(8,128)S(1)}, u32[]{:S(2)}, u32[]{:S(2)}) collective-permute-start(f32[8,72,128]{2,1,0:T(8,128)S(1)} %get-tuple-element.34), channel_id=1, source_target_pairs={{0,1},{1,0},{2,3},{3,2},{4,5},{5,4},{6,7},{7,6},{8,9},{9,8},{10,11... | collective-permute-start | bytes 884744 | tf_op jit(solution)/shard_map/ppermute | solution.py:426
  135.6 4.3 %collective-permute-start.7 = (f32[8,72,128]{2,1,0:T(8,128)S(1)}, f32[8,72,128]{2,1,0:T(8,128)S(1)}, u32[]{:S(2)}, u32[]{:S(2)}) collective-permute-start(f32[8,72,128]{2,1,0:T(8,128)S(1)} %all_to_all.34.roots), channel_id=1, source_target_pairs={{0,1},{1,0},{2,3},{3,2},{4,5},{5,4},{6,7},{7,6},{8,9},{9,8},{10,11... | collective-permute-start | bytes 884744 | tf_op jit(solution)/shard_map/ppermute | solution.py:426

commit v5 on v4

--- a/solution.py
+++ b/solution.py
@@ -264,16 +264,20 @@
     blend(fs, table, info[0], keep, send)
 
 
-def forecast_kernel(table, info, state, low, high, hist, mixing, both, keep, send, ps, fs):
+def forecast_kernel(table, info, state, outer, low, high, hist, mixing, both, keep, send, ps, fs, sides):
     edge = HALO * LEVELS
     span = MINE * LEVELS
+    for f in range(2):
+        rows = pl.ds(f * edge, edge)
+        sides[pl.ds(2 * f * edge, edge), :] = jnp.where(info[3] == 0, outer[rows, :], low[rows, :])
+        sides[pl.ds((2 * f + 1) * edge, edge), :] = jnp.where(info[3] == GROUP - 1, outer[rows, :], high[rows, :])
 
     def sources(f, c):
         if c < HALO:
-            return low, f * edge + c * LEVELS
+            return sides, 2 * f * edge + c * LEVELS
         if c < HALO + MINE:
             return state, f * span + (c - HALO) * LEVELS
-        return high, f * edge + (c - HALO - MINE) * LEVELS
+        return sides, (2 * f + 1) * edge + (c - HALO - MINE) * LEVELS
 
     substeps(sources, both, ps, mixing)
     for four in range(8):
@@ -340,10 +344,13 @@
             at = (fj // 2) * span + 2 * s + fj % 2
             out[pl.ds(at, MINE, stride=LEVELS), :] = result[fj * 32 : fj * 32 + 32, :]
     if second:
-        low, high = refs[2:]
+        low, high, outer = refs[2:]
         for f in range(2):
-            low[pl.ds(f * edge, edge), :] = out[pl.ds(f * span, edge), :]
-            high[pl.ds(f * edge, edge), :] = out[pl.ds((f + 1) * span - edge, edge), :]
+            first = out[pl.ds(f * span, edge), :]
+            final = out[pl.ds((f + 1) * span - edge, edge), :]
+            low[pl.ds(f * edge, edge), :] = first
+            high[pl.ds(f * edge, edge), :] = final
+            outer[pl.ds(f * edge, edge), :] = jnp.where(info[3] == GROUP - 1, final, first)
 
 
 def last_apply_kernel(second, info, both, roots, *refs):
@@ -406,20 +413,19 @@
     return jax.ShapeDtypeStruct(shape, dtype)
 
 
-def across(x, forward):
-    pairs = []
-    for hor in range(16):
-        for block in range(GROUP):
-            here = MEMBER_AT[block]
-            nxt = MEMBER_AT[(block + 1) % GROUP]
-            nhor = (hor + (block + 1) // GROUP) % 16
-
-            def flat(g, h):
-                return ((g >> 2) * 16 + h) * 4 + (g & 3)
-
-            pair = (flat(here ^ (15 * (hor & 1)), hor), flat(nxt ^ (15 * (nhor & 1)), nhor))
-            pairs.append(pair if forward else pair[::-1])
-    return lax.ppermute(x, ALL, pairs)
+def holder(block, hor):
+    g = MEMBER_AT[block] ^ (15 * (hor & 1))
+    return ((g >> 2) * 16 + hor) * 4 + (g & 3)
+
+
+def next_block(x, forward):
+    pairs = [(holder(b, hor), holder(b + 1, hor)) for hor in range(16) for b in range(GROUP - 1)]
+    return lax.ppermute(x, ALL, pairs if forward else [(b, a) for a, b in pairs])
+
+
+def next_tile(x):
+    pairs = [(holder(GROUP - 1, hor), holder(0, (hor + 1) % 16)) for hor in range(16)]
+    return lax.ppermute(x, ALL, pairs + [(b, a) for a, b in pairs])
 
 
 def swap(x):
@@ -436,7 +442,7 @@
     members = ensemble.reshape(512, COLS)
     flip = 15 * (lax.axis_index("hor") & 1)
     block = block_of(lax.axis_index(TILE) ^ flip)
-    info = jnp.stack([lax.axis_index("core"), flip, block & 3]).astype(jnp.int32)
+    info = jnp.stack([lax.axis_index("core"), flip, block & 3, block]).astype(jnp.int32)
     first, last = call(edges_kernel, (arr(HALO, COLS), arr(HALO, COLS)), [vmem()], "edges")(members)
     ring = [(i, (i + 1) % 16) for i in range(16)]
     before = lax.ppermute(last, "hor", ring)
@@ -482,22 +488,23 @@
         "apply",
         cost=cost,
     )(info, received, same)
-    state, low, high = call(
+    state, low, high, outer = call(
         functools.partial(first_apply_kernel, True),
-        (arr(2 * rows, WIDTH), arr(edges, WIDTH), arr(edges, WIDTH)),
+        (arr(2 * rows, WIDTH),) + (arr(edges, WIDTH),) * 3,
         [smem()] + [vmem()] * 3,
         "apply",
         aliases={3: 0},
     )(info, received, other, part)
-    from_low = across(high, True)
-    from_high = across(low, False)
+    from_tile = next_tile(outer)
+    from_low = next_block(high, True)
+    from_high = next_block(low, False)
     both, keep, send = call(
         forecast_kernel,
         (arr(2 * WIDE * LEVELS, WIDTH), arr(8, FOLD, 128), arr(8, FOLD, 128)),
-        [smem(), smem()] + [vmem()] * 5,
+        [smem(), smem()] + [vmem()] * 6,
         "forecast",
-        [wide, folded],
-    )(table, info, state, from_low, from_high, hist, mixing)
+        [wide, folded, pltpu.VMEM((4 * HALO * LEVELS, 128), F32)],
+    )(table, info, state, from_tile, from_low, from_high, hist, mixing)
     same, other = roots(keep, send)
     part = call(
         functools.partial(last_apply_kernel, False),

time: 175 us -> 178 us (1.017)
  starting transfers between devices: 15.4 us -> 21.8 us
  waiting for transfers between devices: 8.87 us -> 4.33 us
    ppermute x2 -> x3, starting transfers between devices: 1.18 us -> 9.89 us  [the longest x2 9.22 us: next_block(): lax.ppermute(x, ALL, pairs if forward else [(b, a) for a, b in pairs])]
    ppermute x2 -> x3, waiting for transfers between devices: 6.09 us -> 1.45 us  [the longest x2 1.45 us: next_block(): lax.ppermute(x, ALL, pairs if forward else [(b, a) for a, b in pairs])]
    ppermute x4, starting transfers between devices: 8.32 us -> 6.02 us  [swap(): return lax.ppermute(x, 'core', [(0, 1), (1, 0)])]
  transfers between devices with their start and end apart: 8 -> 9, of which waited for: 4 -> 3; matrix products, arithmetic and copies ran while one was open for 0% -> 0% of each run, Pallas kernels for 3% -> 3%
where the time goes in v5:
time: 178 us; the launch traced here: 176 us
  blocking collectives  123 us (69%)
  Pallas kernels  25.1 us (14%)
  starting transfers between devices  21.8 us (12%)
  waiting for transfers between devices  4.33 us (2%)
    all_to_all x6, blocking collectives, exchange(): return lax.all_to_all(x, axes, split_axis=0, concat_axis=0, tiled=True)  123 us
    ppermute x2, starting transfers between devices, next_block(): lax.ppermute(x, ALL, pairs if forward else [(b, a) for a, b in pairs])  9.22 us
    pallas_call x2, Pallas kernels, roots(): copies = call(root_kernel, arr(8, FOLD, 128), [vmem()], 'root')(parts)  6.25 us
    ppermute x4, starting transfers between devices, swap(): return lax.ppermute(x, 'core', [(0, 1), (1, 0)])  6.02 us
    ppermute x1, starting transfers between devices, shards(): after = lax.ppermute(first, 'hor', [(b, a) for a, b in ring])  3.81 us
  transfers between devices with their start and end apart: 9, of which 3 were waited for; matrix products, arithmetic and copies ran while one was open for 0% of the time, Pallas kernels for 3%

profile of v5, /device:TPU:1, one launch (start us, length us, event | category | flops | bytes accessed | tf_op | source)
XLA Modules:
  0.0 176.3 jit_solution(9314960122474020483)
XLA Ops:
  0.0 1.2 copy-done
  1.3 0.2 edges.1
  1.5 2.1 %collective-permute-start = (f32[8,512]{1,0:T(8,128)S(1)}, f32[8,512]{1,0:T(8,128)S(1)}, u32[]{:S(2)}, u32[]{:S(2)}) collective-permute-start(f32[8,512]{1,0:T(8,128)S(1)} %get-tuple-element.22), channel_id=1, source_target_pairs={{0,4},{4,8},{8,12},{12,16},{16,20},{20,24},{24,28},{28,32},{32,36}... | collective-permute-start | bytes 49160 | tf_op jit(solution)/shard_map/ppermute | solution.py:448
  3.6 3.8 %collective-permute-start.1 = (f32[8,512]{1,0:T(8,128)S(1)}, f32[8,512]{1,0:T(8,128)S(1)}, u32[]{:S(2)}, u32[]{:S(2)}) collective-permute-start(f32[8,512]{1,0:T(8,128)S(1)} %get-tuple-element.23), channel_id=1, source_target_pairs={{4,0},{8,4},{12,8},{16,12},{20,16},{24,20},{28,24},{32,28},{36,32}... | collective-permute-start | bytes 49160 | tf_op jit(solution)/shard_map/ppermute | solution.py:449
  7.4 0.1 pad_add_fusion.info
  7.5 2.4 %prepare.1 = (f32[2048,128]{1,0:T(8,128)S(1)}, f32[128,128]{1,0:T(8,128)S(1)}, bf16[256,128]{1,0:T(8,128)(2,1)S(1)}) custom-call(s32[4]{0:T(128)S(1)} %pad_add_fusion.info, s32[1,1,2]{2,1,0:T(1,128)S(1)} %copy-done.8, f32[512,512]{1,0:T(8,128)S(1)} %bitcast.16, s32[2,1,1,512]{3,2,1,0:T(1,128)S(1)} %copy-done.3, s32[2,1,1,512]{3,2,1,0:T(1,128)S(1)} %copy-done.4, ...), custom_call_target="tpu_custom_call" | custom-call | tf_op jit(solution)/shard_map/prepare/pallas_call | solution.py:450
  9.9 2.9 %first.1 = f32[2176,128]{1,0:T(8,128)S(1)} custom-call(s32[4]{0:T(128)S(1)} %pad_add_fusion.info, f32[2048,128]{1,0:T(8,128)S(1)} %get-tuple-element.21.state, f32[8,512]{1,0:T(8,128)S(1)} %collective-permute-done.before, f32[8,512]{1,0:T(8,128)S(1)} %collective-permute-done.1.after, f32[128,128]{1,0:T(8,128)S(1)} %get-tuple-element.24.sums, ...), custom_call_target="tpu_custom_call" | custom-call | tf_op jit(solution)/shard_map/first/pallas_call | solution.py:459
  12.9 39.5 %all_to_all.30 = f32[16,136,128]{2,1,0:T(8,128)S(1)} all-to-all(f32[16,136,128]{2,1,0:T(8,128)S(1)} %bitcast.13), channel_id=1, replica_groups=mesh['mem'=4,'hor'=16,'zh'=2,'core'=2] {'mem','zh','core'}, dimensions={0} | all-to-all | bytes 2228224 | tf_op jit(solution)/shard_map/all_to_all | solution.py:436
  52.4 2.2 %gram.1 = (f32[8,72,128]{2,1,0:T(8,128)S(1)}, f32[8,72,128]{2,1,0:T(8,128)S(1)}, f32[16,128]{1,0:T(8,128)S(1)}, s32[16,128]{1,0:T(8,128)S(1)}) custom-call(s32[4]{0:T(128)S(1)} %pad_add_fusion.info, f32[2176,128]{1,0:T(8,128)S(1)} %bitcast.10), custom_call_target="tpu_custom_call" | custom-call | tf_op jit(solution)/shard_map/gram/pallas_call | solution.py:468
  54.6 0.1 collective-permute-start.2
  54.7 1.6 collective-permute-done.2
  56.3 13.4 %all_to_all.31.got = f32[8,72,128]{2,1,0:T(8,128)S(1)} all-to-all(f32[8,72,128]{2,1,0:T(8,128)S(1)} %add.22), channel_id=1, replica_groups=mesh['mem'=4,'hor'=16,'zh'=2,'core'=2] {'mem','zh'}, dimensions={0} | all-to-all | bytes 589824 | tf_op jit(solution)/shard_map/all_to_all | solution.py:436
  69.7 3.1 %root.2 = f32[8,72,128]{2,1,0:T(8,128)S(1)} custom-call(f32[8,72,128]{2,1,0:T(8,128)S(1)} %all_to_all.31.got), custom_call_target="tpu_custom_call" | custom-call | tf_op jit(solution)/shard_map/root/pallas_call | solution.py:478
  72.8 13.3 %all_to_all.32.roots = f32[8,72,128]{2,1,0:T(8,128)S(1)} all-to-all(f32[8,72,128]{2,1,0:T(8,128)S(1)} %root.2), channel_id=1, replica_groups=mesh['mem'=4,'hor'=16,'zh'=2,'core'=2] {'mem','zh'}, dimensions={0} | all-to-all | bytes 589824 | tf_op jit(solution)/shard_map/all_to_all | solution.py:436
  86.0 2.6 %collective-permute-start.3 = (f32[8,72,128]{2,1,0:T(8,128)S(1)}, f32[8,72,128]{2,1,0:T(8,128)S(1)}, u32[]{:S(2)}, u32[]{:S(2)}) collective-permute-start(f32[8,72,128]{2,1,0:T(8,128)S(1)} %all_to_all.32.roots), channel_id=1, source_target_pairs={{0,1},{1,0},{2,3},{3,2},{4,5},{5,4},{6,7},{7,6},{8,9},{9,8},{10,11... | collective-permute-start | bytes 884744 | tf_op jit(solution)/shard_map/ppermute | solution.py:432
  88.6 1.5 apply.2.refs_0_
  90.2 1.6 apply.3
  91.7 0.7 collective-permute-start.4
  92.4 3.0 %collective-permute-start.5 = (f32[512,128]{1,0:T(8,128)S(1)}, f32[512,128]{1,0:T(8,128)S(1)}, u32[]{:S(2)}, u32[]{:S(2)}) collective-permute-start(f32[512,128]{1,0:T(8,128)S(1)} %get-tuple-element.31), channel_id=1, source_target_pairs={{0,1},{1,64},{64,65},{65,128},{128,129},{129,192},{192,193},{193,2... | collective-permute-start | bytes 786440 | tf_op jit(solution)/shard_map/ppermute | solution.py:423
  95.4 6.2 %collective-permute-start.6 = (f32[512,128]{1,0:T(8,128)S(1)}, f32[512,128]{1,0:T(8,128)S(1)}, u32[]{:S(2)}, u32[]{:S(2)}) collective-permute-start(f32[512,128]{1,0:T(8,128)S(1)} %get-tuple-element.32), channel_id=1, source_target_pairs={{1,0},{64,1},{65,64},{128,65},{129,128},{192,129},{193,192},{2,193... | collective-permute-start | bytes 786440 | tf_op jit(solution)/shard_map/ppermute | solution.py:423
  101.7 1.4 collective-permute-done.6.high
  103.1 3.5 %forecast.1 = (f32[3072,128]{1,0:T(8,128)S(1)}, f32[8,72,128]{2,1,0:T(8,128)S(1)}, f32[8,72,128]{2,1,0:T(8,128)S(1)}) custom-call(s32[16,128]{1,0:T(8,128)S(1)} %get-tuple-element.26.table, s32[4]{0:T(128)S(1)} %pad_add_fusion.info, f32[2048,128]{1,0:T(8,128)S(1)} %get-tuple-element.29.state, f32[512,128]{1,0:T(8,128)S(1)} %collective-permute-done.4.outer, ...), custom_call_target="tpu_custom_call" | custom-call | tf_op jit(solution)/shard_map/forecast/pallas_call | solution.py:501
  106.6 0.4 collective-permute-start.7
  107.0 1.3 collective-permute-done.7
  108.3 13.0 %all_to_all.33.got = f32[8,72,128]{2,1,0:T(8,128)S(1)} all-to-all(f32[8,72,128]{2,1,0:T(8,128)S(1)} %add.23), channel_id=1, replica_groups=mesh['mem'=4,'hor'=16,'zh'=2,'core'=2] {'mem','zh'}, dimensions={0} | all-to-all | bytes 589824 | tf_op jit(solution)/shard_map/all_to_all | solution.py:436
  121.3 3.1 %root.3 = f32[8,72,128]{2,1,0:T(8,128)S(1)} custom-call(f32[8,72,128]{2,1,0:T(8,128)S(1)} %all_to_all.33.got), custom_call_target="tpu_custom_call" | custom-call | tf_op jit(solution)/shard_map/root/pallas_call | solution.py:478
  124.5 13.2 %all_to_all.34.roots = f32[8,72,128]{2,1,0:T(8,128)S(1)} all-to-all(f32[8,72,128]{2,1,0:T(8,128)S(1)} %root.3), channel_id=1, replica_groups=mesh['mem'=4,'hor'=16,'zh'=2,'core'=2] {'mem','zh'}, dimensions={0} | all-to-all | bytes 589824 | tf_op jit(solution)/shard_map/all_to_all | solution.py:436
  137.7 3.0 %collective-permute-start.8 = (f32[8,72,128]{2,1,0:T(8,128)S(1)}, f32[8,72,128]{2,1,0:T(8,128)S(1)}, u32[]{:S(2)}, u32[]{:S(2)}) collective-permute-start(f32[8,72,128]{2,1,0:T(8,128)S(1)} %all_to_all.34.roots), channel_id=1, source_target_pairs={{0,1},{1,0},{2,3},{3,2},{4,5},{5,4},{6,7},{7,6},{8,9},{9,8},{10,11... | collective-permute-start | bytes 884744 | tf_op jit(solution)/shard_map/ppermute | solution.py:432
  140.7 1.4 analyse.2.refs_0_
  142.1 1.4 analyse.3
  143.5 30.9 %all_to_all.35 = f32[16,128,128]{2,1,0:T(8,128)S(1)} all-to-all(f32[16,128,128]{2,1,0:T(8,128)S(1)} %bitcast.17), channel_id=1, replica_groups=mesh['mem'=4,'hor'=16,'zh'=2,'core'=2] {'mem','zh','core'}, dimensions={0} | all-to-all | bytes 2097152 | tf_op jit(solution)/shard_map/all_to_all | solution.py:436
  174.4 1.9 %place.1 = f32[512,512]{1,0:T(8,128)} custom-call(s32[4]{0:T(128)S(1)} %pad_add_fusion.info, f32[2048,128]{1,0:T(8,128)S(1)} %bitcast.14), custom_call_target="tpu_custom_call" | custom-call | tf_op jit(solution)/shard_map/place/pallas_call | solution.py:524
  (25 shorter events, 0.1 us)
Async XLA Ops:
  0.0 7.5 %copy-start.8 = (s32[1,1,2]{2,1,0:T(1,128)S(1)}, s32[1,1,2]{2,1,0:T(1,128)}, u32[]{:S(2)}) copy-start(s32[1,1,2]{2,1,0:T(1,128)} %partner.1) | copy-start | bytes 28
  0.0 1.2 copy-start
  1.2 6.2 %copy-start.1 = (f32[8,2,32,512]{3,2,1,0:T(8,128)S(1)}, f32[8,2,32,512]{3,2,1,0:T(8,128)}, u32[]{:S(2)}) copy-start(f32[8,2,32,512]{3,2,1,0:T(8,128)} %param.8) | copy-start | bytes 3145732
  1.2 6.2 %copy-start.2 = (f32[32,32]{1,0:T(8,128)S(1)}, f32[32,32]{1,0:T(8,128)}, u32[]{:S(2)}) copy-start(f32[32,32]{1,0:T(8,128)} %coupling.1) | copy-start | bytes 12292
  1.2 6.3 %copy-start.3 = (s32[2,1,1,512]{3,2,1,0:T(1,128)S(1)}, s32[2,1,1,512]{3,2,1,0:T(1,128)}, u32[]{:S(2)}) copy-start(s32[2,1,1,512]{3,2,1,0:T(1,128)} %column.1) | copy-start | bytes 12292
  1.2 6.3 %copy-start.4 = (s32[2,1,1,512]{3,2,1,0:T(1,128)S(1)}, s32[2,1,1,512]{3,2,1,0:T(1,128)}, u32[]{:S(2)}) copy-start(s32[2,1,1,512]{3,2,1,0:T(1,128)} %level.1) | copy-start | bytes 12292
  1.3 6.3 %copy-start.5 = (f32[2,1,1,512]{3,2,1,0:T(1,128)S(1)}, f32[2,1,1,512]{3,2,1,0:T(1,128)}, u32[]{:S(2)}) copy-start(f32[2,1,1,512]{3,2,1,0:T(1,128)} %value.1) | copy-start | bytes 12292
  1.3 6.3 %copy-start.6 = (f32[2,1,1,512]{3,2,1,0:T(1,128)S(1)}, f32[2,1,1,512]{3,2,1,0:T(1,128)}, u32[]{:S(2)}) copy-start(f32[2,1,1,512]{3,2,1,0:T(1,128)} %error.1) | copy-start | bytes 12292
  1.3 6.3 %copy-start.7 = (s32[2,1,1,512]{3,2,1,0:T(1,128)S(1)}, s32[2,1,1,512]{3,2,1,0:T(1,128)}, u32[]{:S(2)}) copy-start(s32[2,1,1,512]{3,2,1,0:T(1,128)} %live.1) | copy-start | bytes 12292
  1.5 8.4 %collective-permute-start = (f32[8,512]{1,0:T(8,128)S(1)}, f32[8,512]{1,0:T(8,128)S(1)}, u32[]{:S(2)}, u32[]{:S(2)}) collective-permute-start(f32[8,512]{1,0:T(8,128)S(1)} %get-tuple-element.22), channel_id=1, source_target_pairs={{0,4},{4,8},{8,12},{12,16},{16,20},{20,24},{24,28},{28,32},{32,36}... | collective-permute-start | bytes 49160 | tf_op jit(solution)/shard_map/ppermute | solution.py:448
  3.6 6.3 %collective-permute-start.1 = (f32[8,512]{1,0:T(8,128)S(1)}, f32[8,512]{1,0:T(8,128)S(1)}, u32[]{:S(2)}, u32[]{:S(2)}) collective-permute-start(f32[8,512]{1,0:T(8,128)S(1)} %get-tuple-element.23), channel_id=1, source_target_pairs={{4,0},{8,4},{12,8},{16,12},{20,16},{24,20},{28,24},{32,28},{36,32}... | collective-permute-start | bytes 49160 | tf_op jit(solution)/shard_map/ppermute | solution.py:449
  54.6 1.7 collective-permute-start.2
  86.0 4.1 %collective-permute-start.3 = (f32[8,72,128]{2,1,0:T(8,128)S(1)}, f32[8,72,128]{2,1,0:T(8,128)S(1)}, u32[]{:S(2)}, u32[]{:S(2)}) collective-permute-start(f32[8,72,128]{2,1,0:T(8,128)S(1)} %all_to_all.32.roots), channel_id=1, source_target_pairs={{0,1},{1,0},{2,3},{3,2},{4,5},{5,4},{6,7},{7,6},{8,9},{9,8},{10,11... | collective-permute-start | bytes 884744 | tf_op jit(solution)/shard_map/ppermute | solution.py:432
  91.7 9.9 %collective-permute-start.4 = (f32[512,128]{1,0:T(8,128)S(1)}, f32[512,128]{1,0:T(8,128)S(1)}, u32[]{:S(2)}, u32[]{:S(2)}) collective-permute-start(f32[512,128]{1,0:T(8,128)S(1)} %get-tuple-element.30), channel_id=1, source_target_pairs={{195,199},{4,8},{203,207},{12,16},{211,215},{20,24},{219,223},{28,... | collective-permute-start | bytes 786440 | tf_op jit(solution)/shard_map/ppermute | solution.py:428
  92.4 9.2 %collective-permute-start.5 = (f32[512,128]{1,0:T(8,128)S(1)}, f32[512,128]{1,0:T(8,128)S(1)}, u32[]{:S(2)}, u32[]{:S(2)}) collective-permute-start(f32[512,128]{1,0:T(8,128)S(1)} %get-tuple-element.31), channel_id=1, source_target_pairs={{0,1},{1,64},{64,65},{65,128},{128,129},{129,192},{192,193},{193,2... | collective-permute-start | bytes 786440 | tf_op jit(solution)/shard_map/ppermute | solution.py:423
  95.4 7.7 %collective-permute-start.6 = (f32[512,128]{1,0:T(8,128)S(1)}, f32[512,128]{1,0:T(8,128)S(1)}, u32[]{:S(2)}, u32[]{:S(2)}) collective-permute-start(f32[512,128]{1,0:T(8,128)S(1)} %get-tuple-element.32), channel_id=1, source_target_pairs={{1,0},{64,1},{65,64},{128,65},{129,128},{192,129},{193,192},{2,193... | collective-permute-start | bytes 786440 | tf_op jit(solution)/shard_map/ppermute | solution.py:423
  106.6 1.7 collective-permute-start.7
  137.7 4.3 %collective-permute-start.8 = (f32[8,72,128]{2,1,0:T(8,128)S(1)}, f32[8,72,128]{2,1,0:T(8,128)S(1)}, u32[]{:S(2)}, u32[]{:S(2)}) collective-permute-start(f32[8,72,128]{2,1,0:T(8,128)S(1)} %all_to_all.34.roots), channel_id=1, source_target_pairs={{0,1},{1,0},{2,3},{3,2},{4,5},{5,4},{6,7},{7,6},{8,9},{9,8},{10,11... | collective-permute-start | bytes 884744 | tf_op jit(solution)/shard_map/ppermute | solution.py:432

commit v6 on v5

--- a/solution.py
+++ b/solution.py
@@ -63,9 +63,12 @@
     return out
 
 
-def edges_kernel(ens, first, last):
-    first[...] = ens[:, 0:128].T[0:HALO, :]
-    last[...] = ens[:, COLS - 128 : COLS].T[128 - HALO :, :]
+def edges_kernel(info, ens, near, far):
+    first = ens[:, 0:128].T[0:HALO, :]
+    last = ens[:, COLS - 128 : COLS].T[128 - HALO :, :]
+    even = info[1] == 0
+    near[...] = jnp.where(even, last, first)
+    far[...] = jnp.where(even, first, last)
 
 
 def prepare_kernel(
@@ -167,13 +170,15 @@
     return jnp.concatenate(rows, axis=0)
 
 
-def first_kernel(info, state, before, after, sums, mixing, packed, both, ps, sides, spare):
+def first_kernel(info, state, near, far, sums, mixing, packed, both, ps, sides, spare):
     span = MINE * LEVELS
     edge = HALO * LEVELS
     pieces = []
-    for ref in (before, after):
+    even = info[1] == 0
+    for before, after in ((far, near), (near, far)):
         for m in range(8):
-            line = ref[:, pl.ds(128 * (m // 2), 128)]
+            lanes = pl.ds(128 * (m // 2), 128)
+            line = jnp.where(even, before[:, lanes], after[:, lanes])
             spare[pl.ds(8 * m, 8), :] = line if m % 2 == 0 else pltpu.roll(line, 64, 1)
         pieces += [spare[pl.ds(c, 8, stride=8), :] for c in range(8)]
     halo = jnp.concatenate(pieces, axis=0).T
@@ -264,13 +269,14 @@
     blend(fs, table, info[0], keep, send)
 
 
-def forecast_kernel(table, info, state, outer, low, high, hist, mixing, both, keep, send, ps, fs, sides):
+def forecast_kernel(table, info, state, outer, inner, hist, mixing, both, keep, send, ps, fs, sides):
     edge = HALO * LEVELS
     span = MINE * LEVELS
+    odd = (info[3] & 1) == 1
     for f in range(2):
         rows = pl.ds(f * edge, edge)
-        sides[pl.ds(2 * f * edge, edge), :] = jnp.where(info[3] == 0, outer[rows, :], low[rows, :])
-        sides[pl.ds((2 * f + 1) * edge, edge), :] = jnp.where(info[3] == GROUP - 1, outer[rows, :], high[rows, :])
+        sides[pl.ds(2 * f * edge, edge), :] = jnp.where(odd, inner[rows, :], outer[rows, :])
+        sides[pl.ds((2 * f + 1) * edge, edge), :] = jnp.where(odd, outer[rows, :], inner[rows, :])
 
     def sources(f, c):
         if c < HALO:
@@ -344,13 +350,13 @@
             at = (fj // 2) * span + 2 * s + fj % 2
             out[pl.ds(at, MINE, stride=LEVELS), :] = result[fj * 32 : fj * 32 + 32, :]
     if second:
-        low, high, outer = refs[2:]
+        outer, inner = refs[2:]
+        odd = (info[3] & 1) == 1
         for f in range(2):
             first = out[pl.ds(f * span, edge), :]
             final = out[pl.ds((f + 1) * span - edge, edge), :]
-            low[pl.ds(f * edge, edge), :] = first
-            high[pl.ds(f * edge, edge), :] = final
-            outer[pl.ds(f * edge, edge), :] = jnp.where(info[3] == GROUP - 1, final, first)
+            outer[pl.ds(f * edge, edge), :] = jnp.where(odd, final, first)
+            inner[pl.ds(f * edge, edge), :] = jnp.where(odd, first, final)
 
 
 def last_apply_kernel(second, info, both, roots, *refs):
@@ -418,14 +424,14 @@
     return ((g >> 2) * 16 + hor) * 4 + (g & 3)
 
 
-def next_block(x, forward):
-    pairs = [(holder(b, hor), holder(b + 1, hor)) for hor in range(16) for b in range(GROUP - 1)]
-    return lax.ppermute(x, ALL, pairs if forward else [(b, a) for a, b in pairs])
-
-
-def next_tile(x):
-    pairs = [(holder(GROUP - 1, hor), holder(0, (hor + 1) % 16)) for hor in range(16)]
-    return lax.ppermute(x, ALL, pairs + [(b, a) for a, b in pairs])
+def block_pairs(start):
+    pairs = []
+    for hor in range(16):
+        for block in range(start, GROUP, 2):
+            after = block + 1
+            pair = (holder(block, hor), holder(after % GROUP, (hor + after // GROUP) % 16))
+            pairs += [pair, pair[::-1]]
+    return pairs
 
 
 def swap(x):
@@ -443,10 +449,9 @@
     flip = 15 * (lax.axis_index("hor") & 1)
     block = block_of(lax.axis_index(TILE) ^ flip)
     info = jnp.stack([lax.axis_index("core"), flip, block & 3, block]).astype(jnp.int32)
-    first, last = call(edges_kernel, (arr(HALO, COLS), arr(HALO, COLS)), [vmem()], "edges")(members)
-    ring = [(i, (i + 1) % 16) for i in range(16)]
-    before = lax.ppermute(last, "hor", ring)
-    after = lax.ppermute(first, "hor", [(b, a) for a, b in ring])
+    near, far = call(edges_kernel, (arr(HALO, COLS), arr(HALO, COLS)), [smem(), vmem()], "edges")(info, members)
+    near = lax.ppermute(near, "hor", [(i, i ^ 1) for i in range(16)])
+    far = lax.ppermute(far, "hor", [(i, (i - 1 + 2 * (i & 1)) % 16) for i in range(16)])
     state, sums, mixing = call(
         prepare_kernel,
         (arr(2 * rows, 128), arr(128, 128), arr(2 * MIX, MIX, dtype=BF16)),
@@ -462,7 +467,7 @@
         [smem()] + [vmem()] * 5,
         "first",
         [fields, wide, pltpu.VMEM((4 * HALO * LEVELS, 128), F32), pltpu.VMEM((64, 128), F32)],
-    )(info, state, before, after, sums, mixing)
+    )(info, state, near, far, sums, mixing)
     received = exchange(packed.reshape(GROUP, 136, 128), TILE).reshape(GROUP * 136, 128)
     folded = pltpu.VMEM((GROUP, FOLD, 128), F32)
     keep, send, hist, table = call(
@@ -488,23 +493,22 @@
         "apply",
         cost=cost,
     )(info, received, same)
-    state, low, high, outer = call(
+    state, outer, inner = call(
         functools.partial(first_apply_kernel, True),
-        (arr(2 * rows, WIDTH),) + (arr(edges, WIDTH),) * 3,
+        (arr(2 * rows, WIDTH),) + (arr(edges, WIDTH),) * 2,
         [smem()] + [vmem()] * 3,
         "apply",
         aliases={3: 0},
     )(info, received, other, part)
-    from_tile = next_tile(outer)
-    from_low = next_block(high, True)
-    from_high = next_block(low, False)
+    outer = lax.ppermute(outer, ALL, block_pairs(1))
+    inner = lax.ppermute(inner, ALL, block_pairs(0))
     both, keep, send = call(
         forecast_kernel,
         (arr(2 * WIDE * LEVELS, WIDTH), arr(8, FOLD, 128), arr(8, FOLD, 128)),
-        [smem(), smem()] + [vmem()] * 6,
+        [smem(), smem()] + [vmem()] * 5,
         "forecast",
         [wide, folded, pltpu.VMEM((4 * HALO * LEVELS, 128), F32)],
-    )(table, info, state, from_tile, from_low, from_high, hist, mixing)
+    )(table, info, state, outer, inner, hist, mixing)
     same, other = roots(keep, send)
     part = call(
         functools.partial(last_apply_kernel, False),

time: 178 us -> 176 us (0.989)
    ppermute x5 -> x4, starting transfers between devices: 15.8 us -> 11.1 us  [the longest x1 4.27 us: shards(): lax.ppermute(far, 'hor', [(i, (i - 1 + 2 * (i & 1)) % 16) for i in range(...]
    ppermute x4, starting transfers between devices: 6.02 us -> 9.71 us  [swap(): return lax.ppermute(x, 'core', [(0, 1), (1, 0)])]
  transfers between devices with their start and end apart: 9 -> 8, of which waited for: 3 -> 3; matrix products, arithmetic and copies ran while one was open for 0% -> 0% of each run, Pallas kernels for 3% -> 3%
where the time goes in v6:
time: 176 us
  blocking collectives  123 us (70%)
  Pallas kernels  25.7 us (15%)
  starting transfers between devices  20.8 us (12%)
  waiting for transfers between devices  3.96 us (2%)
    all_to_all x6, blocking collectives, exchange(): return lax.all_to_all(x, axes, split_axis=0, concat_axis=0, tiled=True)  123 us
    ppermute x4, starting transfers between devices, swap(): return lax.ppermute(x, 'core', [(0, 1), (1, 0)])  9.71 us
    pallas_call x2, Pallas kernels, roots(): copies = call(root_kernel, arr(8, FOLD, 128), [vmem()], 'root')(parts)  6.25 us
    ppermute x1, starting transfers between devices, shards(): lax.ppermute(far, 'hor', [(i, (i - 1 + 2 * (i & 1)) % 16) for i in range(...  4.27 us
    ppermute x1, starting transfers between devices, shards(): inner = lax.ppermute(inner, ALL, block_pairs(0))  3.53 us
  transfers between devices with their start and end apart: 8, of which 3 were waited for; matrix products, arithmetic and copies ran while one was open for 0% of the time, Pallas kernels for 3%

profile of v6, /device:TPU:1, one launch (start us, length us, event | category | flops | bytes accessed | tf_op | source)
XLA Modules:
  0.0 175.5 jit_solution(13923360059721658910)
XLA Ops:
  0.1 0.1 pad_add_fusion.info
  0.1 1.2 copy-done
  1.4 0.7 edges.1
  2.1 2.1 %collective-permute-start = (f32[8,512]{1,0:T(8,128)S(1)}, f32[8,512]{1,0:T(8,128)S(1)}, u32[]{:S(2)}, u32[]{:S(2)}) collective-permute-start(f32[8,512]{1,0:T(8,128)S(1)} %get-tuple-element.21), channel_id=1, source_target_pairs={{0,4},{4,0},{8,12},{12,8},{16,20},{20,16},{24,28},{28,24},{32,36},... | collective-permute-start | bytes 49160 | tf_op jit(solution)/shard_map/ppermute | solution.py:453
  4.2 4.3 %collective-permute-start.1 = (f32[8,512]{1,0:T(8,128)S(1)}, f32[8,512]{1,0:T(8,128)S(1)}, u32[]{:S(2)}, u32[]{:S(2)}) collective-permute-start(f32[8,512]{1,0:T(8,128)S(1)} %get-tuple-element.22), channel_id=1, source_target_pairs={{0,60},{4,8},{8,4},{12,16},{16,12},{20,24},{24,20},{28,32},{32,28}... | collective-permute-start | bytes 49160 | tf_op jit(solution)/shard_map/ppermute | solution.py:454
  8.6 2.4 %prepare.1 = (f32[2048,128]{1,0:T(8,128)S(1)}, f32[128,128]{1,0:T(8,128)S(1)}, bf16[256,128]{1,0:T(8,128)(2,1)S(1)}) custom-call(s32[4]{0:T(128)S(1)} %pad_add_fusion.info, s32[1,1,2]{2,1,0:T(1,128)S(1)} %copy-done.8, f32[512,512]{1,0:T(8,128)S(1)} %bitcast.16, s32[2,1,1,512]{3,2,1,0:T(1,128)S(1)} %copy-done.3, s32[2,1,1,512]{3,2,1,0:T(1,128)S(1)} %copy-done.4, ...), custom_call_target="tpu_custom_call" | custom-call | tf_op jit(solution)/shard_map/prepare/pallas_call | solution.py:455
  11.0 0.0 collective-permute-done.1.far
  11.0 2.9 %first.1 = f32[2176,128]{1,0:T(8,128)S(1)} custom-call(s32[4]{0:T(128)S(1)} %pad_add_fusion.info, f32[2048,128]{1,0:T(8,128)S(1)} %get-tuple-element.20.state, f32[8,512]{1,0:T(8,128)S(1)} %collective-permute-done.near, f32[8,512]{1,0:T(8,128)S(1)} %collective-permute-done.1.far, f32[128,128]{1,0:T(8,128)S(1)} %get-tuple-element.23.sums, ...), custom_call_target="tpu_custom_call" | custom-call | tf_op jit(solution)/shard_map/first/pallas_call | solution.py:464
  13.9 39.8 %all_to_all.30 = f32[16,136,128]{2,1,0:T(8,128)S(1)} all-to-all(f32[16,136,128]{2,1,0:T(8,128)S(1)} %bitcast.13), channel_id=1, replica_groups=mesh['mem'=4,'hor'=16,'zh'=2,'core'=2] {'mem','zh','core'}, dimensions={0} | all-to-all | bytes 2228224 | tf_op jit(solution)/shard_map/all_to_all | solution.py:442
  53.7 2.2 %gram.1 = (f32[8,72,128]{2,1,0:T(8,128)S(1)}, f32[8,72,128]{2,1,0:T(8,128)S(1)}, f32[16,128]{1,0:T(8,128)S(1)}, s32[16,128]{1,0:T(8,128)S(1)}) custom-call(s32[4]{0:T(128)S(1)} %pad_add_fusion.info, f32[2176,128]{1,0:T(8,128)S(1)} %bitcast.10), custom_call_target="tpu_custom_call" | custom-call | tf_op jit(solution)/shard_map/gram/pallas_call | solution.py:473
  55.9 0.1 collective-permute-start.2
  56.0 1.6 collective-permute-done.2
  57.6 13.4 %all_to_all.31.got = f32[8,72,128]{2,1,0:T(8,128)S(1)} all-to-all(f32[8,72,128]{2,1,0:T(8,128)S(1)} %add.22), channel_id=1, replica_groups=mesh['mem'=4,'hor'=16,'zh'=2,'core'=2] {'mem','zh'}, dimensions={0} | all-to-all | bytes 589824 | tf_op jit(solution)/shard_map/all_to_all | solution.py:442
  71.0 3.1 %root.2 = f32[8,72,128]{2,1,0:T(8,128)S(1)} custom-call(f32[8,72,128]{2,1,0:T(8,128)S(1)} %all_to_all.31.got), custom_call_target="tpu_custom_call" | custom-call | tf_op jit(solution)/shard_map/root/pallas_call | solution.py:483
  74.1 13.3 %all_to_all.32.roots = f32[8,72,128]{2,1,0:T(8,128)S(1)} all-to-all(f32[8,72,128]{2,1,0:T(8,128)S(1)} %root.2), channel_id=1, replica_groups=mesh['mem'=4,'hor'=16,'zh'=2,'core'=2] {'mem','zh'}, dimensions={0} | all-to-all | bytes 589824 | tf_op jit(solution)/shard_map/all_to_all | solution.py:442
  87.4 2.6 %collective-permute-start.3 = (f32[8,72,128]{2,1,0:T(8,128)S(1)}, f32[8,72,128]{2,1,0:T(8,128)S(1)}, u32[]{:S(2)}, u32[]{:S(2)}) collective-permute-start(f32[8,72,128]{2,1,0:T(8,128)S(1)} %all_to_all.32.roots), channel_id=1, source_target_pairs={{0,1},{1,0},{2,3},{3,2},{4,5},{5,4},{6,7},{7,6},{8,9},{9,8},{10,11... | collective-permute-start | bytes 884744 | tf_op jit(solution)/shard_map/ppermute | solution.py:438
  90.0 1.5 apply.2.refs_0_
  91.5 1.5 apply.3
  93.0 1.2 collective-permute-start.4
  94.2 3.5 %collective-permute-start.5 = (f32[512,128]{1,0:T(8,128)S(1)}, f32[512,128]{1,0:T(8,128)S(1)}, u32[]{:S(2)}, u32[]{:S(2)}) collective-permute-start(f32[512,128]{1,0:T(8,128)S(1)} %get-tuple-element.30), channel_id=1, source_target_pairs={{0,1},{1,0},{64,65},{65,64},{128,129},{129,128},{192,193},{193,192... | collective-permute-start | bytes 786440 | tf_op jit(solution)/shard_map/ppermute | solution.py:504
  97.7 1.2 collective-permute-done.4.outer
  98.9 3.5 %forecast.1 = (f32[3072,128]{1,0:T(8,128)S(1)}, f32[8,72,128]{2,1,0:T(8,128)S(1)}, f32[8,72,128]{2,1,0:T(8,128)S(1)}) custom-call(s32[16,128]{1,0:T(8,128)S(1)} %get-tuple-element.25.table, s32[4]{0:T(128)S(1)} %pad_add_fusion.info, f32[2048,128]{1,0:T(8,128)S(1)} %get-tuple-element.28.state, f32[512,128]{1,0:T(8,128)S(1)} %collective-permute-done.4.outer, ...), custom_call_target="tpu_custom_call" | custom-call | tf_op jit(solution)/shard_map/forecast/pallas_call | solution.py:505
  102.4 4.1 %collective-permute-start.6 = (f32[8,72,128]{2,1,0:T(8,128)S(1)}, f32[8,72,128]{2,1,0:T(8,128)S(1)}, u32[]{:S(2)}, u32[]{:S(2)}) collective-permute-start(f32[8,72,128]{2,1,0:T(8,128)S(1)} %get-tuple-element.34), channel_id=1, source_target_pairs={{0,1},{1,0},{2,3},{3,2},{4,5},{5,4},{6,7},{7,6},{8,9},{9,8},{10,11... | collective-permute-start | bytes 884744 | tf_op jit(solution)/shard_map/ppermute | solution.py:438
  106.5 1.2 collective-permute-done.6
  107.7 12.9 %all_to_all.33.got = f32[8,72,128]{2,1,0:T(8,128)S(1)} all-to-all(f32[8,72,128]{2,1,0:T(8,128)S(1)} %add.23), channel_id=1, replica_groups=mesh['mem'=4,'hor'=16,'zh'=2,'core'=2] {'mem','zh'}, dimensions={0} | all-to-all | bytes 589824 | tf_op jit(solution)/shard_map/all_to_all | solution.py:442
  120.7 3.1 %root.3 = f32[8,72,128]{2,1,0:T(8,128)S(1)} custom-call(f32[8,72,128]{2,1,0:T(8,128)S(1)} %all_to_all.33.got), custom_call_target="tpu_custom_call" | custom-call | tf_op jit(solution)/shard_map/root/pallas_call | solution.py:483
  123.8 13.2 %all_to_all.34.roots = f32[8,72,128]{2,1,0:T(8,128)S(1)} all-to-all(f32[8,72,128]{2,1,0:T(8,128)S(1)} %root.3), channel_id=1, replica_groups=mesh['mem'=4,'hor'=16,'zh'=2,'core'=2] {'mem','zh'}, dimensions={0} | all-to-all | bytes 589824 | tf_op jit(solution)/shard_map/all_to_all | solution.py:442
  137.0 2.9 %collective-permute-start.7 = (f32[8,72,128]{2,1,0:T(8,128)S(1)}, f32[8,72,128]{2,1,0:T(8,128)S(1)}, u32[]{:S(2)}, u32[]{:S(2)}) collective-permute-start(f32[8,72,128]{2,1,0:T(8,128)S(1)} %all_to_all.34.roots), channel_id=1, source_target_pairs={{0,1},{1,0},{2,3},{3,2},{4,5},{5,4},{6,7},{7,6},{8,9},{9,8},{10,11... | collective-permute-start | bytes 884744 | tf_op jit(solution)/shard_map/ppermute | solution.py:438
  139.9 1.4 analyse.2.refs_0_
  141.3 1.4 analyse.3
  142.7 30.9 %all_to_all.35 = f32[16,128,128]{2,1,0:T(8,128)S(1)} all-to-all(f32[16,128,128]{2,1,0:T(8,128)S(1)} %bitcast.17), channel_id=1, replica_groups=mesh['mem'=4,'hor'=16,'zh'=2,'core'=2] {'mem','zh','core'}, dimensions={0} | all-to-all | bytes 2097152 | tf_op jit(solution)/shard_map/all_to_all | solution.py:442
  173.6 1.9 %place.1 = f32[512,512]{1,0:T(8,128)} custom-call(s32[4]{0:T(128)S(1)} %pad_add_fusion.info, f32[2048,128]{1,0:T(8,128)S(1)} %bitcast.14), custom_call_target="tpu_custom_call" | custom-call | tf_op jit(solution)/shard_map/place/pallas_call | solution.py:528
  (23 shorter events, 0.1 us)
Async XLA Ops:
  0.0 8.5 %copy-start.8 = (s32[1,1,2]{2,1,0:T(1,128)S(1)}, s32[1,1,2]{2,1,0:T(1,128)}, u32[]{:S(2)}) copy-start(s32[1,1,2]{2,1,0:T(1,128)} %partner.1) | copy-start | bytes 28
  0.0 8.5 %copy-start.7 = (s32[2,1,1,512]{3,2,1,0:T(1,128)S(1)}, s32[2,1,1,512]{3,2,1,0:T(1,128)}, u32[]{:S(2)}) copy-start(s32[2,1,1,512]{3,2,1,0:T(1,128)} %live.1) | copy-start | bytes 12292
  0.0 8.5 %copy-start.6 = (f32[2,1,1,512]{3,2,1,0:T(1,128)S(1)}, f32[2,1,1,512]{3,2,1,0:T(1,128)}, u32[]{:S(2)}) copy-start(f32[2,1,1,512]{3,2,1,0:T(1,128)} %error.1) | copy-start | bytes 12292
  0.0 8.5 %copy-start.5 = (f32[2,1,1,512]{3,2,1,0:T(1,128)S(1)}, f32[2,1,1,512]{3,2,1,0:T(1,128)}, u32[]{:S(2)}) copy-start(f32[2,1,1,512]{3,2,1,0:T(1,128)} %value.1) | copy-start | bytes 12292
  0.0 8.5 %copy-start.4 = (s32[2,1,1,512]{3,2,1,0:T(1,128)S(1)}, s32[2,1,1,512]{3,2,1,0:T(1,128)}, u32[]{:S(2)}) copy-start(s32[2,1,1,512]{3,2,1,0:T(1,128)} %level.1) | copy-start | bytes 12292
  0.0 8.5 %copy-start.3 = (s32[2,1,1,512]{3,2,1,0:T(1,128)S(1)}, s32[2,1,1,512]{3,2,1,0:T(1,128)}, u32[]{:S(2)}) copy-start(s32[2,1,1,512]{3,2,1,0:T(1,128)} %column.1) | copy-start | bytes 12292
  0.0 8.5 %copy-start.2 = (f32[32,32]{1,0:T(8,128)S(1)}, f32[32,32]{1,0:T(8,128)}, u32[]{:S(2)}) copy-start(f32[32,32]{1,0:T(8,128)} %coupling.1) | copy-start | bytes 12292
  0.1 1.2 copy-start
  1.4 7.2 %copy-start.1 = (f32[8,2,32,512]{3,2,1,0:T(8,128)S(1)}, f32[8,2,32,512]{3,2,1,0:T(8,128)}, u32[]{:S(2)}) copy-start(f32[8,2,32,512]{3,2,1,0:T(8,128)} %param.8) | copy-start | bytes 3145732
  2.1 8.8 %collective-permute-start = (f32[8,512]{1,0:T(8,128)S(1)}, f32[8,512]{1,0:T(8,128)S(1)}, u32[]{:S(2)}, u32[]{:S(2)}) collective-permute-start(f32[8,512]{1,0:T(8,128)S(1)} %get-tuple-element.21), channel_id=1, source_target_pairs={{0,4},{4,0},{8,12},{12,8},{16,20},{20,16},{24,28},{28,24},{32,36},... | collective-permute-start | bytes 49160 | tf_op jit(solution)/shard_map/ppermute | solution.py:453
  4.2 6.7 %collective-permute-start.1 = (f32[8,512]{1,0:T(8,128)S(1)}, f32[8,512]{1,0:T(8,128)S(1)}, u32[]{:S(2)}, u32[]{:S(2)}) collective-permute-start(f32[8,512]{1,0:T(8,128)S(1)} %get-tuple-element.22), channel_id=1, source_target_pairs={{0,60},{4,8},{8,4},{12,16},{16,12},{20,24},{24,20},{28,32},{32,28}... | collective-permute-start | bytes 49160 | tf_op jit(solution)/shard_map/ppermute | solution.py:454
  55.9 1.7 collective-permute-start.2
  87.4 4.1 %collective-permute-start.3 = (f32[8,72,128]{2,1,0:T(8,128)S(1)}, f32[8,72,128]{2,1,0:T(8,128)S(1)}, u32[]{:S(2)}, u32[]{:S(2)}) collective-permute-start(f32[8,72,128]{2,1,0:T(8,128)S(1)} %all_to_all.32.roots), channel_id=1, source_target_pairs={{0,1},{1,0},{2,3},{3,2},{4,5},{5,4},{6,7},{7,6},{8,9},{9,8},{10,11... | collective-permute-start | bytes 884744 | tf_op jit(solution)/shard_map/ppermute | solution.py:438
  93.0 5.9 %collective-permute-start.4 = (f32[512,128]{1,0:T(8,128)S(1)}, f32[512,128]{1,0:T(8,128)S(1)}, u32[]{:S(2)}, u32[]{:S(2)}) collective-permute-start(f32[512,128]{1,0:T(8,128)S(1)} %get-tuple-element.29), channel_id=1, source_target_pairs={{1,64},{64,1},{65,128},{128,65},{129,192},{192,129},{193,2},{2,193... | collective-permute-start | bytes 786440 | tf_op jit(solution)/shard_map/ppermute | solution.py:503
  94.2 4.7 %collective-permute-start.5 = (f32[512,128]{1,0:T(8,128)S(1)}, f32[512,128]{1,0:T(8,128)S(1)}, u32[]{:S(2)}, u32[]{:S(2)}) collective-permute-start(f32[512,128]{1,0:T(8,128)S(1)} %get-tuple-element.30), channel_id=1, source_target_pairs={{0,1},{1,0},{64,65},{65,64},{128,129},{129,128},{192,193},{193,192... | collective-permute-start | bytes 786440 | tf_op jit(solution)/shard_map/ppermute | solution.py:504
  102.4 5.3 %collective-permute-start.6 = (f32[8,72,128]{2,1,0:T(8,128)S(1)}, f32[8,72,128]{2,1,0:T(8,128)S(1)}, u32[]{:S(2)}, u32[]{:S(2)}) collective-permute-start(f32[8,72,128]{2,1,0:T(8,128)S(1)} %get-tuple-element.34), channel_id=1, source_target_pairs={{0,1},{1,0},{2,3},{3,2},{4,5},{5,4},{6,7},{7,6},{8,9},{9,8},{10,11... | collective-permute-start | bytes 884744 | tf_op jit(solution)/shard_map/ppermute | solution.py:438
  137.0 4.3 %collective-permute-start.7 = (f32[8,72,128]{2,1,0:T(8,128)S(1)}, f32[8,72,128]{2,1,0:T(8,128)S(1)}, u32[]{:S(2)}, u32[]{:S(2)}) collective-permute-start(f32[8,72,128]{2,1,0:T(8,128)S(1)} %all_to_all.34.roots), channel_id=1, source_target_pairs={{0,1},{1,0},{2,3},{3,2},{4,5},{5,4},{6,7},{7,6},{8,9},{9,8},{10,11... | collective-permute-start | bytes 884744 | tf_op jit(solution)/shard_map/ppermute | solution.py:438

commit v7 on v6

--- a/solution.py
+++ b/solution.py
@@ -35,6 +35,13 @@
 MEMBER_AT = {block_of(g): g for g in range(GROUP)}
 
 
+def my_place():
+    core = lax.axis_index("core")
+    flip = 15 * (lax.axis_index("hor") & 1)
+    g = lax.axis_index("mem") * 4 + lax.axis_index("zh") * 2 + core
+    return core, flip, block_of(jnp.bitwise_xor(g, flip))
+
+
 def split(a):
     high = a.astype(BF16)
     return high, (a - high.astype(F32)).astype(BF16)
@@ -63,16 +70,16 @@
     return out
 
 
-def edges_kernel(info, ens, near, far):
+def edges_kernel(ens, near, far):
     first = ens[:, 0:128].T[0:HALO, :]
     last = ens[:, COLS - 128 : COLS].T[128 - HALO :, :]
-    even = info[1] == 0
+    even = my_place()[1] == 0
     near[...] = jnp.where(even, last, first)
     far[...] = jnp.where(even, first, last)
 
 
 def prepare_kernel(
-    info, partner, ens, column, level, value, error, live, coupling, state, out, mixing, tiles, blocks
+    partner, ens, column, level, value, error, live, coupling, state, out, mixing, tiles, blocks
 ):
     for t in range(4):
         tiles[pl.ds(512 * t, 512), :] = ens[:, pl.ds(128 * t, 128)]
@@ -88,7 +95,7 @@
             for i in range(4):
                 at = f * MINE * LEVELS + 4 * four + i
                 state[pl.ds(at, MINE, stride=LEVELS), :] = turned[32 * i : 32 * i + 32, :]
-    member = jnp.bitwise_xor(iota((GROUP, COLS), 0), info[1])
+    member = jnp.bitwise_xor(iota((GROUP, COLS), 0), my_place()[1])
     place = ((member >> 1) & 1) * 8 + (member >> 2) * 2 + (member & 1)
     spot = iota((64, COLS), 0)
     zero = jnp.zeros((64, COLS), F32)
@@ -107,9 +114,8 @@
         )
         out[pl.ds(cycle, GROUP, stride=8), :] = sums
     lane = iota((GROUP, 128), 1)
-    first = partner[0, 0, 0].astype(F32)
-    second = partner[0, 0, 1].astype(F32)
-    out[pl.ds(2, GROUP, stride=8), :] = jnp.where(lane == 0, first, second)
+    both = partner[0].astype(F32)
+    out[pl.ds(2, GROUP, stride=8), :] = jnp.where(lane == 0, both[:, 0:1], both[:, 1:2])
     wide = jnp.concatenate([coupling[...]] * (MIX // LEVELS), axis=1)
     wide = jnp.concatenate([wide] * (MIX // LEVELS), axis=0)
     wide = jnp.where((iota((MIX, MIX), 0) >> 5) == (iota((MIX, MIX), 1) >> 5), RATE * RATE * wide, 0.0)
@@ -170,11 +176,12 @@
     return jnp.concatenate(rows, axis=0)
 
 
-def first_kernel(info, state, near, far, sums, mixing, packed, both, ps, sides, spare):
+def first_kernel(state, near, far, sums, mixing, packed, both, ps, sides, spare):
     span = MINE * LEVELS
     edge = HALO * LEVELS
     pieces = []
-    even = info[1] == 0
+    flip = my_place()[1]
+    even = flip == 0
     for before, after in ((far, near), (near, far)):
         for m in range(8):
             lanes = pl.ds(128 * (m // 2), 128)
@@ -201,7 +208,7 @@
         return sides, (2 * f + 1) * edge + (c - HALO - MINE) * LEVELS
 
     substeps(sources, both, ps, mixing)
-    starts = [jnp.bitwise_xor(MEMBER_AT[k], info[1]) * 136 for k in range(GROUP)]
+    starts = [jnp.bitwise_xor(MEMBER_AT[k], flip) * 136 for k in range(GROUP)]
     for s in range(GROUP):
         square = slab_rows(both, edge, s).T
         for k in range(GROUP):
@@ -258,7 +265,7 @@
     return anomaly, split(anomaly), mean
 
 
-def first_gram_kernel(info, got, keep, send, later, table_out, fs, table, sem):
+def first_gram_kernel(got, keep, send, later, table_out, fs, table, sem):
     table_out[...] = got[pl.ds(130, GROUP, stride=136), :].astype(jnp.int32)
     copy = pltpu.make_async_copy(table_out, table, sem)
     copy.start()
@@ -266,13 +273,15 @@
     for q in range(GROUP):
         gram_of(fs, q, *centred(square_of(got, q)), got[pl.ds(q * 136 + 128, 1), :], True)
     copy.wait()
-    blend(fs, table, info[0], keep, send)
-
-
-def forecast_kernel(table, info, state, outer, inner, hist, mixing, both, keep, send, ps, fs, sides):
+    blend(fs, table, my_place()[0], keep, send)
+
+
+def forecast_kernel(table_in, state, outer, inner, hist, mixing, both, keep, send, ps, fs, sides, table, sem):
     edge = HALO * LEVELS
     span = MINE * LEVELS
-    odd = (info[3] & 1) == 1
+    copy = pltpu.make_async_copy(table_in, table, sem)
+    copy.start()
+    odd = (my_place()[2] & 1) == 1
     for f in range(2):
         rows = pl.ds(f * edge, edge)
         sides[pl.ds(2 * f * edge, edge), :] = jnp.where(odd, inner[rows, :], outer[rows, :])
@@ -291,7 +300,8 @@
         for half in range(2):
             q = 2 * four + half
             gram_of(fs, q, *parts, hist[pl.ds(q, 1), :], half == 1)
-    blend(fs, table, info[0], keep, send)
+    copy.wait()
+    blend(fs, table, my_place()[0], keep, send)
 
 
 def root_kernel(got, out):
@@ -335,11 +345,12 @@
     return split((half + tail[1:2, :]) + (half + tail[2:3, :]).T)
 
 
-def first_apply_kernel(second, info, got, roots, *refs):
+def first_apply_kernel(second, got, roots, *refs):
     out = refs[1] if second else refs[0]
     span = MINE * LEVELS
     edge = HALO * LEVELS
-    parity = 1 - info[0] if second else info[0]
+    core, _, block = my_place()
+    parity = 1 - core if second else core
     for j in range(8):
         s = 2 * j + parity
         square = jnp.concatenate(
@@ -351,7 +362,7 @@
             out[pl.ds(at, MINE, stride=LEVELS), :] = result[fj * 32 : fj * 32 + 32, :]
     if second:
         outer, inner = refs[2:]
-        odd = (info[3] & 1) == 1
+        odd = (block & 1) == 1
         for f in range(2):
             first = out[pl.ds(f * span, edge), :]
             final = out[pl.ds((f + 1) * span - edge, edge), :]
@@ -359,12 +370,13 @@
             inner[pl.ds(f * edge, edge), :] = jnp.where(odd, first, final)
 
 
-def last_apply_kernel(second, info, both, roots, *refs):
+def last_apply_kernel(second, both, roots, *refs):
     out = refs[-1]
-    parity = 1 - info[0] if second else info[0]
+    core, _, block = my_place()
+    parity = 1 - core if second else core
     starts = []
     for chunk in range(4):
-        fj = (chunk + 4 - info[2]) & 3
+        fj = (chunk + 16 - block) & 3
         starts.append((fj >> 1) * (WIDE * LEVELS) + (fj & 1) + HALO * LEVELS)
     for j in range(8):
         s = 2 * j + parity
@@ -376,8 +388,9 @@
             out[pl.ds(pl.multiple_of((g * GROUP + s) * 8, 8), 8), :] = result[g * 8 : g * 8 + 8, :]
 
 
-def place_kernel(info, got, out, tiles):
-    starts = [jnp.bitwise_xor(MEMBER_AT[k], info[1]) * 128 for k in range(GROUP)]
+def place_kernel(got, out, tiles):
+    flip = my_place()[1]
+    starts = [jnp.bitwise_xor(MEMBER_AT[k], flip) * 128 for k in range(GROUP)]
     lane = iota((16, 128), 1)
     for t in range(4):
         for n in range(8):
@@ -397,10 +410,6 @@
     return pl.BlockSpec(memory_space=pltpu.VMEM)
 
 
-def smem():
-    return pl.BlockSpec(memory_space=pltpu.SMEM)
-
-
 def call(kernel, out, ins, name, scratch=(), aliases=None, cost=None):
     return pl.pallas_call(
         kernel,
@@ -446,37 +455,35 @@
     rows = MINE * LEVELS
     edges = 2 * HALO * LEVELS
     members = ensemble.reshape(512, COLS)
-    flip = 15 * (lax.axis_index("hor") & 1)
-    block = block_of(lax.axis_index(TILE) ^ flip)
-    info = jnp.stack([lax.axis_index("core"), flip, block & 3, block]).astype(jnp.int32)
-    near, far = call(edges_kernel, (arr(HALO, COLS), arr(HALO, COLS)), [smem(), vmem()], "edges")(info, members)
+    near, far = call(edges_kernel, (arr(HALO, COLS), arr(HALO, COLS)), [vmem()], "edges")(members)
+    far = lax.ppermute(far, "hor", [(i, (i - 1 + 2 * (i & 1)) % 16) for i in range(16)])
     near = lax.ppermute(near, "hor", [(i, i ^ 1) for i in range(16)])
-    far = lax.ppermute(far, "hor", [(i, (i - 1 + 2 * (i & 1)) % 16) for i in range(16)])
     state, sums, mixing = call(
         prepare_kernel,
         (arr(2 * rows, 128), arr(128, 128), arr(2 * MIX, MIX, dtype=BF16)),
-        [smem()] * 2 + [vmem()] * 7,
+        [vmem()] * 8,
         "prepare",
         [pltpu.VMEM((2048, 128), F32), pltpu.VMEM((2048, 128), F32)],
-    )(info, partners, members, obs_column, obs_level, obs_value, obs_error, obs_live, coupling)
+    )(partners, members, obs_column, obs_level, obs_value, obs_error, obs_live, coupling)
     wide = pltpu.VMEM((WIDE * LEVELS, WIDTH), F32)
     fields = pltpu.VMEM((2 * WIDE * LEVELS, WIDTH), F32)
     packed = call(
         first_kernel,
         arr(GROUP * 136, 128),
-        [smem()] + [vmem()] * 5,
+        [vmem()] * 5,
         "first",
         [fields, wide, pltpu.VMEM((4 * HALO * LEVELS, 128), F32), pltpu.VMEM((64, 128), F32)],
-    )(info, state, near, far, sums, mixing)
+    )(state, near, far, sums, mixing)
     received = exchange(packed.reshape(GROUP, 136, 128), TILE).reshape(GROUP * 136, 128)
     folded = pltpu.VMEM((GROUP, FOLD, 128), F32)
+    scalars = pltpu.SMEM((GROUP, 128), jnp.int32)
     keep, send, hist, table = call(
         first_gram_kernel,
         (arr(8, FOLD, 128), arr(8, FOLD, 128), arr(GROUP, 128), arr(GROUP, 128, dtype=jnp.int32)),
-        [smem(), vmem()],
+        [vmem()],
         "gram",
-        [folded, pltpu.SMEM((GROUP, 128), jnp.int32), pltpu.SemaphoreType.DMA(())],
-    )(info, received)
+        [folded, scalars, pltpu.SemaphoreType.DMA(())],
+    )(received)
 
     def roots(keep, send):
         parts = exchange(keep + swap(send), CHIPS)
@@ -489,43 +496,43 @@
     part = call(
         functools.partial(first_apply_kernel, False),
         arr(2 * rows, WIDTH),
-        [smem()] + [vmem()] * 2,
+        [vmem()] * 2,
         "apply",
         cost=cost,
-    )(info, received, same)
+    )(received, same)
     state, outer, inner = call(
         functools.partial(first_apply_kernel, True),
         (arr(2 * rows, WIDTH),) + (arr(edges, WIDTH),) * 2,
-        [smem()] + [vmem()] * 3,
+        [vmem()] * 3,
         "apply",
-        aliases={3: 0},
-    )(info, received, other, part)
+        aliases={2: 0},
+    )(received, other, part)
     outer = lax.ppermute(outer, ALL, block_pairs(1))
     inner = lax.ppermute(inner, ALL, block_pairs(0))
     both, keep, send = call(
         forecast_kernel,
         (arr(2 * WIDE * LEVELS, WIDTH), arr(8, FOLD, 128), arr(8, FOLD, 128)),
-        [smem(), smem()] + [vmem()] * 5,
+        [vmem()] * 6,
         "forecast",
-        [wide, folded, pltpu.VMEM((4 * HALO * LEVELS, 128), F32)],
-    )(table, info, state, outer, inner, hist, mixing)
+        [wide, folded, pltpu.VMEM((4 * HALO * LEVELS, 128), F32), scalars, pltpu.SemaphoreType.DMA(())],
+    )(table, state, outer, inner, hist, mixing)
     same, other = roots(keep, send)
     part = call(
         functools.partial(last_apply_kernel, False),
         arr(GROUP * 128, 128),
-        [smem()] + [vmem()] * 2,
+        [vmem()] * 2,
         "analyse",
         cost=cost,
-    )(info, both, same)
+    )(both, same)
     analysed = call(
         functools.partial(last_apply_kernel, True),
         arr(GROUP * 128, 128),
-        [smem()] + [vmem()] * 3,
+        [vmem()] * 3,
         "analyse",
-        aliases={3: 0},
-    )(info, both, other, part)
+        aliases={2: 0},
+    )(both, other, part)
     got = exchange(analysed.reshape(GROUP, 128, 128), TILE).reshape(GROUP * 128, 128)
-    placed = call(place_kernel, arr(512, 512), [smem(), vmem()], "place", [pltpu.VMEM((2048, 128), F32)])(info, got)
+    placed = call(place_kernel, arr(512, 512), [vmem()], "place", [pltpu.VMEM((2048, 128), F32)])(got)
     return placed.reshape(ensemble.shape)
 
 

time: 176 us -> 176 us (level)
  Pallas kernels: 25.7 us -> 20 us
  local copies, waits for them, and re-layouts: 1.26 us -> 6.03 us
  waiting for transfers between devices: 3.96 us -> 7.81 us
  starting transfers between devices: 20.8 us -> 17.9 us
    unnamed x18, local copies, waits for them, and re-layouts: 1.26 us -> 6.03 us
    ppermute x1, starting transfers between devices: 3.53 us -> 0.01 us  [shards(): inner = lax.ppermute(inner, ALL, block_pairs(0))]
    ppermute x1, waiting for transfers between devices: 1.17 us -> 4.39 us  [shards(): outer = lax.ppermute(outer, ALL, block_pairs(1))]
  transfers between devices with their start and end apart: 8 -> 8, of which waited for: 3 -> 5; matrix products, arithmetic and copies ran while one was open for 0% -> 0% of each run, Pallas kernels for 3% -> 2%
where the time goes in v7:
time: 176 us
  blocking collectives  124 us (70%)
  Pallas kernels  20 us (11%)
  starting transfers between devices  17.9 us (10%)
  waiting for transfers between devices  7.81 us (4%)
  local copies, waits for them, and re-layouts  6.03 us (3%)
    all_to_all x6, blocking collectives, exchange(): return lax.all_to_all(x, axes, split_axis=0, concat_axis=0, tiled=True)  124 us
    ppermute x4, starting transfers between devices, swap(): return lax.ppermute(x, 'core', [(0, 1), (1, 0)])  10 us
    pallas_call x2, Pallas kernels, roots(): copies = call(root_kernel, arr(8, FOLD, 128), [vmem()], 'root')(parts)  6.24 us
    unnamed x18, local copies, waits for them, and re-layouts  6.03 us
    ppermute x1, waiting for transfers between devices, shards(): outer = lax.ppermute(outer, ALL, block_pairs(1))  4.39 us
    ppermute x1, starting transfers between devices, shards(): lax.ppermute(far, 'hor', [(i, (i - 1 + 2 * (i & 1)) % 16) for i in range(...  4.27 us
  transfers between devices with their start and end apart: 8, of which 5 were waited for; matrix products, arithmetic and copies ran while one was open for 0% of the time, Pallas kernels for 2%

profile of v7, /device:TPU:1, one launch (start us, length us, event | category | flops | bytes accessed | tf_op | source)
XLA Modules:
  0.0 175.5 jit_solution(5938029194711626421)
XLA Ops:
  0.0 1.2 copy-done
  1.4 2.1 %collective-permute-start = (f32[8,512]{1,0:T(8,128)S(1)}, f32[8,512]{1,0:T(8,128)S(1)}, u32[]{:S(2)}, u32[]{:S(2)}) collective-permute-start(f32[8,512]{1,0:T(8,128)S(1)} %get-tuple-element.21), channel_id=1, source_target_pairs={{0,4},{4,0},{8,12},{12,8},{16,20},{20,16},{24,28},{28,24},{32,36},... | collective-permute-start | bytes 49160 | tf_op jit(solution)/shard_map/ppermute | solution.py:460
  3.6 4.3 %collective-permute-start.1 = (f32[8,512]{1,0:T(8,128)S(1)}, f32[8,512]{1,0:T(8,128)S(1)}, u32[]{:S(2)}, u32[]{:S(2)}) collective-permute-start(f32[8,512]{1,0:T(8,128)S(1)} %get-tuple-element.22), channel_id=1, source_target_pairs={{0,60},{4,8},{8,4},{12,16},{16,12},{20,24},{24,20},{28,32},{32,28}... | collective-permute-start | bytes 49160 | tf_op jit(solution)/shard_map/ppermute | solution.py:459
  7.8 0.7 copy-done.2
  9.2 0.7 copy-done.4
  9.9 0.7 copy-done.5
  10.6 0.7 copy-done.6
  11.3 0.7 copy-done.7
  12.6 1.8 %prepare.1 = (f32[2048,128]{1,0:T(8,128)S(1)}, f32[128,128]{1,0:T(8,128)S(1)}, bf16[256,128]{1,0:T(8,128)(2,1)S(1)}) custom-call(s32[1,1,2]{2,1,0:T(1,128)S(1)} %copy-done.8, f32[512,512]{1,0:T(8,128)S(1)} %bitcast.11, s32[2,1,1,512]{3,2,1,0:T(1,128)S(1)} %copy-done.3, s32[2,1,1,512]{3,2,1,0:T(1,128)S(1)} %copy-done.4, f32[2,1,1,512]{3,2,1,0:T(1,128)S(1)} %copy-done.5, ...), custom_call_target="tpu_custom_call" | custom-call | tf_op jit(solution)/shard_map/prepare/pallas_call | solution.py:461
  14.5 2.4 %first.1 = f32[2176,128]{1,0:T(8,128)S(1)} custom-call(f32[2048,128]{1,0:T(8,128)S(1)} %get-tuple-element.20.state, f32[8,512]{1,0:T(8,128)S(1)} %collective-permute-done.near, f32[8,512]{1,0:T(8,128)S(1)} %collective-permute-done.1.far, f32[128,128]{1,0:T(8,128)S(1)} %get-tuple-element.23.sums, bf16[256,128]{1,0:T(8,128)(2,1)S(1)} %get-tuple-element.24.mixing), custom_call_target="tpu_custom_call" | custom-call | tf_op jit(solution)/shard_map/first/pallas_call | solution.py:470
  16.9 39.7 %all_to_all.30 = f32[16,136,128]{2,1,0:T(8,128)S(1)} all-to-all(f32[16,136,128]{2,1,0:T(8,128)S(1)} %bitcast.9), channel_id=1, replica_groups=mesh['mem'=4,'hor'=16,'zh'=2,'core'=2] {'mem','zh','core'}, dimensions={0} | all-to-all | bytes 2228224 | tf_op jit(solution)/shard_map/all_to_all | solution.py:451
  56.6 1.7 gram.1
  58.4 1.6 collective-permute-done.2
  60.0 13.4 %all_to_all.31.got = f32[8,72,128]{2,1,0:T(8,128)S(1)} all-to-all(f32[8,72,128]{2,1,0:T(8,128)S(1)} %add.6), channel_id=1, replica_groups=mesh['mem'=4,'hor'=16,'zh'=2,'core'=2] {'mem','zh'}, dimensions={0} | all-to-all | bytes 589824 | tf_op jit(solution)/shard_map/all_to_all | solution.py:451
  73.4 3.1 %root.2 = f32[8,72,128]{2,1,0:T(8,128)S(1)} custom-call(f32[8,72,128]{2,1,0:T(8,128)S(1)} %all_to_all.31.got), custom_call_target="tpu_custom_call" | custom-call | tf_op jit(solution)/shard_map/root/pallas_call | solution.py:490
  76.5 13.3 %all_to_all.32.roots = f32[8,72,128]{2,1,0:T(8,128)S(1)} all-to-all(f32[8,72,128]{2,1,0:T(8,128)S(1)} %root.2), channel_id=1, replica_groups=mesh['mem'=4,'hor'=16,'zh'=2,'core'=2] {'mem','zh'}, dimensions={0} | all-to-all | bytes 589824 | tf_op jit(solution)/shard_map/all_to_all | solution.py:451
  89.7 2.6 %collective-permute-start.3 = (f32[8,72,128]{2,1,0:T(8,128)S(1)}, f32[8,72,128]{2,1,0:T(8,128)S(1)}, u32[]{:S(2)}, u32[]{:S(2)}) collective-permute-start(f32[8,72,128]{2,1,0:T(8,128)S(1)} %all_to_all.32.roots), channel_id=1, source_target_pairs={{0,1},{1,0},{2,3},{3,2},{4,5},{5,4},{6,7},{7,6},{8,9},{9,8},{10,11... | collective-permute-start | bytes 884744 | tf_op jit(solution)/shard_map/ppermute | solution.py:447
  92.3 0.9 apply.2.refs_0_
  93.5 1.0 apply.3
  94.6 1.5 collective-permute-start.4
  96.1 4.4 %collective-permute-done.4.outer = f32[512,128]{1,0:T(8,128)S(1)} collective-permute-done((f32[512,128]{1,0:T(8,128)S(1)}, f32[512,128]{1,0:T(8,128)S(1)}, u32[]{:S(2)}, u32[]{:S(2)}) %collective-permute-start.4) | collective-permute-done | bytes 262176 | tf_op jit(solution)/shard_map/ppermute | solution.py:510
  100.5 2.7 %forecast.1 = (f32[3072,128]{1,0:T(8,128)S(1)}, f32[8,72,128]{2,1,0:T(8,128)S(1)}, f32[8,72,128]{2,1,0:T(8,128)S(1)}) custom-call(s32[16,128]{1,0:T(8,128)S(1)} %get-tuple-element.25.table_in, f32[2048,128]{1,0:T(8,128)S(1)} %get-tuple-element.28.state, f32[512,128]{1,0:T(8,128)S(1)} %collective-permute-done.4.outer, ...), custom_call_target="tpu_custom_call" | custom-call | tf_op jit(solution)/shard_map/forecast/pallas_call | solution.py:512
  103.2 4.4 %collective-permute-start.6 = (f32[8,72,128]{2,1,0:T(8,128)S(1)}, f32[8,72,128]{2,1,0:T(8,128)S(1)}, u32[]{:S(2)}, u32[]{:S(2)}) collective-permute-start(f32[8,72,128]{2,1,0:T(8,128)S(1)} %get-tuple-element.34), channel_id=1, source_target_pairs={{0,1},{1,0},{2,3},{3,2},{4,5},{5,4},{6,7},{7,6},{8,9},{9,8},{10,11... | collective-permute-start | bytes 884744 | tf_op jit(solution)/shard_map/ppermute | solution.py:447
  107.6 1.2 collective-permute-done.6
  108.8 12.9 %all_to_all.33.got = f32[8,72,128]{2,1,0:T(8,128)S(1)} all-to-all(f32[8,72,128]{2,1,0:T(8,128)S(1)} %add.7), channel_id=1, replica_groups=mesh['mem'=4,'hor'=16,'zh'=2,'core'=2] {'mem','zh'}, dimensions={0} | all-to-all | bytes 589824 | tf_op jit(solution)/shard_map/all_to_all | solution.py:451
  121.7 3.1 %root.3 = f32[8,72,128]{2,1,0:T(8,128)S(1)} custom-call(f32[8,72,128]{2,1,0:T(8,128)S(1)} %all_to_all.33.got), custom_call_target="tpu_custom_call" | custom-call | tf_op jit(solution)/shard_map/root/pallas_call | solution.py:490
  124.8 13.2 %all_to_all.34.roots = f32[8,72,128]{2,1,0:T(8,128)S(1)} all-to-all(f32[8,72,128]{2,1,0:T(8,128)S(1)} %root.3), channel_id=1, replica_groups=mesh['mem'=4,'hor'=16,'zh'=2,'core'=2] {'mem','zh'}, dimensions={0} | all-to-all | bytes 589824 | tf_op jit(solution)/shard_map/all_to_all | solution.py:451
  138.0 2.9 %collective-permute-start.7 = (f32[8,72,128]{2,1,0:T(8,128)S(1)}, f32[8,72,128]{2,1,0:T(8,128)S(1)}, u32[]{:S(2)}, u32[]{:S(2)}) collective-permute-start(f32[8,72,128]{2,1,0:T(8,128)S(1)} %all_to_all.34.roots), channel_id=1, source_target_pairs={{0,1},{1,0},{2,3},{3,2},{4,5},{5,4},{6,7},{7,6},{8,9},{9,8},{10,11... | collective-permute-start | bytes 884744 | tf_op jit(solution)/shard_map/ppermute | solution.py:447
  141.0 0.8 analyse.2.refs_0_
  142.2 0.9 analyse.3
  143.1 31.1 %all_to_all.35 = f32[16,128,128]{2,1,0:T(8,128)S(1)} all-to-all(f32[16,128,128]{2,1,0:T(8,128)S(1)} %bitcast.13), channel_id=1, replica_groups=mesh['mem'=4,'hor'=16,'zh'=2,'core'=2] {'mem','zh','core'}, dimensions={0} | all-to-all | bytes 2097152 | tf_op jit(solution)/shard_map/all_to_all | solution.py:451
  174.2 1.3 place.1
  (22 shorter events, 2.4 us)
Async XLA Ops:
  0.0 1.2 copy-start
  1.2 6.6 %copy-start.1 = (f32[8,2,32,512]{3,2,1,0:T(8,128)S(1)}, f32[8,2,32,512]{3,2,1,0:T(8,128)}, u32[]{:S(2)}) copy-start(f32[8,2,32,512]{3,2,1,0:T(8,128)} %param.8) | copy-start | bytes 3145732
  1.4 13.0 %collective-permute-start = (f32[8,512]{1,0:T(8,128)S(1)}, f32[8,512]{1,0:T(8,128)S(1)}, u32[]{:S(2)}, u32[]{:S(2)}) collective-permute-start(f32[8,512]{1,0:T(8,128)S(1)} %get-tuple-element.21), channel_id=1, source_target_pairs={{0,4},{4,0},{8,12},{12,8},{16,20},{20,16},{24,28},{28,24},{32,36},... | collective-permute-start | bytes 49160 | tf_op jit(solution)/shard_map/ppermute | solution.py:460
  3.6 10.9 %collective-permute-start.1 = (f32[8,512]{1,0:T(8,128)S(1)}, f32[8,512]{1,0:T(8,128)S(1)}, u32[]{:S(2)}, u32[]{:S(2)}) collective-permute-start(f32[8,512]{1,0:T(8,128)S(1)} %get-tuple-element.22), channel_id=1, source_target_pairs={{0,60},{4,8},{8,4},{12,16},{16,12},{20,24},{24,20},{28,32},{32,28}... | collective-permute-start | bytes 49160 | tf_op jit(solution)/shard_map/ppermute | solution.py:459
  7.8 0.7 copy-start.2
  8.5 0.7 copy-start.3
  9.2 0.7 copy-start.4
  9.9 0.7 copy-start.5
  10.6 0.7 copy-start.6
  11.3 0.7 copy-start.7
  12.0 0.7 copy-start.8
  58.3 1.7 collective-permute-start.2
  89.7 3.8 %collective-permute-start.3 = (f32[8,72,128]{2,1,0:T(8,128)S(1)}, f32[8,72,128]{2,1,0:T(8,128)S(1)}, u32[]{:S(2)}, u32[]{:S(2)}) collective-permute-start(f32[8,72,128]{2,1,0:T(8,128)S(1)} %all_to_all.32.roots), channel_id=1, source_target_pairs={{0,1},{1,0},{2,3},{3,2},{4,5},{5,4},{6,7},{7,6},{8,9},{9,8},{10,11... | collective-permute-start | bytes 884744 | tf_op jit(solution)/shard_map/ppermute | solution.py:447
  94.6 5.9 %collective-permute-start.4 = (f32[512,128]{1,0:T(8,128)S(1)}, f32[512,128]{1,0:T(8,128)S(1)}, u32[]{:S(2)}, u32[]{:S(2)}) collective-permute-start(f32[512,128]{1,0:T(8,128)S(1)} %get-tuple-element.29), channel_id=1, source_target_pairs={{1,64},{64,1},{65,128},{128,65},{129,192},{192,129},{193,2},{2,193... | collective-permute-start | bytes 786440 | tf_op jit(solution)/shard_map/ppermute | solution.py:510
  96.1 4.4 %collective-permute-start.5 = (f32[512,128]{1,0:T(8,128)S(1)}, f32[512,128]{1,0:T(8,128)S(1)}, u32[]{:S(2)}, u32[]{:S(2)}) collective-permute-start(f32[512,128]{1,0:T(8,128)S(1)} %get-tuple-element.30), channel_id=1, source_target_pairs={{0,1},{1,0},{64,65},{65,64},{128,129},{129,128},{192,193},{193,192... | collective-permute-start | bytes 786440 | tf_op jit(solution)/shard_map/ppermute | solution.py:511
  103.2 5.6 %collective-permute-start.6 = (f32[8,72,128]{2,1,0:T(8,128)S(1)}, f32[8,72,128]{2,1,0:T(8,128)S(1)}, u32[]{:S(2)}, u32[]{:S(2)}) collective-permute-start(f32[8,72,128]{2,1,0:T(8,128)S(1)} %get-tuple-element.34), channel_id=1, source_target_pairs={{0,1},{1,0},{2,3},{3,2},{4,5},{5,4},{6,7},{7,6},{8,9},{9,8},{10,11... | collective-permute-start | bytes 884744 | tf_op jit(solution)/shard_map/ppermute | solution.py:447
  138.0 4.1 %collective-permute-start.7 = (f32[8,72,128]{2,1,0:T(8,128)S(1)}, f32[8,72,128]{2,1,0:T(8,128)S(1)}, u32[]{:S(2)}, u32[]{:S(2)}) collective-permute-start(f32[8,72,128]{2,1,0:T(8,128)S(1)} %all_to_all.34.roots), channel_id=1, source_target_pairs={{0,1},{1,0},{2,3},{3,2},{4,5},{5,4},{6,7},{7,6},{8,9},{9,8},{10,11... | collective-permute-start | bytes 884744 | tf_op jit(solution)/shard_map/ppermute | solution.py:447

commit v8 on v7

--- a/solution.py
+++ b/solution.py
@@ -455,7 +455,8 @@
     rows = MINE * LEVELS
     edges = 2 * HALO * LEVELS
     members = ensemble.reshape(512, COLS)
-    near, far = call(edges_kernel, (arr(HALO, COLS), arr(HALO, COLS)), [vmem()], "edges")(members)
+    cost = pl.CostEstimate(flops=10**9, bytes_accessed=3 * 2**20, transcendentals=0)
+    near, far = call(edges_kernel, (arr(HALO, COLS), arr(HALO, COLS)), [vmem()], "edges", cost=cost)(members)
     far = lax.ppermute(far, "hor", [(i, (i - 1 + 2 * (i & 1)) % 16) for i in range(16)])
     near = lax.ppermute(near, "hor", [(i, i ^ 1) for i in range(16)])
     state, sums, mixing = call(

time: 176 us -> 172 us (0.977)
  local copies, waits for them, and re-layouts: 6.03 us -> 1.26 us
  waiting for transfers between devices: 7.81 us -> 4.59 us
  starting transfers between devices: 17.9 us -> 21.1 us
    unnamed x18, local copies, waits for them, and re-layouts: 6.03 us -> 1.26 us
    ppermute x1, waiting for transfers between devices: 4.39 us -> 0.87 us  [shards(): outer = lax.ppermute(outer, ALL, block_pairs(1))]
    ppermute x1, starting transfers between devices: 0.01 us -> 3.52 us  [shards(): inner = lax.ppermute(inner, ALL, block_pairs(0))]
  transfers between devices with their start and end apart: 8 -> 8, of which waited for: 5 -> 6; matrix products, arithmetic and copies ran while one was open for 0% -> 0% of each run, Pallas kernels for 2% -> 2%
where the time goes in v8:
time: 172 us; the launch traced here: 171 us
  blocking collectives  124 us (72%)
  starting transfers between devices  21.1 us (12%)
  Pallas kernels  20 us (12%)
  waiting for transfers between devices  4.59 us (3%)
    all_to_all x6, blocking collectives, exchange(): return lax.all_to_all(x, axes, split_axis=0, concat_axis=0, tiled=True)  124 us
    ppermute x4, starting transfers between devices, swap(): return lax.ppermute(x, 'core', [(0, 1), (1, 0)])  9.71 us
    pallas_call x2, Pallas kernels, roots(): copies = call(root_kernel, arr(8, FOLD, 128), [vmem()], 'root')(parts)  6.25 us
    ppermute x1, starting transfers between devices, shards(): lax.ppermute(far, 'hor', [(i, (i - 1 + 2 * (i & 1)) % 16) for i in range(...  4.27 us
    ppermute x1, starting transfers between devices, shards(): inner = lax.ppermute(inner, ALL, block_pairs(0))  3.52 us
  transfers between devices with their start and end apart: 8, of which 6 were waited for; matrix products, arithmetic and copies ran while one was open for 0% of the time, Pallas kernels for 2%

profile of v8, /device:TPU:1, one launch (start us, length us, event | category | flops | bytes accessed | tf_op | source)
XLA Modules:
  0.0 171.4 jit_solution(2624314592760357188)
XLA Ops:
  0.0 1.2 copy-done
  1.3 0.2 edges.1
  1.5 2.1 %collective-permute-start = (f32[8,512]{1,0:T(8,128)S(1)}, f32[8,512]{1,0:T(8,128)S(1)}, u32[]{:S(2)}, u32[]{:S(2)}) collective-permute-start(f32[8,512]{1,0:T(8,128)S(1)} %get-tuple-element.21), channel_id=1, source_target_pairs={{0,4},{4,0},{8,12},{12,8},{16,20},{20,16},{24,28},{28,24},{32,36},... | collective-permute-start | bytes 49160 | tf_op jit(solution)/shard_map/ppermute | solution.py:461
  3.6 4.3 %collective-permute-start.1 = (f32[8,512]{1,0:T(8,128)S(1)}, f32[8,512]{1,0:T(8,128)S(1)}, u32[]{:S(2)}, u32[]{:S(2)}) collective-permute-start(f32[8,512]{1,0:T(8,128)S(1)} %get-tuple-element.22), channel_id=1, source_target_pairs={{0,60},{4,8},{8,4},{12,16},{16,12},{20,24},{24,20},{28,32},{32,28}... | collective-permute-start | bytes 49160 | tf_op jit(solution)/shard_map/ppermute | solution.py:460
  7.9 1.8 %prepare.1 = (f32[2048,128]{1,0:T(8,128)S(1)}, f32[128,128]{1,0:T(8,128)S(1)}, bf16[256,128]{1,0:T(8,128)(2,1)S(1)}) custom-call(s32[1,1,2]{2,1,0:T(1,128)S(1)} %copy-done.8, f32[512,512]{1,0:T(8,128)S(1)} %bitcast.13, s32[2,1,1,512]{3,2,1,0:T(1,128)S(1)} %copy-done.3, s32[2,1,1,512]{3,2,1,0:T(1,128)S(1)} %copy-done.4, f32[2,1,1,512]{3,2,1,0:T(1,128)S(1)} %copy-done.5, ...), custom_call_target="tpu_custom_call" | custom-call | tf_op jit(solution)/shard_map/prepare/pallas_call | solution.py:462
  9.8 2.4 %first.1 = f32[2176,128]{1,0:T(8,128)S(1)} custom-call(f32[2048,128]{1,0:T(8,128)S(1)} %get-tuple-element.20.state, f32[8,512]{1,0:T(8,128)S(1)} %collective-permute-done.near, f32[8,512]{1,0:T(8,128)S(1)} %collective-permute-done.1.far, f32[128,128]{1,0:T(8,128)S(1)} %get-tuple-element.23.sums, bf16[256,128]{1,0:T(8,128)(2,1)S(1)} %get-tuple-element.24.mixing), custom_call_target="tpu_custom_call" | custom-call | tf_op jit(solution)/shard_map/first/pallas_call | solution.py:471
  12.2 40.3 %all_to_all.30 = f32[16,136,128]{2,1,0:T(8,128)S(1)} all-to-all(f32[16,136,128]{2,1,0:T(8,128)S(1)} %bitcast.9), channel_id=1, replica_groups=mesh['mem'=4,'hor'=16,'zh'=2,'core'=2] {'mem','zh','core'}, dimensions={0} | all-to-all | bytes 2228224 | tf_op jit(solution)/shard_map/all_to_all | solution.py:451
  52.5 1.7 gram.1
  54.3 1.6 collective-permute-done.2
  55.9 13.4 %all_to_all.31.got = f32[8,72,128]{2,1,0:T(8,128)S(1)} all-to-all(f32[8,72,128]{2,1,0:T(8,128)S(1)} %add.6), channel_id=1, replica_groups=mesh['mem'=4,'hor'=16,'zh'=2,'core'=2] {'mem','zh'}, dimensions={0} | all-to-all | bytes 589824 | tf_op jit(solution)/shard_map/all_to_all | solution.py:451
  69.3 3.1 %root.2 = f32[8,72,128]{2,1,0:T(8,128)S(1)} custom-call(f32[8,72,128]{2,1,0:T(8,128)S(1)} %all_to_all.31.got), custom_call_target="tpu_custom_call" | custom-call | tf_op jit(solution)/shard_map/root/pallas_call | solution.py:491
  72.4 13.3 %all_to_all.32.roots = f32[8,72,128]{2,1,0:T(8,128)S(1)} all-to-all(f32[8,72,128]{2,1,0:T(8,128)S(1)} %root.2), channel_id=1, replica_groups=mesh['mem'=4,'hor'=16,'zh'=2,'core'=2] {'mem','zh'}, dimensions={0} | all-to-all | bytes 589824 | tf_op jit(solution)/shard_map/all_to_all | solution.py:451
  85.6 2.6 %collective-permute-start.3 = (f32[8,72,128]{2,1,0:T(8,128)S(1)}, f32[8,72,128]{2,1,0:T(8,128)S(1)}, u32[]{:S(2)}, u32[]{:S(2)}) collective-permute-start(f32[8,72,128]{2,1,0:T(8,128)S(1)} %all_to_all.32.roots), channel_id=1, source_target_pairs={{0,1},{1,0},{2,3},{3,2},{4,5},{5,4},{6,7},{7,6},{8,9},{9,8},{10,11... | collective-permute-start | bytes 884744 | tf_op jit(solution)/shard_map/ppermute | solution.py:447
  88.2 0.9 apply.2.refs_0_
  89.2 0.3 collective-permute-done.3.roots
  89.5 1.0 apply.3
  90.5 1.5 collective-permute-start.4
  92.0 3.5 %collective-permute-start.5 = (f32[512,128]{1,0:T(8,128)S(1)}, f32[512,128]{1,0:T(8,128)S(1)}, u32[]{:S(2)}, u32[]{:S(2)}) collective-permute-start(f32[512,128]{1,0:T(8,128)S(1)} %get-tuple-element.30), channel_id=1, source_target_pairs={{0,1},{1,0},{64,65},{65,64},{128,129},{129,128},{192,193},{193,192... | collective-permute-start | bytes 786440 | tf_op jit(solution)/shard_map/ppermute | solution.py:512
  95.5 0.9 collective-permute-done.4.outer
  96.4 0.3 collective-permute-done.5.inner
  96.7 2.7 %forecast.1 = (f32[3072,128]{1,0:T(8,128)S(1)}, f32[8,72,128]{2,1,0:T(8,128)S(1)}, f32[8,72,128]{2,1,0:T(8,128)S(1)}) custom-call(s32[16,128]{1,0:T(8,128)S(1)} %get-tuple-element.25.table_in, f32[2048,128]{1,0:T(8,128)S(1)} %get-tuple-element.28.state, f32[512,128]{1,0:T(8,128)S(1)} %collective-permute-done.4.outer, ...), custom_call_target="tpu_custom_call" | custom-call | tf_op jit(solution)/shard_map/forecast/pallas_call | solution.py:513
  99.4 4.1 %collective-permute-start.6 = (f32[8,72,128]{2,1,0:T(8,128)S(1)}, f32[8,72,128]{2,1,0:T(8,128)S(1)}, u32[]{:S(2)}, u32[]{:S(2)}) collective-permute-start(f32[8,72,128]{2,1,0:T(8,128)S(1)} %get-tuple-element.34), channel_id=1, source_target_pairs={{0,1},{1,0},{2,3},{3,2},{4,5},{5,4},{6,7},{7,6},{8,9},{9,8},{10,11... | collective-permute-start | bytes 884744 | tf_op jit(solution)/shard_map/ppermute | solution.py:447
  103.5 1.2 collective-permute-done.6
  104.7 12.9 %all_to_all.33.got = f32[8,72,128]{2,1,0:T(8,128)S(1)} all-to-all(f32[8,72,128]{2,1,0:T(8,128)S(1)} %add.7), channel_id=1, replica_groups=mesh['mem'=4,'hor'=16,'zh'=2,'core'=2] {'mem','zh'}, dimensions={0} | all-to-all | bytes 589824 | tf_op jit(solution)/shard_map/all_to_all | solution.py:451
  117.6 3.1 %root.3 = f32[8,72,128]{2,1,0:T(8,128)S(1)} custom-call(f32[8,72,128]{2,1,0:T(8,128)S(1)} %all_to_all.33.got), custom_call_target="tpu_custom_call" | custom-call | tf_op jit(solution)/shard_map/root/pallas_call | solution.py:491
  120.8 13.2 %all_to_all.34.roots = f32[8,72,128]{2,1,0:T(8,128)S(1)} all-to-all(f32[8,72,128]{2,1,0:T(8,128)S(1)} %root.3), channel_id=1, replica_groups=mesh['mem'=4,'hor'=16,'zh'=2,'core'=2] {'mem','zh'}, dimensions={0} | all-to-all | bytes 589824 | tf_op jit(solution)/shard_map/all_to_all | solution.py:451
  133.9 2.9 %collective-permute-start.7 = (f32[8,72,128]{2,1,0:T(8,128)S(1)}, f32[8,72,128]{2,1,0:T(8,128)S(1)}, u32[]{:S(2)}, u32[]{:S(2)}) collective-permute-start(f32[8,72,128]{2,1,0:T(8,128)S(1)} %all_to_all.34.roots), channel_id=1, source_target_pairs={{0,1},{1,0},{2,3},{3,2},{4,5},{5,4},{6,7},{7,6},{8,9},{9,8},{10,11... | collective-permute-start | bytes 884744 | tf_op jit(solution)/shard_map/ppermute | solution.py:447
  136.9 0.8 analyse.2.refs_0_
  137.7 0.4 collective-permute-done.7.roots
  138.1 0.9 analyse.3
  139.0 31.1 %all_to_all.35 = f32[16,128,128]{2,1,0:T(8,128)S(1)} all-to-all(f32[16,128,128]{2,1,0:T(8,128)S(1)} %bitcast.11), channel_id=1, replica_groups=mesh['mem'=4,'hor'=16,'zh'=2,'core'=2] {'mem','zh','core'}, dimensions={0} | all-to-all | bytes 2097152 | tf_op jit(solution)/shard_map/all_to_all | solution.py:451
  170.1 1.3 place.1
  (22 shorter events, 0.2 us)
Async XLA Ops:
  0.0 1.2 copy-start
  1.2 6.6 %copy-start.1 = (f32[8,2,32,512]{3,2,1,0:T(8,128)S(1)}, f32[8,2,32,512]{3,2,1,0:T(8,128)}, u32[]{:S(2)}) copy-start(f32[8,2,32,512]{3,2,1,0:T(8,128)} %param.8) | copy-start | bytes 3145732
  1.2 6.6 %copy-start.2 = (f32[32,32]{1,0:T(8,128)S(1)}, f32[32,32]{1,0:T(8,128)}, u32[]{:S(2)}) copy-start(f32[32,32]{1,0:T(8,128)} %coupling.1) | copy-start | bytes 12292
  1.2 6.6 %copy-start.3 = (s32[2,1,1,512]{3,2,1,0:T(1,128)S(1)}, s32[2,1,1,512]{3,2,1,0:T(1,128)}, u32[]{:S(2)}) copy-start(s32[2,1,1,512]{3,2,1,0:T(1,128)} %column.1) | copy-start | bytes 12292
  1.2 6.6 %copy-start.4 = (s32[2,1,1,512]{3,2,1,0:T(1,128)S(1)}, s32[2,1,1,512]{3,2,1,0:T(1,128)}, u32[]{:S(2)}) copy-start(s32[2,1,1,512]{3,2,1,0:T(1,128)} %level.1) | copy-start | bytes 12292
  1.2 6.6 %copy-start.5 = (f32[2,1,1,512]{3,2,1,0:T(1,128)S(1)}, f32[2,1,1,512]{3,2,1,0:T(1,128)}, u32[]{:S(2)}) copy-start(f32[2,1,1,512]{3,2,1,0:T(1,128)} %value.1) | copy-start | bytes 12292
  1.2 6.6 %copy-start.6 = (f32[2,1,1,512]{3,2,1,0:T(1,128)S(1)}, f32[2,1,1,512]{3,2,1,0:T(1,128)}, u32[]{:S(2)}) copy-start(f32[2,1,1,512]{3,2,1,0:T(1,128)} %error.1) | copy-start | bytes 12292
  1.3 6.6 %copy-start.7 = (s32[2,1,1,512]{3,2,1,0:T(1,128)S(1)}, s32[2,1,1,512]{3,2,1,0:T(1,128)}, u32[]{:S(2)}) copy-start(s32[2,1,1,512]{3,2,1,0:T(1,128)} %live.1) | copy-start | bytes 12292
  1.3 6.6 %copy-start.8 = (s32[1,1,2]{2,1,0:T(1,128)S(1)}, s32[1,1,2]{2,1,0:T(1,128)}, u32[]{:S(2)}) copy-start(s32[1,1,2]{2,1,0:T(1,128)} %partner.1) | copy-start | bytes 28
  1.5 8.3 %collective-permute-start = (f32[8,512]{1,0:T(8,128)S(1)}, f32[8,512]{1,0:T(8,128)S(1)}, u32[]{:S(2)}, u32[]{:S(2)}) collective-permute-start(f32[8,512]{1,0:T(8,128)S(1)} %get-tuple-element.21), channel_id=1, source_target_pairs={{0,4},{4,0},{8,12},{12,8},{16,20},{20,16},{24,28},{28,24},{32,36},... | collective-permute-start | bytes 49160 | tf_op jit(solution)/shard_map/ppermute | solution.py:461
  3.6 6.2 %collective-permute-start.1 = (f32[8,512]{1,0:T(8,128)S(1)}, f32[8,512]{1,0:T(8,128)S(1)}, u32[]{:S(2)}, u32[]{:S(2)}) collective-permute-start(f32[8,512]{1,0:T(8,128)S(1)} %get-tuple-element.22), channel_id=1, source_target_pairs={{0,60},{4,8},{8,4},{12,16},{16,12},{20,24},{24,20},{28,32},{32,28}... | collective-permute-start | bytes 49160 | tf_op jit(solution)/shard_map/ppermute | solution.py:460
  54.2 1.7 collective-permute-start.2
  85.6 3.8 %collective-permute-start.3 = (f32[8,72,128]{2,1,0:T(8,128)S(1)}, f32[8,72,128]{2,1,0:T(8,128)S(1)}, u32[]{:S(2)}, u32[]{:S(2)}) collective-permute-start(f32[8,72,128]{2,1,0:T(8,128)S(1)} %all_to_all.32.roots), channel_id=1, source_target_pairs={{0,1},{1,0},{2,3},{3,2},{4,5},{5,4},{6,7},{7,6},{8,9},{9,8},{10,11... | collective-permute-start | bytes 884744 | tf_op jit(solution)/shard_map/ppermute | solution.py:447
  90.5 5.9 %collective-permute-start.4 = (f32[512,128]{1,0:T(8,128)S(1)}, f32[512,128]{1,0:T(8,128)S(1)}, u32[]{:S(2)}, u32[]{:S(2)}) collective-permute-start(f32[512,128]{1,0:T(8,128)S(1)} %get-tuple-element.29), channel_id=1, source_target_pairs={{1,64},{64,1},{65,128},{128,65},{129,192},{192,129},{193,2},{2,193... | collective-permute-start | bytes 786440 | tf_op jit(solution)/shard_map/ppermute | solution.py:511
  92.0 4.7 %collective-permute-start.5 = (f32[512,128]{1,0:T(8,128)S(1)}, f32[512,128]{1,0:T(8,128)S(1)}, u32[]{:S(2)}, u32[]{:S(2)}) collective-permute-start(f32[512,128]{1,0:T(8,128)S(1)} %get-tuple-element.30), channel_id=1, source_target_pairs={{0,1},{1,0},{64,65},{65,64},{128,129},{129,128},{192,193},{193,192... | collective-permute-start | bytes 786440 | tf_op jit(solution)/shard_map/ppermute | solution.py:512
  99.4 5.3 %collective-permute-start.6 = (f32[8,72,128]{2,1,0:T(8,128)S(1)}, f32[8,72,128]{2,1,0:T(8,128)S(1)}, u32[]{:S(2)}, u32[]{:S(2)}) collective-permute-start(f32[8,72,128]{2,1,0:T(8,128)S(1)} %get-tuple-element.34), channel_id=1, source_target_pairs={{0,1},{1,0},{2,3},{3,2},{4,5},{5,4},{6,7},{7,6},{8,9},{9,8},{10,11... | collective-permute-start | bytes 884744 | tf_op jit(solution)/shard_map/ppermute | solution.py:447
  133.9 4.1 %collective-permute-start.7 = (f32[8,72,128]{2,1,0:T(8,128)S(1)}, f32[8,72,128]{2,1,0:T(8,128)S(1)}, u32[]{:S(2)}, u32[]{:S(2)}) collective-permute-start(f32[8,72,128]{2,1,0:T(8,128)S(1)} %all_to_all.34.roots), channel_id=1, source_target_pairs={{0,1},{1,0},{2,3},{3,2},{4,5},{5,4},{6,7},{7,6},{8,9},{9,8},{10,11... | collective-permute-start | bytes 884744 | tf_op jit(solution)/shard_map/ppermute | solution.py:447

commit v9 on v8

--- a/solution.py
+++ b/solution.py
@@ -19,10 +19,11 @@
 MINE = COLS // GROUP
 HALO = 2 * SUBSTEPS
 WIDE = MINE + 2 * HALO
+FINAL = (4 - 1) * 2 * WIDE * 32
 FOLD = 72
 F32 = jnp.float32
 BF16 = jnp.bfloat16
-VMEM_LIMIT = 48 * 1024 * 1024
+VMEM_LIMIT = 16 * 1024 * 1024
 ALL = ("mem", "hor", "zh", "core")
 TILE = ("mem", "zh", "core")
 CHIPS = ("mem", "zh")
@@ -124,44 +125,81 @@
     mixing[pl.ds(MIX, MIX), :] = rest
 
 
-def substeps(sources, both, ps, mixing):
+def rows_after(sources, levels, step, f, c, count=1):
+    if step == 0:
+        ref, at = sources(f, c)
+        return ref[pl.ds(at, count * LEVELS), :]
+    return levels[pl.ds(((step - 1) * 2 + f) * WIDE * LEVELS + c * LEVELS, count * LEVELS), :]
+
+
+def pressures(step, groups, sources, levels, ps, mixing):
     mix = (mixing[pl.ds(0, MIX), :], mixing[pl.ds(MIX, MIX), :])
-    wide = WIDE * LEVELS
-    for c in (0, WIDE - 2):
-        both[pl.ds(wide + c * LEVELS, 2 * LEVELS), :] = jnp.zeros((2 * LEVELS, WIDTH), F32)
-
-    def rows(step, f, c, count):
-        if step == 0:
-            ref, at = sources(f, c)
-            return ref[pl.ds(at, count * LEVELS), :]
-        return both[pl.ds(f * wide + c * LEVELS, count * LEVELS), :]
-
-    def speed(step, c):
-        return RATE * rows(0, 0, c, 1) if step == 0 else rows(step, 0, c, 1)
-
     many = MIX // LEVELS
-    for step in range(SUBSTEPS):
+    for c in groups:
+        block = jnp.concatenate(
+            [rows_after(sources, levels, step - 1, 1, c, many), rows_after(sources, levels, step - 1, 1, c + many, many)],
+            axis=1,
+        )
+        pressure = dot_split(mix, split(block))
+        ps[pl.ds(c * LEVELS, MIX), :] = pressure[:, :128]
+        ps[pl.ds(c * LEVELS + MIX, MIX), :] = pressure[:, 128:]
+
+
+def sweep(step, start, stop, new, sources, levels, ps):
+    last = step == SUBSTEPS
+
+    def speed(at, c):
+        value = rows_after(sources, levels, at, 0, c)
+        return RATE * value if at in (0, SUBSTEPS) else value
+
+    def slope(c):
+        return ps[pl.ds(c * LEVELS, LEVELS), :]
+
+    def put(f, c, value):
+        levels[pl.ds(((step - 1) * 2 + f) * WIDE * LEVELS + c * LEVELS, LEVELS), :] = value
+
+    flux_two, flux_one, height_one = None, None, None
+    for c in range(start, stop):
+        if new[0] <= c < new[1]:
+            here = speed(step - 1, c)
+            change = here * (speed(step - 1, c + 1) - speed(step - 1, c - 1))
+            moved = (here - change) - (slope(c + 1) - slope(c - 1))
+            put(0, c, moved * (1.0 / RATE) if last else moved)
+        else:
+            moved = speed(step, c)
+        height = rows_after(sources, levels, step - 1, 1, c)
+        flux = moved * height
+        if c >= start + 2:
+            put(1, c - 1, height_one - (flux - flux_two))
+        flux_two, flux_one, height_one = flux_one, flux, height
+
+
+def inner_kernel(state, mixing, levels, ps):
+    span = MINE * LEVELS
+
+    def sources(f, c):
+        return state, f * span + (c - HALO) * LEVELS
+
+    blank = jnp.zeros((LEVELS, 128), F32)
+    for step in range(1, SUBSTEPS + 1):
+        lo, hi = HALO + 2 * step, HALO + MINE - 2 * step
+        if step < SUBSTEPS:
+            for c in [*range(HALO, lo), *range(hi, HALO + MINE)]:
+                levels[pl.ds(((step - 1) * 2 + 1) * WIDE * LEVELS + c * LEVELS, LEVELS), :] = blank
+        pressures(step, range(HALO, HALO + MINE, 8), sources, levels, ps, mixing)
+        sweep(step, lo - 1, hi + 1, (lo - 1, hi + 1), sources, levels, ps)
+
+
+def outer_steps(sources, levels, ps, mixing):
+    blank = jnp.zeros((LEVELS, 128), F32)
+    for step in range(1, SUBSTEPS + 1):
         lo, hi = 2 * step, WIDE - 2 * step
-        for c in range(0, WIDE, 2 * many):
-            block = jnp.concatenate([rows(step, 1, c, many), rows(step, 1, c + many, many)], axis=1)
-            pressure = dot_split(mix, split(block))
-            ps[pl.ds(c * LEVELS, MIX), :] = pressure[:, :128]
-            ps[pl.ds(c * LEVELS + MIX, MIX), :] = pressure[:, 128:]
-        before, here = speed(step, lo), speed(step, lo + 1)
-        slope_one, slope_two = ps[pl.ds(lo * LEVELS, LEVELS), :], ps[pl.ds((lo + 1) * LEVELS, LEVELS), :]
-        flux_two, flux_one, height_one = None, None, None
-        for c in range(lo + 1, hi - 1):
-            after = speed(step, c + 1)
-            slope = ps[pl.ds((c + 1) * LEVELS, LEVELS), :]
-            moved = (here - here * (after - before)) - (slope - slope_one)
-            height = rows(step, 1, c, 1)
-            flux = moved * height
-            if c >= lo + 3:
-                both[pl.ds(wide + (c - 1) * LEVELS, LEVELS), :] = height_one - (flux - flux_two)
-            both[pl.ds(c * LEVELS, LEVELS), :] = moved if step < SUBSTEPS - 1 else moved * (1.0 / RATE)
-            before, here = here, after
-            slope_one, slope_two = slope_two, slope
-            flux_two, flux_one, height_one = flux_one, flux, height
+        if step < SUBSTEPS:
+            for c in [*range(lo), *range(hi, WIDE)]:
+                levels[pl.ds(((step - 1) * 2 + 1) * WIDE * LEVELS + c * LEVELS, LEVELS), :] = blank
+        pressures(step, (0, HALO, WIDE - 2 * HALO, WIDE - HALO), sources, levels, ps, mixing)
+        sweep(step, lo - 1, lo + HALO + 1, (lo - 1, lo + HALO - 1), sources, levels, ps)
+        sweep(step, hi - HALO - 1, hi + 1, (hi - HALO + 1, hi + 1), sources, levels, ps)
 
 
 def four_levels(ref, at, four):
@@ -176,7 +214,8 @@
     return jnp.concatenate(rows, axis=0)
 
 
-def first_kernel(state, near, far, sums, mixing, packed, both, ps, sides, spare):
+def first_kernel(levels_in, state, near, far, sums, mixing, packed, levels, ps, sides, spare):
+    del levels_in
     span = MINE * LEVELS
     edge = HALO * LEVELS
     pieces = []
@@ -207,10 +246,10 @@
             return state, f * span + (c - HALO) * LEVELS
         return sides, (2 * f + 1) * edge + (c - HALO - MINE) * LEVELS
 
-    substeps(sources, both, ps, mixing)
+    outer_steps(sources, levels, ps, mixing)
     starts = [jnp.bitwise_xor(MEMBER_AT[k], flip) * 136 for k in range(GROUP)]
     for s in range(GROUP):
-        square = slab_rows(both, edge, s).T
+        square = slab_rows(levels, FINAL + edge, s).T
         for k in range(GROUP):
             packed[pl.ds(starts[k] + 8 * s, 8), :] = square[8 * k : 8 * k + 8, :]
     for g in range(GROUP):
@@ -276,7 +315,8 @@
     blend(fs, table, my_place()[0], keep, send)
 
 
-def forecast_kernel(table_in, state, outer, inner, hist, mixing, both, keep, send, ps, fs, sides, table, sem):
+def forecast_kernel(levels_in, table_in, state, outer, inner, hist, mixing, levels, keep, send, ps, fs, sides, table, sem):
+    del levels_in
     edge = HALO * LEVELS
     span = MINE * LEVELS
     copy = pltpu.make_async_copy(table_in, table, sem)
@@ -294,9 +334,9 @@
             return state, f * span + (c - HALO) * LEVELS
         return sides, (2 * f + 1) * edge + (c - HALO - MINE) * LEVELS
 
-    substeps(sources, both, ps, mixing)
+    outer_steps(sources, levels, ps, mixing)
     for four in range(8):
-        parts = centred(four_levels(both, WIDE * LEVELS + edge, four).T)
+        parts = centred(four_levels(levels, FINAL + WIDE * LEVELS + edge, four).T)
         for half in range(2):
             q = 2 * four + half
             gram_of(fs, q, *parts, hist[pl.ds(q, 1), :], half == 1)
@@ -377,7 +417,7 @@
     starts = []
     for chunk in range(4):
         fj = (chunk + 16 - block) & 3
-        starts.append((fj >> 1) * (WIDE * LEVELS) + (fj & 1) + HALO * LEVELS)
+        starts.append((fj >> 1) * (WIDE * LEVELS) + (fj & 1) + (FINAL + HALO * LEVELS))
     for j in range(8):
         s = 2 * j + parity
         field = jnp.concatenate(
@@ -455,8 +495,9 @@
     rows = MINE * LEVELS
     edges = 2 * HALO * LEVELS
     members = ensemble.reshape(512, COLS)
+    early = pl.CostEstimate(flops=10**10, bytes_accessed=3 * 2**20, transcendentals=0)
     cost = pl.CostEstimate(flops=10**9, bytes_accessed=3 * 2**20, transcendentals=0)
-    near, far = call(edges_kernel, (arr(HALO, COLS), arr(HALO, COLS)), [vmem()], "edges", cost=cost)(members)
+    near, far = call(edges_kernel, (arr(HALO, COLS), arr(HALO, COLS)), [vmem()], "edges", cost=early)(members)
     far = lax.ppermute(far, "hor", [(i, (i - 1 + 2 * (i & 1)) % 16) for i in range(16)])
     near = lax.ppermute(near, "hor", [(i, i ^ 1) for i in range(16)])
     state, sums, mixing = call(
@@ -467,14 +508,16 @@
         [pltpu.VMEM((2048, 128), F32), pltpu.VMEM((2048, 128), F32)],
     )(partners, members, obs_column, obs_level, obs_value, obs_error, obs_live, coupling)
     wide = pltpu.VMEM((WIDE * LEVELS, WIDTH), F32)
-    fields = pltpu.VMEM((2 * WIDE * LEVELS, WIDTH), F32)
-    packed = call(
+    all_levels = arr(SUBSTEPS * 2 * WIDE * LEVELS, WIDTH)
+    inside = call(inner_kernel, all_levels, [vmem()] * 2, "inside", [wide], cost=cost)
+    packed, _ = call(
         first_kernel,
-        arr(GROUP * 136, 128),
-        [vmem()] * 5,
+        (arr(GROUP * 136, 128), all_levels),
+        [vmem()] * 6,
         "first",
-        [fields, wide, pltpu.VMEM((4 * HALO * LEVELS, 128), F32), pltpu.VMEM((64, 128), F32)],
-    )(state, near, far, sums, mixing)
+        [wide, pltpu.VMEM((4 * HALO * LEVELS, 128), F32), pltpu.VMEM((64, 128), F32)],
+        aliases={0: 1},
+    )(inside(state, mixing), state, near, far, sums, mixing)
     received = exchange(packed.reshape(GROUP, 136, 128), TILE).reshape(GROUP * 136, 128)
     folded = pltpu.VMEM((GROUP, FOLD, 128), F32)
     scalars = pltpu.SMEM((GROUP, 128), jnp.int32)
@@ -492,7 +535,6 @@
         same = exchange(copies, CHIPS)
         return same, swap(same)
 
-    cost = pl.CostEstimate(flops=10**9, bytes_accessed=3 * 2**20, transcendentals=0)
     same, other = roots(keep, send)
     part = call(
         functools.partial(first_apply_kernel, False),
@@ -512,11 +554,12 @@
     inner = lax.ppermute(inner, ALL, block_pairs(0))
     both, keep, send = call(
         forecast_kernel,
-        (arr(2 * WIDE * LEVELS, WIDTH), arr(8, FOLD, 128), arr(8, FOLD, 128)),
-        [vmem()] * 6,
+        (all_levels, arr(8, FOLD, 128), arr(8, FOLD, 128)),
+        [vmem()] * 7,
         "forecast",
         [wide, folded, pltpu.VMEM((4 * HALO * LEVELS, 128), F32), scalars, pltpu.SemaphoreType.DMA(())],
-    )(table, state, outer, inner, hist, mixing)
+        aliases={0: 0},
+    )(inside(state, mixing), table, state, outer, inner, hist, mixing)
     same, other = roots(keep, send)
     part = call(
         functools.partial(last_apply_kernel, False),

time: 172 us -> 172 us (level)
  Pallas kernels: 20 us -> 21.8 us
    pallas_call x2 -> x4, Pallas kernels: 5.12 us -> 6.82 us  [the longest x2 2.42 us: shards(): inside(state, mixing)]
  transfers between devices with their start and end apart: 8 -> 8, of which waited for: 6 -> 5; matrix products, arithmetic and copies ran while one was open for 0% -> 0% of each run, Pallas kernels for 2% -> 4%
where the time goes in v9:
time: 172 us; the launch traced here: 171 us
  blocking collectives  124 us (72%)
  Pallas kernels  21.8 us (13%)
  starting transfers between devices  20.8 us (12%)
  waiting for transfers between devices  3.69 us (2%)
    all_to_all x6, blocking collectives, exchange(): return lax.all_to_all(x, axes, split_axis=0, concat_axis=0, tiled=True)  124 us
    ppermute x4, starting transfers between devices, swap(): return lax.ppermute(x, 'core', [(0, 1), (1, 0)])  9.98 us
    pallas_call x2, Pallas kernels, roots(): copies = call(root_kernel, arr(8, FOLD, 128), [vmem()], 'root')(parts)  6.25 us
    ppermute x1, starting transfers between devices, shards(): lax.ppermute(far, 'hor', [(i, (i - 1 + 2 * (i & 1)) % 16) for i in range(...  4.27 us
  transfers between devices with their start and end apart: 8, of which 5 were waited for; matrix products, arithmetic and copies ran while one was open for 0% of the time, Pallas kernels for 4%

profile of v9, /device:TPU:1, one launch (start us, length us, event | category | flops | bytes accessed | tf_op | source)
XLA Modules:
  0.0 171.3 jit_solution(2801469150181339887)
XLA Ops:
  0.0 1.2 copy-done
  1.5 2.1 %collective-permute-start = (f32[8,512]{1,0:T(8,128)S(1)}, f32[8,512]{1,0:T(8,128)S(1)}, u32[]{:S(2)}, u32[]{:S(2)}) collective-permute-start(f32[8,512]{1,0:T(8,128)S(1)} %get-tuple-element.23), channel_id=1, source_target_pairs={{0,4},{4,0},{8,12},{12,8},{16,20},{20,16},{24,28},{28,24},{32,36},... | collective-permute-start | bytes 49160 | tf_op jit(solution)/shard_map/ppermute | solution.py:502
  3.6 4.3 %collective-permute-start.1 = (f32[8,512]{1,0:T(8,128)S(1)}, f32[8,512]{1,0:T(8,128)S(1)}, u32[]{:S(2)}, u32[]{:S(2)}) collective-permute-start(f32[8,512]{1,0:T(8,128)S(1)} %get-tuple-element.24), channel_id=1, source_target_pairs={{0,60},{4,8},{8,4},{12,16},{16,12},{20,24},{24,20},{28,32},{32,28}... | collective-permute-start | bytes 49160 | tf_op jit(solution)/shard_map/ppermute | solution.py:501
  7.9 1.8 %prepare.1 = (f32[2048,128]{1,0:T(8,128)S(1)}, f32[128,128]{1,0:T(8,128)S(1)}, bf16[256,128]{1,0:T(8,128)(2,1)S(1)}) custom-call(s32[1,1,2]{2,1,0:T(1,128)S(1)} %copy-done.8, f32[512,512]{1,0:T(8,128)S(1)} %bitcast.13, s32[2,1,1,512]{3,2,1,0:T(1,128)S(1)} %copy-done.3, s32[2,1,1,512]{3,2,1,0:T(1,128)S(1)} %copy-done.4, f32[2,1,1,512]{3,2,1,0:T(1,128)S(1)} %copy-done.5, ...), custom_call_target="tpu_custom_call" | custom-call | tf_op jit(solution)/shard_map/prepare/pallas_call | solution.py:503
  9.8 1.2 inside.2.levels_in
  11.0 2.1 %first.1 = (f32[2176,128]{1,0:T(8,128)S(1)}, f32[12288,128]{1,0:T(8,128)S(1)}) custom-call(f32[12288,128]{1,0:T(8,128)S(1)} %inside.2.levels_in, f32[2048,128]{1,0:T(8,128)S(1)} %get-tuple-element.21.state, f32[8,512]{1,0:T(8,128)S(1)} %collective-permute-done.near, f32[8,512]{1,0:T(8,128)S(1)} %collective-permute-done.1.far, ...), custom_call_target="tpu_custom_call", output_to_operand_aliasing={{1}: (0, {})} | custom-call | tf_op jit(solution)/shard_map/first/pallas_call | solution.py:513
  13.1 39.7 %all_to_all.30 = f32[16,136,128]{2,1,0:T(8,128)S(1)} all-to-all(f32[16,136,128]{2,1,0:T(8,128)S(1)} %bitcast.11), channel_id=1, replica_groups=mesh['mem'=4,'hor'=16,'zh'=2,'core'=2] {'mem','zh','core'}, dimensions={0} | all-to-all | bytes 2228224 | tf_op jit(solution)/shard_map/all_to_all | solution.py:491
  52.8 1.7 gram.1
  54.6 1.6 collective-permute-done.2
  56.2 13.4 %all_to_all.31.got = f32[8,72,128]{2,1,0:T(8,128)S(1)} all-to-all(f32[8,72,128]{2,1,0:T(8,128)S(1)} %add.6), channel_id=1, replica_groups=mesh['mem'=4,'hor'=16,'zh'=2,'core'=2] {'mem','zh'}, dimensions={0} | all-to-all | bytes 589824 | tf_op jit(solution)/shard_map/all_to_all | solution.py:491
  69.5 3.1 %root.2 = f32[8,72,128]{2,1,0:T(8,128)S(1)} custom-call(f32[8,72,128]{2,1,0:T(8,128)S(1)} %all_to_all.31.got), custom_call_target="tpu_custom_call" | custom-call | tf_op jit(solution)/shard_map/root/pallas_call | solution.py:534
  72.7 13.3 %all_to_all.32.roots = f32[8,72,128]{2,1,0:T(8,128)S(1)} all-to-all(f32[8,72,128]{2,1,0:T(8,128)S(1)} %root.2), channel_id=1, replica_groups=mesh['mem'=4,'hor'=16,'zh'=2,'core'=2] {'mem','zh'}, dimensions={0} | all-to-all | bytes 589824 | tf_op jit(solution)/shard_map/all_to_all | solution.py:491
  85.9 2.6 %collective-permute-start.3 = (f32[8,72,128]{2,1,0:T(8,128)S(1)}, f32[8,72,128]{2,1,0:T(8,128)S(1)}, u32[]{:S(2)}, u32[]{:S(2)}) collective-permute-start(f32[8,72,128]{2,1,0:T(8,128)S(1)} %all_to_all.32.roots), channel_id=1, source_target_pairs={{0,1},{1,0},{2,3},{3,2},{4,5},{5,4},{6,7},{7,6},{8,9},{9,8},{10,11... | collective-permute-start | bytes 884744 | tf_op jit(solution)/shard_map/ppermute | solution.py:487
  88.5 0.9 apply.2.refs_0_
  89.5 0.3 collective-permute-done.3.roots
  89.7 1.0 apply.3
  90.8 1.5 collective-permute-start.4
  92.2 2.9 %collective-permute-start.5 = (f32[512,128]{1,0:T(8,128)S(1)}, f32[512,128]{1,0:T(8,128)S(1)}, u32[]{:S(2)}, u32[]{:S(2)}) collective-permute-start(f32[512,128]{1,0:T(8,128)S(1)} %get-tuple-element.32), channel_id=1, source_target_pairs={{0,1},{1,0},{64,65},{65,64},{128,129},{129,128},{192,193},{193,192... | collective-permute-start | bytes 786440 | tf_op jit(solution)/shard_map/ppermute | solution.py:554
  95.2 1.2 inside.3.levels_in
  96.4 0.3 collective-permute-done.4.outer
  96.6 2.3 %forecast.1 = (f32[12288,128]{1,0:T(8,128)S(1)}, f32[8,72,128]{2,1,0:T(8,128)S(1)}, f32[8,72,128]{2,1,0:T(8,128)S(1)}) custom-call(f32[12288,128]{1,0:T(8,128)S(1)} %inside.3.levels_in, s32[16,128]{1,0:T(8,128)S(1)} %get-tuple-element.30.table_in, f32[2048,128]{1,0:T(8,128)S(1)} %get-tuple-element.29.state, ...), custom_call_target="tpu_custom_call", output_to_operand_aliasing={{0}: (0, {})} | custom-call | tf_op jit(solution)/shard_map/forecast/pallas_call | solution.py:555
  99.0 4.3 %collective-permute-start.6 = (f32[8,72,128]{2,1,0:T(8,128)S(1)}, f32[8,72,128]{2,1,0:T(8,128)S(1)}, u32[]{:S(2)}, u32[]{:S(2)}) collective-permute-start(f32[8,72,128]{2,1,0:T(8,128)S(1)} %get-tuple-element.36), channel_id=1, source_target_pairs={{0,1},{1,0},{2,3},{3,2},{4,5},{5,4},{6,7},{7,6},{8,9},{9,8},{10,11... | collective-permute-start | bytes 884744 | tf_op jit(solution)/shard_map/ppermute | solution.py:487
  103.3 1.2 collective-permute-done.6
  104.6 12.9 %all_to_all.33.got = f32[8,72,128]{2,1,0:T(8,128)S(1)} all-to-all(f32[8,72,128]{2,1,0:T(8,128)S(1)} %add.7), channel_id=1, replica_groups=mesh['mem'=4,'hor'=16,'zh'=2,'core'=2] {'mem','zh'}, dimensions={0} | all-to-all | bytes 589824 | tf_op jit(solution)/shard_map/all_to_all | solution.py:491
  117.5 3.1 %root.3 = f32[8,72,128]{2,1,0:T(8,128)S(1)} custom-call(f32[8,72,128]{2,1,0:T(8,128)S(1)} %all_to_all.33.got), custom_call_target="tpu_custom_call" | custom-call | tf_op jit(solution)/shard_map/root/pallas_call | solution.py:534
  120.7 13.2 %all_to_all.34.roots = f32[8,72,128]{2,1,0:T(8,128)S(1)} all-to-all(f32[8,72,128]{2,1,0:T(8,128)S(1)} %root.3), channel_id=1, replica_groups=mesh['mem'=4,'hor'=16,'zh'=2,'core'=2] {'mem','zh'}, dimensions={0} | all-to-all | bytes 589824 | tf_op jit(solution)/shard_map/all_to_all | solution.py:491
  133.8 2.9 %collective-permute-start.7 = (f32[8,72,128]{2,1,0:T(8,128)S(1)}, f32[8,72,128]{2,1,0:T(8,128)S(1)}, u32[]{:S(2)}, u32[]{:S(2)}) collective-permute-start(f32[8,72,128]{2,1,0:T(8,128)S(1)} %all_to_all.34.roots), channel_id=1, source_target_pairs={{0,1},{1,0},{2,3},{3,2},{4,5},{5,4},{6,7},{7,6},{8,9},{9,8},{10,11... | collective-permute-start | bytes 884744 | tf_op jit(solution)/shard_map/ppermute | solution.py:487
  136.8 0.8 analyse.2.refs_0_
  137.6 0.4 collective-permute-done.7.roots
  138.0 0.9 analyse.3
  138.9 31.1 %all_to_all.35 = f32[16,128,128]{2,1,0:T(8,128)S(1)} all-to-all(f32[16,128,128]{2,1,0:T(8,128)S(1)} %bitcast.9), channel_id=1, replica_groups=mesh['mem'=4,'hor'=16,'zh'=2,'core'=2] {'mem','zh','core'}, dimensions={0} | all-to-all | bytes 2097152 | tf_op jit(solution)/shard_map/all_to_all | solution.py:491
  170.0 1.3 place.1
  (24 shorter events, 0.4 us)
Async XLA Ops:
  0.0 1.2 copy-start
  1.2 6.6 %copy-start.1 = (f32[8,2,32,512]{3,2,1,0:T(8,128)S(1)}, f32[8,2,32,512]{3,2,1,0:T(8,128)}, u32[]{:S(2)}) copy-start(f32[8,2,32,512]{3,2,1,0:T(8,128)} %param.8) | copy-start | bytes 3145732
  1.2 6.6 %copy-start.2 = (f32[32,32]{1,0:T(8,128)S(1)}, f32[32,32]{1,0:T(8,128)}, u32[]{:S(2)}) copy-start(f32[32,32]{1,0:T(8,128)} %coupling.1) | copy-start | bytes 12292
  1.2 6.6 %copy-start.3 = (s32[2,1,1,512]{3,2,1,0:T(1,128)S(1)}, s32[2,1,1,512]{3,2,1,0:T(1,128)}, u32[]{:S(2)}) copy-start(s32[2,1,1,512]{3,2,1,0:T(1,128)} %column.1) | copy-start | bytes 12292
  1.2 6.6 %copy-start.4 = (s32[2,1,1,512]{3,2,1,0:T(1,128)S(1)}, s32[2,1,1,512]{3,2,1,0:T(1,128)}, u32[]{:S(2)}) copy-start(s32[2,1,1,512]{3,2,1,0:T(1,128)} %level.1) | copy-start | bytes 12292
  1.2 6.6 %copy-start.5 = (f32[2,1,1,512]{3,2,1,0:T(1,128)S(1)}, f32[2,1,1,512]{3,2,1,0:T(1,128)}, u32[]{:S(2)}) copy-start(f32[2,1,1,512]{3,2,1,0:T(1,128)} %value.1) | copy-start | bytes 12292
  1.2 6.6 %copy-start.6 = (f32[2,1,1,512]{3,2,1,0:T(1,128)S(1)}, f32[2,1,1,512]{3,2,1,0:T(1,128)}, u32[]{:S(2)}) copy-start(f32[2,1,1,512]{3,2,1,0:T(1,128)} %error.1) | copy-start | bytes 12292
  1.3 6.6 %copy-start.7 = (s32[2,1,1,512]{3,2,1,0:T(1,128)S(1)}, s32[2,1,1,512]{3,2,1,0:T(1,128)}, u32[]{:S(2)}) copy-start(s32[2,1,1,512]{3,2,1,0:T(1,128)} %live.1) | copy-start | bytes 12292
  1.3 6.6 %copy-start.8 = (s32[1,1,2]{2,1,0:T(1,128)S(1)}, s32[1,1,2]{2,1,0:T(1,128)}, u32[]{:S(2)}) copy-start(s32[1,1,2]{2,1,0:T(1,128)} %partner.1) | copy-start | bytes 28
  1.5 9.5 %collective-permute-start = (f32[8,512]{1,0:T(8,128)S(1)}, f32[8,512]{1,0:T(8,128)S(1)}, u32[]{:S(2)}, u32[]{:S(2)}) collective-permute-start(f32[8,512]{1,0:T(8,128)S(1)} %get-tuple-element.23), channel_id=1, source_target_pairs={{0,4},{4,0},{8,12},{12,8},{16,20},{20,16},{24,28},{28,24},{32,36},... | collective-permute-start | bytes 49160 | tf_op jit(solution)/shard_map/ppermute | solution.py:502
  3.6 7.4 %collective-permute-start.1 = (f32[8,512]{1,0:T(8,128)S(1)}, f32[8,512]{1,0:T(8,128)S(1)}, u32[]{:S(2)}, u32[]{:S(2)}) collective-permute-start(f32[8,512]{1,0:T(8,128)S(1)} %get-tuple-element.24), channel_id=1, source_target_pairs={{0,60},{4,8},{8,4},{12,16},{16,12},{20,24},{24,20},{28,32},{32,28}... | collective-permute-start | bytes 49160 | tf_op jit(solution)/shard_map/ppermute | solution.py:501
  54.5 1.7 collective-permute-start.2
  85.9 3.8 %collective-permute-start.3 = (f32[8,72,128]{2,1,0:T(8,128)S(1)}, f32[8,72,128]{2,1,0:T(8,128)S(1)}, u32[]{:S(2)}, u32[]{:S(2)}) collective-permute-start(f32[8,72,128]{2,1,0:T(8,128)S(1)} %all_to_all.32.roots), channel_id=1, source_target_pairs={{0,1},{1,0},{2,3},{3,2},{4,5},{5,4},{6,7},{7,6},{8,9},{9,8},{10,11... | collective-permute-start | bytes 884744 | tf_op jit(solution)/shard_map/ppermute | solution.py:487
  90.8 5.9 %collective-permute-start.4 = (f32[512,128]{1,0:T(8,128)S(1)}, f32[512,128]{1,0:T(8,128)S(1)}, u32[]{:S(2)}, u32[]{:S(2)}) collective-permute-start(f32[512,128]{1,0:T(8,128)S(1)} %get-tuple-element.31), channel_id=1, source_target_pairs={{1,64},{64,1},{65,128},{128,65},{129,192},{192,129},{193,2},{2,193... | collective-permute-start | bytes 786440 | tf_op jit(solution)/shard_map/ppermute | solution.py:553
  92.2 4.4 %collective-permute-start.5 = (f32[512,128]{1,0:T(8,128)S(1)}, f32[512,128]{1,0:T(8,128)S(1)}, u32[]{:S(2)}, u32[]{:S(2)}) collective-permute-start(f32[512,128]{1,0:T(8,128)S(1)} %get-tuple-element.32), channel_id=1, source_target_pairs={{0,1},{1,0},{64,65},{65,64},{128,129},{129,128},{192,193},{193,192... | collective-permute-start | bytes 786440 | tf_op jit(solution)/shard_map/ppermute | solution.py:554
  99.0 5.6 %collective-permute-start.6 = (f32[8,72,128]{2,1,0:T(8,128)S(1)}, f32[8,72,128]{2,1,0:T(8,128)S(1)}, u32[]{:S(2)}, u32[]{:S(2)}) collective-permute-start(f32[8,72,128]{2,1,0:T(8,128)S(1)} %get-tuple-element.36), channel_id=1, source_target_pairs={{0,1},{1,0},{2,3},{3,2},{4,5},{5,4},{6,7},{7,6},{8,9},{9,8},{10,11... | collective-permute-start | bytes 884744 | tf_op jit(solution)/shard_map/ppermute | solution.py:487
  133.8 4.1 %collective-permute-start.7 = (f32[8,72,128]{2,1,0:T(8,128)S(1)}, f32[8,72,128]{2,1,0:T(8,128)S(1)}, u32[]{:S(2)}, u32[]{:S(2)}) collective-permute-start(f32[8,72,128]{2,1,0:T(8,128)S(1)} %all_to_all.34.roots), channel_id=1, source_target_pairs={{0,1},{1,0},{2,3},{3,2},{4,5},{5,4},{6,7},{7,6},{8,9},{9,8},{10,11... | collective-permute-start | bytes 884744 | tf_op jit(solution)/shard_map/ppermute | solution.py:487

commit v10 on v9

--- a/solution.py
+++ b/solution.py
@@ -214,7 +214,7 @@
     return jnp.concatenate(rows, axis=0)
 
 
-def first_kernel(levels_in, state, near, far, sums, mixing, packed, levels, ps, sides, spare):
+def first_kernel(levels_in, far, near, state, sums, mixing, packed, levels, ps, sides, spare):
     del levels_in
     span = MINE * LEVELS
     edge = HALO * LEVELS
@@ -517,7 +517,7 @@
         "first",
         [wide, pltpu.VMEM((4 * HALO * LEVELS, 128), F32), pltpu.VMEM((64, 128), F32)],
         aliases={0: 1},
-    )(inside(state, mixing), state, near, far, sums, mixing)
+    )(inside(state, mixing), far, near, state, sums, mixing)
     received = exchange(packed.reshape(GROUP, 136, 128), TILE).reshape(GROUP * 136, 128)
     folded = pltpu.VMEM((GROUP, FOLD, 128), F32)
     scalars = pltpu.SMEM((GROUP, 128), jnp.int32)

time: 172 us -> 171 us (level)
    ppermute x1, starting transfers between devices: 2.13 us -> 0.01 us  [shards(): near = lax.ppermute(near, 'hor', [(i, i ^ 1) for i in range(16)])]
where the time goes in v10:
time: 171 us
  blocking collectives  124 us (73%)
  Pallas kernels  21.7 us (13%)
  starting transfers between devices  19.6 us (11%)
  waiting for transfers between devices  4.3 us (3%)
    all_to_all x6, blocking collectives, exchange(): return lax.all_to_all(x, axes, split_axis=0, concat_axis=0, tiled=True)  124 us
    ppermute x4, starting transfers between devices, swap(): return lax.ppermute(x, 'core', [(0, 1), (1, 0)])  10 us
    pallas_call x2, Pallas kernels, roots(): copies = call(root_kernel, arr(8, FOLD, 128), [vmem()], 'root')(parts)  6.25 us
    ppermute x1, starting transfers between devices, shards(): lax.ppermute(far, 'hor', [(i, (i - 1 + 2 * (i & 1)) % 16) for i in range(...  5.84 us
  transfers between devices with their start and end apart: 8, of which 5 were waited for; matrix products, arithmetic and copies ran while one was open for 0% of the time, Pallas kernels for 4%

profile of v10, /device:TPU:1, one launch (start us, length us, event | category | flops | bytes accessed | tf_op | source)
XLA Modules:
  0.0 171.1 jit_solution(7106425209244997926)
XLA Ops:
  0.0 1.2 copy-done
  1.3 0.2 edges.1
  1.5 5.8 %collective-permute-start = (f32[8,512]{1,0:T(8,128)S(1)}, f32[8,512]{1,0:T(8,128)S(1)}, u32[]{:S(2)}, u32[]{:S(2)}) collective-permute-start(f32[8,512]{1,0:T(8,128)S(1)} %get-tuple-element.23), channel_id=1, source_target_pairs={{0,60},{4,8},{8,4},{12,16},{16,12},{20,24},{24,20},{28,32},{32,28}... | collective-permute-start | bytes 49160 | tf_op jit(solution)/shard_map/ppermute | solution.py:501
  7.4 1.8 %prepare.1 = (f32[2048,128]{1,0:T(8,128)S(1)}, f32[128,128]{1,0:T(8,128)S(1)}, bf16[256,128]{1,0:T(8,128)(2,1)S(1)}) custom-call(s32[1,1,2]{2,1,0:T(1,128)S(1)} %copy-done.8, f32[512,512]{1,0:T(8,128)S(1)} %bitcast.13, s32[2,1,1,512]{3,2,1,0:T(1,128)S(1)} %copy-done.3, s32[2,1,1,512]{3,2,1,0:T(1,128)S(1)} %copy-done.4, f32[2,1,1,512]{3,2,1,0:T(1,128)S(1)} %copy-done.5, ...), custom_call_target="tpu_custom_call" | custom-call | tf_op jit(solution)/shard_map/prepare/pallas_call | solution.py:503
  9.2 1.2 inside.2.levels_in
  10.5 2.1 %first.1 = (f32[2176,128]{1,0:T(8,128)S(1)}, f32[12288,128]{1,0:T(8,128)S(1)}) custom-call(f32[12288,128]{1,0:T(8,128)S(1)} %inside.2.levels_in, f32[8,512]{1,0:T(8,128)S(1)} %collective-permute-done.far, f32[8,512]{1,0:T(8,128)S(1)} %collective-permute-done.1.near, f32[2048,128]{1,0:T(8,128)S(1)} %get-tuple-element.21.state, ...), custom_call_target="tpu_custom_call", output_to_operand_aliasing={{1}: (0, {})} | custom-call | tf_op jit(solution)/shard_map/first/pallas_call | solution.py:513
  12.5 40.0 %all_to_all.30 = f32[16,136,128]{2,1,0:T(8,128)S(1)} all-to-all(f32[16,136,128]{2,1,0:T(8,128)S(1)} %bitcast.11), channel_id=1, replica_groups=mesh['mem'=4,'hor'=16,'zh'=2,'core'=2] {'mem','zh','core'}, dimensions={0} | all-to-all | bytes 2228224 | tf_op jit(solution)/shard_map/all_to_all | solution.py:491
  52.6 1.7 gram.1
  54.3 1.6 collective-permute-done.2
  55.9 13.4 %all_to_all.31.got = f32[8,72,128]{2,1,0:T(8,128)S(1)} all-to-all(f32[8,72,128]{2,1,0:T(8,128)S(1)} %add.6), channel_id=1, replica_groups=mesh['mem'=4,'hor'=16,'zh'=2,'core'=2] {'mem','zh'}, dimensions={0} | all-to-all | bytes 589824 | tf_op jit(solution)/shard_map/all_to_all | solution.py:491
  69.3 3.1 %root.2 = f32[8,72,128]{2,1,0:T(8,128)S(1)} custom-call(f32[8,72,128]{2,1,0:T(8,128)S(1)} %all_to_all.31.got), custom_call_target="tpu_custom_call" | custom-call | tf_op jit(solution)/shard_map/root/pallas_call | solution.py:534
  72.4 13.3 %all_to_all.32.roots = f32[8,72,128]{2,1,0:T(8,128)S(1)} all-to-all(f32[8,72,128]{2,1,0:T(8,128)S(1)} %root.2), channel_id=1, replica_groups=mesh['mem'=4,'hor'=16,'zh'=2,'core'=2] {'mem','zh'}, dimensions={0} | all-to-all | bytes 589824 | tf_op jit(solution)/shard_map/all_to_all | solution.py:491
  85.7 2.6 %collective-permute-start.3 = (f32[8,72,128]{2,1,0:T(8,128)S(1)}, f32[8,72,128]{2,1,0:T(8,128)S(1)}, u32[]{:S(2)}, u32[]{:S(2)}) collective-permute-start(f32[8,72,128]{2,1,0:T(8,128)S(1)} %all_to_all.32.roots), channel_id=1, source_target_pairs={{0,1},{1,0},{2,3},{3,2},{4,5},{5,4},{6,7},{7,6},{8,9},{9,8},{10,11... | collective-permute-start | bytes 884744 | tf_op jit(solution)/shard_map/ppermute | solution.py:487
  88.3 0.9 apply.2.refs_0_
  89.2 0.3 collective-permute-done.3.roots
  89.5 1.0 apply.3
  90.5 1.5 collective-permute-start.4
  92.0 2.3 %collective-permute-start.5 = (f32[512,128]{1,0:T(8,128)S(1)}, f32[512,128]{1,0:T(8,128)S(1)}, u32[]{:S(2)}, u32[]{:S(2)}) collective-permute-start(f32[512,128]{1,0:T(8,128)S(1)} %get-tuple-element.32), channel_id=1, source_target_pairs={{0,1},{1,0},{64,65},{65,64},{128,129},{129,128},{192,193},{193,192... | collective-permute-start | bytes 786440 | tf_op jit(solution)/shard_map/ppermute | solution.py:554
  94.3 1.2 inside.3.levels_in
  95.5 0.9 collective-permute-done.4.outer
  96.4 2.3 %forecast.1 = (f32[12288,128]{1,0:T(8,128)S(1)}, f32[8,72,128]{2,1,0:T(8,128)S(1)}, f32[8,72,128]{2,1,0:T(8,128)S(1)}) custom-call(f32[12288,128]{1,0:T(8,128)S(1)} %inside.3.levels_in, s32[16,128]{1,0:T(8,128)S(1)} %get-tuple-element.30.table_in, f32[2048,128]{1,0:T(8,128)S(1)} %get-tuple-element.29.state, ...), custom_call_target="tpu_custom_call", output_to_operand_aliasing={{0}: (0, {})} | custom-call | tf_op jit(solution)/shard_map/forecast/pallas_call | solution.py:555
  98.8 4.4 %collective-permute-start.6 = (f32[8,72,128]{2,1,0:T(8,128)S(1)}, f32[8,72,128]{2,1,0:T(8,128)S(1)}, u32[]{:S(2)}, u32[]{:S(2)}) collective-permute-start(f32[8,72,128]{2,1,0:T(8,128)S(1)} %get-tuple-element.36), channel_id=1, source_target_pairs={{0,1},{1,0},{2,3},{3,2},{4,5},{5,4},{6,7},{7,6},{8,9},{9,8},{10,11... | collective-permute-start | bytes 884744 | tf_op jit(solution)/shard_map/ppermute | solution.py:487
  103.1 1.2 collective-permute-done.6
  104.4 12.9 %all_to_all.33.got = f32[8,72,128]{2,1,0:T(8,128)S(1)} all-to-all(f32[8,72,128]{2,1,0:T(8,128)S(1)} %add.7), channel_id=1, replica_groups=mesh['mem'=4,'hor'=16,'zh'=2,'core'=2] {'mem','zh'}, dimensions={0} | all-to-all | bytes 589824 | tf_op jit(solution)/shard_map/all_to_all | solution.py:491
  117.3 3.1 %root.3 = f32[8,72,128]{2,1,0:T(8,128)S(1)} custom-call(f32[8,72,128]{2,1,0:T(8,128)S(1)} %all_to_all.33.got), custom_call_target="tpu_custom_call" | custom-call | tf_op jit(solution)/shard_map/root/pallas_call | solution.py:534
  120.4 13.2 %all_to_all.34.roots = f32[8,72,128]{2,1,0:T(8,128)S(1)} all-to-all(f32[8,72,128]{2,1,0:T(8,128)S(1)} %root.3), channel_id=1, replica_groups=mesh['mem'=4,'hor'=16,'zh'=2,'core'=2] {'mem','zh'}, dimensions={0} | all-to-all | bytes 589824 | tf_op jit(solution)/shard_map/all_to_all | solution.py:491
  133.6 2.9 %collective-permute-start.7 = (f32[8,72,128]{2,1,0:T(8,128)S(1)}, f32[8,72,128]{2,1,0:T(8,128)S(1)}, u32[]{:S(2)}, u32[]{:S(2)}) collective-permute-start(f32[8,72,128]{2,1,0:T(8,128)S(1)} %all_to_all.34.roots), channel_id=1, source_target_pairs={{0,1},{1,0},{2,3},{3,2},{4,5},{5,4},{6,7},{7,6},{8,9},{9,8},{10,11... | collective-permute-start | bytes 884744 | tf_op jit(solution)/shard_map/ppermute | solution.py:487
  136.6 0.8 analyse.2.refs_0_
  137.4 0.4 collective-permute-done.7.roots
  137.8 0.9 analyse.3
  138.6 31.1 %all_to_all.35 = f32[16,128,128]{2,1,0:T(8,128)S(1)} all-to-all(f32[16,128,128]{2,1,0:T(8,128)S(1)} %bitcast.9), channel_id=1, replica_groups=mesh['mem'=4,'hor'=16,'zh'=2,'core'=2] {'mem','zh','core'}, dimensions={0} | all-to-all | bytes 2097152 | tf_op jit(solution)/shard_map/all_to_all | solution.py:491
  169.7 1.3 place.1
  (24 shorter events, 0.2 us)
Async XLA Ops:
  0.0 1.2 copy-start
  1.2 6.1 %copy-start.1 = (f32[8,2,32,512]{3,2,1,0:T(8,128)S(1)}, f32[8,2,32,512]{3,2,1,0:T(8,128)}, u32[]{:S(2)}) copy-start(f32[8,2,32,512]{3,2,1,0:T(8,128)} %param.8) | copy-start | bytes 3145732
  1.2 6.1 %copy-start.2 = (f32[32,32]{1,0:T(8,128)S(1)}, f32[32,32]{1,0:T(8,128)}, u32[]{:S(2)}) copy-start(f32[32,32]{1,0:T(8,128)} %coupling.1) | copy-start | bytes 12292
  1.2 6.1 %copy-start.3 = (s32[2,1,1,512]{3,2,1,0:T(1,128)S(1)}, s32[2,1,1,512]{3,2,1,0:T(1,128)}, u32[]{:S(2)}) copy-start(s32[2,1,1,512]{3,2,1,0:T(1,128)} %column.1) | copy-start | bytes 12292
  1.2 6.1 %copy-start.4 = (s32[2,1,1,512]{3,2,1,0:T(1,128)S(1)}, s32[2,1,1,512]{3,2,1,0:T(1,128)}, u32[]{:S(2)}) copy-start(s32[2,1,1,512]{3,2,1,0:T(1,128)} %level.1) | copy-start | bytes 12292
  1.2 6.1 %copy-start.5 = (f32[2,1,1,512]{3,2,1,0:T(1,128)S(1)}, f32[2,1,1,512]{3,2,1,0:T(1,128)}, u32[]{:S(2)}) copy-start(f32[2,1,1,512]{3,2,1,0:T(1,128)} %value.1) | copy-start | bytes 12292
  1.2 6.1 %copy-start.6 = (f32[2,1,1,512]{3,2,1,0:T(1,128)S(1)}, f32[2,1,1,512]{3,2,1,0:T(1,128)}, u32[]{:S(2)}) copy-start(f32[2,1,1,512]{3,2,1,0:T(1,128)} %error.1) | copy-start | bytes 12292
  1.3 6.1 %copy-start.7 = (s32[2,1,1,512]{3,2,1,0:T(1,128)S(1)}, s32[2,1,1,512]{3,2,1,0:T(1,128)}, u32[]{:S(2)}) copy-start(s32[2,1,1,512]{3,2,1,0:T(1,128)} %live.1) | copy-start | bytes 12292
  1.3 6.1 %copy-start.8 = (s32[1,1,2]{2,1,0:T(1,128)S(1)}, s32[1,1,2]{2,1,0:T(1,128)}, u32[]{:S(2)}) copy-start(s32[1,1,2]{2,1,0:T(1,128)} %partner.1) | copy-start | bytes 28
  1.5 9.0 %collective-permute-start = (f32[8,512]{1,0:T(8,128)S(1)}, f32[8,512]{1,0:T(8,128)S(1)}, u32[]{:S(2)}, u32[]{:S(2)}) collective-permute-start(f32[8,512]{1,0:T(8,128)S(1)} %get-tuple-element.23), channel_id=1, source_target_pairs={{0,60},{4,8},{8,4},{12,16},{16,12},{20,24},{24,20},{28,32},{32,28}... | collective-permute-start | bytes 49160 | tf_op jit(solution)/shard_map/ppermute | solution.py:501
  7.3 3.1 %collective-permute-start.1 = (f32[8,512]{1,0:T(8,128)S(1)}, f32[8,512]{1,0:T(8,128)S(1)}, u32[]{:S(2)}, u32[]{:S(2)}) collective-permute-start(f32[8,512]{1,0:T(8,128)S(1)} %get-tuple-element.24), channel_id=1, source_target_pairs={{0,4},{4,0},{8,12},{12,8},{16,20},{20,16},{24,28},{28,24},{32,36},... | collective-permute-start | bytes 49160 | tf_op jit(solution)/shard_map/ppermute | solution.py:502
  54.2 1.7 collective-permute-start.2
  85.7 3.8 %collective-permute-start.3 = (f32[8,72,128]{2,1,0:T(8,128)S(1)}, f32[8,72,128]{2,1,0:T(8,128)S(1)}, u32[]{:S(2)}, u32[]{:S(2)}) collective-permute-start(f32[8,72,128]{2,1,0:T(8,128)S(1)} %all_to_all.32.roots), channel_id=1, source_target_pairs={{0,1},{1,0},{2,3},{3,2},{4,5},{5,4},{6,7},{7,6},{8,9},{9,8},{10,11... | collective-permute-start | bytes 884744 | tf_op jit(solution)/shard_map/ppermute | solution.py:487
  90.5 5.9 %collective-permute-start.4 = (f32[512,128]{1,0:T(8,128)S(1)}, f32[512,128]{1,0:T(8,128)S(1)}, u32[]{:S(2)}, u32[]{:S(2)}) collective-permute-start(f32[512,128]{1,0:T(8,128)S(1)} %get-tuple-element.31), channel_id=1, source_target_pairs={{1,64},{64,1},{65,128},{128,65},{129,192},{192,129},{193,2},{2,193... | collective-permute-start | bytes 786440 | tf_op jit(solution)/shard_map/ppermute | solution.py:553
  92.0 4.4 %collective-permute-start.5 = (f32[512,128]{1,0:T(8,128)S(1)}, f32[512,128]{1,0:T(8,128)S(1)}, u32[]{:S(2)}, u32[]{:S(2)}) collective-permute-start(f32[512,128]{1,0:T(8,128)S(1)} %get-tuple-element.32), channel_id=1, source_target_pairs={{0,1},{1,0},{64,65},{65,64},{128,129},{129,128},{192,193},{193,192... | collective-permute-start | bytes 786440 | tf_op jit(solution)/shard_map/ppermute | solution.py:554
  98.8 5.6 %collective-permute-start.6 = (f32[8,72,128]{2,1,0:T(8,128)S(1)}, f32[8,72,128]{2,1,0:T(8,128)S(1)}, u32[]{:S(2)}, u32[]{:S(2)}) collective-permute-start(f32[8,72,128]{2,1,0:T(8,128)S(1)} %get-tuple-element.36), channel_id=1, source_target_pairs={{0,1},{1,0},{2,3},{3,2},{4,5},{5,4},{6,7},{7,6},{8,9},{9,8},{10,11... | collective-permute-start | bytes 884744 | tf_op jit(solution)/shard_map/ppermute | solution.py:487
  133.6 4.1 %collective-permute-start.7 = (f32[8,72,128]{2,1,0:T(8,128)S(1)}, f32[8,72,128]{2,1,0:T(8,128)S(1)}, u32[]{:S(2)}, u32[]{:S(2)}) collective-permute-start(f32[8,72,128]{2,1,0:T(8,128)S(1)} %all_to_all.34.roots), channel_id=1, source_target_pairs={{0,1},{1,0},{2,3},{3,2},{4,5},{5,4},{6,7},{7,6},{8,9},{9,8},{10,11... | collective-permute-start | bytes 884744 | tf_op jit(solution)/shard_map/ppermute | solution.py:487

commit v11 on v9

--- a/solution.py
+++ b/solution.py
@@ -135,14 +135,14 @@
 def pressures(step, groups, sources, levels, ps, mixing):
     mix = (mixing[pl.ds(0, MIX), :], mixing[pl.ds(MIX, MIX), :])
     many = MIX // LEVELS
-    for c in groups:
+    for one, two in groups:
         block = jnp.concatenate(
-            [rows_after(sources, levels, step - 1, 1, c, many), rows_after(sources, levels, step - 1, 1, c + many, many)],
+            [rows_after(sources, levels, step - 1, 1, one, many), rows_after(sources, levels, step - 1, 1, two, many)],
             axis=1,
         )
         pressure = dot_split(mix, split(block))
-        ps[pl.ds(c * LEVELS, MIX), :] = pressure[:, :128]
-        ps[pl.ds(c * LEVELS + MIX, MIX), :] = pressure[:, 128:]
+        ps[pl.ds(one * LEVELS, MIX), :] = pressure[:, :128]
+        ps[pl.ds(two * LEVELS, MIX), :] = pressure[:, 128:]
 
 
 def sweep(step, start, stop, new, sources, levels, ps):
@@ -186,7 +186,9 @@
         if step < SUBSTEPS:
             for c in [*range(HALO, lo), *range(hi, HALO + MINE)]:
                 levels[pl.ds(((step - 1) * 2 + 1) * WIDE * LEVELS + c * LEVELS, LEVELS), :] = blank
-        pressures(step, range(HALO, HALO + MINE, 8), sources, levels, ps, mixing)
+        begin = (lo - 2) // 4 * 4
+        groups = [(c, c + 4) for c in range(begin, WIDE - begin, 8)]
+        pressures(step, groups, sources, levels, ps, mixing)
         sweep(step, lo - 1, hi + 1, (lo - 1, hi + 1), sources, levels, ps)
 
 
@@ -197,7 +199,9 @@
         if step < SUBSTEPS:
             for c in [*range(lo), *range(hi, WIDE)]:
                 levels[pl.ds(((step - 1) * 2 + 1) * WIDE * LEVELS + c * LEVELS, LEVELS), :] = blank
-        pressures(step, (0, HALO, WIDE - 2 * HALO, WIDE - HALO), sources, levels, ps, mixing)
+        begin = (lo - 2) // 4 * 4
+        groups = [(c, WIDE - 4 - c) for c in range(begin, begin + 12, 4)]
+        pressures(step, groups, sources, levels, ps, mixing)
         sweep(step, lo - 1, lo + HALO + 1, (lo - 1, lo + HALO - 1), sources, levels, ps)
         sweep(step, hi - HALO - 1, hi + 1, (hi - HALO + 1, hi + 1), sources, levels, ps)
 
@@ -358,19 +362,18 @@
     norm = jnp.sqrt(squared)
     a = blended / norm
     newton = 1.5 * eye - 0.5 * a
-    a = dot_split(split(a), split(newton))
-    z = newton
+    inner = jnp.broadcast_to(pull, (8, WIDTH))
+    both = dot_split(split(jnp.concatenate([a, inner], axis=0)), split(newton))
+    a, z, inner = both[:WIDTH], newton, both[WIDTH:]
     for step in range(1, ROOT_STEPS):
         newton = 1.5 * eye - 0.5 * dot_split(split(z), split(a))
         if step < ROOT_STEPS - 1:
-            both = dot_split(split(jnp.concatenate([a, z], axis=0)), split(newton))
-            a, z = both[:WIDTH], both[WIDTH:]
+            both = dot_split(split(jnp.concatenate([a, z, inner], axis=0)), split(newton))
+            a, z, inner = both[:WIDTH], both[WIDTH : 2 * WIDTH], both[2 * WIDTH :]
         else:
-            z = dot_split(split(z), split(newton))
-    halves = split(z)
-    wide = jnp.broadcast_to(pull, (8, WIDTH))
-    inner = dot_split(split(wide), halves, turned=True)
-    shift = dot_split(split(inner), halves, turned=True)[0:1, :] / norm
+            both = dot_split(split(jnp.concatenate([z, inner], axis=0)), split(newton))
+            z, inner = both[:WIDTH], both[WIDTH:]
+    shift = dot_split(split(inner), split(z), turned=True)[0:1, :] / norm
     spread = z * (math.sqrt(WIDTH - 1.0) / jnp.sqrt(norm))
     sums = jnp.sum(spread, axis=0, keepdims=True) + jnp.sum(shift, axis=1, keepdims=True)
     body, tail = fold(spread[:64], spread[64:], shift, (1.0 - sums) * (1.0 / WIDTH))

time: 172 us -> 172 us (level)
  transfers between devices with their start and end apart: 8 -> 8, of which waited for: 5 -> 5; matrix products, arithmetic and copies ran while one was open for 0% -> 0% of each run, Pallas kernels for 4% -> 3%
where the time goes in v11:
time: 172 us
  blocking collectives  124 us (72%)
  Pallas kernels  22.5 us (13%)
  starting transfers between devices  20.8 us (12%)
  waiting for transfers between devices  3.67 us (2%)
    all_to_all x6, blocking collectives, exchange(): return lax.all_to_all(x, axes, split_axis=0, concat_axis=0, tiled=True)  124 us
    ppermute x4, starting transfers between devices, swap(): return lax.ppermute(x, 'core', [(0, 1), (1, 0)])  10 us
    pallas_call x2, Pallas kernels, roots(): copies = call(root_kernel, arr(8, FOLD, 128), [vmem()], 'root')(parts)  6.87 us
    ppermute x1, starting transfers between devices, shards(): lax.ppermute(far, 'hor', [(i, (i - 1 + 2 * (i & 1)) % 16) for i in range(...  4.27 us
  transfers between devices with their start and end apart: 8, of which 5 were waited for; matrix products, arithmetic and copies ran while one was open for 0% of the time, Pallas kernels for 3%

profile of v11, /device:TPU:1, one launch (start us, length us, event | category | flops | bytes accessed | tf_op | source)
XLA Modules:
  0.0 172.1 jit_solution(2244371441952477773)
XLA Ops:
  0.0 1.2 copy-done
  1.5 2.1 %collective-permute-start = (f32[8,512]{1,0:T(8,128)S(1)}, f32[8,512]{1,0:T(8,128)S(1)}, u32[]{:S(2)}, u32[]{:S(2)}) collective-permute-start(f32[8,512]{1,0:T(8,128)S(1)} %get-tuple-element.23), channel_id=1, source_target_pairs={{0,4},{4,0},{8,12},{12,8},{16,20},{20,16},{24,28},{28,24},{32,36},... | collective-permute-start | bytes 49160 | tf_op jit(solution)/shard_map/ppermute | solution.py:505
  3.6 4.3 %collective-permute-start.1 = (f32[8,512]{1,0:T(8,128)S(1)}, f32[8,512]{1,0:T(8,128)S(1)}, u32[]{:S(2)}, u32[]{:S(2)}) collective-permute-start(f32[8,512]{1,0:T(8,128)S(1)} %get-tuple-element.24), channel_id=1, source_target_pairs={{0,60},{4,8},{8,4},{12,16},{16,12},{20,24},{24,20},{28,32},{32,28}... | collective-permute-start | bytes 49160 | tf_op jit(solution)/shard_map/ppermute | solution.py:504
  7.9 1.8 %prepare.1 = (f32[2048,128]{1,0:T(8,128)S(1)}, f32[128,128]{1,0:T(8,128)S(1)}, bf16[256,128]{1,0:T(8,128)(2,1)S(1)}) custom-call(s32[1,1,2]{2,1,0:T(1,128)S(1)} %copy-done.8, f32[512,512]{1,0:T(8,128)S(1)} %bitcast.13, s32[2,1,1,512]{3,2,1,0:T(1,128)S(1)} %copy-done.3, s32[2,1,1,512]{3,2,1,0:T(1,128)S(1)} %copy-done.4, f32[2,1,1,512]{3,2,1,0:T(1,128)S(1)} %copy-done.5, ...), custom_call_target="tpu_custom_call" | custom-call | tf_op jit(solution)/shard_map/prepare/pallas_call | solution.py:506
  9.8 1.2 inside.2.levels_in
  11.0 2.2 %first.1 = (f32[2176,128]{1,0:T(8,128)S(1)}, f32[12288,128]{1,0:T(8,128)S(1)}) custom-call(f32[12288,128]{1,0:T(8,128)S(1)} %inside.2.levels_in, f32[2048,128]{1,0:T(8,128)S(1)} %get-tuple-element.21.state, f32[8,512]{1,0:T(8,128)S(1)} %collective-permute-done.near, f32[8,512]{1,0:T(8,128)S(1)} %collective-permute-done.1.far, ...), custom_call_target="tpu_custom_call", output_to_operand_aliasing={{1}: (0, {})} | custom-call | tf_op jit(solution)/shard_map/first/pallas_call | solution.py:516
  13.2 39.7 %all_to_all.30 = f32[16,136,128]{2,1,0:T(8,128)S(1)} all-to-all(f32[16,136,128]{2,1,0:T(8,128)S(1)} %bitcast.11), channel_id=1, replica_groups=mesh['mem'=4,'hor'=16,'zh'=2,'core'=2] {'mem','zh','core'}, dimensions={0} | all-to-all | bytes 2228224 | tf_op jit(solution)/shard_map/all_to_all | solution.py:494
  52.9 1.6 gram.1
  54.7 1.6 collective-permute-done.2
  56.3 13.4 %all_to_all.31.got = f32[8,72,128]{2,1,0:T(8,128)S(1)} all-to-all(f32[8,72,128]{2,1,0:T(8,128)S(1)} %add.6), channel_id=1, replica_groups=mesh['mem'=4,'hor'=16,'zh'=2,'core'=2] {'mem','zh'}, dimensions={0} | all-to-all | bytes 589824 | tf_op jit(solution)/shard_map/all_to_all | solution.py:494
  69.6 3.4 %root.2 = f32[8,72,128]{2,1,0:T(8,128)S(1)} custom-call(f32[8,72,128]{2,1,0:T(8,128)S(1)} %all_to_all.31.got), custom_call_target="tpu_custom_call" | custom-call | tf_op jit(solution)/shard_map/root/pallas_call | solution.py:537
  73.1 13.3 %all_to_all.32.roots = f32[8,72,128]{2,1,0:T(8,128)S(1)} all-to-all(f32[8,72,128]{2,1,0:T(8,128)S(1)} %root.2), channel_id=1, replica_groups=mesh['mem'=4,'hor'=16,'zh'=2,'core'=2] {'mem','zh'}, dimensions={0} | all-to-all | bytes 589824 | tf_op jit(solution)/shard_map/all_to_all | solution.py:494
  86.3 2.6 %collective-permute-start.3 = (f32[8,72,128]{2,1,0:T(8,128)S(1)}, f32[8,72,128]{2,1,0:T(8,128)S(1)}, u32[]{:S(2)}, u32[]{:S(2)}) collective-permute-start(f32[8,72,128]{2,1,0:T(8,128)S(1)} %all_to_all.32.roots), channel_id=1, source_target_pairs={{0,1},{1,0},{2,3},{3,2},{4,5},{5,4},{6,7},{7,6},{8,9},{9,8},{10,11... | collective-permute-start | bytes 884744 | tf_op jit(solution)/shard_map/ppermute | solution.py:490
  88.9 1.0 apply.2.refs_0_
  89.9 0.2 collective-permute-done.3.roots
  90.1 1.0 apply.3
  91.2 1.5 collective-permute-start.4
  92.6 2.9 %collective-permute-start.5 = (f32[512,128]{1,0:T(8,128)S(1)}, f32[512,128]{1,0:T(8,128)S(1)}, u32[]{:S(2)}, u32[]{:S(2)}) collective-permute-start(f32[512,128]{1,0:T(8,128)S(1)} %get-tuple-element.32), channel_id=1, source_target_pairs={{0,1},{1,0},{64,65},{65,64},{128,129},{129,128},{192,193},{193,192... | collective-permute-start | bytes 786440 | tf_op jit(solution)/shard_map/ppermute | solution.py:557
  95.6 1.2 inside.3.levels_in
  96.8 0.3 collective-permute-done.4.outer
  97.0 2.4 %forecast.1 = (f32[12288,128]{1,0:T(8,128)S(1)}, f32[8,72,128]{2,1,0:T(8,128)S(1)}, f32[8,72,128]{2,1,0:T(8,128)S(1)}) custom-call(f32[12288,128]{1,0:T(8,128)S(1)} %inside.3.levels_in, s32[16,128]{1,0:T(8,128)S(1)} %get-tuple-element.30.table_in, f32[2048,128]{1,0:T(8,128)S(1)} %get-tuple-element.29.state, ...), custom_call_target="tpu_custom_call", output_to_operand_aliasing={{0}: (0, {})} | custom-call | tf_op jit(solution)/shard_map/forecast/pallas_call | solution.py:558
  99.4 4.4 %collective-permute-start.6 = (f32[8,72,128]{2,1,0:T(8,128)S(1)}, f32[8,72,128]{2,1,0:T(8,128)S(1)}, u32[]{:S(2)}, u32[]{:S(2)}) collective-permute-start(f32[8,72,128]{2,1,0:T(8,128)S(1)} %get-tuple-element.36), channel_id=1, source_target_pairs={{0,1},{1,0},{2,3},{3,2},{4,5},{5,4},{6,7},{7,6},{8,9},{9,8},{10,11... | collective-permute-start | bytes 884744 | tf_op jit(solution)/shard_map/ppermute | solution.py:490
  103.8 1.2 collective-permute-done.6
  105.1 12.9 %all_to_all.33.got = f32[8,72,128]{2,1,0:T(8,128)S(1)} all-to-all(f32[8,72,128]{2,1,0:T(8,128)S(1)} %add.7), channel_id=1, replica_groups=mesh['mem'=4,'hor'=16,'zh'=2,'core'=2] {'mem','zh'}, dimensions={0} | all-to-all | bytes 589824 | tf_op jit(solution)/shard_map/all_to_all | solution.py:494
  118.0 3.4 %root.3 = f32[8,72,128]{2,1,0:T(8,128)S(1)} custom-call(f32[8,72,128]{2,1,0:T(8,128)S(1)} %all_to_all.33.got), custom_call_target="tpu_custom_call" | custom-call | tf_op jit(solution)/shard_map/root/pallas_call | solution.py:537
  121.4 13.2 %all_to_all.34.roots = f32[8,72,128]{2,1,0:T(8,128)S(1)} all-to-all(f32[8,72,128]{2,1,0:T(8,128)S(1)} %root.3), channel_id=1, replica_groups=mesh['mem'=4,'hor'=16,'zh'=2,'core'=2] {'mem','zh'}, dimensions={0} | all-to-all | bytes 589824 | tf_op jit(solution)/shard_map/all_to_all | solution.py:494
  134.6 2.9 %collective-permute-start.7 = (f32[8,72,128]{2,1,0:T(8,128)S(1)}, f32[8,72,128]{2,1,0:T(8,128)S(1)}, u32[]{:S(2)}, u32[]{:S(2)}) collective-permute-start(f32[8,72,128]{2,1,0:T(8,128)S(1)} %all_to_all.34.roots), channel_id=1, source_target_pairs={{0,1},{1,0},{2,3},{3,2},{4,5},{5,4},{6,7},{7,6},{8,9},{9,8},{10,11... | collective-permute-start | bytes 884744 | tf_op jit(solution)/shard_map/ppermute | solution.py:490
  137.5 0.8 analyse.2.refs_0_
  138.4 0.4 collective-permute-done.7.roots
  138.8 0.9 analyse.3
  139.6 31.1 %all_to_all.35 = f32[16,128,128]{2,1,0:T(8,128)S(1)} all-to-all(f32[16,128,128]{2,1,0:T(8,128)S(1)} %bitcast.9), channel_id=1, replica_groups=mesh['mem'=4,'hor'=16,'zh'=2,'core'=2] {'mem','zh','core'}, dimensions={0} | all-to-all | bytes 2097152 | tf_op jit(solution)/shard_map/all_to_all | solution.py:494
  170.7 1.3 place.1
  (24 shorter events, 0.4 us)
Async XLA Ops:
  0.0 1.2 copy-start
  1.2 6.6 %copy-start.1 = (f32[8,2,32,512]{3,2,1,0:T(8,128)S(1)}, f32[8,2,32,512]{3,2,1,0:T(8,128)}, u32[]{:S(2)}) copy-start(f32[8,2,32,512]{3,2,1,0:T(8,128)} %param.8) | copy-start | bytes 3145732
  1.2 6.6 %copy-start.2 = (f32[32,32]{1,0:T(8,128)S(1)}, f32[32,32]{1,0:T(8,128)}, u32[]{:S(2)}) copy-start(f32[32,32]{1,0:T(8,128)} %coupling.1) | copy-start | bytes 12292
  1.2 6.6 %copy-start.3 = (s32[2,1,1,512]{3,2,1,0:T(1,128)S(1)}, s32[2,1,1,512]{3,2,1,0:T(1,128)}, u32[]{:S(2)}) copy-start(s32[2,1,1,512]{3,2,1,0:T(1,128)} %column.1) | copy-start | bytes 12292
  1.2 6.6 %copy-start.4 = (s32[2,1,1,512]{3,2,1,0:T(1,128)S(1)}, s32[2,1,1,512]{3,2,1,0:T(1,128)}, u32[]{:S(2)}) copy-start(s32[2,1,1,512]{3,2,1,0:T(1,128)} %level.1) | copy-start | bytes 12292
  1.2 6.6 %copy-start.5 = (f32[2,1,1,512]{3,2,1,0:T(1,128)S(1)}, f32[2,1,1,512]{3,2,1,0:T(1,128)}, u32[]{:S(2)}) copy-start(f32[2,1,1,512]{3,2,1,0:T(1,128)} %value.1) | copy-start | bytes 12292
  1.2 6.6 %copy-start.6 = (f32[2,1,1,512]{3,2,1,0:T(1,128)S(1)}, f32[2,1,1,512]{3,2,1,0:T(1,128)}, u32[]{:S(2)}) copy-start(f32[2,1,1,512]{3,2,1,0:T(1,128)} %error.1) | copy-start | bytes 12292
  1.3 6.6 %copy-start.7 = (s32[2,1,1,512]{3,2,1,0:T(1,128)S(1)}, s32[2,1,1,512]{3,2,1,0:T(1,128)}, u32[]{:S(2)}) copy-start(s32[2,1,1,512]{3,2,1,0:T(1,128)} %live.1) | copy-start | bytes 12292
  1.3 6.6 %copy-start.8 = (s32[1,1,2]{2,1,0:T(1,128)S(1)}, s32[1,1,2]{2,1,0:T(1,128)}, u32[]{:S(2)}) copy-start(s32[1,1,2]{2,1,0:T(1,128)} %partner.1) | copy-start | bytes 28
  1.5 9.5 %collective-permute-start = (f32[8,512]{1,0:T(8,128)S(1)}, f32[8,512]{1,0:T(8,128)S(1)}, u32[]{:S(2)}, u32[]{:S(2)}) collective-permute-start(f32[8,512]{1,0:T(8,128)S(1)} %get-tuple-element.23), channel_id=1, source_target_pairs={{0,4},{4,0},{8,12},{12,8},{16,20},{20,16},{24,28},{28,24},{32,36},... | collective-permute-start | bytes 49160 | tf_op jit(solution)/shard_map/ppermute | solution.py:505
  3.6 7.4 %collective-permute-start.1 = (f32[8,512]{1,0:T(8,128)S(1)}, f32[8,512]{1,0:T(8,128)S(1)}, u32[]{:S(2)}, u32[]{:S(2)}) collective-permute-start(f32[8,512]{1,0:T(8,128)S(1)} %get-tuple-element.24), channel_id=1, source_target_pairs={{0,60},{4,8},{8,4},{12,16},{16,12},{20,24},{24,20},{28,32},{32,28}... | collective-permute-start | bytes 49160 | tf_op jit(solution)/shard_map/ppermute | solution.py:504
  54.6 1.7 collective-permute-start.2
  86.3 3.8 %collective-permute-start.3 = (f32[8,72,128]{2,1,0:T(8,128)S(1)}, f32[8,72,128]{2,1,0:T(8,128)S(1)}, u32[]{:S(2)}, u32[]{:S(2)}) collective-permute-start(f32[8,72,128]{2,1,0:T(8,128)S(1)} %all_to_all.32.roots), channel_id=1, source_target_pairs={{0,1},{1,0},{2,3},{3,2},{4,5},{5,4},{6,7},{7,6},{8,9},{9,8},{10,11... | collective-permute-start | bytes 884744 | tf_op jit(solution)/shard_map/ppermute | solution.py:490
  91.2 5.9 %collective-permute-start.4 = (f32[512,128]{1,0:T(8,128)S(1)}, f32[512,128]{1,0:T(8,128)S(1)}, u32[]{:S(2)}, u32[]{:S(2)}) collective-permute-start(f32[512,128]{1,0:T(8,128)S(1)} %get-tuple-element.31), channel_id=1, source_target_pairs={{1,64},{64,1},{65,128},{128,65},{129,192},{192,129},{193,2},{2,193... | collective-permute-start | bytes 786440 | tf_op jit(solution)/shard_map/ppermute | solution.py:556
  92.6 4.4 %collective-permute-start.5 = (f32[512,128]{1,0:T(8,128)S(1)}, f32[512,128]{1,0:T(8,128)S(1)}, u32[]{:S(2)}, u32[]{:S(2)}) collective-permute-start(f32[512,128]{1,0:T(8,128)S(1)} %get-tuple-element.32), channel_id=1, source_target_pairs={{0,1},{1,0},{64,65},{65,64},{128,129},{129,128},{192,193},{193,192... | collective-permute-start | bytes 786440 | tf_op jit(solution)/shard_map/ppermute | solution.py:557
  99.4 5.6 %collective-permute-start.6 = (f32[8,72,128]{2,1,0:T(8,128)S(1)}, f32[8,72,128]{2,1,0:T(8,128)S(1)}, u32[]{:S(2)}, u32[]{:S(2)}) collective-permute-start(f32[8,72,128]{2,1,0:T(8,128)S(1)} %get-tuple-element.36), channel_id=1, source_target_pairs={{0,1},{1,0},{2,3},{3,2},{4,5},{5,4},{6,7},{7,6},{8,9},{9,8},{10,11... | collective-permute-start | bytes 884744 | tf_op jit(solution)/shard_map/ppermute | solution.py:490
  134.6 4.1 %collective-permute-start.7 = (f32[8,72,128]{2,1,0:T(8,128)S(1)}, f32[8,72,128]{2,1,0:T(8,128)S(1)}, u32[]{:S(2)}, u32[]{:S(2)}) collective-permute-start(f32[8,72,128]{2,1,0:T(8,128)S(1)} %all_to_all.34.roots), channel_id=1, source_target_pairs={{0,1},{1,0},{2,3},{3,2},{4,5},{5,4},{6,7},{7,6},{8,9},{9,8},{10,11... | collective-permute-start | bytes 884744 | tf_op jit(solution)/shard_map/ppermute | solution.py:490

commit v12 on v9

--- a/solution.py
+++ b/solution.py
@@ -367,10 +367,8 @@
             a, z = both[:WIDTH], both[WIDTH:]
         else:
             z = dot_split(split(z), split(newton))
-    halves = split(z)
-    wide = jnp.broadcast_to(pull, (8, WIDTH))
-    inner = dot_split(split(wide), halves, turned=True)
-    shift = dot_split(split(inner), halves, turned=True)[0:1, :] / norm
+    inner = jnp.sum(z * pull, axis=1, keepdims=True)
+    shift = jnp.sum(z * inner, axis=0, keepdims=True) / norm
     spread = z * (math.sqrt(WIDTH - 1.0) / jnp.sqrt(norm))
     sums = jnp.sum(spread, axis=0, keepdims=True) + jnp.sum(shift, axis=1, keepdims=True)
     body, tail = fold(spread[:64], spread[64:], shift, (1.0 - sums) * (1.0 / WIDTH))

time: 172 us -> 171 us (level)
  no operation moved by 1% of the time
where the time goes in v12:
time: 171 us
  blocking collectives  124 us (73%)
  Pallas kernels  21.4 us (13%)
  starting transfers between devices  20.8 us (12%)
  waiting for transfers between devices  3.69 us (2%)
    all_to_all x6, blocking collectives, exchange(): return lax.all_to_all(x, axes, split_axis=0, concat_axis=0, tiled=True)  124 us
    ppermute x4, starting transfers between devices, swap(): return lax.ppermute(x, 'core', [(0, 1), (1, 0)])  10 us
    pallas_call x2, Pallas kernels, roots(): copies = call(root_kernel, arr(8, FOLD, 128), [vmem()], 'root')(parts)  5.9 us
    ppermute x1, starting transfers between devices, shards(): lax.ppermute(far, 'hor', [(i, (i - 1 + 2 * (i & 1)) % 16) for i in range(...  4.27 us
  transfers between devices with their start and end apart: 8, of which 5 were waited for; matrix products, arithmetic and copies ran while one was open for 0% of the time, Pallas kernels for 4%

profile of v12, /device:TPU:1, one launch (start us, length us, event | category | flops | bytes accessed | tf_op | source)
XLA Modules:
  0.0 170.9 jit_solution(11259064409148910454)
XLA Ops:
  0.0 1.2 copy-done
  1.5 2.1 %collective-permute-start = (f32[8,512]{1,0:T(8,128)S(1)}, f32[8,512]{1,0:T(8,128)S(1)}, u32[]{:S(2)}, u32[]{:S(2)}) collective-permute-start(f32[8,512]{1,0:T(8,128)S(1)} %get-tuple-element.23), channel_id=1, source_target_pairs={{0,4},{4,0},{8,12},{12,8},{16,20},{20,16},{24,28},{28,24},{32,36},... | collective-permute-start | bytes 49160 | tf_op jit(solution)/shard_map/ppermute | solution.py:500
  3.6 4.3 %collective-permute-start.1 = (f32[8,512]{1,0:T(8,128)S(1)}, f32[8,512]{1,0:T(8,128)S(1)}, u32[]{:S(2)}, u32[]{:S(2)}) collective-permute-start(f32[8,512]{1,0:T(8,128)S(1)} %get-tuple-element.24), channel_id=1, source_target_pairs={{0,60},{4,8},{8,4},{12,16},{16,12},{20,24},{24,20},{28,32},{32,28}... | collective-permute-start | bytes 49160 | tf_op jit(solution)/shard_map/ppermute | solution.py:499
  7.9 1.8 %prepare.1 = (f32[2048,128]{1,0:T(8,128)S(1)}, f32[128,128]{1,0:T(8,128)S(1)}, bf16[256,128]{1,0:T(8,128)(2,1)S(1)}) custom-call(s32[1,1,2]{2,1,0:T(1,128)S(1)} %copy-done.8, f32[512,512]{1,0:T(8,128)S(1)} %bitcast.13, s32[2,1,1,512]{3,2,1,0:T(1,128)S(1)} %copy-done.3, s32[2,1,1,512]{3,2,1,0:T(1,128)S(1)} %copy-done.4, f32[2,1,1,512]{3,2,1,0:T(1,128)S(1)} %copy-done.5, ...), custom_call_target="tpu_custom_call" | custom-call | tf_op jit(solution)/shard_map/prepare/pallas_call | solution.py:501
  9.8 1.2 inside.2.levels_in
  11.0 2.1 %first.1 = (f32[2176,128]{1,0:T(8,128)S(1)}, f32[12288,128]{1,0:T(8,128)S(1)}) custom-call(f32[12288,128]{1,0:T(8,128)S(1)} %inside.2.levels_in, f32[2048,128]{1,0:T(8,128)S(1)} %get-tuple-element.21.state, f32[8,512]{1,0:T(8,128)S(1)} %collective-permute-done.near, f32[8,512]{1,0:T(8,128)S(1)} %collective-permute-done.1.far, ...), custom_call_target="tpu_custom_call", output_to_operand_aliasing={{1}: (0, {})} | custom-call | tf_op jit(solution)/shard_map/first/pallas_call | solution.py:511
  13.1 39.7 %all_to_all.30 = f32[16,136,128]{2,1,0:T(8,128)S(1)} all-to-all(f32[16,136,128]{2,1,0:T(8,128)S(1)} %bitcast.11), channel_id=1, replica_groups=mesh['mem'=4,'hor'=16,'zh'=2,'core'=2] {'mem','zh','core'}, dimensions={0} | all-to-all | bytes 2228224 | tf_op jit(solution)/shard_map/all_to_all | solution.py:489
  52.8 1.7 gram.1
  54.6 1.6 collective-permute-done.2
  56.2 13.4 %all_to_all.31.got = f32[8,72,128]{2,1,0:T(8,128)S(1)} all-to-all(f32[8,72,128]{2,1,0:T(8,128)S(1)} %add.6), channel_id=1, replica_groups=mesh['mem'=4,'hor'=16,'zh'=2,'core'=2] {'mem','zh'}, dimensions={0} | all-to-all | bytes 589824 | tf_op jit(solution)/shard_map/all_to_all | solution.py:489
  69.5 2.9 %root.2 = f32[8,72,128]{2,1,0:T(8,128)S(1)} custom-call(f32[8,72,128]{2,1,0:T(8,128)S(1)} %all_to_all.31.got), custom_call_target="tpu_custom_call" | custom-call | tf_op jit(solution)/shard_map/root/pallas_call | solution.py:532
  72.5 13.2 %all_to_all.32.roots = f32[8,72,128]{2,1,0:T(8,128)S(1)} all-to-all(f32[8,72,128]{2,1,0:T(8,128)S(1)} %root.2), channel_id=1, replica_groups=mesh['mem'=4,'hor'=16,'zh'=2,'core'=2] {'mem','zh'}, dimensions={0} | all-to-all | bytes 589824 | tf_op jit(solution)/shard_map/all_to_all | solution.py:489
  85.7 2.6 %collective-permute-start.3 = (f32[8,72,128]{2,1,0:T(8,128)S(1)}, f32[8,72,128]{2,1,0:T(8,128)S(1)}, u32[]{:S(2)}, u32[]{:S(2)}) collective-permute-start(f32[8,72,128]{2,1,0:T(8,128)S(1)} %all_to_all.32.roots), channel_id=1, source_target_pairs={{0,1},{1,0},{2,3},{3,2},{4,5},{5,4},{6,7},{7,6},{8,9},{9,8},{10,11... | collective-permute-start | bytes 884744 | tf_op jit(solution)/shard_map/ppermute | solution.py:485
  88.3 0.9 apply.2.refs_0_
  89.3 0.3 collective-permute-done.3.roots
  89.5 1.0 apply.3
  90.6 1.5 collective-permute-start.4
  92.0 2.9 %collective-permute-start.5 = (f32[512,128]{1,0:T(8,128)S(1)}, f32[512,128]{1,0:T(8,128)S(1)}, u32[]{:S(2)}, u32[]{:S(2)}) collective-permute-start(f32[512,128]{1,0:T(8,128)S(1)} %get-tuple-element.32), channel_id=1, source_target_pairs={{0,1},{1,0},{64,65},{65,64},{128,129},{129,128},{192,193},{193,192... | collective-permute-start | bytes 786440 | tf_op jit(solution)/shard_map/ppermute | solution.py:552
  95.0 1.2 inside.3.levels_in
  96.2 0.3 collective-permute-done.4.outer
  96.4 2.3 %forecast.1 = (f32[12288,128]{1,0:T(8,128)S(1)}, f32[8,72,128]{2,1,0:T(8,128)S(1)}, f32[8,72,128]{2,1,0:T(8,128)S(1)}) custom-call(f32[12288,128]{1,0:T(8,128)S(1)} %inside.3.levels_in, s32[16,128]{1,0:T(8,128)S(1)} %get-tuple-element.30.table_in, f32[2048,128]{1,0:T(8,128)S(1)} %get-tuple-element.29.state, ...), custom_call_target="tpu_custom_call", output_to_operand_aliasing={{0}: (0, {})} | custom-call | tf_op jit(solution)/shard_map/forecast/pallas_call | solution.py:553
  98.8 4.4 %collective-permute-start.6 = (f32[8,72,128]{2,1,0:T(8,128)S(1)}, f32[8,72,128]{2,1,0:T(8,128)S(1)}, u32[]{:S(2)}, u32[]{:S(2)}) collective-permute-start(f32[8,72,128]{2,1,0:T(8,128)S(1)} %get-tuple-element.36), channel_id=1, source_target_pairs={{0,1},{1,0},{2,3},{3,2},{4,5},{5,4},{6,7},{7,6},{8,9},{9,8},{10,11... | collective-permute-start | bytes 884744 | tf_op jit(solution)/shard_map/ppermute | solution.py:485
  103.2 1.2 collective-permute-done.6
  104.4 12.9 %all_to_all.33.got = f32[8,72,128]{2,1,0:T(8,128)S(1)} all-to-all(f32[8,72,128]{2,1,0:T(8,128)S(1)} %add.7), channel_id=1, replica_groups=mesh['mem'=4,'hor'=16,'zh'=2,'core'=2] {'mem','zh'}, dimensions={0} | all-to-all | bytes 589824 | tf_op jit(solution)/shard_map/all_to_all | solution.py:489
  117.3 2.9 %root.3 = f32[8,72,128]{2,1,0:T(8,128)S(1)} custom-call(f32[8,72,128]{2,1,0:T(8,128)S(1)} %all_to_all.33.got), custom_call_target="tpu_custom_call" | custom-call | tf_op jit(solution)/shard_map/root/pallas_call | solution.py:532
  120.3 13.2 %all_to_all.34.roots = f32[8,72,128]{2,1,0:T(8,128)S(1)} all-to-all(f32[8,72,128]{2,1,0:T(8,128)S(1)} %root.3), channel_id=1, replica_groups=mesh['mem'=4,'hor'=16,'zh'=2,'core'=2] {'mem','zh'}, dimensions={0} | all-to-all | bytes 589824 | tf_op jit(solution)/shard_map/all_to_all | solution.py:489
  133.4 2.9 %collective-permute-start.7 = (f32[8,72,128]{2,1,0:T(8,128)S(1)}, f32[8,72,128]{2,1,0:T(8,128)S(1)}, u32[]{:S(2)}, u32[]{:S(2)}) collective-permute-start(f32[8,72,128]{2,1,0:T(8,128)S(1)} %all_to_all.34.roots), channel_id=1, source_target_pairs={{0,1},{1,0},{2,3},{3,2},{4,5},{5,4},{6,7},{7,6},{8,9},{9,8},{10,11... | collective-permute-start | bytes 884744 | tf_op jit(solution)/shard_map/ppermute | solution.py:485
  136.4 0.8 analyse.2.refs_0_
  137.2 0.4 collective-permute-done.7.roots
  137.6 0.9 analyse.3
  138.5 31.1 %all_to_all.35 = f32[16,128,128]{2,1,0:T(8,128)S(1)} all-to-all(f32[16,128,128]{2,1,0:T(8,128)S(1)} %bitcast.9), channel_id=1, replica_groups=mesh['mem'=4,'hor'=16,'zh'=2,'core'=2] {'mem','zh','core'}, dimensions={0} | all-to-all | bytes 2097152 | tf_op jit(solution)/shard_map/all_to_all | solution.py:489
  169.6 1.3 place.1
  (24 shorter events, 0.4 us)
Async XLA Ops:
  0.0 1.2 copy-start
  1.2 6.6 %copy-start.1 = (f32[8,2,32,512]{3,2,1,0:T(8,128)S(1)}, f32[8,2,32,512]{3,2,1,0:T(8,128)}, u32[]{:S(2)}) copy-start(f32[8,2,32,512]{3,2,1,0:T(8,128)} %param.8) | copy-start | bytes 3145732
  1.2 6.6 %copy-start.2 = (f32[32,32]{1,0:T(8,128)S(1)}, f32[32,32]{1,0:T(8,128)}, u32[]{:S(2)}) copy-start(f32[32,32]{1,0:T(8,128)} %coupling.1) | copy-start | bytes 12292
  1.2 6.6 %copy-start.3 = (s32[2,1,1,512]{3,2,1,0:T(1,128)S(1)}, s32[2,1,1,512]{3,2,1,0:T(1,128)}, u32[]{:S(2)}) copy-start(s32[2,1,1,512]{3,2,1,0:T(1,128)} %column.1) | copy-start | bytes 12292
  1.2 6.6 %copy-start.4 = (s32[2,1,1,512]{3,2,1,0:T(1,128)S(1)}, s32[2,1,1,512]{3,2,1,0:T(1,128)}, u32[]{:S(2)}) copy-start(s32[2,1,1,512]{3,2,1,0:T(1,128)} %level.1) | copy-start | bytes 12292
  1.2 6.6 %copy-start.5 = (f32[2,1,1,512]{3,2,1,0:T(1,128)S(1)}, f32[2,1,1,512]{3,2,1,0:T(1,128)}, u32[]{:S(2)}) copy-start(f32[2,1,1,512]{3,2,1,0:T(1,128)} %value.1) | copy-start | bytes 12292
  1.2 6.6 %copy-start.6 = (f32[2,1,1,512]{3,2,1,0:T(1,128)S(1)}, f32[2,1,1,512]{3,2,1,0:T(1,128)}, u32[]{:S(2)}) copy-start(f32[2,1,1,512]{3,2,1,0:T(1,128)} %error.1) | copy-start | bytes 12292
  1.3 6.6 %copy-start.7 = (s32[2,1,1,512]{3,2,1,0:T(1,128)S(1)}, s32[2,1,1,512]{3,2,1,0:T(1,128)}, u32[]{:S(2)}) copy-start(s32[2,1,1,512]{3,2,1,0:T(1,128)} %live.1) | copy-start | bytes 12292
  1.3 6.6 %copy-start.8 = (s32[1,1,2]{2,1,0:T(1,128)S(1)}, s32[1,1,2]{2,1,0:T(1,128)}, u32[]{:S(2)}) copy-start(s32[1,1,2]{2,1,0:T(1,128)} %partner.1) | copy-start | bytes 28
  1.5 9.5 %collective-permute-start = (f32[8,512]{1,0:T(8,128)S(1)}, f32[8,512]{1,0:T(8,128)S(1)}, u32[]{:S(2)}, u32[]{:S(2)}) collective-permute-start(f32[8,512]{1,0:T(8,128)S(1)} %get-tuple-element.23), channel_id=1, source_target_pairs={{0,4},{4,0},{8,12},{12,8},{16,20},{20,16},{24,28},{28,24},{32,36},... | collective-permute-start | bytes 49160 | tf_op jit(solution)/shard_map/ppermute | solution.py:500
  3.6 7.4 %collective-permute-start.1 = (f32[8,512]{1,0:T(8,128)S(1)}, f32[8,512]{1,0:T(8,128)S(1)}, u32[]{:S(2)}, u32[]{:S(2)}) collective-permute-start(f32[8,512]{1,0:T(8,128)S(1)} %get-tuple-element.24), channel_id=1, source_target_pairs={{0,60},{4,8},{8,4},{12,16},{16,12},{20,24},{24,20},{28,32},{32,28}... | collective-permute-start | bytes 49160 | tf_op jit(solution)/shard_map/ppermute | solution.py:499
  54.5 1.7 collective-permute-start.2
  85.7 3.8 %collective-permute-start.3 = (f32[8,72,128]{2,1,0:T(8,128)S(1)}, f32[8,72,128]{2,1,0:T(8,128)S(1)}, u32[]{:S(2)}, u32[]{:S(2)}) collective-permute-start(f32[8,72,128]{2,1,0:T(8,128)S(1)} %all_to_all.32.roots), channel_id=1, source_target_pairs={{0,1},{1,0},{2,3},{3,2},{4,5},{5,4},{6,7},{7,6},{8,9},{9,8},{10,11... | collective-permute-start | bytes 884744 | tf_op jit(solution)/shard_map/ppermute | solution.py:485
  90.6 5.9 %collective-permute-start.4 = (f32[512,128]{1,0:T(8,128)S(1)}, f32[512,128]{1,0:T(8,128)S(1)}, u32[]{:S(2)}, u32[]{:S(2)}) collective-permute-start(f32[512,128]{1,0:T(8,128)S(1)} %get-tuple-element.31), channel_id=1, source_target_pairs={{1,64},{64,1},{65,128},{128,65},{129,192},{192,129},{193,2},{2,193... | collective-permute-start | bytes 786440 | tf_op jit(solution)/shard_map/ppermute | solution.py:551
  92.0 4.4 %collective-permute-start.5 = (f32[512,128]{1,0:T(8,128)S(1)}, f32[512,128]{1,0:T(8,128)S(1)}, u32[]{:S(2)}, u32[]{:S(2)}) collective-permute-start(f32[512,128]{1,0:T(8,128)S(1)} %get-tuple-element.32), channel_id=1, source_target_pairs={{0,1},{1,0},{64,65},{65,64},{128,129},{129,128},{192,193},{193,192... | collective-permute-start | bytes 786440 | tf_op jit(solution)/shard_map/ppermute | solution.py:552
  98.8 5.6 %collective-permute-start.6 = (f32[8,72,128]{2,1,0:T(8,128)S(1)}, f32[8,72,128]{2,1,0:T(8,128)S(1)}, u32[]{:S(2)}, u32[]{:S(2)}) collective-permute-start(f32[8,72,128]{2,1,0:T(8,128)S(1)} %get-tuple-element.36), channel_id=1, source_target_pairs={{0,1},{1,0},{2,3},{3,2},{4,5},{5,4},{6,7},{7,6},{8,9},{9,8},{10,11... | collective-permute-start | bytes 884744 | tf_op jit(solution)/shard_map/ppermute | solution.py:485
  133.4 4.1 %collective-permute-start.7 = (f32[8,72,128]{2,1,0:T(8,128)S(1)}, f32[8,72,128]{2,1,0:T(8,128)S(1)}, u32[]{:S(2)}, u32[]{:S(2)}) collective-permute-start(f32[8,72,128]{2,1,0:T(8,128)S(1)} %all_to_all.34.roots), channel_id=1, source_target_pairs={{0,1},{1,0},{2,3},{3,2},{4,5},{5,4},{6,7},{7,6},{8,9},{9,8},{10,11... | collective-permute-start | bytes 884744 | tf_op jit(solution)/shard_map/ppermute | solution.py:485

commit v13 on v12

--- a/solution.py
+++ b/solution.py
@@ -383,23 +383,39 @@
     return split((half + tail[1:2, :]) + (half + tail[2:3, :]).T)
 
 
-def first_apply_kernel(second, got, roots, *refs):
-    out = refs[1] if second else refs[0]
+def keep_halves(ready, j, halves):
+    ready[j, pl.ds(0, 128), :] = halves[0]
+    ready[j, pl.ds(128, 128), :] = halves[1]
+
+
+def kept_halves(ready, j):
+    return ready[j, pl.ds(0, 128), :], ready[j, pl.ds(128, 128), :]
+
+
+def first_apply_kernel(second, roots, *refs):
+    core, _, block = my_place()
+    if second:
+        _, ready, out, outer, inner = refs
+    else:
+        got, out, ready = refs
     span = MINE * LEVELS
     edge = HALO * LEVELS
-    core, _, block = my_place()
-    parity = 1 - core if second else core
-    for j in range(8):
-        s = 2 * j + parity
-        square = jnp.concatenate(
+
+    def square(s):
+        return jnp.concatenate(
             [got[pl.ds(pl.multiple_of(g * 136 + s * 8, 8), 8), :] for g in range(GROUP)], axis=0
         )
-        result = dot_split(weights_of(roots, j), split(square)).T
+
+    for j in range(8):
+        s = 2 * j + (1 - core if second else core)
+        halves = kept_halves(ready, j) if second else split(square(s))
+        result = dot_split(weights_of(roots, j), halves).T
         for fj in range(4):
             at = (fj // 2) * span + 2 * s + fj % 2
             out[pl.ds(at, MINE, stride=LEVELS), :] = result[fj * 32 : fj * 32 + 32, :]
+        if not second:
+            keep_halves(ready, j, split(square(2 * j + 1 - core)))
     if second:
-        outer, inner = refs[2:]
         odd = (block & 1) == 1
         for f in range(2):
             first = out[pl.ds(f * span, edge), :]
@@ -408,22 +424,28 @@
             inner[pl.ds(f * edge, edge), :] = jnp.where(odd, first, final)
 
 
-def last_apply_kernel(second, both, roots, *refs):
-    out = refs[-1]
+def last_apply_kernel(second, roots, *refs):
     core, _, block = my_place()
-    parity = 1 - core if second else core
+    if second:
+        _, ready, out = refs
+    else:
+        both, out, ready = refs
     starts = []
     for chunk in range(4):
         fj = (chunk + 16 - block) & 3
         starts.append((fj >> 1) * (WIDE * LEVELS) + (fj & 1) + (FINAL + HALO * LEVELS))
+
+    def field(s):
+        return jnp.concatenate([both[pl.ds(at + 2 * s, MINE, stride=LEVELS), :] for at in starts], axis=0)
+
     for j in range(8):
-        s = 2 * j + parity
-        field = jnp.concatenate(
-            [both[pl.ds(at + 2 * s, MINE, stride=LEVELS), :] for at in starts], axis=0
-        )
-        result = dot_split(weights_of(roots, j), split(field), turned=True)
+        s = 2 * j + (1 - core if second else core)
+        halves = kept_halves(ready, j) if second else split(field(s))
+        result = dot_split(weights_of(roots, j), halves, turned=True)
         for g in range(GROUP):
             out[pl.ds(pl.multiple_of((g * GROUP + s) * 8, 8), 8), :] = result[g * 8 : g * 8 + 8, :]
+        if not second:
+            keep_halves(ready, j, split(field(2 * j + 1 - core)))
 
 
 def place_kernel(got, out, tiles):
@@ -534,20 +556,21 @@
         return same, swap(same)
 
     same, other = roots(keep, send)
-    part = call(
+    ready = arr(8, 256, 128, dtype=BF16)
+    part, halves = call(
         functools.partial(first_apply_kernel, False),
-        arr(2 * rows, WIDTH),
+        (arr(2 * rows, WIDTH), ready),
         [vmem()] * 2,
         "apply",
         cost=cost,
-    )(received, same)
+    )(same, received)
     state, outer, inner = call(
         functools.partial(first_apply_kernel, True),
         (arr(2 * rows, WIDTH),) + (arr(edges, WIDTH),) * 2,
         [vmem()] * 3,
         "apply",
-        aliases={2: 0},
-    )(received, other, part)
+        aliases={1: 0},
+    )(other, part, halves)
     outer = lax.ppermute(outer, ALL, block_pairs(1))
     inner = lax.ppermute(inner, ALL, block_pairs(0))
     both, keep, send = call(
@@ -559,20 +582,20 @@
         aliases={0: 0},
     )(inside(state, mixing), table, state, outer, inner, hist, mixing)
     same, other = roots(keep, send)
-    part = call(
+    part, halves = call(
         functools.partial(last_apply_kernel, False),
-        arr(GROUP * 128, 128),
+        (arr(GROUP * 128, 128), ready),
         [vmem()] * 2,
         "analyse",
         cost=cost,
-    )(both, same)
+    )(same, both)
     analysed = call(
         functools.partial(last_apply_kernel, True),
         arr(GROUP * 128, 128),
         [vmem()] * 3,
         "analyse",
-        aliases={2: 0},
-    )(both, other, part)
+        aliases={1: 0},
+    )(other, part, halves)
     got = exchange(analysed.reshape(GROUP, 128, 128), TILE).reshape(GROUP * 128, 128)
     placed = call(place_kernel, arr(512, 512), [vmem()], "place", [pltpu.VMEM((2048, 128), F32)])(got)
     return placed.reshape(ensemble.shape)

time: 171 us -> 171 us (level)
  transfers between devices with their start and end apart: 8 -> 8, of which waited for: 5 -> 4; matrix products, arithmetic and copies ran while one was open for 0% -> 0% of each run, Pallas kernels for 4% -> 4%
where the time goes in v13:
time: 171 us
  blocking collectives  123 us (72%)
  Pallas kernels  21.7 us (13%)
  starting transfers between devices  20.8 us (12%)
  waiting for transfers between devices  3.28 us (2%)
    all_to_all x6, blocking collectives, exchange(): return lax.all_to_all(x, axes, split_axis=0, concat_axis=0, tiled=True)  123 us
    ppermute x4, starting transfers between devices, swap(): return lax.ppermute(x, 'core', [(0, 1), (1, 0)])  10 us
    pallas_call x2, Pallas kernels, roots(): copies = call(root_kernel, arr(8, FOLD, 128), [vmem()], 'root')(parts)  5.9 us
    ppermute x1, starting transfers between devices, shards(): lax.ppermute(far, 'hor', [(i, (i - 1 + 2 * (i & 1)) % 16) for i in range(...  4.27 us
  transfers between devices with their start and end apart: 8, of which 4 were waited for; matrix products, arithmetic and copies ran while one was open for 0% of the time, Pallas kernels for 4%

profile of v13, /device:TPU:1, one launch (start us, length us, event | category | flops | bytes accessed | tf_op | source)
XLA Modules:
  0.0 170.7 jit_solution(4770729322051409209)
XLA Ops:
  0.0 1.2 copy-done
  1.3 0.2 edges.1
  1.5 2.1 %collective-permute-start = (f32[8,512]{1,0:T(8,128)S(1)}, f32[8,512]{1,0:T(8,128)S(1)}, u32[]{:S(2)}, u32[]{:S(2)}) collective-permute-start(f32[8,512]{1,0:T(8,128)S(1)} %get-tuple-element.27), channel_id=1, source_target_pairs={{0,4},{4,0},{8,12},{12,8},{16,20},{20,16},{24,28},{28,24},{32,36},... | collective-permute-start | bytes 49160 | tf_op jit(solution)/shard_map/ppermute | solution.py:522
  3.6 4.3 %collective-permute-start.1 = (f32[8,512]{1,0:T(8,128)S(1)}, f32[8,512]{1,0:T(8,128)S(1)}, u32[]{:S(2)}, u32[]{:S(2)}) collective-permute-start(f32[8,512]{1,0:T(8,128)S(1)} %get-tuple-element.28), channel_id=1, source_target_pairs={{0,60},{4,8},{8,4},{12,16},{16,12},{20,24},{24,20},{28,32},{32,28}... | collective-permute-start | bytes 49160 | tf_op jit(solution)/shard_map/ppermute | solution.py:521
  7.9 1.8 %prepare.1 = (f32[2048,128]{1,0:T(8,128)S(1)}, f32[128,128]{1,0:T(8,128)S(1)}, bf16[256,128]{1,0:T(8,128)(2,1)S(1)}) custom-call(s32[1,1,2]{2,1,0:T(1,128)S(1)} %copy-done.8, f32[512,512]{1,0:T(8,128)S(1)} %bitcast.12, s32[2,1,1,512]{3,2,1,0:T(1,128)S(1)} %copy-done.3, s32[2,1,1,512]{3,2,1,0:T(1,128)S(1)} %copy-done.4, f32[2,1,1,512]{3,2,1,0:T(1,128)S(1)} %copy-done.5, ...), custom_call_target="tpu_custom_call" | custom-call | tf_op jit(solution)/shard_map/prepare/pallas_call | solution.py:523
  9.8 1.2 inside.2.levels_in
  11.0 2.1 %first.1 = (f32[2176,128]{1,0:T(8,128)S(1)}, f32[12288,128]{1,0:T(8,128)S(1)}) custom-call(f32[12288,128]{1,0:T(8,128)S(1)} %inside.2.levels_in, f32[2048,128]{1,0:T(8,128)S(1)} %get-tuple-element.25.state, f32[8,512]{1,0:T(8,128)S(1)} %collective-permute-done.near, f32[8,512]{1,0:T(8,128)S(1)} %collective-permute-done.1.far, ...), custom_call_target="tpu_custom_call", output_to_operand_aliasing={{1}: (0, {})} | custom-call | tf_op jit(solution)/shard_map/first/pallas_call | solution.py:533
  13.1 39.7 %all_to_all.30 = f32[16,136,128]{2,1,0:T(8,128)S(1)} all-to-all(f32[16,136,128]{2,1,0:T(8,128)S(1)} %bitcast.10), channel_id=1, replica_groups=mesh['mem'=4,'hor'=16,'zh'=2,'core'=2] {'mem','zh','core'}, dimensions={0} | all-to-all | bytes 2228224 | tf_op jit(solution)/shard_map/all_to_all | solution.py:511
  52.8 1.7 gram.1
  54.6 1.6 collective-permute-done.2
  56.2 13.4 %all_to_all.31.got = f32[8,72,128]{2,1,0:T(8,128)S(1)} all-to-all(f32[8,72,128]{2,1,0:T(8,128)S(1)} %add.6), channel_id=1, replica_groups=mesh['mem'=4,'hor'=16,'zh'=2,'core'=2] {'mem','zh'}, dimensions={0} | all-to-all | bytes 589824 | tf_op jit(solution)/shard_map/all_to_all | solution.py:511
  69.5 2.9 %root.2 = f32[8,72,128]{2,1,0:T(8,128)S(1)} custom-call(f32[8,72,128]{2,1,0:T(8,128)S(1)} %all_to_all.31.got), custom_call_target="tpu_custom_call" | custom-call | tf_op jit(solution)/shard_map/root/pallas_call | solution.py:554
  72.5 13.2 %all_to_all.32.roots = f32[8,72,128]{2,1,0:T(8,128)S(1)} all-to-all(f32[8,72,128]{2,1,0:T(8,128)S(1)} %root.2), channel_id=1, replica_groups=mesh['mem'=4,'hor'=16,'zh'=2,'core'=2] {'mem','zh'}, dimensions={0} | all-to-all | bytes 589824 | tf_op jit(solution)/shard_map/all_to_all | solution.py:511
  85.7 2.6 %collective-permute-start.3 = (f32[8,72,128]{2,1,0:T(8,128)S(1)}, f32[8,72,128]{2,1,0:T(8,128)S(1)}, u32[]{:S(2)}, u32[]{:S(2)}) collective-permute-start(f32[8,72,128]{2,1,0:T(8,128)S(1)} %all_to_all.32.roots), channel_id=1, source_target_pairs={{0,1},{1,0},{2,3},{3,2},{4,5},{5,4},{6,7},{7,6},{8,9},{9,8},{10,11... | collective-permute-start | bytes 884744 | tf_op jit(solution)/shard_map/ppermute | solution.py:507
  88.3 1.0 apply.2
  89.3 0.2 collective-permute-done.3.roots
  89.5 1.0 apply.3
  90.5 1.5 collective-permute-start.4
  92.0 2.9 %collective-permute-start.5 = (f32[512,128]{1,0:T(8,128)S(1)}, f32[512,128]{1,0:T(8,128)S(1)}, u32[]{:S(2)}, u32[]{:S(2)}) collective-permute-start(f32[512,128]{1,0:T(8,128)S(1)} %get-tuple-element.38), channel_id=1, source_target_pairs={{0,1},{1,0},{64,65},{65,64},{128,129},{129,128},{192,193},{193,192... | collective-permute-start | bytes 786440 | tf_op jit(solution)/shard_map/ppermute | solution.py:575
  94.9 1.2 inside.3.levels_in
  96.2 0.3 collective-permute-done.4.outer
  96.4 2.3 %forecast.1 = (f32[12288,128]{1,0:T(8,128)S(1)}, f32[8,72,128]{2,1,0:T(8,128)S(1)}, f32[8,72,128]{2,1,0:T(8,128)S(1)}) custom-call(f32[12288,128]{1,0:T(8,128)S(1)} %inside.3.levels_in, s32[16,128]{1,0:T(8,128)S(1)} %get-tuple-element.36.table_in, f32[2048,128]{1,0:T(8,128)S(1)} %get-tuple-element.35.state, ...), custom_call_target="tpu_custom_call", output_to_operand_aliasing={{0}: (0, {})} | custom-call | tf_op jit(solution)/shard_map/forecast/pallas_call | solution.py:576
  98.8 4.4 %collective-permute-start.6 = (f32[8,72,128]{2,1,0:T(8,128)S(1)}, f32[8,72,128]{2,1,0:T(8,128)S(1)}, u32[]{:S(2)}, u32[]{:S(2)}) collective-permute-start(f32[8,72,128]{2,1,0:T(8,128)S(1)} %get-tuple-element.41), channel_id=1, source_target_pairs={{0,1},{1,0},{2,3},{3,2},{4,5},{5,4},{6,7},{7,6},{8,9},{9,8},{10,11... | collective-permute-start | bytes 884744 | tf_op jit(solution)/shard_map/ppermute | solution.py:507
  103.1 1.2 collective-permute-done.6
  104.4 12.9 %all_to_all.33.got = f32[8,72,128]{2,1,0:T(8,128)S(1)} all-to-all(f32[8,72,128]{2,1,0:T(8,128)S(1)} %add.7), channel_id=1, replica_groups=mesh['mem'=4,'hor'=16,'zh'=2,'core'=2] {'mem','zh'}, dimensions={0} | all-to-all | bytes 589824 | tf_op jit(solution)/shard_map/all_to_all | solution.py:511
  117.3 2.9 %root.3 = f32[8,72,128]{2,1,0:T(8,128)S(1)} custom-call(f32[8,72,128]{2,1,0:T(8,128)S(1)} %all_to_all.33.got), custom_call_target="tpu_custom_call" | custom-call | tf_op jit(solution)/shard_map/root/pallas_call | solution.py:554
  120.3 13.2 %all_to_all.34.roots = f32[8,72,128]{2,1,0:T(8,128)S(1)} all-to-all(f32[8,72,128]{2,1,0:T(8,128)S(1)} %root.3), channel_id=1, replica_groups=mesh['mem'=4,'hor'=16,'zh'=2,'core'=2] {'mem','zh'}, dimensions={0} | all-to-all | bytes 589824 | tf_op jit(solution)/shard_map/all_to_all | solution.py:511
  133.4 2.9 %collective-permute-start.7 = (f32[8,72,128]{2,1,0:T(8,128)S(1)}, f32[8,72,128]{2,1,0:T(8,128)S(1)}, u32[]{:S(2)}, u32[]{:S(2)}) collective-permute-start(f32[8,72,128]{2,1,0:T(8,128)S(1)} %all_to_all.34.roots), channel_id=1, source_target_pairs={{0,1},{1,0},{2,3},{3,2},{4,5},{5,4},{6,7},{7,6},{8,9},{9,8},{10,11... | collective-permute-start | bytes 884744 | tf_op jit(solution)/shard_map/ppermute | solution.py:507
  136.4 1.3 analyse.2
  137.7 0.7 analyse.3
  138.4 31.0 %all_to_all.35 = f32[16,128,128]{2,1,0:T(8,128)S(1)} all-to-all(f32[16,128,128]{2,1,0:T(8,128)S(1)} %bitcast.9), channel_id=1, replica_groups=mesh['mem'=4,'hor'=16,'zh'=2,'core'=2] {'mem','zh','core'}, dimensions={0} | all-to-all | bytes 2097152 | tf_op jit(solution)/shard_map/all_to_all | solution.py:511
  169.4 1.3 place.1
  (24 shorter events, 0.2 us)
Async XLA Ops:
  0.0 1.2 copy-start
  1.2 6.6 %copy-start.1 = (f32[8,2,32,512]{3,2,1,0:T(8,128)S(1)}, f32[8,2,32,512]{3,2,1,0:T(8,128)}, u32[]{:S(2)}) copy-start(f32[8,2,32,512]{3,2,1,0:T(8,128)} %param.8) | copy-start | bytes 3145732
  1.2 6.6 %copy-start.2 = (f32[32,32]{1,0:T(8,128)S(1)}, f32[32,32]{1,0:T(8,128)}, u32[]{:S(2)}) copy-start(f32[32,32]{1,0:T(8,128)} %coupling.1) | copy-start | bytes 12292
  1.2 6.6 %copy-start.3 = (s32[2,1,1,512]{3,2,1,0:T(1,128)S(1)}, s32[2,1,1,512]{3,2,1,0:T(1,128)}, u32[]{:S(2)}) copy-start(s32[2,1,1,512]{3,2,1,0:T(1,128)} %column.1) | copy-start | bytes 12292
  1.2 6.6 %copy-start.4 = (s32[2,1,1,512]{3,2,1,0:T(1,128)S(1)}, s32[2,1,1,512]{3,2,1,0:T(1,128)}, u32[]{:S(2)}) copy-start(s32[2,1,1,512]{3,2,1,0:T(1,128)} %level.1) | copy-start | bytes 12292
  1.2 6.6 %copy-start.5 = (f32[2,1,1,512]{3,2,1,0:T(1,128)S(1)}, f32[2,1,1,512]{3,2,1,0:T(1,128)}, u32[]{:S(2)}) copy-start(f32[2,1,1,512]{3,2,1,0:T(1,128)} %value.1) | copy-start | bytes 12292
  1.2 6.6 %copy-start.6 = (f32[2,1,1,512]{3,2,1,0:T(1,128)S(1)}, f32[2,1,1,512]{3,2,1,0:T(1,128)}, u32[]{:S(2)}) copy-start(f32[2,1,1,512]{3,2,1,0:T(1,128)} %error.1) | copy-start | bytes 12292
  1.3 6.6 %copy-start.7 = (s32[2,1,1,512]{3,2,1,0:T(1,128)S(1)}, s32[2,1,1,512]{3,2,1,0:T(1,128)}, u32[]{:S(2)}) copy-start(s32[2,1,1,512]{3,2,1,0:T(1,128)} %live.1) | copy-start | bytes 12292
  1.3 6.6 %copy-start.8 = (s32[1,1,2]{2,1,0:T(1,128)S(1)}, s32[1,1,2]{2,1,0:T(1,128)}, u32[]{:S(2)}) copy-start(s32[1,1,2]{2,1,0:T(1,128)} %partner.1) | copy-start | bytes 28
  1.5 9.5 %collective-permute-start = (f32[8,512]{1,0:T(8,128)S(1)}, f32[8,512]{1,0:T(8,128)S(1)}, u32[]{:S(2)}, u32[]{:S(2)}) collective-permute-start(f32[8,512]{1,0:T(8,128)S(1)} %get-tuple-element.27), channel_id=1, source_target_pairs={{0,4},{4,0},{8,12},{12,8},{16,20},{20,16},{24,28},{28,24},{32,36},... | collective-permute-start | bytes 49160 | tf_op jit(solution)/shard_map/ppermute | solution.py:522
  3.6 7.4 %collective-permute-start.1 = (f32[8,512]{1,0:T(8,128)S(1)}, f32[8,512]{1,0:T(8,128)S(1)}, u32[]{:S(2)}, u32[]{:S(2)}) collective-permute-start(f32[8,512]{1,0:T(8,128)S(1)} %get-tuple-element.28), channel_id=1, source_target_pairs={{0,60},{4,8},{8,4},{12,16},{16,12},{20,24},{24,20},{28,32},{32,28}... | collective-permute-start | bytes 49160 | tf_op jit(solution)/shard_map/ppermute | solution.py:521
  54.5 1.7 collective-permute-start.2
  85.7 3.8 %collective-permute-start.3 = (f32[8,72,128]{2,1,0:T(8,128)S(1)}, f32[8,72,128]{2,1,0:T(8,128)S(1)}, u32[]{:S(2)}, u32[]{:S(2)}) collective-permute-start(f32[8,72,128]{2,1,0:T(8,128)S(1)} %all_to_all.32.roots), channel_id=1, source_target_pairs={{0,1},{1,0},{2,3},{3,2},{4,5},{5,4},{6,7},{7,6},{8,9},{9,8},{10,11... | collective-permute-start | bytes 884744 | tf_op jit(solution)/shard_map/ppermute | solution.py:507
  90.5 5.9 %collective-permute-start.4 = (f32[512,128]{1,0:T(8,128)S(1)}, f32[512,128]{1,0:T(8,128)S(1)}, u32[]{:S(2)}, u32[]{:S(2)}) collective-permute-start(f32[512,128]{1,0:T(8,128)S(1)} %get-tuple-element.37), channel_id=1, source_target_pairs={{1,64},{64,1},{65,128},{128,65},{129,192},{192,129},{193,2},{2,193... | collective-permute-start | bytes 786440 | tf_op jit(solution)/shard_map/ppermute | solution.py:574
  92.0 4.4 %collective-permute-start.5 = (f32[512,128]{1,0:T(8,128)S(1)}, f32[512,128]{1,0:T(8,128)S(1)}, u32[]{:S(2)}, u32[]{:S(2)}) collective-permute-start(f32[512,128]{1,0:T(8,128)S(1)} %get-tuple-element.38), channel_id=1, source_target_pairs={{0,1},{1,0},{64,65},{65,64},{128,129},{129,128},{192,193},{193,192... | collective-permute-start | bytes 786440 | tf_op jit(solution)/shard_map/ppermute | solution.py:575
  98.8 5.6 %collective-permute-start.6 = (f32[8,72,128]{2,1,0:T(8,128)S(1)}, f32[8,72,128]{2,1,0:T(8,128)S(1)}, u32[]{:S(2)}, u32[]{:S(2)}) collective-permute-start(f32[8,72,128]{2,1,0:T(8,128)S(1)} %get-tuple-element.41), channel_id=1, source_target_pairs={{0,1},{1,0},{2,3},{3,2},{4,5},{5,4},{6,7},{7,6},{8,9},{9,8},{10,11... | collective-permute-start | bytes 884744 | tf_op jit(solution)/shard_map/ppermute | solution.py:507
  133.4 4.3 %collective-permute-start.7 = (f32[8,72,128]{2,1,0:T(8,128)S(1)}, f32[8,72,128]{2,1,0:T(8,128)S(1)}, u32[]{:S(2)}, u32[]{:S(2)}) collective-permute-start(f32[8,72,128]{2,1,0:T(8,128)S(1)} %all_to_all.34.roots), channel_id=1, source_target_pairs={{0,1},{1,0},{2,3},{3,2},{4,5},{5,4},{6,7},{7,6},{8,9},{9,8},{10,11... | collective-permute-start | bytes 884744 | tf_op jit(solution)/shard_map/ppermute | solution.py:507
